TPU v7x, 256 devices: a whole 4x4x8 slice. The times are simulated.
256 devices in a mesh: band: 16 (over z, y_lo), col: 16 (over x, y_hi, core).
Axes of the slice: x: 4, y: 4 (y_hi: 2, y_lo: 2; y = y_hi * 2 + y_lo), z: 8, core: 2. Of those that a mesh axis runs over, the one named last changes fastest.
Arguments:
- valence_wave: bfloat16 [16, 96, 9216], P('band', 'col'), may hold values from -6 to 6
- conduction_wave: bfloat16 [16, 96, 9216], P('band', 'col'), may hold values from -6 to 6
- valence_index: int32 [16], replicated, may hold values from 0 to 4095
- occupied_energy: float32 [4096], replicated, may hold values from -6 to -0.5
- conduction_energy: float32 [16], replicated, may hold values from 0.5 to 8
- frequency: float32 [4], replicated, may hold values from 0.5 to 16
- gvec_cell: int32 [32768], P('col'), may hold values from 0 to 55295, as said below
- block_cell: int32 [16], P('col'), may hold values from 0 to 55295, as said below
Outputs:
- chi: float32 [32768, 128], P(('col', 'band'))
Inputs may be any that keep to these rules, and one draw needn't show every extreme that they name: `gvec_cell`: for rows j of owner k (k * 2048 <= j < (k + 1) * 2048) the entry is (kx 6 + ky - k * 6) * 96 + kz for the G vector's grid point (kx, ky, kz), whose ky lies in [k * 6, (k + 1) * 6); no point appears twice among the rows and block columns of one owner. `block_cell`: block column m has owner k = m // 1 and is encoded as for gvec_cell; its points differ from every row point of the same owner.
All inputs are finite; a program needn't handle non-finite values.
Results may differ from a plain program's by a relative error of at most 0.018.
Values may be sent and summed in bfloat16 or wider, within the bound.
No kernel may reach another device: no remote copies, remote signals or barrier semaphores. Data moves between devices by JAX's collectives and lax.ppermute only.
A program may use at most 128 MiB of HBM per device.

v0:
```python
import math

import jax
import jax.numpy as jnp
from jax import lax
from jax.sharding import PartitionSpec as P

GY = 96


def joined_along(pieces, dim):
    dims = list(pieces.shape[1:])
    dims[dim] *= pieces.shape[0]
    return jnp.moveaxis(pieces, 0, dim).reshape(dims)


def copy_for_each(x, axis):
    devices = lax.axis_size(axis)
    return lax.all_to_all(jnp.broadcast_to(x[None], (devices, *x.shape)), axis, 0, 0, tiled=True)


def collect(x, axis, dim):
    return joined_along(copy_for_each(x, axis), dim)


def cut_along(x, dim, devices):
    dims = x.shape
    pieces = x.reshape(*dims[:dim], devices, dims[dim] // devices, *dims[dim + 1 :])
    return jnp.moveaxis(pieces, dim, 0)


def sent_and_summed(x, axis, dim):
    pieces = cut_along(x, dim, lax.axis_size(axis))
    arrived = lax.all_to_all(pieces, axis, split_axis=0, concat_axis=0, tiled=True)
    return arrived.astype(jnp.float32).sum(axis=0)


def dft_tables(length, factor, out_type):
    indices = jnp.arange(length, dtype=jnp.int32)
    phases = indices[:, None] * indices[None, :] % length
    angles = phases.astype(jnp.float32) * (2.0 * math.pi / length)
    return (
        (jnp.cos(angles) * factor).astype(out_type),
        (-jnp.sin(angles) * factor).astype(out_type),
    )


def weighted_columns(block, weights):
    columns = block.astype(jnp.float32)
    stacked = jnp.stack([columns, jnp.stack([-columns[1], columns[0]])])
    scaled = stacked[None] * weights[:, None, None, :, None]
    scaled = scaled.transpose(2, 3, 0, 1, 4).astype(jnp.bfloat16)
    return scaled.reshape(2, block.shape[1], -1)


def pair_weights(
    pair_ids, valence_energy, conduction_energy, frequency, per_band, pairs_dev, norm_factor
):
    band_of = pair_ids // pairs_dev
    within = pair_ids % pairs_dev
    valence_of = within // per_band
    conduction_of = band_of * per_band + within % per_band
    valence_range = jnp.arange(valence_energy.shape[0], dtype=jnp.int32)
    conduction_range = jnp.arange(conduction_energy.shape[0], dtype=jnp.int32)
    valence_pick = jnp.sum(
        jnp.where(valence_of[:, None] == valence_range[None, :], valence_energy[None, :], 0.0),
        axis=1,
    )
    conduction_pick = jnp.sum(
        jnp.where(
            conduction_of[:, None] == conduction_range[None, :], conduction_energy[None, :], 0.0
        ),
        axis=1,
    )
    gap = conduction_pick - valence_pick
    freq_column = frequency[:, None]
    return (
        -4.0
        * gap[None, :]
        / (gap[None, :] * gap[None, :] + freq_column * freq_column)
        * norm_factor
    )


def per_device(
    valence_wave,
    conduction_wave,
    valence_index,
    occupied_energy,
    conduction_energy,
    frequency,
    gvec_cell,
    block_cell,
):
    local_valence, slab_x, plane_size = valence_wave.shape
    per_band = conduction_wave.shape[0]
    band_count = lax.axis_size("band")
    col_count = lax.axis_size("col")
    grid_x = slab_x * col_count
    grid_y = GY
    grid_z = plane_size // grid_y
    total_valence = local_valence * band_count
    pairs_dev = total_valence * per_band
    total_conduction = conduction_energy.shape[0]
    norm_factor = 1.0 / math.sqrt(total_valence * total_conduction)
    high = lax.Precision.HIGH
    z_cosine, z_sine = dft_tables(grid_z, 1.0, jnp.float32)
    y_cosine, y_sine = dft_tables(grid_y, 1.0 / math.sqrt(grid_y * grid_z), jnp.float32)
    x_cosine, x_sine = dft_tables(grid_x, 1.0 / math.sqrt(grid_x), jnp.bfloat16)
    x_table = jnp.stack([jnp.stack([x_cosine, -x_sine]), jnp.stack([x_sine, x_cosine])])
    conduction_float = conduction_wave.astype(jnp.float32)
    products = (
        collect(valence_wave, "band", 0).astype(jnp.float32)[:, None] * conduction_float[None]
    )
    products = products.reshape(-1, slab_x, grid_y, grid_z)
    z_real = jnp.einsum("kz,pxyz->pxyk", z_cosine, products, precision=high)
    z_imag = jnp.einsum("kz,pxyz->pxyk", z_sine, products, precision=high)
    y_real = jnp.einsum("jy,pxyk->pxjk", y_cosine, z_real, precision=high) - jnp.einsum(
        "jy,pxyk->pxjk", y_sine, z_imag, precision=high
    )
    y_imag = jnp.einsum("jy,pxyk->pxjk", y_sine, z_real, precision=high) + jnp.einsum(
        "jy,pxyk->pxjk", y_cosine, z_imag, precision=high
    )
    planes = jnp.stack([y_real, y_imag]).astype(jnp.bfloat16)
    exchanged = lax.all_to_all(planes, "col", split_axis=3, concat_axis=2, tiled=True)
    items = exchanged.shape[1]
    flat = exchanged.reshape(2, items, grid_x, -1)
    density = jnp.einsum(
        "orkx,rpxf->opkf", x_table, flat, preferred_element_type=jnp.float32
    ).astype(jnp.bfloat16)
    density = density.reshape(2, items, -1)
    row_density = jnp.take(density, gvec_cell, axis=2)
    block_density = jnp.take(density, block_cell, axis=2)
    block_all = collect(block_density, "col", 2)
    occupied_range = jnp.arange(occupied_energy.shape[0], dtype=jnp.int32)
    valence_energy = jnp.sum(
        jnp.where(valence_index[:, None] == occupied_range[None, :], occupied_energy[None, :], 0.0),
        axis=1,
    )
    pair_ids = lax.axis_index("band") * pairs_dev + jnp.arange(pairs_dev, dtype=jnp.int32)
    weights = pair_weights(
        pair_ids, valence_energy, conduction_energy, frequency, per_band, pairs_dev, norm_factor
    )
    right_side = weighted_columns(block_all, weights)
    return sent_and_summed(
        jnp.einsum(
            "rpg,rpc->gc", row_density, right_side, preferred_element_type=jnp.float32
        ).astype(jnp.bfloat16),
        "band",
        0,
    )


def solution(mesh):
    return jax.shard_map(
        per_device,
        mesh=mesh,
        in_specs=(
            P("band", "col", None),
            P("band", "col", None),
            P(),
            P(),
            P(),
            P(),
            P("col"),
            P("col"),
        ),
        out_specs=P(("col", "band"), None),
        check_vma=False,
    )
```

profile of v0, /device:TPU:6, one launch (start us, length us, event | category | flops | bytes accessed | tf_op | source)
XLA Modules:
  0.0 309.5 jit_solution(16333228598212090025)
XLA Ops:
  0.0 2.6 broadcast_in_dim.93
  2.6 9.6 %all-to-all-start = ((bf16[16,1,6,9216]{3,2,1,0:T(8,128)(2,1)}), bf16[16,1,6,9216]{3,2,1,0:T(8,128)(2,1)S(1)}, u32[]{:S(2)}, u32[]{:S(2)}) async-start(bf16[16,1,6,9216]{3,2,1,0:T(8,128)(2,1)} %broadcast_in_dim.93), calls=%async_computation | async-start | bytes 4718592 | tf_op jit(solution)/shard_map/all_to_all | solution.py:19
  12.2 55.8 %all-to-all-done = bf16[16,1,6,9216]{3,2,1,0:T(8,128)(2,1)S(1)} async-done(((bf16[16,1,6,9216]{3,2,1,0:T(8,128)(2,1)}), bf16[16,1,6,9216]{3,2,1,0:T(8,128)(2,1)S(1)}, u32[]{:S(2)}, u32[]{:S(2)}) %all-to-all-start) | async-done | bytes 1769504 | tf_op jit(solution)/shard_map/all_to_all | solution.py:19
  68.0 2.6 convert_multiply_fusion
  70.6 5.9 %reshape.293 = f32[16,6,96,96]{3,2,1,0:T(8,128)} reshape(f32[16,1,6,9216]{3,2,1,0:T(8,128)} %convert_multiply_fusion) | data formatting | bytes 7077888 | tf_op jit(solution)/shard_map/reshape | solution.py:115
  76.5 7.9 %fusion.18 = f32[16,6,96,96]{2,3,1,0:T(8,128)S(1)} fusion(f32[16,6,96,96]{3,2,1,0:T(8,128)} %reshape.293), kind=kOutput, calls=%fused_computation.33 | convolution fusion | flops 509690880 | bytes 7077888 | tf_op jit(solution)/shard_map/kz,pxyz->pxyk/dot_general | solution.py:116
  84.4 5.4 %fusion.16 = f32[16,6,96,96]{2,3,1,0:T(8,128)S(1)} fusion(f32[16,6,96,96]{3,2,1,0:T(8,128)S(1)} %copy-done), kind=kOutput, calls=%fused_computation.31 | convolution fusion | flops 509700096 | bytes 7077888 | tf_op jit(solution)/shard_map/kz,pxyz->pxyk/dot_general | solution.py:117
  89.8 2.3 fusion.23
  92.1 2.2 fusion.21
  94.3 2.9 fusion.7
  97.2 2.7 fusion.6
  100.0 3.2 %pad_maximum_fusion = bf16[2,16,6,96,96]{3,4,2,1,0:T(8,128)(2,1)} fusion(bf16[1,16,6,96,96]{3,4,2,1,0:T(8,128)(2,1)S(1)} %fusion.7, bf16[1,16,6,96,96]{3,4,2,1,0:T(8,128)(2,1)S(1)} %fusion.6), kind=kLoop, calls=%fused_computation.2 | loop fusion | flops 1769472 | bytes 7077888 | tf_op jit(solution)/shard_map/stack | solution.py:124
  103.2 9.2 %copy.84 = bf16[2,16,6,96,96]{4,1,2,0,3:T(8,128)(2,1)} copy(bf16[2,16,6,96,96]{3,4,2,1,0:T(8,128)(2,1)} %pad_maximum_fusion) | data formatting | bytes 7077888 | tf_op jit(solution)/shard_map/stack | solution.py:124
  112.4 7.3 %all-to-all-start.1 = ((bf16[2,16,6,96,96]{4,1,2,0,3:T(8,128)(2,1)}), bf16[2,16,6,96,96]{4,1,2,0,3:T(8,128)(2,1)}, u32[]{:S(2)}, u32[]{:S(2)}) async-start(bf16[2,16,6,96,96]{4,1,2,0,3:T(8,128)(2,1)} %copy.84), calls=%async_computation.1 | async-start | bytes 9437184 | tf_op jit(solution)/shard_map/all_to_all | solution.py:125
  120.4 0.2 select_reduce_fusion.2
  120.6 0.2 select_reduce_fusion
  120.8 0.2 select_reduce_fusion.1
  121.3 0.2 fusion.62
  121.6 0.2 multiply_convert_fusion
  121.9 63.9 %all-to-all-done.1 = bf16[2,16,6,96,96]{4,1,2,0,3:T(8,128)(2,1)} async-done(((bf16[2,16,6,96,96]{4,1,2,0,3:T(8,128)(2,1)}), bf16[2,16,6,96,96]{4,1,2,0,3:T(8,128)(2,1)}, u32[]{:S(2)}, u32[]{:S(2)}) %all-to-all-start.1) | async-done | bytes 3538976 | tf_op jit(solution)/shard_map/all_to_all | solution.py:125
  185.8 8.2 %copy.102 = bf16[2,16,16,6,6,96]{5,4,3,2,0,1:T(8,128)(2,1)} copy(bf16[2,16,16,6,6,96]{5,1,3,0,4,2:T(8,128)(2,1)} %bitcast.18) | data formatting | bytes 7077888 | tf_op jit(solution)/shard_map/reshape | solution.py:127
  194.0 9.6 %reshape.287 = bf16[2,16,96,576,1]{3,2,0,1,4:T(8,128)(2,1)} reshape(bf16[2,16,16,6,6,96]{5,4,3,2,0,1:T(8,128)(2,1)} %copy.102) | data formatting | bytes 7077888 | tf_op jit(solution)/shard_map/reshape | solution.py:127
  203.7 5.3 %fusion = bf16[2,16,96,576]{3,2,0,1:T(8,128)(2,1)} fusion(bf16[2,16,96,576,1]{3,2,0,1,4:T(8,128)(2,1)} %reshape.287, bf16[1,2,96,96]{3,2,1,0:T(8,128)(2,1)S(1)} %get-tuple-element.17, bf16[1,2,96,96]{3,2,1,0:T(8,128)(2,1)S(1)} %get-tuple-element.16), kind=kOutput, calls=%fused_computation.6 | convolution fusion | flops 681394176 | bytes 7151616 | tf_op jit(solution)/shard_map/orkx,rpxf->opkf/dot_general | solution.py:128
  209.0 44.3 %copy.105 = bf16[2,16,96,576]{1,0,3,2:T(2,128)(2,1)} copy(bf16[2,16,96,576]{3,2,0,1:T(8,128)(2,1)} %fusion) | data formatting | bytes 7077888 | tf_op jit(solution)/shard_map/reshape | solution.py:131
  253.2 16.1 %gather_fusion = bf16[2048,2,16]{2,1,0:T(2,128)(2,1)S(1)} fusion(bf16[2,16,55296]{1,0,2:T(2,128)(2,1)} %bitcast.91, s32[2048]{0:T(1024)S(1)} %fusion.65), kind=kCustom, calls=%fused_computation | custom fusion | bytes 270336 | tf_op jit(solution)/shard_map/jit(_take)/gather | solution.py:132
  269.3 0.7 fusion.66
  270.0 0.6 broadcast_in_dim.99
  270.6 8.5 %all-to-all-start.2 = ((bf16[16,2,16,1]{2,1,3,0:T(2,128)(2,1)}), bf16[16,2,16,1]{2,1,3,0:T(2,128)(2,1)S(1)}, u32[]{:S(2)}, u32[]{:S(2)}) async-start(bf16[16,2,16,1]{2,1,3,0:T(2,128)(2,1)} %broadcast_in_dim.99), calls=%async_computation.2 | async-start | bytes 16384 | tf_op jit(solution)/shard_map/all_to_all | solution.py:19
  279.1 7.4 %fusion.9 = bf16[2,16,2048]{1,0,2:T(2,128)(2,1)S(1)} fusion(bf16[2048,2,16]{2,1,0:T(2,128)(2,1)S(1)} %gather_fusion, pred[2048]{0:T(1024)(128)(4,1)S(1)} %compare_and_fusion), kind=kLoop, calls=%fused_computation.16 | loop fusion | flops 65536 | bytes 264192 | tf_op jit(solution)/shard_map/jit(_take)/select_n | solution.py:132
  286.9 0.4 fusion.5
  287.3 21.5 %all_to_all.30 = bf16[16,128,128]{2,1,0:T(8,128)(2,1)S(1)} all-to-all(bf16[16,128,128]{2,1,0:T(8,128)(2,1)S(1)} %bitcast.93), channel_id=1, replica_groups=mesh['band'=16,'col'=16] {'band'}, dimensions={0} | all-to-all | bytes 1048576 | tf_op jit(solution)/shard_map/all_to_all | solution.py:34
  308.8 0.7 convert_reduce_fusion
  (33 shorter events, 0.8 us)
Async XLA Ops:
  0.0 12.2 %copy-start.1 = (bf16[1,6,9216]{2,1,0:T(8,128)(2,1)S(1)}, bf16[1,6,9216]{2,1,0:T(8,128)(2,1)}, u32[]{:S(2)}) copy-start(bf16[1,6,9216]{2,1,0:T(8,128)(2,1)} %param.9) | copy-start | bytes 331780
  2.6 65.4 %all-to-all-start = ((bf16[16,1,6,9216]{3,2,1,0:T(8,128)(2,1)}), bf16[16,1,6,9216]{3,2,1,0:T(8,128)(2,1)S(1)}, u32[]{:S(2)}, u32[]{:S(2)}) async-start(bf16[16,1,6,9216]{3,2,1,0:T(8,128)(2,1)} %broadcast_in_dim.93), calls=%async_computation | async-start | bytes 4718592 | tf_op jit(solution)/shard_map/all_to_all | solution.py:19
  76.5 7.9 %copy-start = (f32[16,6,96,96]{3,2,1,0:T(8,128)S(1)}, f32[16,6,96,96]{3,2,1,0:T(8,128)}, u32[]{:S(2)}) copy-start(f32[16,6,96,96]{3,2,1,0:T(8,128)} %reshape.293) | copy-start | bytes 10616836
  112.4 8.0 %copy-start.5 = (f32[4]{0:T(128)S(1)}, f32[4]{0:T(128)}, u32[]{:S(2)}) copy-start(f32[4]{0:T(128)} %param.13) | copy-start | bytes 52
  112.4 8.0 %copy-start.6 = (f32[16]{0:T(128)S(1)}, f32[16]{0:T(128)}, u32[]{:S(2)}) copy-start(f32[16]{0:T(128)} %param.12) | copy-start | bytes 196
  112.4 8.2 %copy-start.3 = (f32[4096]{0:T(1024)S(1)}, f32[4096]{0:T(1024)}, u32[]{:S(2)}) copy-start(f32[4096]{0:T(1024)} %param.11) | copy-start | bytes 49156
  112.4 8.2 %copy-start.4 = (s32[16]{0:T(128)S(1)}, s32[16]{0:T(128)}, u32[]{:S(2)}) copy-start(s32[16]{0:T(128)} %param.10) | copy-start | bytes 196
  112.4 9.4 %copy-start.2 = (s32[2048]{0:T(1024)S(1)}, s32[2048]{0:T(1024)}, u32[]{:S(2)}) copy-start(s32[2048]{0:T(1024)} %param.14) | copy-start | bytes 24580
  112.4 73.4 %all-to-all-start.1 = ((bf16[2,16,6,96,96]{4,1,2,0,3:T(8,128)(2,1)}), bf16[2,16,6,96,96]{4,1,2,0,3:T(8,128)(2,1)}, u32[]{:S(2)}, u32[]{:S(2)}) async-start(bf16[2,16,6,96,96]{4,1,2,0,3:T(8,128)(2,1)} %copy.84), calls=%async_computation.1 | async-start | bytes 9437184 | tf_op jit(solution)/shard_map/all_to_all | solution.py:125
  270.6 15.9 %all-to-all-start.2 = ((bf16[16,2,16,1]{2,1,3,0:T(2,128)(2,1)}), bf16[16,2,16,1]{2,1,3,0:T(2,128)(2,1)S(1)}, u32[]{:S(2)}, u32[]{:S(2)}) async-start(bf16[16,2,16,1]{2,1,3,0:T(2,128)(2,1)} %broadcast_in_dim.99), calls=%async_computation.2 | async-start | bytes 16384 | tf_op jit(solution)/shard_map/all_to_all | solution.py:19
where the time goes:
time: 313 us; the launch traced here: 309 us
  waiting for transfers between devices  120 us (38%)
  local copies, waits for them, and re-layouts  97.1 us (31%)
  matrix products  29.1 us (9%)
  starting transfers between devices  25.3 us (8%)
  blocking collectives  21.5 us (7%)
  other arithmetic  15.8 us (5%)
    all_to_all x1, waiting for transfers between devices, per_device(): lax.all_to_all(planes, 'col', split_axis=3, concat_axis=2, tiled=True)  63.9 us
    all_to_all x2, waiting for transfers between devices, copy_for_each(): lax.all_to_all(jnp.broadcast_to(x[None], (devices, *x.shape)), axis, 0, 0...  55.8 us
    reshape x1, local copies, waits for them, and re-layouts, per_device(): density = density.reshape(2, items, -1)  44.3 us
    all_to_all x1, blocking collectives, sent_and_summed(): lax.all_to_all(pieces, axis, split_axis=0, concat_axis=0, tiled=True)  21.5 us
    all_to_all x2, starting transfers between devices, copy_for_each(): lax.all_to_all(jnp.broadcast_to(x[None], (devices, *x.shape)), axis, 0, 0...  18 us
    reshape x2, local copies, waits for them, and re-layouts, per_device(): flat = exchanged.reshape(2, items, grid_x, -1)  17.8 us
    gather x1, local copies, waits for them, and re-layouts, per_device(): row_density = jnp.take(density, gvec_cell, axis=2)  16.1 us
    another operation x1, local copies, waits for them, and re-layouts, per_device(): planes = jnp.stack([y_real, y_imag]).astype(jnp.bfloat16)  9.18 us
  transfers between devices with their start and end apart: 3, of which 2 were waited for; matrix products, arithmetic and copies ran while one was open for 3% of the time, Pallas kernels for 0%

commit v1 on v0

v1 whole, which is shorter than its diff:
```python
import functools
import math

import jax
import jax.numpy as jnp
import ml_dtypes
import numpy as np
from jax import lax
from jax.experimental import pallas as pl
from jax.experimental.pallas import tpu as pltpu
from jax.sharding import Mesh
from jax.sharding import PartitionSpec as P

BF16 = jnp.bfloat16
F32 = jnp.float32

N = 96
SLABS = 16
X6 = 6
Y6 = 6
Y16 = 16
K7 = 7
FLAT = K7 * N
WIDE = 768
ITEMS = 4
CHUNKS = 2
C_OF_CHUNK = ((0, 1), (3, 2))
G_DEV = 2048
NBLOCK = 16
TILE = 512

BAND = ("z1", "z0", "yl")
VGROUP = ("z0", "yl")
COL = ("x", "yh", "co")


def unit(phase, period):
    angle = 2.0 * np.pi * (np.asarray(phase) % period) / period
    return np.cos(angle), -np.sin(angle)


def bf16(table):
    return np.asarray(table, np.float32).astype(ml_dtypes.bfloat16)


@functools.cache
def lane_table():
    y6, z = np.divmod(np.arange(Y6 * N), N)
    k7, kz = np.divmod(np.arange(FLAT), N)
    phase = 16 * y6[:, None] * k7[None, :] + z[:, None] * kz[None, :]
    cosine, sine = unit(phase, N)
    table = np.zeros((Y6 * N, 2 * WIDE))
    table[:, :FLAT] = cosine
    table[:, WIDE : WIDE + FLAT] = sine
    return bf16(table)


@functools.cache
def twiddle_table():
    k7 = np.arange(FLAT) // N
    cosine, sine = unit(np.arange(Y16)[:, None] * k7[None, :], N)
    table = np.zeros((2, Y16, WIDE), np.float32)
    table[0, :, :FLAT] = cosine / N
    table[1, :, :FLAT] = sine / N
    return table


@functools.cache
def row_table():
    table = np.zeros((SLABS, ITEMS, 2, X6, 2, ITEMS, X6, Y16))
    cosine, sine = unit(np.arange(SLABS)[:, None] * np.arange(Y16)[None, :], SLABS)
    for item in range(ITEMS):
        for x in range(X6):
            table[:, item, 0, x, 0, item, x] = cosine
            table[:, item, 0, x, 1, item, x] = -sine
            table[:, item, 1, x, 0, item, x] = sine
            table[:, item, 1, x, 1, item, x] = cosine
    return bf16(table.reshape(SLABS * ITEMS * 2 * X6, 2 * ITEMS * X6 * Y16))


@functools.cache
def x_table():
    table = np.zeros((2, ITEMS, N, SLABS, ITEMS, 2, X6))
    cosine, sine = unit(np.arange(N)[:, None] * np.arange(N)[None, :], N)
    cosine = (cosine * 0.5 / math.sqrt(N)).reshape(N, SLABS, X6)
    sine = (sine * 0.5 / math.sqrt(N)).reshape(N, SLABS, X6)
    for item in range(ITEMS):
        table[0, item, :, :, item, 0] = cosine
        table[0, item, :, :, item, 1] = -sine
        table[1, item, :, :, item, 0] = sine
        table[1, item, :, :, item, 1] = cosine
    return bf16(table.reshape(2 * ITEMS * N, SLABS * ITEMS * 2 * X6))


@functools.cache
def pair_table():
    valence, conduction, imaginary = [], [], []
    for band in range(16):
        z1, group = divmod(band, 4)
        for slots in C_OF_CHUNK:
            for kind in range(4):
                for item in range(ITEMS):
                    slot_v = 2 * (item // 2) + kind // 2
                    slot_c = slots[item % 2]
                    valence.append(z1 * 4 + (group ^ slot_v))
                    conduction.append((z1 - slot_c) % 4 * 4 + group)
                    imaginary.append(kind % 2)
    return np.array(valence), np.array(conduction), np.array(imaginary)


def plane_kernel(v_ref, c_ref, lane_ref, twiddle_ref, row_ref, out_ref, low_ref):
    rows = X6 * Y16
    twiddle_c = twiddle_ref[0][None]
    twiddle_s = twiddle_ref[1][None]
    for item in range(ITEMS):
        wave_c = c_ref[item % 2]
        pairs = jnp.concatenate(
            [v_ref[2 * (item // 2)] * wave_c, v_ref[2 * (item // 2) + 1] * wave_c], axis=0
        )
        moved = jnp.dot(pairs, lane_ref[...], preferred_element_type=F32)
        real = moved[:rows, :WIDE] - moved[rows:, WIDE:]
        imag = moved[:rows, WIDE:] + moved[rows:, :WIDE]
        real = real.reshape(X6, Y16, WIDE)
        imag = imag.reshape(X6, Y16, WIDE)
        turned_r = real * twiddle_c - imag * twiddle_s
        turned_i = real * twiddle_s + imag * twiddle_c
        low_ref[item * rows : (item + 1) * rows, :] = turned_r.reshape(rows, WIDE).astype(BF16)
        low_ref[(ITEMS + item) * rows : (ITEMS + item + 1) * rows, :] = turned_i.reshape(
            rows, WIDE
        ).astype(BF16)
    per_slab = ITEMS * 2 * X6
    for part in range(4):
        count = SLABS // 4
        planes = jnp.dot(
            row_ref[part * count * per_slab : (part + 1) * count * per_slab, :],
            low_ref[...],
            preferred_element_type=F32,
        )
        out_ref[part * count : (part + 1) * count] = planes.astype(BF16).reshape(
            count, per_slab, WIDE
        )


def planes_of(v, c, tables):
    per_slab = ITEMS * 2 * X6
    return pl.pallas_call(
        plane_kernel,
        out_shape=jax.ShapeDtypeStruct((SLABS, per_slab, WIDE), BF16),
        scratch_shapes=[pltpu.VMEM((2 * ITEMS * X6 * Y16, WIDE), BF16)],
        compiler_params=pltpu.CompilerParams(vmem_limit_bytes=40 << 20),
        cost_estimate=pl.CostEstimate(
            flops=2_700_000_000, bytes_accessed=6_000_000, transcendentals=0
        ),
        name="planes",
    )(v, c, *tables)


def pick_kernel(t_ref, x_ref, flat_ref, kx_ref, out_ref, density_ref):
    rows = SLABS * ITEMS * 2 * X6
    density_ref[...] = jnp.dot(
        x_ref[...], t_ref[...].reshape(rows, WIDE), preferred_element_type=F32
    ).astype(BF16)

    def body(step, carry):
        lanes = pl.ds(pl.multiple_of(step * TILE, TILE), TILE)
        spot = lax.broadcasted_iota(jnp.int32, (WIDE, TILE), 0)
        chosen = jnp.where(spot == flat_ref[:, lanes], 1.0, 0.0).astype(BF16)
        values = jnp.dot(density_ref[...], chosen, preferred_element_type=F32)
        kx = lax.broadcasted_iota(jnp.int32, (N, TILE), 0) == kx_ref[:, lanes]
        values = jnp.where(kx[None], values.reshape(2 * ITEMS, N, TILE), 0.0)
        out_ref[:, lanes] = values.sum(axis=1)
        return carry

    lax.fori_loop(0, 2 * G_DEV // TILE, body, 0)


def points_of(planes, table, flat, kx):
    return pl.pallas_call(
        pick_kernel,
        out_shape=jax.ShapeDtypeStruct((2 * ITEMS, 2 * G_DEV), F32),
        scratch_shapes=[pltpu.VMEM((2 * ITEMS * N, WIDE), BF16)],
        compiler_params=pltpu.CompilerParams(vmem_limit_bytes=40 << 20),
        cost_estimate=pl.CostEstimate(
            flops=5_700_000_000, bytes_accessed=3_000_000, transcendentals=0
        ),
        name="points",
    )(planes, table, flat, kx)


def split_kernel(own0_ref, own1_ref, far_ref, out_ref):
    for chunk, own_ref in enumerate((own0_ref, own1_ref)):
        own_r = own_ref[:ITEMS, :G_DEV]
        own_i = own_ref[ITEMS:, :G_DEV]
        far_r = far_ref[chunk, :ITEMS, :].astype(F32)
        far_i = far_ref[chunk, ITEMS:, :].astype(F32)
        pairs = jnp.concatenate(
            [own_r + far_r, own_i - far_i, own_i + far_i, far_r - own_r], axis=0
        ).astype(BF16)
        for band in range(16):
            out_ref[band, chunk * 16 : (chunk + 1) * 16, :] = pairs[
                :, band * 128 : (band + 1) * 128
            ]


def split_pairs(own0, own1, far):
    return pl.pallas_call(
        split_kernel,
        out_shape=jax.ShapeDtypeStruct((16, 32, 128), BF16),
        cost_estimate=pl.CostEstimate(
            flops=1_000_000, bytes_accessed=500_000, transcendentals=0
        ),
        name="split",
    )(own0, own1, far)


def block_kernel(v_ref, c_ref, lane_ref, row_ref, out_ref):
    for chunk, slots in enumerate(C_OF_CHUNK):
        for half in range(2):
            for item in range(ITEMS):
                pair = v_ref[2 * (item // 2) + half] * c_ref[chunk, item % 2]
                sums = jnp.dot(pair, lane_ref[...], preferred_element_type=F32) * row_ref[...]
                index = (chunk * 2 + half) * ITEMS + item
                out_ref[index : index + 1, :] = sums.sum(axis=0, keepdims=True)


def block_sums(v, c, lanes, rows):
    return pl.pallas_call(
        block_kernel,
        out_shape=jax.ShapeDtypeStruct((16, 128), F32),
        cost_estimate=pl.CostEstimate(
            flops=250_000_000, bytes_accessed=1_500_000, transcendentals=0
        ),
        name="block",
    )(v, c, lanes, rows)


def sum_kernel(left_ref, right_ref, out_ref):
    out_ref[...] = lax.dot_general(
        left_ref[...],
        right_ref[...],
        (((0,), (0,)), ((), ())),
        preferred_element_type=F32,
    )


def copy_for_each(x, axis, devices):
    return lax.all_to_all(
        jnp.broadcast_to(x[None], (devices, *x.shape)), axis, 0, 0, tiled=True
    )


def wave_rows(wave):
    return wave.reshape(X6, Y6, Y16, N).transpose(0, 2, 1, 3).reshape(X6 * Y16, Y6 * N)


def turn(phase):
    angle = (phase % N).astype(F32) * (2.0 * math.pi / N)
    return jnp.cos(angle), -jnp.sin(angle)


def per_device(
    valence_wave,
    conduction_wave,
    valence_index,
    occupied_energy,
    conduction_energy,
    frequency,
    gvec_cell,
    block_cell,
):
    col = lax.axis_index(COL)
    wave_v = wave_rows(valence_wave)
    wave_c = wave_rows(conduction_wave)
    all_v = [wave_v]
    for mask in (1, 2, 3):
        all_v.append(lax.ppermute(wave_v, VGROUP, [(i, i ^ mask) for i in range(4)]))
    all_c = [wave_c] + [None] * 3
    for shift in (1, 3, 2):
        all_c[shift] = lax.ppermute(wave_c, "z1", [(i, (i + shift) % 4) for i in range(4)])
    v = jnp.stack(all_v)
    c = [jnp.stack([all_c[slot] for slot in slots]) for slots in C_OF_CHUNK]

    mirror_of = [(k, SLABS - 1 - k) for k in range(SLABS)]
    far_cell = lax.ppermute(gvec_cell, COL, mirror_of)
    far_x, far_y, far_z = far_cell // 576, far_cell // N % 6, far_cell % N
    flat = jnp.concatenate([gvec_cell % 576, (6 - far_y) * N + (N - far_z) % N])[None]
    kx = jnp.concatenate([gvec_cell // 576, (N - far_x) % N])[None]

    cells = copy_for_each(block_cell, COL, SLABS).reshape(NBLOCK)
    block_x = cells // 576
    block_y = jnp.arange(NBLOCK, dtype=jnp.int32) * 6 + cells // N % 6
    block_z = cells % N

    tables = (lane_table(), twiddle_table(), row_table())
    sent = [lax.all_to_all(planes_of(v, part, tables), COL, 0, 0, tiled=True) for part in c]

    lane = jnp.arange(Y6 * N, dtype=jnp.int32)
    lane_c, lane_s = turn(
        (lane // N * 16)[:, None] * block_y[None] + (lane % N)[:, None] * block_z[None]
    )
    row = jnp.arange(X6 * Y16, dtype=jnp.int32)
    row_c, row_s = turn(
        (row // Y16 + X6 * col)[:, None] * block_x[None] + (row % Y16)[:, None] * block_y[None]
    )
    scale = 1.0 / (N * math.sqrt(N))
    zeros = jnp.zeros((Y6 * N, 64), F32)
    lanes = jnp.concatenate([lane_c, lane_s, lane_c, lane_s, zeros], axis=1).astype(BF16)
    rows = jnp.concatenate([row_c, -row_s, row_s, row_c, zeros[: X6 * Y16]], axis=1) * scale
    partial = block_sums(v, jnp.stack(c), lanes, rows)
    here = copy_for_each(partial, COL, SLABS).reshape(SLABS, 16, 128).sum(axis=0)
    here = jnp.concatenate(
        [here[:, :16] + here[:, 16:32], here[:, 32:48] + here[:, 48:64]], axis=1
    )
    block = copy_for_each(here.astype(BF16), BAND, 16).reshape(16, CHUNKS, 2, ITEMS, 2, NBLOCK)

    pair_v, pair_c, pair_part = pair_table()
    occupied = jnp.arange(occupied_energy.shape[0], dtype=jnp.int32)
    valence_energy = jnp.sum(
        jnp.where(valence_index[:, None] == occupied[None, :], occupied_energy[None, :], 0.0),
        axis=1,
    )
    count_v, count_c = valence_index.shape[0], conduction_energy.shape[0]
    energy_v = jnp.sum(
        jnp.where(pair_v[:, None] == np.arange(count_v)[None], valence_energy[None], 0.0), axis=1
    )
    energy_c = jnp.sum(
        jnp.where(pair_c[:, None] == np.arange(count_c)[None], conduction_energy[None], 0.0),
        axis=1,
    )
    gap = (energy_c - energy_v)[:, None]
    weight = (
        -4.0 * gap / (gap * gap + frequency[None] * frequency[None])
        * (1.0 / math.sqrt(count_v * count_c))
    )
    block = block.astype(F32)
    real, imag = block[..., 0, :], block[..., 1, :]
    columns = jnp.stack(
        [jnp.stack([real, -imag], axis=-2), jnp.stack([imag, real], axis=-2)], axis=3
    )
    columns = columns.reshape(512, 1, 2, NBLOCK)
    right = (columns * weight[:, :, None, None]).astype(BF16).reshape(512, -1)

    found = [points_of(planes, x_table(), flat, kx) for planes in sent]
    mirrored = jnp.stack([part[:, G_DEV:].astype(BF16) for part in found])
    far = lax.ppermute(mirrored, COL, mirror_of)
    pairs = split_pairs(found[0], found[1], far)
    left = lax.all_to_all(pairs, BAND, 0, 0, tiled=True).reshape(512, 128)
    return pl.pallas_call(
        sum_kernel,
        out_shape=jax.ShapeDtypeStruct((128, right.shape[1]), F32),
        name="pair_sum",
    )(left, right)


def solution(mesh):
    fine = Mesh(
        mesh.devices.reshape(4, 2, 2, 4, 2, 2), ("z1", "z0", "yl", "x", "yh", "co")
    )
    return jax.shard_map(
        per_device,
        mesh=fine,
        in_specs=(
            P(BAND, COL, None),
            P(BAND, COL, None),
            P(),
            P(),
            P(),
            P(),
            P(COL),
            P(COL),
        ),
        out_specs=P(COL + BAND, None),
        check_vma=False,
    )
```

time: 313 us -> 156 us (0.50)
  local copies, waits for them, and re-layouts: 97.1 us -> 16.3 us
  waiting for transfers between devices: 120 us -> 47.7 us
  Pallas kernels: 0 us -> 29.2 us
  matrix products: 29.1 us -> 0 us
  starting transfers between devices: 25.3 us -> 51.7 us
  blocking collectives: 21.5 us -> 0 us
  other arithmetic: 15.8 us -> 7.37 us
    reshape x4 -> x6, local copies, waits for them, and re-layouts: 68 us -> 2.57 us  [wave_rows(): wave.reshape(X6, Y6, Y16, N).transpose(0, 2, 1, 3).reshape(X6 * Y16, Y6 * N)]
    all_to_all x2 -> x3, waiting for transfers between devices: 55.8 us -> 13.5 us  [copy_for_each(): lax.all_to_all(jnp.broadcast_to(x[None], (devices, *x.shape)), axis, 0, 0...]
    all_to_all x1 -> x3, waiting for transfers between devices: 63.9 us -> 26.3 us  [the longest x2 18 us: per_device(): lax.all_to_all(planes_of(v, part, tables), COL, 0, 0, tiled=True)]
    pallas_call x0 -> x7, Pallas kernels: none -> 29.2 us  [the longest x2 14.8 us: points_of(): pl.pallas_call(pick_kernel, out_shape=jax.ShapeDtypeStruct((2 * ITEMS, 2...]
    dot_general x8 -> x0, matrix products: 29.1 us -> none  [the longest x1 7.89 us: per_device(): z_real = jnp.einsum('kz,pxyz->pxyk', z_cosine, products, precision=high)]
    all_to_all x1 -> x0, blocking collectives: 21.5 us -> none  [sent_and_summed(): lax.all_to_all(pieces, axis, split_axis=0, concat_axis=0, tiled=True)]
    ppermute x0 -> x8, starting transfers between devices: none -> 17.5 us  [the longest x3 10.2 us: per_device(): lax.ppermute(wave_c, 'z1', [(i, (i + shift) % 4) for i in range(4)])]
    gather x1 -> x0, local copies, waits for them, and re-layouts: 16.1 us -> none  [per_device(): row_density = jnp.take(density, gvec_cell, axis=2)]
  transfers between devices with their start and end apart: 3 -> 14, of which waited for: 2 -> 8; matrix products, arithmetic and copies ran while one was open for 3% -> 9% of each run, Pallas kernels for 0% -> 12%
where the time goes in v1:
time: 156 us; the launch traced here: 153 us
  starting transfers between devices  51.7 us (33%)
  waiting for transfers between devices  47.7 us (31%)
  Pallas kernels  29.2 us (19%)
  local copies, waits for them, and re-layouts  16.3 us (10%)
  other arithmetic  7.37 us (5%)
    all_to_all x2, waiting for transfers between devices, per_device(): lax.all_to_all(planes_of(v, part, tables), COL, 0, 0, tiled=True)  18 us
    all_to_all x3, starting transfers between devices, copy_for_each(): lax.all_to_all(jnp.broadcast_to(x[None], (devices, *x.shape)), axis, 0, 0...  17.2 us
    pallas_call x2, Pallas kernels, points_of(): pl.pallas_call(pick_kernel, out_shape=jax.ShapeDtypeStruct((2 * ITEMS, 2...  14.8 us
    all_to_all x3, waiting for transfers between devices, copy_for_each(): lax.all_to_all(jnp.broadcast_to(x[None], (devices, *x.shape)), axis, 0, 0...  13.5 us
    all_to_all x2, starting transfers between devices, per_device(): lax.all_to_all(planes_of(v, part, tables), COL, 0, 0, tiled=True)  11.6 us
    ppermute x3, starting transfers between devices, per_device(): lax.ppermute(wave_c, 'z1', [(i, (i + shift) % 4) for i in range(4)])  10.2 us
    unnamed x40, local copies, waits for them, and re-layouts  8.89 us
    all_to_all x1, waiting for transfers between devices, per_device(): left = lax.all_to_all(pairs, BAND, 0, 0, tiled=True).reshape(512, 128)  8.32 us
  transfers between devices with their start and end apart: 14, of which 8 were waited for; matrix products, arithmetic and copies ran while one was open for 9% of the time, Pallas kernels for 12%

profile of v1, /device:TPU:6, one launch (start us, length us, event | category | flops | bytes accessed | tf_op | source)
XLA Modules:
  0.0 153.5 jit_solution(3356727890441032112)
XLA Ops:
  1.3 6.4 %collective-permute-start.5 = (bf16[96,576]{1,0:T(8,128)(2,1)S(1)}, bf16[96,576]{1,0:T(8,128)(2,1)S(1)}, u32[]{:S(2)}, u32[]{:S(2)}) collective-permute-start(bf16[96,576]{1,0:T(8,128)(2,1)S(1)} %reshape.220), channel_id=1, source_target_pairs={{0,192},{64,0},{128,64},{192,128},{1,193},{65,1},{129,65},{193,129... | collective-permute-start | bytes 331784 | tf_op jit(solution)/shard_map/ppermute | solution.py:279
  8.7 2.8 %collective-permute-start.3 = (bf16[96,576]{1,0:T(8,128)(2,1)S(1)}, bf16[96,576]{1,0:T(8,128)(2,1)S(1)}, u32[]{:S(2)}, u32[]{:S(2)}) collective-permute-start(bf16[96,576]{1,0:T(8,128)(2,1)S(1)} %reshape.220), channel_id=1, source_target_pairs={{0,64},{64,128},{128,192},{192,0},{1,65},{65,129},{129,193},{193,1... | collective-permute-start | bytes 331784 | tf_op jit(solution)/shard_map/ppermute | solution.py:279
  12.8 1.7 %collective-permute-start = (bf16[96,576]{1,0:T(8,128)(2,1)S(1)}, bf16[96,576]{1,0:T(8,128)(2,1)S(1)}, u32[]{:S(2)}, u32[]{:S(2)}) collective-permute-start(bf16[96,576]{1,0:T(8,128)(2,1)S(1)} %reshape.218), channel_id=1, source_target_pairs={{0,16},{16,0},{32,48},{48,32},{1,17},{17,1},{33,49},{49,33},{2,18}... | collective-permute-start | bytes 331784 | tf_op jit(solution)/shard_map/ppermute | solution.py:276
  16.7 7.1 %all-to-all-start.3 = ((s32[16,1,1]{2,1,0:T(1,128)}), s32[16,1,1]{2,1,0:T(1,128)S(1)}, u32[]{:S(2)}, u32[]{:S(2)}) async-start(s32[16,1,1]{2,1,0:T(1,128)} %broadcast_in_dim.47), calls=%async_computation.3 | async-start | bytes 16384 | tf_op jit(solution)/shard_map/all_to_all | solution.py:247
  24.2 5.2 %all-to-all-done.3 = s32[16,1,1]{2,1,0:T(1,128)S(1)} async-done(((s32[16,1,1]{2,1,0:T(1,128)}), s32[16,1,1]{2,1,0:T(1,128)S(1)}, u32[]{:S(2)}, u32[]{:S(2)}) %all-to-all-start.3) | async-done | bytes 96 | tf_op jit(solution)/shard_map/all_to_all | solution.py:247
  35.1 1.9 %collective-permute-start.4 = (s32[2048]{0:T(1024)S(1)}, s32[2048]{0:T(1024)S(1)}, u32[]{:S(2)}, u32[]{:S(2)}) collective-permute-start(s32[2048]{0:T(1024)S(1)} %copy-done.13), channel_id=1, source_target_pairs={{0,15},{1,14},{2,13},{3,12},{4,11},{5,10},{6,9},{7,8},{8,7},{9,6},... | collective-permute-start | bytes 24584 | tf_op jit(solution)/shard_map/ppermute | solution.py:284
  38.0 2.7 %collective-permute-done.2 = bf16[96,576]{1,0:T(8,128)(2,1)S(1)} collective-permute-done((bf16[96,576]{1,0:T(8,128)(2,1)S(1)}, bf16[96,576]{1,0:T(8,128)(2,1)S(1)}, u32[]{:S(2)}, u32[]{:S(2)}) %collective-permute-start.2) | collective-permute-done | bytes 110624 | tf_op jit(solution)/shard_map/ppermute | solution.py:276
  41.6 2.6 %block.1 = f32[16,128]{1,0:T(8,128)} custom-call(bf16[4,96,576]{2,1,0:T(8,128)(2,1)} %pad_maximum_fusion.1.v_ref, bf16[2,2,96,576]{3,2,1,0:T(8,128)(2,1)} %pad_maximum_fusion.2.c_ref, bf16[576,128]{1,0:T(8,128)(2,1)} %concatenate.23.lane_ref, f32[96,128]{1,0:T(8,128)} %broadcast_multiply_fusion.row_ref), custom_call_target="tpu_custom_call" | custom-call | flops 250000000 | bytes 1500000 | tf_op jit(solution)/shard_map/block/pallas_call | solution.py:227
  44.2 1.4 broadcast_in_dim.81
  45.6 5.4 %all-to-all-start.4 = ((f32[16,16,128]{2,1,0:T(8,128)}), f32[16,16,128]{2,1,0:T(8,128)S(1)}, u32[]{:S(2)}, u32[]{:S(2)}) async-start(f32[16,16,128]{2,1,0:T(8,128)} %broadcast_in_dim.81), calls=%async_computation.4 | async-start | bytes 262144 | tf_op jit(solution)/shard_map/all_to_all | solution.py:247
  51.4 5.5 %all-to-all-done.4 = f32[16,16,128]{2,1,0:T(8,128)S(1)} async-done(((f32[16,16,128]{2,1,0:T(8,128)}), f32[16,16,128]{2,1,0:T(8,128)S(1)}, u32[]{:S(2)}, u32[]{:S(2)}) %all-to-all-start.4) | async-done | bytes 131104 | tf_op jit(solution)/shard_map/all_to_all | solution.py:247
  57.8 4.6 %all-to-all-start.5 = ((bf16[16,2,256]{2,1,0:T(2,128)(2,1)}), bf16[16,2,256]{2,1,0:T(2,128)(2,1)S(1)}, u32[]{:S(2)}, u32[]{:S(2)}) async-start(bf16[16,2,256]{2,1,0:T(2,128)(2,1)} %reshape.228), calls=%async_computation.5 | async-start | bytes 32768 | tf_op jit(solution)/shard_map/all_to_all | solution.py:247
  62.5 1.5 copy-done.3
  64.0 4.2 %planes.3 = bf16[16,48,768]{2,1,0:T(8,128)(2,1)} custom-call(bf16[4,96,576]{2,1,0:T(8,128)(2,1)S(1)} %copy-done, bf16[2,96,576]{2,1,0:T(8,128)(2,1)S(1)} %get-tuple-element.18.c_ref, bf16[576,1536]{1,0:T(8,128)(2,1)S(1)} %copy-done.3, f32[2,16,768]{2,1,0:T(8,128)S(1)} %copy-done.9, bf16[768,768]{1,0:T(8,128)(2,1)S(1)} %copy-done.7), custom_call_target="tpu_custom_call" | custom-call | flops 2700000000 | bytes 6000000 | tf_op jit(solution)/shard_map/planes/pallas_call | solution.py:146
  68.1 2.9 %all-to-all-done.5 = bf16[16,2,256]{2,1,0:T(2,128)(2,1)S(1)} async-done(((bf16[16,2,256]{2,1,0:T(2,128)(2,1)}), bf16[16,2,256]{2,1,0:T(2,128)(2,1)S(1)}, u32[]{:S(2)}, u32[]{:S(2)}) %all-to-all-start.5) | async-done | bytes 16416 | tf_op jit(solution)/shard_map/all_to_all | solution.py:247
  71.0 5.8 %all-to-all-start.1 = ((bf16[16,48,768]{2,1,0:T(8,128)(2,1)}), bf16[16,48,768]{2,1,0:T(8,128)(2,1)S(1)}, u32[]{:S(2)}, u32[]{:S(2)}) async-start(bf16[16,48,768]{2,1,0:T(8,128)(2,1)} %planes.3), calls=%async_computation.1 | async-start | bytes 2359296 | tf_op jit(solution)/shard_map/all_to_all | solution.py:295
  77.0 1.5 copy-done.4
  78.4 1.3 copy-done.8
  79.7 4.1 %planes.2 = bf16[16,48,768]{2,1,0:T(8,128)(2,1)} custom-call(bf16[4,96,576]{2,1,0:T(8,128)(2,1)S(1)} %copy-done, bf16[2,96,576]{2,1,0:T(8,128)(2,1)S(1)} %get-tuple-element.16.c_ref, bf16[576,1536]{1,0:T(8,128)(2,1)S(1)} %copy-done.4, f32[2,16,768]{2,1,0:T(8,128)S(1)} %copy-done.9, bf16[768,768]{1,0:T(8,128)(2,1)S(1)} %copy-done.8), custom_call_target="tpu_custom_call" | custom-call | flops 2700000000 | bytes 6000000 | tf_op jit(solution)/shard_map/planes/pallas_call | solution.py:146
  84.1 9.8 %all-to-all-done.1.t_ref = bf16[16,48,768]{2,1,0:T(8,128)(2,1)S(1)} async-done(((bf16[16,48,768]{2,1,0:T(8,128)(2,1)}), bf16[16,48,768]{2,1,0:T(8,128)(2,1)S(1)}, u32[]{:S(2)}, u32[]{:S(2)}) %all-to-all-start.1) | async-done | bytes 1179680 | tf_op jit(solution)/shard_map/all_to_all | solution.py:295
  93.9 5.9 %all-to-all-start = ((bf16[16,48,768]{2,1,0:T(8,128)(2,1)}), bf16[16,48,768]{2,1,0:T(8,128)(2,1)S(1)}, u32[]{:S(2)}, u32[]{:S(2)}) async-start(bf16[16,48,768]{2,1,0:T(8,128)(2,1)} %planes.2), calls=%async_computation | async-start | bytes 2359296 | tf_op jit(solution)/shard_map/all_to_all | solution.py:295
  100.1 1.3 copy-done.5
  101.3 7.4 %points.3.own1_ref = f32[8,4096]{1,0:T(8,128)S(1)} custom-call(bf16[16,48,768]{2,1,0:T(8,128)(2,1)S(1)} %all-to-all-done.1.t_ref, bf16[768,768]{1,0:T(8,128)(2,1)S(1)} %copy-done.5, s32[1,4096]{1,0:T(1,128)S(1)} %bitcast.31, s32[1,4096]{1,0:T(1,128)S(1)} %bitcast.33), custom_call_target="tpu_custom_call" | custom-call | flops 5699999744 | bytes 3000000 | tf_op jit(solution)/shard_map/points/pallas_call | solution.py:178
  108.8 8.2 %all-to-all-done.t_ref = bf16[16,48,768]{2,1,0:T(8,128)(2,1)S(1)} async-done(((bf16[16,48,768]{2,1,0:T(8,128)(2,1)}), bf16[16,48,768]{2,1,0:T(8,128)(2,1)S(1)}, u32[]{:S(2)}, u32[]{:S(2)}) %all-to-all-start) | async-done | bytes 1179680 | tf_op jit(solution)/shard_map/all_to_all | solution.py:295
  117.0 1.3 copy-done.6
  118.3 7.4 %points.2.own0_ref = f32[8,4096]{1,0:T(8,128)S(1)} custom-call(bf16[16,48,768]{2,1,0:T(8,128)(2,1)S(1)} %all-to-all-done.t_ref, bf16[768,768]{1,0:T(8,128)(2,1)S(1)} %copy-done.6, s32[1,4096]{1,0:T(1,128)S(1)} %bitcast.32, s32[1,4096]{1,0:T(1,128)S(1)} %bitcast.34), custom_call_target="tpu_custom_call" | custom-call | flops 5699999744 | bytes 3000000 | tf_op jit(solution)/shard_map/points/pallas_call | solution.py:178
  125.7 2.2 %collective-permute-start.7 = (bf16[2,8,2048]{2,1,0:T(8,128)(2,1)S(1)}, bf16[2,8,2048]{2,1,0:T(8,128)(2,1)S(1)}, u32[]{:S(2)}, u32[]{:S(2)}) collective-permute-start(bf16[2,8,2048]{2,1,0:T(8,128)(2,1)S(1)} %pad_maximum_fusion.5), channel_id=1, source_target_pairs={{0,15},{1,14},{2,13},{3,12},{4,11},{5,10},{6,9},{7,8},{8,7},{9,6},... | collective-permute-start | bytes 196616 | tf_op jit(solution)/shard_map/ppermute | solution.py:345
  128.5 5.1 %collective-permute-done.7.far_ref = bf16[2,8,2048]{2,1,0:T(8,128)(2,1)S(1)} collective-permute-done((bf16[2,8,2048]{2,1,0:T(8,128)(2,1)S(1)}, bf16[2,8,2048]{2,1,0:T(8,128)(2,1)S(1)}, u32[]{:S(2)}, u32[]{:S(2)}) %collective-permute-start.7) | collective-permute-done | bytes 65568 | tf_op jit(solution)/shard_map/ppermute | solution.py:345
  134.3 1.7 %split.1 = bf16[16,32,128]{2,1,0:T(8,128)(2,1)} custom-call(f32[8,4096]{1,0:T(8,128)} %copy-done.2, f32[8,4096]{1,0:T(8,128)} %copy-done.1, bf16[2,8,2048]{2,1,0:T(8,128)(2,1)} %copy-done.11), custom_call_target="tpu_custom_call" | custom-call | flops 1000000 | bytes 500000 | tf_op jit(solution)/shard_map/split/pallas_call | solution.py:206
  135.9 5.4 %all-to-all-start.2 = ((bf16[16,32,128]{2,1,0:T(8,128)(2,1)}), bf16[16,32,128]{2,1,0:T(8,128)(2,1)S(1)}, u32[]{:S(2)}, u32[]{:S(2)}) async-start(bf16[16,32,128]{2,1,0:T(8,128)(2,1)} %split.1), calls=%async_computation.2 | async-start | bytes 262144 | tf_op jit(solution)/shard_map/all_to_all | solution.py:347
  142.7 8.3 %all-to-all-done.2 = bf16[16,32,128]{2,1,0:T(8,128)(2,1)S(1)} async-done(((bf16[16,32,128]{2,1,0:T(8,128)(2,1)}), bf16[16,32,128]{2,1,0:T(8,128)(2,1)S(1)}, u32[]{:S(2)}, u32[]{:S(2)}) %all-to-all-start.2) | async-done | bytes 131104 | tf_op jit(solution)/shard_map/all_to_all | solution.py:347
  151.7 1.8 %pair_sum.1 = f32[128,128]{1,0:T(8,128)} custom-call(bf16[512,128]{1,0:T(8,128)(2,1)} %bitcast.40, bf16[512,128]{1,0:T(8,128)(2,1)} %copy.48.right_ref), custom_call_target="tpu_custom_call" | custom-call | tf_op jit(solution)/shard_map/pair_sum/pallas_call | solution.py:348
  (96 shorter events, 18.2 us)
Async XLA Ops:
  1.3 33.2 %collective-permute-start.5 = (bf16[96,576]{1,0:T(8,128)(2,1)S(1)}, bf16[96,576]{1,0:T(8,128)(2,1)S(1)}, u32[]{:S(2)}, u32[]{:S(2)}) collective-permute-start(bf16[96,576]{1,0:T(8,128)(2,1)S(1)} %reshape.220), channel_id=1, source_target_pairs={{0,192},{64,0},{128,64},{192,128},{1,193},{65,1},{129,65},{193,129... | collective-permute-start | bytes 331784 | tf_op jit(solution)/shard_map/ppermute | solution.py:279
  7.7 27.5 %collective-permute-start.6 = (bf16[96,576]{1,0:T(8,128)(2,1)S(1)}, bf16[96,576]{1,0:T(8,128)(2,1)S(1)}, u32[]{:S(2)}, u32[]{:S(2)}) collective-permute-start(bf16[96,576]{1,0:T(8,128)(2,1)S(1)} %reshape.220), channel_id=1, source_target_pairs={{0,128},{64,192},{128,0},{192,64},{1,129},{65,193},{129,1},{193,65... | collective-permute-start | bytes 331784 | tf_op jit(solution)/shard_map/ppermute | solution.py:279
  8.7 28.4 %collective-permute-start.3 = (bf16[96,576]{1,0:T(8,128)(2,1)S(1)}, bf16[96,576]{1,0:T(8,128)(2,1)S(1)}, u32[]{:S(2)}, u32[]{:S(2)}) collective-permute-start(bf16[96,576]{1,0:T(8,128)(2,1)S(1)} %reshape.220), channel_id=1, source_target_pairs={{0,64},{64,128},{128,192},{192,0},{1,65},{65,129},{129,193},{193,1... | collective-permute-start | bytes 331784 | tf_op jit(solution)/shard_map/ppermute | solution.py:279
  12.8 25.2 %collective-permute-start = (bf16[96,576]{1,0:T(8,128)(2,1)S(1)}, bf16[96,576]{1,0:T(8,128)(2,1)S(1)}, u32[]{:S(2)}, u32[]{:S(2)}) collective-permute-start(bf16[96,576]{1,0:T(8,128)(2,1)S(1)} %reshape.218), channel_id=1, source_target_pairs={{0,16},{16,0},{32,48},{48,32},{1,17},{17,1},{33,49},{49,33},{2,18}... | collective-permute-start | bytes 331784 | tf_op jit(solution)/shard_map/ppermute | solution.py:276
  14.5 23.5 %collective-permute-start.1 = (bf16[96,576]{1,0:T(8,128)(2,1)S(1)}, bf16[96,576]{1,0:T(8,128)(2,1)S(1)}, u32[]{:S(2)}, u32[]{:S(2)}) collective-permute-start(bf16[96,576]{1,0:T(8,128)(2,1)S(1)} %reshape.218), channel_id=1, source_target_pairs={{0,32},{16,48},{32,0},{48,16},{1,33},{17,49},{33,1},{49,17},{2,34}... | collective-permute-start | bytes 331784 | tf_op jit(solution)/shard_map/ppermute | solution.py:276
  16.7 12.6 %all-to-all-start.3 = ((s32[16,1,1]{2,1,0:T(1,128)}), s32[16,1,1]{2,1,0:T(1,128)S(1)}, u32[]{:S(2)}, u32[]{:S(2)}) async-start(s32[16,1,1]{2,1,0:T(1,128)} %broadcast_in_dim.47), calls=%async_computation.3 | async-start | bytes 16384 | tf_op jit(solution)/shard_map/all_to_all | solution.py:247
  31.5 3.6 %copy-start.13 = (s32[2048]{0:T(1024)S(1)}, s32[2048]{0:T(1024)}, u32[]{:S(2)}) copy-start(s32[2048]{0:T(1024)} %param.20) | copy-start | bytes 24580
  34.5 6.1 %collective-permute-start.2 = (bf16[96,576]{1,0:T(8,128)(2,1)S(1)}, bf16[96,576]{1,0:T(8,128)(2,1)S(1)}, u32[]{:S(2)}, u32[]{:S(2)}) collective-permute-start(bf16[96,576]{1,0:T(8,128)(2,1)S(1)} %reshape.218), channel_id=1, source_target_pairs={{0,48},{16,32},{32,16},{48,0},{1,49},{17,33},{33,17},{49,1},{2,50}... | collective-permute-start | bytes 331784 | tf_op jit(solution)/shard_map/ppermute | solution.py:276
  35.1 41.7 %collective-permute-start.4 = (s32[2048]{0:T(1024)S(1)}, s32[2048]{0:T(1024)S(1)}, u32[]{:S(2)}, u32[]{:S(2)}) collective-permute-start(s32[2048]{0:T(1024)S(1)} %copy-done.13), channel_id=1, source_target_pairs={{0,15},{1,14},{2,13},{3,12},{4,11},{5,10},{6,9},{7,8},{8,7},{9,6},... | collective-permute-start | bytes 24584 | tf_op jit(solution)/shard_map/ppermute | solution.py:284
  40.7 10.4 %copy-start.12 = (f32[4096]{0:T(1024)S(1)}, f32[4096]{0:T(1024)}, u32[]{:S(2)}) copy-start(f32[4096]{0:T(1024)} %param.17) | copy-start | bytes 49156
  40.7 10.4 %copy-start.16 = (s32[16]{0:T(128)S(1)}, s32[16]{0:T(128)}, u32[]{:S(2)}) copy-start(s32[16]{0:T(128)} %param.16) | copy-start | bytes 196
  40.7 10.6 %copy-start.14 = (pred[512,16]{0,1:T(8,128)(4,1)S(1)}, pred[512,16]{0,1:T(8,128)(4,1)}, u32[]{:S(2)}) copy-start(pred[512,16]{0,1:T(8,128)(4,1)} %constant.165.clone) | copy-start | bytes 24580
  40.7 10.6 %copy-start.15 = (pred[512,16]{0,1:T(8,128)(4,1)S(1)}, pred[512,16]{0,1:T(8,128)(4,1)}, u32[]{:S(2)}) copy-start(pred[512,16]{0,1:T(8,128)(4,1)} %constant.166.clone) | copy-start | bytes 24580
  40.7 10.6 %copy-start.17 = (f32[16]{0:T(128)S(1)}, f32[16]{0:T(128)}, u32[]{:S(2)}) copy-start(f32[16]{0:T(128)} %param.18) | copy-start | bytes 196
  41.6 20.8 %copy-start = (bf16[4,96,576]{2,1,0:T(8,128)(2,1)S(1)}, bf16[4,96,576]{2,1,0:T(8,128)(2,1)}, u32[]{:S(2)}) copy-start(bf16[4,96,576]{2,1,0:T(8,128)(2,1)} %pad_maximum_fusion.1.v_ref) | copy-start | bytes 1327108
  41.6 20.8 %copy-start.7 = (bf16[768,768]{1,0:T(8,128)(2,1)S(1)}, bf16[768,768]{1,0:T(8,128)(2,1)}, u32[]{:S(2)}) copy-start(bf16[768,768]{1,0:T(8,128)(2,1)} %constant.164.clone.row_ref) | copy-start | bytes 3538948
  41.6 20.9 %copy-start.9 = (f32[2,16,768]{2,1,0:T(8,128)S(1)}, f32[2,16,768]{2,1,0:T(8,128)}, u32[]{:S(2)}) copy-start(f32[2,16,768]{2,1,0:T(8,128)} %constant.163.clone.twiddle_ref) | copy-start | bytes 294916
  45.6 11.3 %all-to-all-start.4 = ((f32[16,16,128]{2,1,0:T(8,128)}), f32[16,16,128]{2,1,0:T(8,128)S(1)}, u32[]{:S(2)}, u32[]{:S(2)}) async-start(f32[16,16,128]{2,1,0:T(8,128)} %broadcast_in_dim.81), calls=%async_computation.4 | async-start | bytes 262144 | tf_op jit(solution)/shard_map/all_to_all | solution.py:247
  57.8 13.2 %all-to-all-start.5 = ((bf16[16,2,256]{2,1,0:T(2,128)(2,1)}), bf16[16,2,256]{2,1,0:T(2,128)(2,1)S(1)}, u32[]{:S(2)}, u32[]{:S(2)}) async-start(bf16[16,2,256]{2,1,0:T(2,128)(2,1)} %reshape.228), calls=%async_computation.5 | async-start | bytes 32768 | tf_op jit(solution)/shard_map/all_to_all | solution.py:247
  62.5 1.5 copy-start.3
  68.1 8.6 %copy-start.18 = (f32[4]{0:T(128)S(1)}, f32[4]{0:T(128)}, u32[]{:S(2)}) copy-start(f32[4]{0:T(128)} %param.19) | copy-start | bytes 52
  71.0 22.9 %all-to-all-start.1 = ((bf16[16,48,768]{2,1,0:T(8,128)(2,1)}), bf16[16,48,768]{2,1,0:T(8,128)(2,1)S(1)}, u32[]{:S(2)}, u32[]{:S(2)}) async-start(bf16[16,48,768]{2,1,0:T(8,128)(2,1)} %planes.3), calls=%async_computation.1 | async-start | bytes 2359296 | tf_op jit(solution)/shard_map/all_to_all | solution.py:295
  76.9 1.5 copy-start.4
  78.4 1.3 copy-start.8
  93.9 23.1 %all-to-all-start = ((bf16[16,48,768]{2,1,0:T(8,128)(2,1)}), bf16[16,48,768]{2,1,0:T(8,128)(2,1)S(1)}, u32[]{:S(2)}, u32[]{:S(2)}) async-start(bf16[16,48,768]{2,1,0:T(8,128)(2,1)} %planes.2), calls=%async_computation | async-start | bytes 2359296 | tf_op jit(solution)/shard_map/all_to_all | solution.py:295
  100.1 1.3 copy-start.5
  108.8 16.9 %copy-start.1 = (f32[8,4096]{1,0:T(8,128)}, f32[8,4096]{1,0:T(8,128)S(1)}, u32[]{:S(2)}) copy-start(f32[8,4096]{1,0:T(8,128)S(1)} %points.3.own1_ref) | copy-start | bytes 393220
  117.0 1.3 copy-start.6
  125.7 8.0 %copy-start.2 = (f32[8,4096]{1,0:T(8,128)}, f32[8,4096]{1,0:T(8,128)S(1)}, u32[]{:S(2)}) copy-start(f32[8,4096]{1,0:T(8,128)S(1)} %points.2.own0_ref) | copy-start | bytes 393220
  125.7 7.9 %collective-permute-start.7 = (bf16[2,8,2048]{2,1,0:T(8,128)(2,1)S(1)}, bf16[2,8,2048]{2,1,0:T(8,128)(2,1)S(1)}, u32[]{:S(2)}, u32[]{:S(2)}) collective-permute-start(bf16[2,8,2048]{2,1,0:T(8,128)(2,1)S(1)} %pad_maximum_fusion.5), channel_id=1, source_target_pairs={{0,15},{1,14},{2,13},{3,12},{4,11},{5,10},{6,9},{7,8},{8,7},{9,6},... | collective-permute-start | bytes 196616 | tf_op jit(solution)/shard_map/ppermute | solution.py:345
  135.9 15.1 %all-to-all-start.2 = ((bf16[16,32,128]{2,1,0:T(8,128)(2,1)}), bf16[16,32,128]{2,1,0:T(8,128)(2,1)S(1)}, u32[]{:S(2)}, u32[]{:S(2)}) async-start(bf16[16,32,128]{2,1,0:T(8,128)(2,1)} %split.1), calls=%async_computation.2 | async-start | bytes 262144 | tf_op jit(solution)/shard_map/all_to_all | solution.py:347
  151.0 0.7 copy-start.10
  (1 other events, 0.6 us)

commit v2 on v1

v2 whole, which is shorter than its diff:
```python
import functools
import math

import jax
import jax.numpy as jnp
import ml_dtypes
import numpy as np
from jax import lax
from jax.experimental import pallas as pl
from jax.experimental.pallas import tpu as pltpu
from jax.sharding import Mesh
from jax.sharding import PartitionSpec as P

BF16 = jnp.bfloat16
F32 = jnp.float32

N = 96
SLABS = 16
X6 = 6
Y6 = 6
Y16 = 16
K7 = 7
FLAT = K7 * N
WIDE = 768
ITEMS = 4
CHUNKS = 2
SPARE = 640
G_DEV = 2048
NBLOCK = 16
TILE = 512

BAND = ("z1", "z0", "yl")
VGROUP = ("z0", "yl")
COL = ("x", "yh", "co")


def unit(phase, period):
    angle = 2.0 * np.pi * (np.asarray(phase) % period) / period
    return np.cos(angle), -np.sin(angle)


def bf16(table):
    return np.asarray(table, np.float32).astype(ml_dtypes.bfloat16)


@functools.cache
def lane_table():
    y6, z = np.divmod(np.arange(Y6 * N), N)
    k7, kz = np.divmod(np.arange(FLAT), N)
    phase = 16 * y6[:, None] * k7[None, :] + z[:, None] * kz[None, :]
    cosine, sine = unit(phase, N)
    table = np.zeros((Y6 * N, 2 * WIDE))
    table[:, :FLAT] = cosine
    table[:, WIDE : WIDE + FLAT] = sine
    return bf16(table)


@functools.cache
def twiddle_table():
    k7 = np.arange(FLAT) // N
    cosine, sine = unit(np.arange(Y16)[:, None] * k7[None, :], N)
    table = np.zeros((2, Y16, WIDE), np.float32)
    table[0, :, :FLAT] = cosine / N
    table[1, :, :FLAT] = sine / N
    return table


@functools.cache
def row_table():
    table = np.zeros((SLABS, ITEMS, 2, X6, 2, ITEMS, X6, Y16))
    cosine, sine = unit(np.arange(SLABS)[:, None] * np.arange(Y16)[None, :], SLABS)
    for item in range(ITEMS):
        for x in range(X6):
            table[:, item, 0, x, 0, item, x] = cosine
            table[:, item, 0, x, 1, item, x] = -sine
            table[:, item, 1, x, 0, item, x] = sine
            table[:, item, 1, x, 1, item, x] = cosine
    return bf16(table.reshape(SLABS * ITEMS * 2 * X6, 2 * ITEMS * X6 * Y16))


@functools.cache
def x_table():
    table = np.zeros((2, ITEMS, N, SLABS, ITEMS, 2, X6))
    cosine, sine = unit(np.arange(N)[:, None] * np.arange(N)[None, :], N)
    cosine = (cosine * 0.5 / math.sqrt(N)).reshape(N, SLABS, X6)
    sine = (sine * 0.5 / math.sqrt(N)).reshape(N, SLABS, X6)
    for item in range(ITEMS):
        table[0, item, :, :, item, 0] = cosine
        table[0, item, :, :, item, 1] = -sine
        table[1, item, :, :, item, 0] = sine
        table[1, item, :, :, item, 1] = cosine
    return bf16(table.reshape(2 * ITEMS * N, SLABS * ITEMS * 2 * X6))


@functools.cache
def pair_table():
    valence, conduction = [], []
    for band in range(16):
        z1, group = divmod(band, 4)
        for chunk in range(CHUNKS):
            for half in range(2):
                for item in range(ITEMS):
                    slot_v = 2 * (item // 2) + half
                    slot_c = 2 * chunk + item % 2
                    valence.append(z1 * 4 + (group ^ slot_v))
                    conduction.append((z1 ^ slot_c) * 4 + group)
    return np.array(valence), np.array(conduction)


@functools.cache
def column_tables():
    tables = np.zeros((2, 128, 4, 2, NBLOCK))
    m = np.arange(NBLOCK)
    tables[0, 32 + m, :, 0, m] = 1.0
    tables[0, 64 + m, :, 1, m] = -1.0
    tables[1, 64 + m, :, 0, m] = 1.0
    tables[1, 32 + m, :, 1, m] = 1.0
    return bf16(tables.reshape(2, 128, 128))


def plane_kernel(v0, v1, v2, v3, c_ref, lane_ref, twiddle_ref, row_ref, *refs):
    *block_ref, out_ref, low_ref = refs
    waves = (v0, v1, v2, v3)
    rows = X6 * Y16
    twiddle_c = twiddle_ref[0][None]
    twiddle_s = twiddle_ref[1][None]
    for item in range(ITEMS):
        wave_c = c_ref[item % 2]
        pairs = jnp.concatenate(
            [waves[2 * (item // 2)][...] * wave_c, waves[2 * (item // 2) + 1][...] * wave_c],
            axis=0,
        )
        moved = jnp.dot(pairs, lane_ref[...], preferred_element_type=F32)
        real = moved[:rows, :WIDE] - moved[rows:, WIDE:]
        imag = moved[:rows, WIDE:] + moved[rows:, :WIDE]
        real = real.reshape(X6, Y16, WIDE)
        imag = imag.reshape(X6, Y16, WIDE)
        turned_r = real * twiddle_c - imag * twiddle_s
        turned_i = real * twiddle_s + imag * twiddle_c
        low_ref[item * rows : (item + 1) * rows, :] = turned_r.reshape(rows, WIDE).astype(BF16)
        low_ref[(ITEMS + item) * rows : (ITEMS + item + 1) * rows, :] = turned_i.reshape(
            rows, WIDE
        ).astype(BF16)
    per_slab = ITEMS * 2 * X6
    count = SLABS // 4
    for part in range(4):
        planes = jnp.dot(
            row_ref[part * count * per_slab : (part + 1) * count * per_slab, :],
            low_ref[...],
            preferred_element_type=F32,
        ).reshape(count, per_slab, WIDE)
        slabs = slice(part * count, (part + 1) * count)
        out_ref[slabs] = planes.astype(BF16)
        if block_ref:
            spare = planes[:, :32, SPARE:] + block_ref[0][...][None]
            out_ref[slabs, :32, SPARE:] = spare.astype(BF16)


def planes_of(v, c, tables, *block):
    per_slab = ITEMS * 2 * X6
    return pl.pallas_call(
        plane_kernel,
        out_shape=jax.ShapeDtypeStruct((SLABS, per_slab, WIDE), BF16),
        scratch_shapes=[pltpu.VMEM((2 * ITEMS * X6 * Y16, WIDE), BF16)],
        compiler_params=pltpu.CompilerParams(vmem_limit_bytes=40 << 20),
        cost_estimate=pl.CostEstimate(
            flops=2_700_000_000, bytes_accessed=6_000_000, transcendentals=0
        ),
        name="planes",
    )(*v, c, *tables, *block)


def pick(density_ref, flat_ref, kx_ref, store):
    def body(step, carry):
        lanes = pl.ds(pl.multiple_of(step * TILE, TILE), TILE)
        spot = lax.broadcasted_iota(jnp.int32, (WIDE, TILE), 0)
        chosen = jnp.where(spot == flat_ref[:, lanes], 1.0, 0.0).astype(BF16)
        values = jnp.dot(density_ref[...], chosen, preferred_element_type=F32)
        kx = lax.broadcasted_iota(jnp.int32, (N, TILE), 0) == kx_ref[:, lanes]
        values = jnp.where(kx[None], values.reshape(2 * ITEMS, N, TILE), 0.0)
        store(lanes, values.sum(axis=1))
        return carry

    lax.fori_loop(0, G_DEV // TILE, body, 0)


def transform_x(t_ref, x_ref, density_ref):
    density_ref[...] = jnp.dot(
        x_ref[...],
        t_ref[...].reshape(SLABS * ITEMS * 2 * X6, WIDE),
        preferred_element_type=F32,
    ).astype(BF16)


def first_kernel(t_ref, x_ref, own_ref, own_kx_ref, far_ref, far_kx_ref, own_out, far_out, low):
    transform_x(t_ref, x_ref, low)

    def store_far(lanes, values):
        far_out[:, lanes] = values.astype(BF16)

    def store_own(lanes, values):
        own_out[:, lanes] = values

    pick(low, far_ref, far_kx_ref, store_far)
    pick(low, own_ref, own_kx_ref, store_own)


def second_far_kernel(t_ref, x_ref, far_ref, far_kx_ref, first_ref, far_out, low, block_out):
    transform_x(t_ref, x_ref, low)
    far_out[0] = first_ref[...]

    def store_far(lanes, values):
        far_out[1, :, lanes] = values.astype(BF16)

    pick(low, far_ref, far_kx_ref, store_far)
    spare = t_ref[:, :32, SPARE:].astype(F32).sum(axis=0)
    spare = spare[:16] + spare[16:]
    spare = spare + pltpu.roll(spare, 128 - NBLOCK, 1)
    block_out[...] = spare


def second_own_kernel(low, own_ref, own_kx_ref, own_out):
    def store_own(lanes, values):
        own_out[:, lanes] = values

    pick(low, own_ref, own_kx_ref, store_own)


OWN = jax.ShapeDtypeStruct((2 * ITEMS, G_DEV), F32)
LOW = (2 * ITEMS * N, WIDE)


def first_points(planes, table, own, far):
    return pl.pallas_call(
        first_kernel,
        out_shape=(OWN, jax.ShapeDtypeStruct((2 * ITEMS, G_DEV), BF16)),
        scratch_shapes=[pltpu.VMEM(LOW, BF16)],
        compiler_params=pltpu.CompilerParams(vmem_limit_bytes=40 << 20),
        cost_estimate=pl.CostEstimate(
            flops=5_700_000_000, bytes_accessed=3_000_000, transcendentals=0
        ),
        name="first_points",
    )(planes, table, *own, *far)


def second_far_points(planes, table, far, first):
    return pl.pallas_call(
        second_far_kernel,
        out_shape=(
            jax.ShapeDtypeStruct((CHUNKS, 2 * ITEMS, G_DEV), BF16),
            jax.ShapeDtypeStruct(LOW, BF16),
            jax.ShapeDtypeStruct((16, 128), F32),
        ),
        compiler_params=pltpu.CompilerParams(vmem_limit_bytes=40 << 20),
        cost_estimate=pl.CostEstimate(
            flops=3_300_000_000, bytes_accessed=4_000_000, transcendentals=0
        ),
        name="second_far_points",
    )(planes, table, *far, first)


def second_own_points(low, own):
    return pl.pallas_call(
        second_own_kernel,
        out_shape=OWN,
        compiler_params=pltpu.CompilerParams(vmem_limit_bytes=40 << 20),
        cost_estimate=pl.CostEstimate(
            flops=2_400_000_000, bytes_accessed=1_300_000, transcendentals=0
        ),
        name="second_own_points",
    )(low, *own)


def split_kernel(own0_ref, own1_ref, far_ref, block_ref, out_ref):
    real, imag = [], []
    for chunk, own_ref in enumerate((own0_ref, own1_ref)):
        own_r = own_ref[:ITEMS, :]
        own_i = own_ref[ITEMS:, :]
        far_r = far_ref[chunk, :ITEMS, :].astype(F32)
        far_i = far_ref[chunk, ITEMS:, :].astype(F32)
        real += [own_r + far_r, own_i + far_i]
        imag += [own_i - far_i, far_r - own_r]
    pairs = jnp.concatenate(real + imag, axis=0).astype(BF16)
    block = block_ref[...].astype(BF16)
    for band in range(16):
        out_ref[band, :32, :] = pairs[:, band * 128 : (band + 1) * 128]
        out_ref[band, 32:, :] = block


def split_pairs(own0, own1, far, block):
    return pl.pallas_call(
        split_kernel,
        out_shape=jax.ShapeDtypeStruct((16, 48, 128), BF16),
        cost_estimate=pl.CostEstimate(
            flops=1_000_000, bytes_accessed=500_000, transcendentals=0
        ),
        name="split",
    )(own0, own1, far, block)


def block_kernel(v0, v1, v2, v3, c0_ref, c1_ref, lane_ref, row_ref, out_ref):
    waves = (v0, v1, v2, v3)
    for chunk, c_ref in enumerate((c0_ref, c1_ref)):
        for half in range(2):
            for item in range(ITEMS):
                pair = waves[2 * (item // 2) + half][...] * c_ref[item % 2]
                sums = jnp.dot(pair, lane_ref[...], preferred_element_type=F32) * row_ref[...]
                total = sums.sum(axis=0, keepdims=True)
                high = total.astype(BF16).astype(F32)
                index = (chunk * 2 + half) * ITEMS + item
                out_ref[index : index + 1, :] = high
                out_ref[16 + index : 17 + index, :] = total - high


def block_sums(v, c, lanes, rows):
    return pl.pallas_call(
        block_kernel,
        out_shape=jax.ShapeDtypeStruct((32, 128), F32),
        cost_estimate=pl.CostEstimate(
            flops=250_000_000, bytes_accessed=1_500_000, transcendentals=0
        ),
        name="block",
    )(*v, *c, lanes, rows)


def sum_kernel(pairs_ref, weight_ref, column_ref, out_ref):
    pairs = 16 * 16
    block = pairs_ref[:, 32:, :].reshape(pairs, 128)
    total = None
    for part in range(2):
        left = pairs_ref[:, 16 * part : 16 * (part + 1), :].reshape(pairs, 128)
        columns = jnp.dot(block, column_ref[part], preferred_element_type=F32)
        right = (columns * weight_ref[...]).astype(BF16)
        term = lax.dot_general(
            left, right, (((0,), (0,)), ((), ())), preferred_element_type=F32
        )
        total = term if total is None else total + term
    out_ref[...] = total


def wave_rows(wave):
    return wave.reshape(X6, Y6, Y16, N).transpose(0, 2, 1, 3).reshape(X6 * Y16, Y6 * N)


def turn(phase):
    angle = (phase % N).astype(F32) * (2.0 * math.pi / N)
    return jnp.cos(angle), -jnp.sin(angle)


def per_device(
    valence_wave,
    conduction_wave,
    valence_index,
    occupied_energy,
    conduction_energy,
    frequency,
    gvec_cell,
    block_cell,
):
    col = lax.axis_index(COL)
    wave_v = wave_rows(valence_wave)
    wave_c = wave_rows(conduction_wave)
    v = [wave_v]
    for mask in (1, 2, 3):
        v.append(lax.ppermute(wave_v, VGROUP, [(i, i ^ mask) for i in range(4)]))
    c = [jnp.stack([wave_c, lax.ppermute(wave_c, "z1", [(i, i ^ 1) for i in range(4)])])]
    c.append(lax.ppermute(c[0], "z1", [(i, i ^ 2) for i in range(4)]))

    tables = (lane_table(), twiddle_table(), row_table())
    sent0 = lax.all_to_all(planes_of(v, c[0], tables), COL, 0, 0, tiled=True)

    mirror_of = [(k, SLABS - 1 - k) for k in range(SLABS)]
    far_cell = lax.ppermute(gvec_cell, COL, mirror_of)
    far_x, far_y, far_z = far_cell // 576, far_cell // N % 6, far_cell % N
    own = ((gvec_cell % 576)[None], (gvec_cell // 576)[None])
    far = (((6 - far_y) * N + (N - far_z) % N)[None], ((N - far_x) % N)[None])

    spots = jnp.arange(NBLOCK, dtype=jnp.int32)
    cells = jnp.where(spots == col, block_cell[0], 0)
    for mask in (1, 2, 4, 8):
        cells = cells + lax.ppermute(cells, COL, [(k, k ^ mask) for k in range(SLABS)])
    block_x = cells // 576
    block_y = spots * 6 + cells // N % 6
    block_z = cells % N
    lane = jnp.arange(Y6 * N, dtype=jnp.int32)
    lane_c, lane_s = turn(
        (lane // N * 16)[:, None] * block_y[None] + (lane % N)[:, None] * block_z[None]
    )
    row = jnp.arange(X6 * Y16, dtype=jnp.int32)
    row_c, row_s = turn(
        (row // Y16 + X6 * col)[:, None] * block_x[None] + (row % Y16)[:, None] * block_y[None]
    )
    scale = 1.0 / (N * math.sqrt(N))
    zeros = jnp.zeros((Y6 * N, 32), F32)
    lanes = jnp.concatenate([zeros, lane_c, lane_s, lane_c, lane_s, zeros], axis=1).astype(BF16)
    zeros = zeros[: X6 * Y16]
    rows = jnp.concatenate([zeros, row_c, -row_s, row_s, row_c, zeros], axis=1) * scale
    block = block_sums(v, c, lanes, rows)
    sent1 = lax.all_to_all(planes_of(v, c[1], tables, block), COL, 0, 0, tiled=True)

    pair_v, pair_c = pair_table()
    occupied = jnp.arange(occupied_energy.shape[0], dtype=jnp.int32)
    valence_energy = jnp.sum(
        jnp.where(valence_index[:, None] == occupied[None, :], occupied_energy[None, :], 0.0),
        axis=1,
    )
    count_v, count_c = valence_index.shape[0], conduction_energy.shape[0]
    energy_v = jnp.sum(
        jnp.where(pair_v[:, None] == np.arange(count_v)[None], valence_energy[None], 0.0), axis=1
    )
    energy_c = jnp.sum(
        jnp.where(pair_c[:, None] == np.arange(count_c)[None], conduction_energy[None], 0.0),
        axis=1,
    )
    gap = (energy_c - energy_v)[:, None]
    omega = jnp.repeat(frequency, 2 * NBLOCK)[None]
    weight = -4.0 * gap / (gap * gap + omega * omega) * (1.0 / math.sqrt(count_v * count_c))

    own0, far0 = first_points(sent0, x_table(), own, far)
    mirrored, low, columns = second_far_points(sent1, x_table(), far, far0)
    mirrored = lax.ppermute(mirrored, COL, mirror_of)
    own1 = second_own_points(low, own)
    pairs = split_pairs(own0, own1, mirrored, columns)
    pairs = lax.all_to_all(pairs, BAND, 0, 0, tiled=True)
    return pl.pallas_call(
        sum_kernel,
        out_shape=jax.ShapeDtypeStruct((128, 128), F32),
        name="pair_sum",
    )(pairs, weight, column_tables())


def solution(mesh):
    fine = Mesh(
        mesh.devices.reshape(4, 2, 2, 4, 2, 2), ("z1", "z0", "yl", "x", "yh", "co")
    )
    return jax.shard_map(
        per_device,
        mesh=fine,
        in_specs=(
            P(BAND, COL, None),
            P(BAND, COL, None),
            P(),
            P(),
            P(),
            P(),
            P(COL),
            P(COL),
        ),
        out_specs=P(COL + BAND, None),
        check_vma=False,
    )
```

time: 156 us -> 133 us (0.85)
  waiting for transfers between devices: 47.7 us -> 35.6 us
  starting transfers between devices: 51.7 us -> 46.3 us
  other arithmetic: 7.37 us -> 3.38 us
    all_to_all x6 -> x3, waiting for transfers between devices: 39.9 us -> 17.4 us  [the longest x1 10.2 us: per_device(): pairs = lax.all_to_all(pairs, BAND, 0, 0, tiled=True)]
    ppermute x7 -> x10, waiting for transfers between devices: 7.86 us -> 18.2 us  [the longest x4 9.13 us: per_device(): lax.ppermute(cells, COL, [(k, k ^ mask) for k in range(SLABS)])]
    all_to_all x6 -> x3, starting transfers between devices: 34.2 us -> 26 us  [the longest x1 10.9 us: per_device(): pairs = lax.all_to_all(pairs, BAND, 0, 0, tiled=True)]
    ppermute x7 -> x10, starting transfers between devices: 15.7 us -> 20.3 us  [the longest x1 5.66 us: per_device(): c.append(lax.ppermute(c[0], 'z1', [(i, i ^ 2) for i in range(4)]))]
    another operation x9 -> x2, other arithmetic: 3.87 us -> 1.15 us
    unnamed x40 -> x60, local copies, waits for them, and re-layouts: 8.89 us -> 11.2 us
    broadcast_in_dim x4 -> x2, local copies, waits for them, and re-layouts: 2 us -> 0.09 us  [the longest x1 0.07 us: per_device(): omega = jnp.repeat(frequency, 2 * NBLOCK)[None]]
    ppermute x1, starting transfers between devices: 1.86 us -> 0.01 us  [per_device(): far_cell = lax.ppermute(gvec_cell, COL, mirror_of)]
  transfers between devices with their start and end apart: 14 -> 14, of which waited for: 8 -> 8; matrix products, arithmetic and copies ran while one was open for 9% -> 5% of each run, Pallas kernels for 12% -> 16%
where the time goes in v2:
time: 133 us; the launch traced here: 131 us
  starting transfers between devices  46.3 us (35%)
  waiting for transfers between devices  35.6 us (27%)
  Pallas kernels  29.4 us (22%)
  local copies, waits for them, and re-layouts  15.4 us (12%)
  other arithmetic  3.38 us (3%)
    unnamed x60, local copies, waits for them, and re-layouts  11.2 us
    all_to_all x1, starting transfers between devices, per_device(): pairs = lax.all_to_all(pairs, BAND, 0, 0, tiled=True)  10.9 us
    all_to_all x1, waiting for transfers between devices, per_device(): pairs = lax.all_to_all(pairs, BAND, 0, 0, tiled=True)  10.2 us
    ppermute x4, waiting for transfers between devices, per_device(): lax.ppermute(cells, COL, [(k, k ^ mask) for k in range(SLABS)])  9.13 us
    pallas_call x2, Pallas kernels, planes_of(): pl.pallas_call(plane_kernel, out_shape=jax.ShapeDtypeStruct((SLABS, per_s...  8.24 us
    all_to_all x1, starting transfers between devices, per_device(): sent0 = lax.all_to_all(planes_of(v, c[0], tables), COL, 0, 0, tiled=True)  7.69 us
    pallas_call x1, Pallas kernels, first_points(): pl.pallas_call(first_kernel, out_shape=(OWN, jax.ShapeDtypeStruct((2 * IT...  7.45 us
    all_to_all x1, starting transfers between devices, per_device(): lax.all_to_all(planes_of(v, c[1], tables, block), COL, 0, 0, tiled=True)  7.36 us
  transfers between devices with their start and end apart: 14, of which 8 were waited for; matrix products, arithmetic and copies ran while one was open for 5% of the time, Pallas kernels for 16%

profile of v2, /device:TPU:6, one launch (start us, length us, event | category | flops | bytes accessed | tf_op | source)
XLA Modules:
  0.0 131.2 jit_solution(3493708458370168003)
XLA Ops:
  0.0 1.1 reshape.83
  1.4 1.7 %collective-permute-start = (bf16[96,576]{1,0:T(8,128)(2,1)S(1)}, bf16[96,576]{1,0:T(8,128)(2,1)S(1)}, u32[]{:S(2)}, u32[]{:S(2)}) collective-permute-start(bf16[96,576]{1,0:T(8,128)(2,1)S(1)} %reshape.84.v0), channel_id=1, source_target_pairs={{0,16},{16,0},{32,48},{48,32},{1,17},{17,1},{33,49},{49,33},{2,18}... | collective-permute-start | bytes 331784 | tf_op jit(solution)/shard_map/ppermute | solution.py:365
  3.0 1.9 %collective-permute-start.1 = (bf16[96,576]{1,0:T(8,128)(2,1)S(1)}, bf16[96,576]{1,0:T(8,128)(2,1)S(1)}, u32[]{:S(2)}, u32[]{:S(2)}) collective-permute-start(bf16[96,576]{1,0:T(8,128)(2,1)S(1)} %reshape.84.v0), channel_id=1, source_target_pairs={{0,32},{16,48},{32,0},{48,16},{1,33},{17,49},{33,1},{49,17},{2,34}... | collective-permute-start | bytes 331784 | tf_op jit(solution)/shard_map/ppermute | solution.py:365
  4.9 1.1 reshape.85
  6.2 3.4 %collective-permute-start.3 = (bf16[96,576]{1,0:T(8,128)(2,1)S(1)}, bf16[96,576]{1,0:T(8,128)(2,1)S(1)}, u32[]{:S(2)}, u32[]{:S(2)}) collective-permute-start(bf16[96,576]{1,0:T(8,128)(2,1)S(1)} %reshape.86), channel_id=1, source_target_pairs={{0,64},{64,0},{128,192},{192,128},{1,65},{65,1},{129,193},{193,129... | collective-permute-start | bytes 331784 | tf_op jit(solution)/shard_map/ppermute | solution.py:366
  11.5 3.2 %collective-permute-start.7 = (s32[16]{0:T(128)S(1)}, s32[16]{0:T(128)S(1)}, u32[]{:S(2)}, u32[]{:S(2)}) collective-permute-start(s32[16]{0:T(128)S(1)} %fusion.29), channel_id=1, source_target_pairs={{0,2},{1,3},{2,0},{3,1},{4,6},{5,7},{6,4},{7,5},{8,10},{9,11},{10,... | collective-permute-start | bytes 200 | tf_op jit(solution)/shard_map/ppermute | solution.py:381
  14.7 1.9 %collective-permute-done.7 = s32[16]{0:T(128)S(1)} collective-permute-done((s32[16]{0:T(128)S(1)}, s32[16]{0:T(128)S(1)}, u32[]{:S(2)}, u32[]{:S(2)}) %collective-permute-start.7) | collective-permute-done | bytes 96 | tf_op jit(solution)/shard_map/ppermute | solution.py:381
  17.4 2.7 %collective-permute-done.8 = s32[16]{0:T(128)S(1)} collective-permute-done((s32[16]{0:T(128)S(1)}, s32[16]{0:T(128)S(1)}, u32[]{:S(2)}, u32[]{:S(2)}) %collective-permute-start.8) | collective-permute-done | bytes 96 | tf_op jit(solution)/shard_map/ppermute | solution.py:381
  20.1 1.4 %collective-permute-start.9 = (s32[16]{0:T(128)S(1)}, s32[16]{0:T(128)S(1)}, u32[]{:S(2)}, u32[]{:S(2)}) collective-permute-start(s32[16]{0:T(128)S(1)} %add.142), channel_id=1, source_target_pairs={{0,8},{1,9},{2,10},{3,11},{4,12},{5,13},{6,14},{7,15},{8,0},{9,1},... | collective-permute-start | bytes 200 | tf_op jit(solution)/shard_map/ppermute | solution.py:381
  21.6 3.5 %collective-permute-done.9 = s32[16]{0:T(128)S(1)} collective-permute-done((s32[16]{0:T(128)S(1)}, s32[16]{0:T(128)S(1)}, u32[]{:S(2)}, u32[]{:S(2)}) %collective-permute-start.9) | collective-permute-done | bytes 96 | tf_op jit(solution)/shard_map/ppermute | solution.py:381
  25.6 1.6 %copy-done.15 = bf16[576,1536]{1,0:T(8,128)(2,1)S(1)} copy-done((bf16[576,1536]{1,0:T(8,128)(2,1)S(1)}, bf16[576,1536]{1,0:T(8,128)(2,1)}, u32[]{:S(2)}) %copy-start.15) | copy-done | bytes 1769496
  27.1 4.1 %planes.2 = bf16[16,48,768]{2,1,0:T(8,128)(2,1)} custom-call(bf16[96,576]{1,0:T(8,128)(2,1)S(1)} %reshape.84.v0, bf16[96,576]{1,0:T(8,128)(2,1)S(1)} %collective-permute-done.v1, bf16[96,576]{1,0:T(8,128)(2,1)S(1)} %collective-permute-done.1.v2, bf16[96,576]{1,0:T(8,128)(2,1)S(1)} %collective-permute-done.2.v3, ...), custom_call_target="tpu_custom_call" | custom-call | flops 2700000000 | bytes 6000000 | tf_op jit(solution)/shard_map/planes/pallas_call | solution.py:161
  31.3 7.7 %all-to-all-start = ((bf16[16,48,768]{2,1,0:T(8,128)(2,1)}), bf16[16,48,768]{2,1,0:T(8,128)(2,1)S(1)}, u32[]{:S(2)}, u32[]{:S(2)}) async-start(bf16[16,48,768]{2,1,0:T(8,128)(2,1)} %planes.2), calls=%async_computation | async-start | bytes 2359296 | tf_op jit(solution)/shard_map/all_to_all | solution.py:370
  39.1 1.1 negate_convert_fusion
  41.7 5.7 %collective-permute-start.5 = (bf16[2,96,576]{2,1,0:T(8,128)(2,1)S(1)}, bf16[2,96,576]{2,1,0:T(8,128)(2,1)S(1)}, u32[]{:S(2)}, u32[]{:S(2)}) collective-permute-start(bf16[2,96,576]{2,1,0:T(8,128)(2,1)S(1)} %pad_maximum_fusion.c_ref.c0_ref), channel_id=1, source_target_pairs={{0,128},{64,192},{128,0},{192,64},{1,129},{65,193},{129,1},{193,65... | collective-permute-start | bytes 663560 | tf_op jit(solution)/shard_map/ppermute | solution.py:367
  47.9 7.2 %collective-permute-done.5.c1_ref.c_ref = bf16[2,96,576]{2,1,0:T(8,128)(2,1)S(1)} collective-permute-done((bf16[2,96,576]{2,1,0:T(8,128)(2,1)S(1)}, bf16[2,96,576]{2,1,0:T(8,128)(2,1)S(1)}, u32[]{:S(2)}, u32[]{:S(2)}) %collective-permute-start.5) | collective-permute-done | bytes 221216 | tf_op jit(solution)/shard_map/ppermute | solution.py:367
  55.8 2.6 %block.1.refs_0_ = f32[32,128]{1,0:T(8,128)} custom-call(bf16[96,576]{1,0:T(8,128)(2,1)} %copy-done.1, bf16[96,576]{1,0:T(8,128)(2,1)} %copy-done.5, bf16[96,576]{1,0:T(8,128)(2,1)} %copy-done.7, bf16[96,576]{1,0:T(8,128)(2,1)} %copy-done.9, bf16[2,96,576]{2,1,0:T(8,128)(2,1)} %copy-done, bf16[2,96,576]{2,1,0:T(8,128)(2,1)} %copy-done.3, ...), custom_call_target="tpu_custom_call" | custom-call | flops 250000000 | bytes 1500000 | tf_op jit(solution)/shard_map/block/pallas_call | solution.py:316
  60.1 1.5 %copy-done.16 = bf16[576,1536]{1,0:T(8,128)(2,1)S(1)} copy-done((bf16[576,1536]{1,0:T(8,128)(2,1)S(1)}, bf16[576,1536]{1,0:T(8,128)(2,1)}, u32[]{:S(2)}) %copy-start.16) | copy-done | bytes 1769496
  61.6 4.1 %planes.3 = bf16[16,48,768]{2,1,0:T(8,128)(2,1)} custom-call(bf16[96,576]{1,0:T(8,128)(2,1)S(1)} %copy-done.2, bf16[96,576]{1,0:T(8,128)(2,1)S(1)} %copy-done.6, bf16[96,576]{1,0:T(8,128)(2,1)S(1)} %copy-done.8, bf16[96,576]{1,0:T(8,128)(2,1)S(1)} %copy-done.10, bf16[2,96,576]{2,1,0:T(8,128)(2,1)S(1)} %copy-done.4, bf16[576,1536]{1,0:T(8,128)(2,1)S(1)} %copy-done.16, ...), custom_call_target="tpu_custom_call" | custom-call | flops 2700000000 | bytes 6000000 | tf_op jit(solution)/shard_map/planes/pallas_call | solution.py:161
  65.8 7.4 %all-to-all-start.1 = ((bf16[16,48,768]{2,1,0:T(8,128)(2,1)}), bf16[16,48,768]{2,1,0:T(8,128)(2,1)S(1)}, u32[]{:S(2)}, u32[]{:S(2)}) async-start(bf16[16,48,768]{2,1,0:T(8,128)(2,1)} %planes.3), calls=%async_computation.1 | async-start | bytes 2359296 | tf_op jit(solution)/shard_map/all_to_all | solution.py:399
  73.7 1.3 copy-done.17
  75.0 7.5 %first_points.1 = (f32[8,2048]{1,0:T(8,128)S(1)}, bf16[8,2048]{1,0:T(8,128)(2,1)S(1)}) custom-call(bf16[16,48,768]{2,1,0:T(8,128)(2,1)S(1)} %all-to-all-done.t_ref, bf16[768,768]{1,0:T(8,128)(2,1)S(1)} %copy-done.17, s32[1,2048]{1,0:T(1,128)S(1)} %bitcast.17, s32[1,2048]{1,0:T(1,128)S(1)} %bitcast.15, s32[1,2048]{1,0:T(1,128)S(1)} %bitcast.21, ...), custom_call_target="tpu_custom_call" | custom-call | flops 5699999744 | bytes 3000000 | tf_op jit(solution)/shard_map/first_points/pallas_call | solution.py:234
  83.1 7.2 %all-to-all-done.1.t_ref = bf16[16,48,768]{2,1,0:T(8,128)(2,1)S(1)} async-done(((bf16[16,48,768]{2,1,0:T(8,128)(2,1)}), bf16[16,48,768]{2,1,0:T(8,128)(2,1)S(1)}, u32[]{:S(2)}, u32[]{:S(2)}) %all-to-all-start.1) | async-done | bytes 1179680 | tf_op jit(solution)/shard_map/all_to_all | solution.py:399
  90.3 1.3 copy-done.18
  91.6 4.3 %second_far_points.1 = (bf16[2,8,2048]{2,1,0:T(8,128)(2,1)S(1)}, bf16[768,768]{1,0:T(8,128)(2,1)S(1)}, f32[16,128]{1,0:T(8,128)S(1)}) custom-call(bf16[16,48,768]{2,1,0:T(8,128)(2,1)S(1)} %all-to-all-done.1.t_ref, bf16[768,768]{1,0:T(8,128)(2,1)S(1)} %copy-done.18, s32[1,2048]{1,0:T(1,128)S(1)} %bitcast.22, s32[1,2048]{1,0:T(1,128)S(1)} %bitcast.20, ...), custom_call_target="tpu_custom_call" | custom-call | flops 3300000000 | bytes 4000000 | tf_op jit(solution)/shard_map/second_far_points/pallas_call | solution.py:247
  96.5 2.2 %collective-permute-start.10 = (bf16[2,8,2048]{2,1,0:T(8,128)(2,1)S(1)}, bf16[2,8,2048]{2,1,0:T(8,128)(2,1)S(1)}, u32[]{:S(2)}, u32[]{:S(2)}) collective-permute-start(bf16[2,8,2048]{2,1,0:T(8,128)(2,1)S(1)} %get-tuple-element.13), channel_id=1, source_target_pairs={{0,15},{1,14},{2,13},{3,12},{4,11},{5,10},{6,9},{7,8},{8,7},{9,6},... | collective-permute-start | bytes 196616 | tf_op jit(solution)/shard_map/ppermute | solution.py:421
  98.7 3.2 %second_own_points.1.own1_ref = f32[8,2048]{1,0:T(8,128)S(1)} custom-call(bf16[768,768]{1,0:T(8,128)(2,1)S(1)} %get-tuple-element.12.low, s32[1,2048]{1,0:T(1,128)S(1)} %bitcast.18, s32[1,2048]{1,0:T(1,128)S(1)} %bitcast.16), custom_call_target="tpu_custom_call" | custom-call | flops 2400000000 | bytes 1300000 | tf_op jit(solution)/shard_map/second_own_points/pallas_call | solution.py:263
  102.5 1.9 %collective-permute-done.10.far_ref = bf16[2,8,2048]{2,1,0:T(8,128)(2,1)S(1)} collective-permute-done((bf16[2,8,2048]{2,1,0:T(8,128)(2,1)S(1)}, bf16[2,8,2048]{2,1,0:T(8,128)(2,1)S(1)}, u32[]{:S(2)}, u32[]{:S(2)}) %collective-permute-start.10) | collective-permute-done | bytes 65568 | tf_op jit(solution)/shard_map/ppermute | solution.py:421
  105.0 1.6 %split.1 = bf16[16,48,128]{2,1,0:T(8,128)(2,1)} custom-call(f32[8,2048]{1,0:T(8,128)} %copy-done.11, f32[8,2048]{1,0:T(8,128)} %copy-done.12, bf16[2,8,2048]{2,1,0:T(8,128)(2,1)} %copy-done.22, f32[16,128]{1,0:T(8,128)} %copy-done.14), custom_call_target="tpu_custom_call" | custom-call | flops 1000000 | bytes 500000 | tf_op jit(solution)/shard_map/split/pallas_call | solution.py:291
  106.6 10.9 %all-to-all-start.2 = ((bf16[16,48,128]{2,1,0:T(8,128)(2,1)}), bf16[16,48,128]{2,1,0:T(8,128)(2,1)S(1)}, u32[]{:S(2)}, u32[]{:S(2)}) async-start(bf16[16,48,128]{2,1,0:T(8,128)(2,1)} %split.1), calls=%async_computation.2 | async-start | bytes 393216 | tf_op jit(solution)/shard_map/all_to_all | solution.py:424
  118.4 10.2 %all-to-all-done.2.pairs_ref = bf16[16,48,128]{2,1,0:T(8,128)(2,1)S(1)} async-done(((bf16[16,48,128]{2,1,0:T(8,128)(2,1)}), bf16[16,48,128]{2,1,0:T(8,128)(2,1)S(1)}, u32[]{:S(2)}, u32[]{:S(2)}) %all-to-all-start.2) | async-done | bytes 196640 | tf_op jit(solution)/shard_map/all_to_all | solution.py:424
  129.2 2.0 %pair_sum.1 = f32[128,128]{1,0:T(8,128)} custom-call(bf16[16,48,128]{2,1,0:T(8,128)(2,1)} %copy-done.21, f32[256,128]{1,0:T(8,128)} %divide_multiply_fusion.weight_ref, bf16[2,128,128]{2,1,0:T(8,128)(2,1)} %constant.171.clone.column_ref), custom_call_target="tpu_custom_call" | custom-call | tf_op jit(solution)/shard_map/pair_sum/pallas_call | solution.py:425
  (100 shorter events, 12.0 us)
Async XLA Ops:
  0.0 25.1 %copy-start.24 = (s32[2048]{0:T(1024)S(1)}, s32[2048]{0:T(1024)}, u32[]{:S(2)}) copy-start(s32[2048]{0:T(1024)} %param.21) | copy-start | bytes 24580
  1.3 30.0 %copy-start.1 = (bf16[96,576]{1,0:T(8,128)(2,1)}, bf16[96,576]{1,0:T(8,128)(2,1)S(1)}, u32[]{:S(2)}) copy-start(bf16[96,576]{1,0:T(8,128)(2,1)S(1)} %reshape.84.v0) | copy-start | bytes 331780
  1.3 24.2 %copy-start.19 = (bf16[768,768]{1,0:T(8,128)(2,1)S(1)}, bf16[768,768]{1,0:T(8,128)(2,1)}, u32[]{:S(2)}) copy-start(bf16[768,768]{1,0:T(8,128)(2,1)} %constant.167.clone.row_ref) | copy-start | bytes 3538948
  1.3 24.2 %copy-start.20 = (f32[2,16,768]{2,1,0:T(8,128)S(1)}, f32[2,16,768]{2,1,0:T(8,128)}, u32[]{:S(2)}) copy-start(f32[2,16,768]{2,1,0:T(8,128)} %constant.166.clone.twiddle_ref) | copy-start | bytes 294916
  1.4 24.1 %collective-permute-start = (bf16[96,576]{1,0:T(8,128)(2,1)S(1)}, bf16[96,576]{1,0:T(8,128)(2,1)S(1)}, u32[]{:S(2)}, u32[]{:S(2)}) collective-permute-start(bf16[96,576]{1,0:T(8,128)(2,1)S(1)} %reshape.84.v0), channel_id=1, source_target_pairs={{0,16},{16,0},{32,48},{48,32},{1,17},{17,1},{33,49},{49,33},{2,18}... | collective-permute-start | bytes 331784 | tf_op jit(solution)/shard_map/ppermute | solution.py:365
  3.0 22.5 %collective-permute-start.1 = (bf16[96,576]{1,0:T(8,128)(2,1)S(1)}, bf16[96,576]{1,0:T(8,128)(2,1)S(1)}, u32[]{:S(2)}, u32[]{:S(2)}) collective-permute-start(bf16[96,576]{1,0:T(8,128)(2,1)S(1)} %reshape.84.v0), channel_id=1, source_target_pairs={{0,32},{16,48},{32,0},{48,16},{1,33},{17,49},{33,1},{49,17},{2,34}... | collective-permute-start | bytes 331784 | tf_op jit(solution)/shard_map/ppermute | solution.py:365
  4.9 20.6 %collective-permute-start.2 = (bf16[96,576]{1,0:T(8,128)(2,1)S(1)}, bf16[96,576]{1,0:T(8,128)(2,1)S(1)}, u32[]{:S(2)}, u32[]{:S(2)}) collective-permute-start(bf16[96,576]{1,0:T(8,128)(2,1)S(1)} %reshape.84.v0), channel_id=1, source_target_pairs={{0,48},{16,32},{32,16},{48,0},{1,49},{17,33},{33,17},{49,1},{2,50}... | collective-permute-start | bytes 331784 | tf_op jit(solution)/shard_map/ppermute | solution.py:365
  6.2 19.2 %collective-permute-start.3 = (bf16[96,576]{1,0:T(8,128)(2,1)S(1)}, bf16[96,576]{1,0:T(8,128)(2,1)S(1)}, u32[]{:S(2)}, u32[]{:S(2)}) collective-permute-start(bf16[96,576]{1,0:T(8,128)(2,1)S(1)} %reshape.86), channel_id=1, source_target_pairs={{0,64},{64,0},{128,192},{192,128},{1,65},{65,1},{129,193},{193,129... | collective-permute-start | bytes 331784 | tf_op jit(solution)/shard_map/ppermute | solution.py:366
  10.3 1.2 collective-permute-start.6
  11.5 5.0 %collective-permute-start.7 = (s32[16]{0:T(128)S(1)}, s32[16]{0:T(128)S(1)}, u32[]{:S(2)}, u32[]{:S(2)}) collective-permute-start(s32[16]{0:T(128)S(1)} %fusion.29), channel_id=1, source_target_pairs={{0,2},{1,3},{2,0},{3,1},{4,6},{5,7},{6,4},{7,5},{8,10},{9,11},{10,... | collective-permute-start | bytes 200 | tf_op jit(solution)/shard_map/ppermute | solution.py:381
  16.5 3.5 %collective-permute-start.8 = (s32[16]{0:T(128)S(1)}, s32[16]{0:T(128)S(1)}, u32[]{:S(2)}, u32[]{:S(2)}) collective-permute-start(s32[16]{0:T(128)S(1)} %fusion.30), channel_id=1, source_target_pairs={{0,4},{1,5},{2,6},{3,7},{4,0},{5,1},{6,2},{7,3},{8,12},{9,13},{10,... | collective-permute-start | bytes 200 | tf_op jit(solution)/shard_map/ppermute | solution.py:381
  20.1 5.0 %collective-permute-start.9 = (s32[16]{0:T(128)S(1)}, s32[16]{0:T(128)S(1)}, u32[]{:S(2)}, u32[]{:S(2)}) collective-permute-start(s32[16]{0:T(128)S(1)} %add.142), channel_id=1, source_target_pairs={{0,8},{1,9},{2,10},{3,11},{4,12},{5,13},{6,14},{7,15},{8,0},{9,1},... | collective-permute-start | bytes 200 | tf_op jit(solution)/shard_map/ppermute | solution.py:381
  25.1 48.5 %collective-permute-start.4 = (s32[2048]{0:T(1024)S(1)}, s32[2048]{0:T(1024)S(1)}, u32[]{:S(2)}, u32[]{:S(2)}) collective-permute-start(s32[2048]{0:T(1024)S(1)} %copy-done.24), channel_id=1, source_target_pairs={{0,15},{1,14},{2,13},{3,12},{4,11},{5,10},{6,9},{7,8},{8,7},{9,6},... | collective-permute-start | bytes 24584 | tf_op jit(solution)/shard_map/ppermute | solution.py:373
  25.5 16.2 %copy-start = (bf16[2,96,576]{2,1,0:T(8,128)(2,1)}, bf16[2,96,576]{2,1,0:T(8,128)(2,1)S(1)}, u32[]{:S(2)}) copy-start(bf16[2,96,576]{2,1,0:T(8,128)(2,1)S(1)} %pad_maximum_fusion.c_ref.c0_ref) | copy-start | bytes 663556
  25.5 5.8 %copy-start.5 = (bf16[96,576]{1,0:T(8,128)(2,1)}, bf16[96,576]{1,0:T(8,128)(2,1)S(1)}, u32[]{:S(2)}) copy-start(bf16[96,576]{1,0:T(8,128)(2,1)S(1)} %collective-permute-done.v1) | copy-start | bytes 331780
  25.5 5.8 %copy-start.7 = (bf16[96,576]{1,0:T(8,128)(2,1)}, bf16[96,576]{1,0:T(8,128)(2,1)S(1)}, u32[]{:S(2)}) copy-start(bf16[96,576]{1,0:T(8,128)(2,1)S(1)} %collective-permute-done.1.v2) | copy-start | bytes 331780
  27.1 4.1 %copy-start.9 = (bf16[96,576]{1,0:T(8,128)(2,1)}, bf16[96,576]{1,0:T(8,128)(2,1)S(1)}, u32[]{:S(2)}) copy-start(bf16[96,576]{1,0:T(8,128)(2,1)S(1)} %collective-permute-done.2.v3) | copy-start | bytes 331780
  31.3 34.5 %all-to-all-start = ((bf16[16,48,768]{2,1,0:T(8,128)(2,1)}), bf16[16,48,768]{2,1,0:T(8,128)(2,1)S(1)}, u32[]{:S(2)}, u32[]{:S(2)}) async-start(bf16[16,48,768]{2,1,0:T(8,128)(2,1)} %planes.2), calls=%async_computation | async-start | bytes 2359296 | tf_op jit(solution)/shard_map/all_to_all | solution.py:370
  41.3 17.1 %copy-start.2 = (bf16[96,576]{1,0:T(8,128)(2,1)S(1)}, bf16[96,576]{1,0:T(8,128)(2,1)}, u32[]{:S(2)}) copy-start(bf16[96,576]{1,0:T(8,128)(2,1)} %copy-done.1) | copy-start | bytes 331780
  41.3 17.1 %copy-start.6 = (bf16[96,576]{1,0:T(8,128)(2,1)S(1)}, bf16[96,576]{1,0:T(8,128)(2,1)}, u32[]{:S(2)}) copy-start(bf16[96,576]{1,0:T(8,128)(2,1)} %copy-done.5) | copy-start | bytes 331780
  41.3 17.1 %copy-start.8 = (bf16[96,576]{1,0:T(8,128)(2,1)S(1)}, bf16[96,576]{1,0:T(8,128)(2,1)}, u32[]{:S(2)}) copy-start(bf16[96,576]{1,0:T(8,128)(2,1)} %copy-done.7) | copy-start | bytes 331780
  41.3 17.1 %copy-start.10 = (bf16[96,576]{1,0:T(8,128)(2,1)S(1)}, bf16[96,576]{1,0:T(8,128)(2,1)}, u32[]{:S(2)}) copy-start(bf16[96,576]{1,0:T(8,128)(2,1)} %copy-done.9) | copy-start | bytes 331780
  41.7 13.4 %collective-permute-start.5 = (bf16[2,96,576]{2,1,0:T(8,128)(2,1)S(1)}, bf16[2,96,576]{2,1,0:T(8,128)(2,1)S(1)}, u32[]{:S(2)}, u32[]{:S(2)}) collective-permute-start(bf16[2,96,576]{2,1,0:T(8,128)(2,1)S(1)} %pad_maximum_fusion.c_ref.c0_ref), channel_id=1, source_target_pairs={{0,128},{64,192},{128,0},{192,64},{1,129},{65,193},{129,1},{193,65... | collective-permute-start | bytes 663560 | tf_op jit(solution)/shard_map/ppermute | solution.py:367
  65.7 7.4 %copy-start.23 = (f32[4096]{0:T(1024)S(1)}, f32[4096]{0:T(1024)}, u32[]{:S(2)}) copy-start(f32[4096]{0:T(1024)} %param.18) | copy-start | bytes 49156
  65.7 7.4 %copy-start.27 = (s32[16]{0:T(128)S(1)}, s32[16]{0:T(128)}, u32[]{:S(2)}) copy-start(s32[16]{0:T(128)} %param.17) | copy-start | bytes 196
  65.7 7.7 %copy-start.25 = (pred[256,16]{0,1:T(8,128)(4,1)S(1)}, pred[256,16]{0,1:T(8,128)(4,1)}, u32[]{:S(2)}) copy-start(pred[256,16]{0,1:T(8,128)(4,1)} %constant.168.clone) | copy-start | bytes 12292
  65.7 7.7 %copy-start.26 = (pred[256,16]{0,1:T(8,128)(4,1)S(1)}, pred[256,16]{0,1:T(8,128)(4,1)}, u32[]{:S(2)}) copy-start(pred[256,16]{0,1:T(8,128)(4,1)} %constant.169.clone) | copy-start | bytes 12292
  65.7 7.7 %copy-start.28 = (f32[16]{0:T(128)S(1)}, f32[16]{0:T(128)}, u32[]{:S(2)}) copy-start(f32[16]{0:T(128)} %param.19) | copy-start | bytes 196
  65.7 7.8 %copy-start.29 = (f32[4]{0:T(128)S(1)}, f32[4]{0:T(128)}, u32[]{:S(2)}) copy-start(f32[4]{0:T(128)} %param.20) | copy-start | bytes 52
  65.8 24.6 %all-to-all-start.1 = ((bf16[16,48,768]{2,1,0:T(8,128)(2,1)}), bf16[16,48,768]{2,1,0:T(8,128)(2,1)S(1)}, u32[]{:S(2)}, u32[]{:S(2)}) async-start(bf16[16,48,768]{2,1,0:T(8,128)(2,1)} %planes.3), calls=%async_computation.1 | async-start | bytes 2359296 | tf_op jit(solution)/shard_map/all_to_all | solution.py:399
  96.5 7.8 %collective-permute-start.10 = (bf16[2,8,2048]{2,1,0:T(8,128)(2,1)S(1)}, bf16[2,8,2048]{2,1,0:T(8,128)(2,1)S(1)}, u32[]{:S(2)}, u32[]{:S(2)}) collective-permute-start(bf16[2,8,2048]{2,1,0:T(8,128)(2,1)S(1)} %get-tuple-element.13), channel_id=1, source_target_pairs={{0,15},{1,14},{2,13},{3,12},{4,11},{5,10},{6,9},{7,8},{8,7},{9,6},... | collective-permute-start | bytes 196616 | tf_op jit(solution)/shard_map/ppermute | solution.py:421
  106.6 21.9 %all-to-all-start.2 = ((bf16[16,48,128]{2,1,0:T(8,128)(2,1)}), bf16[16,48,128]{2,1,0:T(8,128)(2,1)S(1)}, u32[]{:S(2)}, u32[]{:S(2)}) async-start(bf16[16,48,128]{2,1,0:T(8,128)(2,1)} %split.1), calls=%async_computation.2 | async-start | bytes 393216 | tf_op jit(solution)/shard_map/all_to_all | solution.py:424
  (12 other events, 11.1 us)

commit v3 on v2

--- a/solution.py
+++ b/solution.py
@@ -101,9 +101,9 @@
             for half in range(2):
                 for item in range(ITEMS):
                     slot_v = 2 * (item // 2) + half
-                    slot_c = 2 * chunk + item % 2
+                    slot_c = (0, 1, 3, 2)[2 * chunk + item % 2]
                     valence.append(z1 * 4 + (group ^ slot_v))
-                    conduction.append((z1 ^ slot_c) * 4 + group)
+                    conduction.append((z1 - slot_c) % 4 * 4 + group)
     return np.array(valence), np.array(conduction)
 
 
@@ -118,19 +118,70 @@
     return bf16(tables.reshape(2, 128, 128))
 
 
-def plane_kernel(v0, v1, v2, v3, c_ref, lane_ref, twiddle_ref, row_ref, *refs):
-    *block_ref, out_ref, low_ref = refs
+VMEM = pl.BlockSpec(memory_space=pltpu.VMEM)
+HBM = pl.BlockSpec(memory_space=pltpu.HBM)
+LANE_CUTS = 3
+
+
+def in_hbm(x):
+    return pltpu.with_memory_space_constraint(jnp.asarray(x), pltpu.HBM)
+
+
+X_CUTS = 3
+
+
+def cut_copies(source, target, sems, cuts, dim):
+    size = source.shape[dim] // cuts
+    moves = []
+    for i in range(cuts):
+        window = pl.ds(i * size, size)
+        spot = (window,) if dim == 0 else (slice(None), window)
+        moves.append(pltpu.make_async_copy(source.at[spot], target.at[spot], sems.at[i]))
+        moves[-1].start()
+    return moves
+
+
+def plane_kernel(v0, v1, v2, v3, c0, c1, lane_hbm, row_hbm, twiddle_ref, *refs, through):
+    *refs, low_ref, lane_ref, row_ref, slab_ref, lane_sems, row_sem, slab_sems, keep_sems = refs
+    lane_moves = cut_copies(lane_hbm, lane_ref, lane_sems, LANE_CUTS, 1)
+    row_move = pltpu.make_async_copy(row_hbm, row_ref, row_sem)
+    row_move.start()
+    if through:
+        block_ref = None
+        out_ref = refs[through]
+        kept = [
+            pltpu.make_async_copy(refs[i], refs[through + 1 + i], keep_sems.at[i])
+            for i in range(through)
+        ]
+    else:
+        block_ref, out_ref = refs
+        kept = []
+    for move in kept:
+        move.start()
     waves = (v0, v1, v2, v3)
+    waves_c = (c0, c1)
     rows = X6 * Y16
     twiddle_c = twiddle_ref[0][None]
     twiddle_s = twiddle_ref[1][None]
+    width = 2 * WIDE // LANE_CUTS
     for item in range(ITEMS):
-        wave_c = c_ref[item % 2]
+        wave_c = waves_c[item % 2][...]
         pairs = jnp.concatenate(
             [waves[2 * (item // 2)][...] * wave_c, waves[2 * (item // 2) + 1][...] * wave_c],
             axis=0,
         )
-        moved = jnp.dot(pairs, lane_ref[...], preferred_element_type=F32)
+        parts = []
+        for i in range(LANE_CUTS):
+            if item == 0:
+                lane_moves[i].wait()
+            parts.append(
+                jnp.dot(
+                    pairs,
+                    lane_ref[:, i * width : (i + 1) * width],
+                    preferred_element_type=F32,
+                )
+            )
+        moved = jnp.concatenate(parts, axis=1)
         real = moved[:rows, :WIDE] - moved[rows:, WIDE:]
         imag = moved[:rows, WIDE:] + moved[rows:, :WIDE]
         real = real.reshape(X6, Y16, WIDE)
@@ -141,8 +192,10 @@
         low_ref[(ITEMS + item) * rows : (ITEMS + item + 1) * rows, :] = turned_i.reshape(
             rows, WIDE
         ).astype(BF16)
+    row_move.wait()
     per_slab = ITEMS * 2 * X6
     count = SLABS // 4
+    moves = []
     for part in range(4):
         planes = jnp.dot(
             row_ref[part * count * per_slab : (part + 1) * count * per_slab, :],
@@ -150,24 +203,56 @@
             preferred_element_type=F32,
         ).reshape(count, per_slab, WIDE)
         slabs = slice(part * count, (part + 1) * count)
-        out_ref[slabs] = planes.astype(BF16)
-        if block_ref:
-            spare = planes[:, :32, SPARE:] + block_ref[0][...][None]
-            out_ref[slabs, :32, SPARE:] = spare.astype(BF16)
-
-
-def planes_of(v, c, tables, *block):
+        slab_ref[slabs] = planes.astype(BF16)
+        if block_ref is not None:
+            spare = planes[:, :32, SPARE:] + block_ref[...][None]
+            slab_ref[slabs, :32, SPARE:] = spare.astype(BF16)
+        moves.append(
+            pltpu.make_async_copy(
+                slab_ref.at[pl.ds(part * count, count)],
+                out_ref.at[pl.ds(part * count, count)],
+                slab_sems.at[part],
+            )
+        )
+        moves[-1].start()
+    for move in (*moves, *kept):
+        move.wait()
+
+
+def planes_of(v, c, tables, block=(), through=()):
     per_slab = ITEMS * 2 * X6
-    return pl.pallas_call(
-        plane_kernel,
-        out_shape=jax.ShapeDtypeStruct((SLABS, per_slab, WIDE), BF16),
-        scratch_shapes=[pltpu.VMEM((2 * ITEMS * X6 * Y16, WIDE), BF16)],
-        compiler_params=pltpu.CompilerParams(vmem_limit_bytes=40 << 20),
+    lane, row, twiddle = tables
+    extra = (*block, *through)
+    return pl.pallas_call(
+        functools.partial(plane_kernel, through=len(through)),
+        out_shape=[
+            pltpu.HBM((SLABS, per_slab, WIDE), BF16),
+            *(pltpu.HBM(x.shape, x.dtype) for x in through),
+        ],
+        in_specs=[VMEM] * 6
+        + [HBM] * 2
+        + [VMEM] * (1 + len(block))
+        + [pl.BlockSpec(memory_space=pl.ANY)] * len(through),
+        out_specs=[HBM] * (1 + len(through)),
+        scratch_shapes=[
+            pltpu.VMEM((2 * ITEMS * X6 * Y16, WIDE), BF16),
+            pltpu.VMEM(lane.shape, BF16),
+            pltpu.VMEM(row.shape, BF16),
+            pltpu.VMEM((SLABS, per_slab, WIDE), BF16),
+            pltpu.SemaphoreType.DMA((LANE_CUTS,)),
+            pltpu.SemaphoreType.DMA,
+            pltpu.SemaphoreType.DMA((4,)),
+            pltpu.SemaphoreType.DMA((max(len(through), 1),)),
+        ],
+        compiler_params=pltpu.CompilerParams(vmem_limit_bytes=16 << 20),
         cost_estimate=pl.CostEstimate(
-            flops=2_700_000_000, bytes_accessed=6_000_000, transcendentals=0
+            flops=PLANES_FLOPS, bytes_accessed=100_000, transcendentals=0
         ),
         name="planes",
-    )(*v, c, *tables, *block)
+    )(*v, *c, in_hbm(lane), in_hbm(row), twiddle, *extra)
+
+
+PLANES_FLOPS = 50_000_000
 
 
 def pick(density_ref, flat_ref, kx_ref, store):
@@ -184,16 +269,22 @@
     lax.fori_loop(0, G_DEV // TILE, body, 0)
 
 
-def transform_x(t_ref, x_ref, density_ref):
-    density_ref[...] = jnp.dot(
-        x_ref[...],
-        t_ref[...].reshape(SLABS * ITEMS * 2 * X6, WIDE),
-        preferred_element_type=F32,
-    ).astype(BF16)
-
-
-def first_kernel(t_ref, x_ref, own_ref, own_kx_ref, far_ref, far_kx_ref, own_out, far_out, low):
-    transform_x(t_ref, x_ref, low)
+def transform_x(t_ref, x_hbm, x_ref, sems, density_ref):
+    moves = cut_copies(x_hbm, x_ref, sems, X_CUTS, 0)
+    size = x_ref.shape[0] // X_CUTS
+    planes = t_ref[...].reshape(SLABS * ITEMS * 2 * X6, WIDE)
+    for i in range(X_CUTS):
+        moves[i].wait()
+        window = slice(i * size, (i + 1) * size)
+        density_ref[window, :] = jnp.dot(
+            x_ref[window, :], planes, preferred_element_type=F32
+        ).astype(BF16)
+
+
+def first_kernel(
+    t_ref, x_hbm, own_ref, own_kx_ref, far_ref, far_kx_ref, own_out, far_out, low, x_ref, sems
+):
+    transform_x(t_ref, x_hbm, x_ref, sems, low)
 
     def store_far(lanes, values):
         far_out[:, lanes] = values.astype(BF16)
@@ -205,8 +296,10 @@
     pick(low, own_ref, own_kx_ref, store_own)
 
 
-def second_far_kernel(t_ref, x_ref, far_ref, far_kx_ref, first_ref, far_out, low, block_out):
-    transform_x(t_ref, x_ref, low)
+def second_far_kernel(
+    t_ref, x_hbm, far_ref, far_kx_ref, first_ref, far_out, low, block_out, x_ref, sems
+):
+    transform_x(t_ref, x_hbm, x_ref, sems, low)
     far_out[0] = first_ref[...]
 
     def store_far(lanes, values):
@@ -228,19 +321,24 @@
 
 OWN = jax.ShapeDtypeStruct((2 * ITEMS, G_DEV), F32)
 LOW = (2 * ITEMS * N, WIDE)
+X_SCRATCH = [
+    pltpu.VMEM((2 * ITEMS * N, SLABS * ITEMS * 2 * X6), BF16),
+    pltpu.SemaphoreType.DMA((X_CUTS,)),
+]
 
 
 def first_points(planes, table, own, far):
     return pl.pallas_call(
         first_kernel,
         out_shape=(OWN, jax.ShapeDtypeStruct((2 * ITEMS, G_DEV), BF16)),
-        scratch_shapes=[pltpu.VMEM(LOW, BF16)],
-        compiler_params=pltpu.CompilerParams(vmem_limit_bytes=40 << 20),
+        in_specs=[VMEM, HBM] + [VMEM] * 4,
+        scratch_shapes=[pltpu.VMEM(LOW, BF16), *X_SCRATCH],
+        compiler_params=pltpu.CompilerParams(vmem_limit_bytes=16 << 20),
         cost_estimate=pl.CostEstimate(
-            flops=5_700_000_000, bytes_accessed=3_000_000, transcendentals=0
+            flops=100_000_000, bytes_accessed=100_000, transcendentals=0
         ),
         name="first_points",
-    )(planes, table, *own, *far)
+    )(planes, in_hbm(table), *own, *far)
 
 
 def second_far_points(planes, table, far, first):
@@ -251,19 +349,21 @@
             jax.ShapeDtypeStruct(LOW, BF16),
             jax.ShapeDtypeStruct((16, 128), F32),
         ),
-        compiler_params=pltpu.CompilerParams(vmem_limit_bytes=40 << 20),
+        in_specs=[VMEM, HBM] + [VMEM] * 3,
+        scratch_shapes=X_SCRATCH,
+        compiler_params=pltpu.CompilerParams(vmem_limit_bytes=16 << 20),
         cost_estimate=pl.CostEstimate(
-            flops=3_300_000_000, bytes_accessed=4_000_000, transcendentals=0
+            flops=100_000_000, bytes_accessed=100_000, transcendentals=0
         ),
         name="second_far_points",
-    )(planes, table, *far, first)
+    )(planes, in_hbm(table), *far, first)
 
 
 def second_own_points(low, own):
     return pl.pallas_call(
         second_own_kernel,
         out_shape=OWN,
-        compiler_params=pltpu.CompilerParams(vmem_limit_bytes=40 << 20),
+        compiler_params=pltpu.CompilerParams(vmem_limit_bytes=16 << 20),
         cost_estimate=pl.CostEstimate(
             flops=2_400_000_000, bytes_accessed=1_300_000, transcendentals=0
         ),
@@ -291,6 +391,7 @@
     return pl.pallas_call(
         split_kernel,
         out_shape=jax.ShapeDtypeStruct((16, 48, 128), BF16),
+        compiler_params=pltpu.CompilerParams(vmem_limit_bytes=4 << 20),
         cost_estimate=pl.CostEstimate(
             flops=1_000_000, bytes_accessed=500_000, transcendentals=0
         ),
@@ -298,12 +399,12 @@
     )(own0, own1, far, block)
 
 
-def block_kernel(v0, v1, v2, v3, c0_ref, c1_ref, lane_ref, row_ref, out_ref):
+def block_kernel(v0, v1, v2, v3, c0, c1, c2, c3, lane_ref, row_ref, out_ref):
     waves = (v0, v1, v2, v3)
-    for chunk, c_ref in enumerate((c0_ref, c1_ref)):
+    for chunk, waves_c in enumerate(((c0, c1), (c2, c3))):
         for half in range(2):
             for item in range(ITEMS):
-                pair = waves[2 * (item // 2) + half][...] * c_ref[item % 2]
+                pair = waves[2 * (item // 2) + half][...] * waves_c[item % 2][...]
                 sums = jnp.dot(pair, lane_ref[...], preferred_element_type=F32) * row_ref[...]
                 total = sums.sum(axis=0, keepdims=True)
                 high = total.astype(BF16).astype(F32)
@@ -316,8 +417,9 @@
     return pl.pallas_call(
         block_kernel,
         out_shape=jax.ShapeDtypeStruct((32, 128), F32),
+        compiler_params=pltpu.CompilerParams(vmem_limit_bytes=4 << 20),
         cost_estimate=pl.CostEstimate(
-            flops=250_000_000, bytes_accessed=1_500_000, transcendentals=0
+            flops=10_000_000, bytes_accessed=100_000, transcendentals=0
         ),
         name="block",
     )(*v, *c, lanes, rows)
@@ -342,9 +444,13 @@
     return wave.reshape(X6, Y6, Y16, N).transpose(0, 2, 1, 3).reshape(X6 * Y16, Y6 * N)
 
 
-def turn(phase):
-    angle = (phase % N).astype(F32) * (2.0 * math.pi / N)
-    return jnp.cos(angle), -jnp.sin(angle)
+def spread(cells, masks):
+    arrived = [lax.ppermute(cells, COL, [(k, k ^ mask) for k in range(SLABS)]) for mask in masks]
+    return sum(arrived, cells)
+
+
+def cosine(phase):
+    return jnp.cos((phase % N).astype(F32) * (2.0 * math.pi / N))
 
 
 def per_device(
@@ -363,40 +469,45 @@
     v = [wave_v]
     for mask in (1, 2, 3):
         v.append(lax.ppermute(wave_v, VGROUP, [(i, i ^ mask) for i in range(4)]))
-    c = [jnp.stack([wave_c, lax.ppermute(wave_c, "z1", [(i, i ^ 1) for i in range(4)])])]
-    c.append(lax.ppermute(c[0], "z1", [(i, i ^ 2) for i in range(4)]))
-
-    tables = (lane_table(), twiddle_table(), row_table())
-    sent0 = lax.all_to_all(planes_of(v, c[0], tables), COL, 0, 0, tiled=True)
+    ahead = [(i, (i + 1) % 4) for i in range(4)]
+    behind = [(i, (i + 3) % 4) for i in range(4)]
+    c = [wave_c, lax.ppermute(wave_c, "z1", ahead)]
+
+    spots = jnp.arange(128, dtype=jnp.int32)
+    cells = jnp.where(spots % NBLOCK == col, block_cell[0], 0)
+    cells = spread(cells, (1, 2, 3))
+
+    tables = (lane_table(), row_table(), twiddle_table())
+    through = (wave_c, c[1], cells[None], gvec_cell.reshape(16, 128))
+    planes0, wave_c, wave_c1, cells, list_cell = planes_of(v, c, tables, through=through)
+    sent0 = lax.all_to_all(planes0, COL, 0, 0, tiled=True)
+    c.append(lax.ppermute(wave_c, "z1", behind))
+    c.append(lax.ppermute(wave_c1, "z1", ahead))
+
+    cells = spread(cells[0], (4, 8, 12))
+    block_x = cells // 576
+    block_y = spots % NBLOCK * 6 + cells // N % 6
+    block_z = cells % N
+    group = spots // NBLOCK - 2
+    quarter = N // 4
+    lane = jnp.arange(Y6 * N, dtype=jnp.int32)[:, None]
+    lanes = cosine(
+        lane // N * 16 * block_y + lane % N * block_z + jnp.where(group % 2 == 1, quarter, 0)
+    ).astype(BF16)
+    row = jnp.arange(X6 * Y16, dtype=jnp.int32)[:, None]
+    shift = jnp.where(group == 1, 3 * quarter, jnp.where(group == 2, quarter, 0))
+    rows = cosine((row // Y16 + X6 * col) * block_x + row % Y16 * block_y + shift)
+    scale = 1.0 / (N * math.sqrt(N))
+    rows = jnp.where((group >= 0) & (group < 4), rows * scale, 0.0)
+    block = block_sums(v, c, lanes, rows)
+    (planes1,) = planes_of(v, c[2:], tables, block=(block,))
+    sent1 = lax.all_to_all(planes1, COL, 0, 0, tiled=True)
 
     mirror_of = [(k, SLABS - 1 - k) for k in range(SLABS)]
-    far_cell = lax.ppermute(gvec_cell, COL, mirror_of)
+    far_cell = lax.ppermute(list_cell, COL, mirror_of).reshape(G_DEV)
     far_x, far_y, far_z = far_cell // 576, far_cell // N % 6, far_cell % N
     own = ((gvec_cell % 576)[None], (gvec_cell // 576)[None])
     far = (((6 - far_y) * N + (N - far_z) % N)[None], ((N - far_x) % N)[None])
-
-    spots = jnp.arange(NBLOCK, dtype=jnp.int32)
-    cells = jnp.where(spots == col, block_cell[0], 0)
-    for mask in (1, 2, 4, 8):
-        cells = cells + lax.ppermute(cells, COL, [(k, k ^ mask) for k in range(SLABS)])
-    block_x = cells // 576
-    block_y = spots * 6 + cells // N % 6
-    block_z = cells % N
-    lane = jnp.arange(Y6 * N, dtype=jnp.int32)
-    lane_c, lane_s = turn(
-        (lane // N * 16)[:, None] * block_y[None] + (lane % N)[:, None] * block_z[None]
-    )
-    row = jnp.arange(X6 * Y16, dtype=jnp.int32)
-    row_c, row_s = turn(
-        (row // Y16 + X6 * col)[:, None] * block_x[None] + (row % Y16)[:, None] * block_y[None]
-    )
-    scale = 1.0 / (N * math.sqrt(N))
-    zeros = jnp.zeros((Y6 * N, 32), F32)
-    lanes = jnp.concatenate([zeros, lane_c, lane_s, lane_c, lane_s, zeros], axis=1).astype(BF16)
-    zeros = zeros[: X6 * Y16]
-    rows = jnp.concatenate([zeros, row_c, -row_s, row_s, row_c, zeros], axis=1) * scale
-    block = block_sums(v, c, lanes, rows)
-    sent1 = lax.all_to_all(planes_of(v, c[1], tables, block), COL, 0, 0, tiled=True)
 
     pair_v, pair_c = pair_table()
     occupied = jnp.arange(occupied_energy.shape[0], dtype=jnp.int32)
@@ -425,6 +536,7 @@
     return pl.pallas_call(
         sum_kernel,
         out_shape=jax.ShapeDtypeStruct((128, 128), F32),
+        compiler_params=pltpu.CompilerParams(vmem_limit_bytes=4 << 20),
         name="pair_sum",
     )(pairs, weight, column_tables())
 

time: 133 us -> 129 us (0.970)
  waiting for transfers between devices: 35.6 us -> 49 us
  local copies, waits for them, and re-layouts: 15.4 us -> 2.83 us
  starting transfers between devices: 46.3 us -> 38.6 us
  Pallas kernels: 29.4 us -> 32.1 us
    ppermute x7 -> x10, waiting for transfers between devices: 16.3 us -> 31.3 us  [the longest x1 13.3 us: per_device(): far_cell = lax.ppermute(list_cell, COL, mirror_of).reshape(G_DEV)]
    unnamed x60 -> x26, local copies, waits for them, and re-layouts: 11.2 us -> 0.07 us
    all_to_all x1, starting transfers between devices: 10.9 us -> 3.53 us  [per_device(): pairs = lax.all_to_all(pairs, BAND, 0, 0, tiled=True)]
    all_to_all x2, waiting for transfers between devices: 7.24 us -> 0.01 us  [the longest x1 0.01 us: per_device(): sent1 = lax.all_to_all(planes1, COL, 0, 0, tiled=True)]
    pallas_call x2, Pallas kernels: 8.24 us -> 11.6 us  [planes_of(): pl.pallas_call(functools.partial(plane_kernel, through=len(through)), out...]
    ppermute x1, waiting for transfers between devices: 1.86 us -> 4.37 us  [per_device(): mirrored = lax.ppermute(mirrored, COL, mirror_of)]
    ppermute x7 -> x10, starting transfers between devices: 14.5 us -> 16.6 us  [the longest x6 7.63 us: spread(): lax.ppermute(cells, COL, [(k, k ^ mask) for k in range(SLABS)])]
    ppermute x1, starting transfers between devices: 2.17 us -> 0.09 us  [per_device(): mirrored = lax.ppermute(mirrored, COL, mirror_of)]
  transfers between devices with their start and end apart: 14 -> 17, of which waited for: 8 -> 8; matrix products, arithmetic and copies ran while one was open for 5% -> 4% of each run, Pallas kernels for 16% -> 15%
where the time goes in v3:
time: 129 us; the launch traced here: 127 us
  waiting for transfers between devices  49 us (38%)
  starting transfers between devices  38.6 us (30%)
  Pallas kernels  32.1 us (25%)
  other arithmetic  3.33 us (3%)
  local copies, waits for them, and re-layouts  2.83 us (2%)
    ppermute x1, waiting for transfers between devices, per_device(): far_cell = lax.ppermute(list_cell, COL, mirror_of).reshape(G_DEV)  13.3 us
    all_to_all x1, waiting for transfers between devices, per_device(): pairs = lax.all_to_all(pairs, BAND, 0, 0, tiled=True)  11.7 us
    pallas_call x2, Pallas kernels, planes_of(): pl.pallas_call(functools.partial(plane_kernel, through=len(through)), out...  11.6 us
    ppermute x6, waiting for transfers between devices, spread(): lax.ppermute(cells, COL, [(k, k ^ mask) for k in range(SLABS)])  9.52 us
    pallas_call x1, Pallas kernels, first_points(): pl.pallas_call(first_kernel, out_shape=(OWN, jax.ShapeDtypeStruct((2 * IT...  9.02 us
    ppermute x1, waiting for transfers between devices, per_device(): c = [wave_c, lax.ppermute(wave_c, 'z1', ahead)]  8.49 us
    ppermute x6, starting transfers between devices, spread(): lax.ppermute(cells, COL, [(k, k ^ mask) for k in range(SLABS)])  7.63 us
    all_to_all x1, starting transfers between devices, per_device(): sent0 = lax.all_to_all(planes0, COL, 0, 0, tiled=True)  7.57 us
  transfers between devices with their start and end apart: 17, of which 8 were waited for; matrix products, arithmetic and copies ran while one was open for 4% of the time, Pallas kernels for 15%

profile of v3, /device:TPU:6, one launch (start us, length us, event | category | flops | bytes accessed | tf_op | source)
XLA Modules:
  0.0 127.0 jit_solution(3434339623620125275)
XLA Ops:
  0.0 1.1 reshape.339
  1.3 1.7 %collective-permute-start = (bf16[96,576]{1,0:T(8,128)(2,1)S(1)}, bf16[96,576]{1,0:T(8,128)(2,1)S(1)}, u32[]{:S(2)}, u32[]{:S(2)}) collective-permute-start(bf16[96,576]{1,0:T(8,128)(2,1)S(1)} %reshape.340.v0), channel_id=1, source_target_pairs={{0,16},{16,0},{32,48},{48,32},{1,17},{17,1},{33,49},{49,33},{2,18}... | collective-permute-start | bytes 331784 | tf_op jit(solution)/shard_map/ppermute | solution.py:471
  3.0 1.9 %collective-permute-start.1 = (bf16[96,576]{1,0:T(8,128)(2,1)S(1)}, bf16[96,576]{1,0:T(8,128)(2,1)S(1)}, u32[]{:S(2)}, u32[]{:S(2)}) collective-permute-start(bf16[96,576]{1,0:T(8,128)(2,1)S(1)} %reshape.340.v0), channel_id=1, source_target_pairs={{0,32},{16,48},{32,0},{48,16},{1,33},{17,49},{33,1},{49,17},{2,34}... | collective-permute-start | bytes 331784 | tf_op jit(solution)/shard_map/ppermute | solution.py:471
  5.6 1.9 %collective-permute-start.6 = (s32[128]{0:T(128)S(1)}, s32[128]{0:T(128)S(1)}, u32[]{:S(2)}, u32[]{:S(2)}) collective-permute-start(s32[128]{0:T(128)S(1)} %compare_select_fusion.5), channel_id=1, source_target_pairs={{0,3},{1,2},{2,1},{3,0},{4,7},{5,6},{6,5},{7,4},{8,11},{9,10},{10,... | collective-permute-start | bytes 1544 | tf_op jit(solution)/shard_map/ppermute | solution.py:448
  7.5 1.2 collective-permute-start.5
  9.8 1.1 reshape.341
  11.2 1.3 %collective-permute-done.5 = s32[128]{0:T(128)S(1)} collective-permute-done((s32[128]{0:T(128)S(1)}, s32[128]{0:T(128)S(1)}, u32[]{:S(2)}, u32[]{:S(2)}) %collective-permute-start.5) | collective-permute-done | bytes 544 | tf_op jit(solution)/shard_map/ppermute | solution.py:448
  12.5 3.3 %collective-permute-start.3 = (bf16[96,576]{1,0:T(8,128)(2,1)S(1)}, bf16[96,576]{1,0:T(8,128)(2,1)S(1)}, u32[]{:S(2)}, u32[]{:S(2)}) collective-permute-start(bf16[96,576]{1,0:T(8,128)(2,1)S(1)} %reshape.342.c0.refs_0_), channel_id=1, source_target_pairs={{0,64},{64,128},{128,192},{192,0},{1,65},{65,129},{129,193},{193,1... | collective-permute-start | bytes 331784 | tf_op jit(solution)/shard_map/ppermute | solution.py:474
  15.8 1.7 %collective-permute-done.2.v3 = bf16[96,576]{1,0:T(8,128)(2,1)S(1)} collective-permute-done((bf16[96,576]{1,0:T(8,128)(2,1)S(1)}, bf16[96,576]{1,0:T(8,128)(2,1)S(1)}, u32[]{:S(2)}, u32[]{:S(2)}) %collective-permute-start.2) | collective-permute-done | bytes 110624 | tf_op jit(solution)/shard_map/ppermute | solution.py:471
  17.5 8.5 %collective-permute-done.3.c1.refs_1_ = bf16[96,576]{1,0:T(8,128)(2,1)S(1)} collective-permute-done((bf16[96,576]{1,0:T(8,128)(2,1)S(1)}, bf16[96,576]{1,0:T(8,128)(2,1)S(1)}, u32[]{:S(2)}, u32[]{:S(2)}) %collective-permute-start.3) | collective-permute-done | bytes 110624 | tf_op jit(solution)/shard_map/ppermute | solution.py:474
  26.0 5.7 %planes.2 = (bf16[16,48,768]{2,1,0:T(8,128)(2,1)}, bf16[96,576]{1,0:T(8,128)(2,1)}, bf16[96,576]{1,0:T(8,128)(2,1)}, s32[1,128]{1,0:T(1,128)}, s32[16,128]{1,0:T(8,128)}) custom-call(bf16[96,576]{1,0:T(8,128)(2,1)S(1)} %reshape.340.v0, bf16[96,576]{1,0:T(8,128)(2,1)S(1)} %collective-permute-done.v1, bf16[96,576]{1,0:T(8,128)(2,1)S(1)} %collective-permute-done.1.v2, ...), custom_call_target="tpu_custom_call" | custom-call | flops 50000000 | bytes 100000 | tf_op jit(solution)/shard_map/planes/pallas_call | solution.py:226
  31.8 7.6 %all-to-all-start = ((bf16[16,48,768]{2,1,0:T(8,128)(2,1)}), bf16[16,48,768]{2,1,0:T(8,128)(2,1)S(1)}, u32[]{:S(2)}, u32[]{:S(2)}) async-start(bf16[16,48,768]{2,1,0:T(8,128)(2,1)} %get-tuple-element.15), calls=%async_computation | async-start | bytes 2359296 | tf_op jit(solution)/shard_map/all_to_all | solution.py:483
  39.5 2.8 %collective-permute-start.11 = (s32[128]{0:T(128)S(1)}, s32[128]{0:T(128)S(1)}, u32[]{:S(2)}, u32[]{:S(2)}) collective-permute-start(s32[128]{0:T(128)S(1)} %bitcast.52), channel_id=1, source_target_pairs={{0,8},{1,9},{2,10},{3,11},{4,12},{5,13},{6,14},{7,15},{8,0},{9,1},... | collective-permute-start | bytes 1544 | tf_op jit(solution)/shard_map/ppermute | solution.py:448
  42.4 1.2 collective-permute-start.10
  43.5 1.5 %collective-permute-start.8 = (bf16[96,576]{1,0:T(8,128)(2,1)S(1)}, bf16[96,576]{1,0:T(8,128)(2,1)S(1)}, u32[]{:S(2)}, u32[]{:S(2)}) collective-permute-start(bf16[96,576]{1,0:T(8,128)(2,1)S(1)} %copy-done.10), channel_id=1, source_target_pairs={{0,192},{64,0},{128,64},{192,128},{1,193},{65,1},{129,65},{193,129... | collective-permute-start | bytes 331784 | tf_op jit(solution)/shard_map/ppermute | solution.py:484
  45.0 1.5 %collective-permute-start.9 = (bf16[96,576]{1,0:T(8,128)(2,1)S(1)}, bf16[96,576]{1,0:T(8,128)(2,1)S(1)}, u32[]{:S(2)}, u32[]{:S(2)}) collective-permute-start(bf16[96,576]{1,0:T(8,128)(2,1)S(1)} %copy-done.9), channel_id=1, source_target_pairs={{0,64},{64,128},{128,192},{192,0},{1,65},{65,129},{129,193},{193,1... | collective-permute-start | bytes 331784 | tf_op jit(solution)/shard_map/ppermute | solution.py:485
  46.5 7.2 %collective-permute-done.12 = s32[128]{0:T(128)S(1)} collective-permute-done((s32[128]{0:T(128)S(1)}, s32[128]{0:T(128)S(1)}, u32[]{:S(2)}, u32[]{:S(2)}) %collective-permute-start.12) | collective-permute-done | bytes 544 | tf_op jit(solution)/shard_map/ppermute | solution.py:448
  53.7 1.0 collective-permute-done.11
  54.8 1.6 %fusion.3.lane_ref = bf16[576,128]{1,0:T(8,128)(2,1)S(1)} fusion(s32[128]{0:T(128)S(1)} %compare_select_fusion.4, s32[128]{0:T(128)S(1)} %get-tuple-element.39, s32[576]{0:T(1024)S(1)} %get-tuple-element.40, s32[128]{0:T(128)S(1)} %get-tuple-element.38, s32[576]{0:T(1024)S(1)} %get-tuple-element.41), kind=kLoop, calls=%fused_computation.4 | loop fusion | flops 958464 | bytes 153600 | tf_op jit(solution)/shard_map/convert_element_type | solution.py:496
  56.7 0.8 block.1.refs_0_
  57.5 5.8 %planes.3 = bf16[16,48,768]{2,1,0:T(8,128)(2,1)} custom-call(bf16[96,576]{1,0:T(8,128)(2,1)S(1)} %reshape.340.v0, bf16[96,576]{1,0:T(8,128)(2,1)S(1)} %collective-permute-done.v1, bf16[96,576]{1,0:T(8,128)(2,1)S(1)} %collective-permute-done.1.v2, bf16[96,576]{1,0:T(8,128)(2,1)S(1)} %collective-permute-done.2.v3, ...), custom_call_target="tpu_custom_call" | custom-call | flops 50000000 | bytes 100000 | tf_op jit(solution)/shard_map/planes/pallas_call | solution.py:226
  63.4 7.1 %all-to-all-start.1 = ((bf16[16,48,768]{2,1,0:T(8,128)(2,1)}), bf16[16,48,768]{2,1,0:T(8,128)(2,1)S(1)}, u32[]{:S(2)}, u32[]{:S(2)}) async-start(bf16[16,48,768]{2,1,0:T(8,128)(2,1)} %planes.3), calls=%async_computation.1 | async-start | bytes 2359296 | tf_op jit(solution)/shard_map/all_to_all | solution.py:504
  70.8 2.8 %collective-permute-start.7 = (s32[16,128]{1,0:T(8,128)S(1)}, s32[16,128]{1,0:T(8,128)S(1)}, u32[]{:S(2)}, u32[]{:S(2)}) collective-permute-start(s32[16,128]{1,0:T(8,128)S(1)} %copy-done.11), channel_id=1, source_target_pairs={{0,15},{1,14},{2,13},{3,12},{4,11},{5,10},{6,9},{7,8},{8,7},{9,6},... | collective-permute-start | bytes 24584 | tf_op jit(solution)/shard_map/ppermute | solution.py:507
  73.8 13.3 %collective-permute-done.7 = s32[16,128]{1,0:T(8,128)S(1)} collective-permute-done((s32[16,128]{1,0:T(8,128)S(1)}, s32[16,128]{1,0:T(8,128)S(1)}, u32[]{:S(2)}, u32[]{:S(2)}) %collective-permute-start.7) | collective-permute-done | bytes 8224 | tf_op jit(solution)/shard_map/ppermute | solution.py:507
  87.3 9.0 %first_points.1 = (f32[8,2048]{1,0:T(8,128)S(1)}, bf16[8,2048]{1,0:T(8,128)(2,1)S(1)}) custom-call(bf16[16,48,768]{2,1,0:T(8,128)(2,1)S(1)} %all-to-all-done.t_ref, bf16[768,768]{1,0:T(8,128)(2,1)} %constant.206.clone.x_hbm, s32[1,2048]{1,0:T(1,128)S(1)} %bitcast.44, s32[1,2048]{1,0:T(1,128)S(1)} %bitcast.42, s32[1,2048]{1,0:T(1,128)S(1)} %get-tuple-element.37.far_ref, ...), custom_call_target="tpu_custom_call" | custom-call | flops 100000000 | bytes 100000 | tf_op jit(solution)/shard_map/first_points/pallas_call | solution.py:331
  96.4 5.9 %second_far_points.1 = (bf16[2,8,2048]{2,1,0:T(8,128)(2,1)S(1)}, bf16[768,768]{1,0:T(8,128)(2,1)S(1)}, f32[16,128]{1,0:T(8,128)S(1)}) custom-call(bf16[16,48,768]{2,1,0:T(8,128)(2,1)S(1)} %all-to-all-done.1.t_ref, bf16[768,768]{1,0:T(8,128)(2,1)} %constant.206.clone.x_hbm, s32[1,2048]{1,0:T(1,128)S(1)} %get-tuple-element.37.far_ref, ...), custom_call_target="tpu_custom_call" | custom-call | flops 100000000 | bytes 100000 | tf_op jit(solution)/shard_map/second_far_points/pallas_call | solution.py:345
  102.4 3.2 %second_own_points.1.own1_ref = f32[8,2048]{1,0:T(8,128)S(1)} custom-call(bf16[768,768]{1,0:T(8,128)(2,1)S(1)} %get-tuple-element.22.low, s32[1,2048]{1,0:T(1,128)S(1)} %bitcast.45, s32[1,2048]{1,0:T(1,128)S(1)} %bitcast.43), custom_call_target="tpu_custom_call" | custom-call | flops 2400000000 | bytes 1300000 | tf_op jit(solution)/shard_map/second_own_points/pallas_call | solution.py:363
  105.6 4.4 %collective-permute-done.13.far_ref = bf16[2,8,2048]{2,1,0:T(8,128)(2,1)S(1)} collective-permute-done((bf16[2,8,2048]{2,1,0:T(8,128)(2,1)S(1)}, bf16[2,8,2048]{2,1,0:T(8,128)(2,1)S(1)}, u32[]{:S(2)}, u32[]{:S(2)}) %collective-permute-start.13) | collective-permute-done | bytes 65568 | tf_op jit(solution)/shard_map/ppermute | solution.py:532
  109.9 0.7 split.1
  110.6 3.5 %all-to-all-start.2 = ((bf16[16,48,128]{2,1,0:T(8,128)(2,1)}), bf16[16,48,128]{2,1,0:T(8,128)(2,1)S(1)}, u32[]{:S(2)}, u32[]{:S(2)}) async-start(bf16[16,48,128]{2,1,0:T(8,128)(2,1)} %split.1), calls=%async_computation.2 | async-start | bytes 393216 | tf_op jit(solution)/shard_map/all_to_all | solution.py:535
  114.3 11.7 %all-to-all-done.2.pairs_ref = bf16[16,48,128]{2,1,0:T(8,128)(2,1)S(1)} async-done(((bf16[16,48,128]{2,1,0:T(8,128)(2,1)}), bf16[16,48,128]{2,1,0:T(8,128)(2,1)S(1)}, u32[]{:S(2)}, u32[]{:S(2)}) %all-to-all-start.2) | async-done | bytes 196640 | tf_op jit(solution)/shard_map/all_to_all | solution.py:535
  126.0 1.0 pair_sum.1
  (65 shorter events, 3.1 us)
Async XLA Ops:
  0.0 26.0 %copy-start = (f32[2,16,768]{2,1,0:T(8,128)S(1)}, f32[2,16,768]{2,1,0:T(8,128)}, u32[]{:S(2)}) copy-start(f32[2,16,768]{2,1,0:T(8,128)} %constant.203.clone.twiddle_ref) | copy-start | bytes 294916
  0.0 26.0 %copy-start.2 = (s32[2048]{0:T(1024)S(1)}, s32[2048]{0:T(1024)}, u32[]{:S(2)}) copy-start(s32[2048]{0:T(1024)} %param.21) | copy-start | bytes 24580
  1.3 14.4 %collective-permute-start = (bf16[96,576]{1,0:T(8,128)(2,1)S(1)}, bf16[96,576]{1,0:T(8,128)(2,1)S(1)}, u32[]{:S(2)}, u32[]{:S(2)}) collective-permute-start(bf16[96,576]{1,0:T(8,128)(2,1)S(1)} %reshape.340.v0), channel_id=1, source_target_pairs={{0,16},{16,0},{32,48},{48,32},{1,17},{17,1},{33,49},{49,33},{2,18}... | collective-permute-start | bytes 331784 | tf_op jit(solution)/shard_map/ppermute | solution.py:471
  3.0 12.8 %collective-permute-start.1 = (bf16[96,576]{1,0:T(8,128)(2,1)S(1)}, bf16[96,576]{1,0:T(8,128)(2,1)S(1)}, u32[]{:S(2)}, u32[]{:S(2)}) collective-permute-start(bf16[96,576]{1,0:T(8,128)(2,1)S(1)} %reshape.340.v0), channel_id=1, source_target_pairs={{0,32},{16,48},{32,0},{48,16},{1,33},{17,49},{33,1},{49,17},{2,34}... | collective-permute-start | bytes 331784 | tf_op jit(solution)/shard_map/ppermute | solution.py:471
  5.6 5.5 %collective-permute-start.6 = (s32[128]{0:T(128)S(1)}, s32[128]{0:T(128)S(1)}, u32[]{:S(2)}, u32[]{:S(2)}) collective-permute-start(s32[128]{0:T(128)S(1)} %compare_select_fusion.5), channel_id=1, source_target_pairs={{0,3},{1,2},{2,1},{3,0},{4,7},{5,6},{6,5},{7,4},{8,11},{9,10},{10,... | collective-permute-start | bytes 1544 | tf_op jit(solution)/shard_map/ppermute | solution.py:448
  7.5 5.0 %collective-permute-start.5 = (s32[128]{0:T(128)S(1)}, s32[128]{0:T(128)S(1)}, u32[]{:S(2)}, u32[]{:S(2)}) collective-permute-start(s32[128]{0:T(128)S(1)} %compare_select_fusion.5), channel_id=1, source_target_pairs={{0,2},{1,3},{2,0},{3,1},{4,6},{5,7},{6,4},{7,5},{8,10},{9,11},{10,... | collective-permute-start | bytes 1544 | tf_op jit(solution)/shard_map/ppermute | solution.py:448
  8.7 7.1 %collective-permute-start.4 = (s32[128]{0:T(128)S(1)}, s32[128]{0:T(128)S(1)}, u32[]{:S(2)}, u32[]{:S(2)}) collective-permute-start(s32[128]{0:T(128)S(1)} %compare_select_fusion.5), channel_id=1, source_target_pairs={{0,1},{1,0},{2,3},{3,2},{4,5},{5,4},{6,7},{7,6},{8,9},{9,8},{10,11... | collective-permute-start | bytes 1544 | tf_op jit(solution)/shard_map/ppermute | solution.py:448
  11.1 6.4 %collective-permute-start.2 = (bf16[96,576]{1,0:T(8,128)(2,1)S(1)}, bf16[96,576]{1,0:T(8,128)(2,1)S(1)}, u32[]{:S(2)}, u32[]{:S(2)}) collective-permute-start(bf16[96,576]{1,0:T(8,128)(2,1)S(1)} %reshape.340.v0), channel_id=1, source_target_pairs={{0,48},{16,32},{32,16},{48,0},{1,49},{17,33},{33,17},{49,1},{2,50}... | collective-permute-start | bytes 331784 | tf_op jit(solution)/shard_map/ppermute | solution.py:471
  12.5 13.5 %collective-permute-start.3 = (bf16[96,576]{1,0:T(8,128)(2,1)S(1)}, bf16[96,576]{1,0:T(8,128)(2,1)S(1)}, u32[]{:S(2)}, u32[]{:S(2)}) collective-permute-start(bf16[96,576]{1,0:T(8,128)(2,1)S(1)} %reshape.342.c0.refs_0_), channel_id=1, source_target_pairs={{0,64},{64,128},{128,192},{192,0},{1,65},{65,129},{129,193},{193,1... | collective-permute-start | bytes 331784 | tf_op jit(solution)/shard_map/ppermute | solution.py:474
  31.7 7.6 %copy-start.8 = (s32[1,128]{1,0:T(1,128)S(1)}, s32[1,128]{1,0:T(1,128)}, u32[]{:S(2)}) copy-start(s32[1,128]{1,0:T(1,128)} %get-tuple-element.20) | copy-start | bytes 1540
  31.7 11.8 %copy-start.10 = (bf16[96,576]{1,0:T(8,128)(2,1)S(1)}, bf16[96,576]{1,0:T(8,128)(2,1)}, u32[]{:S(2)}) copy-start(bf16[96,576]{1,0:T(8,128)(2,1)} %get-tuple-element.18) | copy-start | bytes 331780
  31.8 13.2 %copy-start.9 = (bf16[96,576]{1,0:T(8,128)(2,1)S(1)}, bf16[96,576]{1,0:T(8,128)(2,1)}, u32[]{:S(2)}) copy-start(bf16[96,576]{1,0:T(8,128)(2,1)} %get-tuple-element.19) | copy-start | bytes 331780
  31.8 31.6 %all-to-all-start = ((bf16[16,48,768]{2,1,0:T(8,128)(2,1)}), bf16[16,48,768]{2,1,0:T(8,128)(2,1)S(1)}, u32[]{:S(2)}, u32[]{:S(2)}) async-start(bf16[16,48,768]{2,1,0:T(8,128)(2,1)} %get-tuple-element.15), calls=%async_computation | async-start | bytes 2359296 | tf_op jit(solution)/shard_map/all_to_all | solution.py:483
  39.4 14.3 %collective-permute-start.12 = (s32[128]{0:T(128)S(1)}, s32[128]{0:T(128)S(1)}, u32[]{:S(2)}, u32[]{:S(2)}) collective-permute-start(s32[128]{0:T(128)S(1)} %bitcast.51), channel_id=1, source_target_pairs={{0,12},{1,13},{2,14},{3,15},{4,8},{5,9},{6,10},{7,11},{8,4},{9,5},... | collective-permute-start | bytes 1544 | tf_op jit(solution)/shard_map/ppermute | solution.py:448
  39.5 15.2 %collective-permute-start.11 = (s32[128]{0:T(128)S(1)}, s32[128]{0:T(128)S(1)}, u32[]{:S(2)}, u32[]{:S(2)}) collective-permute-start(s32[128]{0:T(128)S(1)} %bitcast.52), channel_id=1, source_target_pairs={{0,8},{1,9},{2,10},{3,11},{4,12},{5,13},{6,14},{7,15},{8,0},{9,1},... | collective-permute-start | bytes 1544 | tf_op jit(solution)/shard_map/ppermute | solution.py:448
  42.4 12.4 %collective-permute-start.10 = (s32[128]{0:T(128)S(1)}, s32[128]{0:T(128)S(1)}, u32[]{:S(2)}, u32[]{:S(2)}) collective-permute-start(s32[128]{0:T(128)S(1)} %bitcast.53), channel_id=1, source_target_pairs={{0,4},{1,5},{2,6},{3,7},{4,0},{5,1},{6,2},{7,3},{8,12},{9,13},{10,... | collective-permute-start | bytes 1544 | tf_op jit(solution)/shard_map/ppermute | solution.py:448
  43.5 13.1 %collective-permute-start.8 = (bf16[96,576]{1,0:T(8,128)(2,1)S(1)}, bf16[96,576]{1,0:T(8,128)(2,1)S(1)}, u32[]{:S(2)}, u32[]{:S(2)}) collective-permute-start(bf16[96,576]{1,0:T(8,128)(2,1)S(1)} %copy-done.10), channel_id=1, source_target_pairs={{0,192},{64,0},{128,64},{192,128},{1,193},{65,1},{129,65},{193,129... | collective-permute-start | bytes 331784 | tf_op jit(solution)/shard_map/ppermute | solution.py:484
  45.0 11.7 %collective-permute-start.9 = (bf16[96,576]{1,0:T(8,128)(2,1)S(1)}, bf16[96,576]{1,0:T(8,128)(2,1)S(1)}, u32[]{:S(2)}, u32[]{:S(2)}) collective-permute-start(bf16[96,576]{1,0:T(8,128)(2,1)S(1)} %copy-done.9), channel_id=1, source_target_pairs={{0,64},{64,128},{128,192},{192,0},{1,65},{65,129},{129,193},{193,1... | collective-permute-start | bytes 331784 | tf_op jit(solution)/shard_map/ppermute | solution.py:485
  63.3 7.2 %copy-start.3 = (f32[4096]{0:T(1024)S(1)}, f32[4096]{0:T(1024)}, u32[]{:S(2)}) copy-start(f32[4096]{0:T(1024)} %param.18) | copy-start | bytes 49156
  63.3 7.2 %copy-start.6 = (s32[16]{0:T(128)S(1)}, s32[16]{0:T(128)}, u32[]{:S(2)}) copy-start(s32[16]{0:T(128)} %param.17) | copy-start | bytes 196
  63.3 7.4 %copy-start.11 = (s32[16,128]{1,0:T(8,128)S(1)}, s32[16,128]{1,0:T(8,128)}, u32[]{:S(2)}) copy-start(s32[16,128]{1,0:T(8,128)} %get-tuple-element.16) | copy-start | bytes 24580
  63.3 10.2 %copy-start.4 = (pred[256,16]{0,1:T(8,128)(4,1)S(1)}, pred[256,16]{0,1:T(8,128)(4,1)}, u32[]{:S(2)}) copy-start(pred[256,16]{0,1:T(8,128)(4,1)} %constant.204.clone) | copy-start | bytes 12292
  63.3 10.2 %copy-start.5 = (pred[256,16]{0,1:T(8,128)(4,1)S(1)}, pred[256,16]{0,1:T(8,128)(4,1)}, u32[]{:S(2)}) copy-start(pred[256,16]{0,1:T(8,128)(4,1)} %constant.205.clone) | copy-start | bytes 12292
  63.4 10.2 %copy-start.7 = (f32[16]{0:T(128)S(1)}, f32[16]{0:T(128)}, u32[]{:S(2)}) copy-start(f32[16]{0:T(128)} %param.19) | copy-start | bytes 196
  63.4 10.3 %copy-start.12 = (f32[4]{0:T(128)S(1)}, f32[4]{0:T(128)}, u32[]{:S(2)}) copy-start(f32[4]{0:T(128)} %param.20) | copy-start | bytes 52
  63.4 32.9 %all-to-all-start.1 = ((bf16[16,48,768]{2,1,0:T(8,128)(2,1)}), bf16[16,48,768]{2,1,0:T(8,128)(2,1)S(1)}, u32[]{:S(2)}, u32[]{:S(2)}) async-start(bf16[16,48,768]{2,1,0:T(8,128)(2,1)} %planes.3), calls=%async_computation.1 | async-start | bytes 2359296 | tf_op jit(solution)/shard_map/all_to_all | solution.py:504
  70.8 16.3 %collective-permute-start.7 = (s32[16,128]{1,0:T(8,128)S(1)}, s32[16,128]{1,0:T(8,128)S(1)}, u32[]{:S(2)}, u32[]{:S(2)}) collective-permute-start(s32[16,128]{1,0:T(8,128)S(1)} %copy-done.11), channel_id=1, source_target_pairs={{0,15},{1,14},{2,13},{3,12},{4,11},{5,10},{6,9},{7,8},{8,7},{9,6},... | collective-permute-start | bytes 24584 | tf_op jit(solution)/shard_map/ppermute | solution.py:507
  102.3 7.6 %collective-permute-start.13 = (bf16[2,8,2048]{2,1,0:T(8,128)(2,1)S(1)}, bf16[2,8,2048]{2,1,0:T(8,128)(2,1)S(1)}, u32[]{:S(2)}, u32[]{:S(2)}) collective-permute-start(bf16[2,8,2048]{2,1,0:T(8,128)(2,1)S(1)} %get-tuple-element.23), channel_id=1, source_target_pairs={{0,15},{1,14},{2,13},{3,12},{4,11},{5,10},{6,9},{7,8},{8,7},{9,6},... | collective-permute-start | bytes 196616 | tf_op jit(solution)/shard_map/ppermute | solution.py:532
  102.4 23.6 %copy-start.1 = (bf16[2,128,128]{2,1,0:T(8,128)(2,1)S(1)}, bf16[2,128,128]{2,1,0:T(8,128)(2,1)}, u32[]{:S(2)}) copy-start(bf16[2,128,128]{2,1,0:T(8,128)(2,1)} %constant.207.clone.column_ref) | copy-start | bytes 196612
  110.6 15.3 %all-to-all-start.2 = ((bf16[16,48,128]{2,1,0:T(8,128)(2,1)}), bf16[16,48,128]{2,1,0:T(8,128)(2,1)S(1)}, u32[]{:S(2)}, u32[]{:S(2)}) async-start(bf16[16,48,128]{2,1,0:T(8,128)(2,1)} %split.1), calls=%async_computation.2 | async-start | bytes 393216 | tf_op jit(solution)/shard_map/all_to_all | solution.py:535

commit v4 on v3

v4 whole, which is shorter than its diff:
```python
import functools
import math

import jax
import jax.numpy as jnp
import ml_dtypes
import numpy as np
from jax import lax
from jax.experimental import pallas as pl
from jax.experimental.pallas import tpu as pltpu
from jax.sharding import Mesh
from jax.sharding import PartitionSpec as P

BF16 = jnp.bfloat16
F32 = jnp.float32

N = 96
SLABS = 16
X6 = 6
Y6 = 6
Y16 = 16
K7 = 7
FLAT = K7 * N
WIDE = 768
GROUPS = (
    (((0, 0), (0, 1)),),
    (((1, 0), (1, 1), (0, 3), (1, 3)), ((0, 2), (1, 2))),
)
ITEM_LIST = [item for chunk in GROUPS for group in chunk for item in group]
SPARE = 640
G_DEV = 2048
NBLOCK = 16
TILE = 512

ITEM_ROWS = 2 * X6
BAND = ("z1", "z0", "yl")
VGROUP = ("z0", "yl")
COL = ("x", "yh", "co")


def unit(phase, period):
    angle = 2.0 * np.pi * (np.asarray(phase) % period) / period
    return np.cos(angle), -np.sin(angle)


def bf16(table):
    return np.asarray(table, np.float32).astype(ml_dtypes.bfloat16)


@functools.cache
def lane_table():
    y6, z = np.divmod(np.arange(Y6 * N), N)
    k7, kz = np.divmod(np.arange(FLAT), N)
    phase = 16 * y6[:, None] * k7[None, :] + z[:, None] * kz[None, :]
    cosine, sine = unit(phase, N)
    table = np.zeros((Y6 * N, 2 * WIDE))
    table[:, :FLAT] = cosine
    table[:, WIDE : WIDE + FLAT] = sine
    return bf16(table)


@functools.cache
def twiddle_table():
    k7 = np.arange(FLAT) // N
    cosine, sine = unit(np.arange(Y16)[:, None] * k7[None, :], N)
    table = np.zeros((2, Y16, WIDE), np.float32)
    table[0, :, :FLAT] = cosine / N
    table[1, :, :FLAT] = sine / N
    return table


@functools.cache
def row_table(items):
    table = np.zeros((SLABS, items, 2, X6, 2, items, X6, Y16))
    cosine, sine = unit(np.arange(SLABS)[:, None] * np.arange(Y16)[None, :], SLABS)
    for item in range(items):
        for x in range(X6):
            table[:, item, 0, x, 0, item, x] = cosine
            table[:, item, 0, x, 1, item, x] = -sine
            table[:, item, 1, x, 0, item, x] = sine
            table[:, item, 1, x, 1, item, x] = cosine
    return bf16(table.reshape(SLABS * items * 2 * X6, 2 * items * X6 * Y16))


@functools.cache
def x_table(items):
    table = np.zeros((2, items, N, SLABS, items, 2, X6))
    cosine, sine = unit(np.arange(N)[:, None] * np.arange(N)[None, :], N)
    cosine = (cosine * 0.5 / math.sqrt(N)).reshape(N, SLABS, X6)
    sine = (sine * 0.5 / math.sqrt(N)).reshape(N, SLABS, X6)
    for item in range(items):
        table[0, item, :, :, item, 0] = cosine
        table[0, item, :, :, item, 1] = -sine
        table[1, item, :, :, item, 0] = sine
        table[1, item, :, :, item, 1] = cosine
    return bf16(table.reshape(2 * items * N, SLABS * items * 2 * X6))


@functools.cache
def pair_table():
    valence, conduction = [], []
    for band in range(16):
        z1, group = divmod(band, 4)
        for half in range(2):
            for pair, slot in ITEM_LIST:
                valence.append(z1 * 4 + (group ^ (2 * pair + half)))
                conduction.append((z1 - slot) % 4 * 4 + group)
    return np.array(valence), np.array(conduction)


@functools.cache
def column_tables():
    tables = np.zeros((2, 128, 4, 2, NBLOCK))
    m = np.arange(NBLOCK)
    tables[0, 32 + m, :, 0, m] = 1.0
    tables[0, 64 + m, :, 1, m] = -1.0
    tables[1, 64 + m, :, 0, m] = 1.0
    tables[1, 32 + m, :, 1, m] = 1.0
    return bf16(tables.reshape(2, 128, 128))


VMEM = pl.BlockSpec(memory_space=pltpu.VMEM)
HBM = pl.BlockSpec(memory_space=pltpu.HBM)
ANY = pl.BlockSpec(memory_space=pl.ANY)
SLAB_CUTS = 4


def plane_kernel(*refs, groups, slots, through):
    refs = list(refs)
    take = lambda count: [refs.pop(0) for _ in range(count)]
    waves = dict(zip(slots[0], take(len(slots[0]))))
    waves_c = dict(zip(slots[1], take(len(slots[1]))))
    lane_ref, twiddle_ref = take(2)
    row_refs = take(len(groups))
    kept = take(through)
    block_refs = take(len(refs) - 4 - through - len(groups))
    (out_ref,) = take(1)
    kept_out = take(through)
    low_refs = take(len(groups))
    slab_ref, slab_sems, keep_sems = refs
    moves = [
        pltpu.make_async_copy(source, target, keep_sems.at[i])
        for i, (source, target) in enumerate(zip(kept, kept_out))
    ]
    for move in moves:
        move.start()
    rows = X6 * Y16
    twiddle_c = twiddle_ref[0][None]
    twiddle_s = twiddle_ref[1][None]
    for group, low_ref in zip(groups, low_refs):
        for index, (pair, slot) in enumerate(group):
            wave_c = waves_c[slot][...]
            pairs = jnp.concatenate(
                [waves[2 * pair][...] * wave_c, waves[2 * pair + 1][...] * wave_c], axis=0
            )
            moved = jnp.dot(pairs, lane_ref[...], preferred_element_type=F32)
            real = moved[:rows, :WIDE] - moved[rows:, WIDE:]
            imag = moved[:rows, WIDE:] + moved[rows:, :WIDE]
            real = real.reshape(X6, Y16, WIDE)
            imag = imag.reshape(X6, Y16, WIDE)
            turned_r = real * twiddle_c - imag * twiddle_s
            turned_i = real * twiddle_s + imag * twiddle_c
            low_ref[index * rows : (index + 1) * rows, :] = turned_r.reshape(rows, WIDE).astype(
                BF16
            )
            index += len(group)
            low_ref[index * rows : (index + 1) * rows, :] = turned_i.reshape(rows, WIDE).astype(
                BF16
            )
    count = SLABS // SLAB_CUTS
    for part in range(SLAB_CUTS):
        slabs = slice(part * count, (part + 1) * count)
        first = 0
        for group, low_ref, row_ref in zip(groups, low_refs, row_refs):
            size = len(group) * ITEM_ROWS
            planes = jnp.dot(
                row_ref[part * count * size : (part + 1) * count * size, :],
                low_ref[...],
                preferred_element_type=F32,
            ).reshape(count, size, WIDE)
            slab_ref[slabs, first : first + size, :] = planes.astype(BF16)
            if first == 0 and block_refs:
                spare = planes[:, :32, SPARE:] + block_refs[0][...][None]
                slab_ref[slabs, :32, SPARE:] = spare.astype(BF16)
            first += size
        window = pl.ds(part * count, count)
        moves.append(
            pltpu.make_async_copy(slab_ref.at[window], out_ref.at[window], slab_sems.at[part])
        )
        moves[-1].start()
    for move in moves:
        move.wait()


def planes_of(chunk, v, c, through=(), block=()):
    groups = GROUPS[chunk]
    items = [item for group in groups for item in group]
    slots_v = sorted({2 * pair + half for pair, _ in items for half in range(2)})
    slots_c = sorted({slot for _, slot in items})
    rows = len(items) * ITEM_ROWS
    tables = [row_table(len(group)) for group in groups]
    return pl.pallas_call(
        functools.partial(
            plane_kernel, groups=groups, slots=(slots_v, slots_c), through=len(through)
        ),
        out_shape=[
            pltpu.HBM((SLABS, rows, WIDE), BF16),
            *(pltpu.HBM(x.shape, x.dtype) for x in through),
        ],
        in_specs=[VMEM] * (len(slots_v) + len(slots_c) + 2 + len(tables))
        + [ANY] * len(through)
        + [VMEM] * len(block),
        out_specs=[HBM] * (1 + len(through)),
        scratch_shapes=[
            *(pltpu.VMEM((2 * len(group) * X6 * Y16, WIDE), BF16) for group in groups),
            pltpu.VMEM((SLABS, rows, WIDE), BF16),
            pltpu.SemaphoreType.DMA((SLAB_CUTS,)),
            pltpu.SemaphoreType.DMA((max(len(through), 1),)),
        ],
        compiler_params=pltpu.CompilerParams(vmem_limit_bytes=16 << 20),
        cost_estimate=pl.CostEstimate(
            flops=50_000_000, bytes_accessed=100_000, transcendentals=0
        ),
        name="planes",
    )(
        *(v[slot] for slot in slots_v),
        *(c[slot] for slot in slots_c),
        lane_table(),
        twiddle_table(),
        *tables,
        *through,
        *block,
    )


def pick(density_ref, flat_ref, kx_ref, store):
    rows = density_ref.shape[0]

    def body(step, carry):
        lanes = pl.ds(pl.multiple_of(step * TILE, TILE), TILE)
        spot = lax.broadcasted_iota(jnp.int32, (WIDE, TILE), 0)
        chosen = jnp.where(spot == flat_ref[:, lanes], 1.0, 0.0).astype(BF16)
        values = jnp.dot(density_ref[...], chosen, preferred_element_type=F32)
        kx = lax.broadcasted_iota(jnp.int32, (N, TILE), 0) == kx_ref[:, lanes]
        values = jnp.where(kx[None], values.reshape(rows // N, N, TILE), 0.0)
        store(lanes, values.sum(axis=1))
        return carry

    lax.fori_loop(0, G_DEV // TILE, body, 0)


def transform_x(chunk, t_ref, x_refs, low):
    first, place = 0, 0
    for group, x_ref in zip(GROUPS[chunk], x_refs):
        size = len(group) * ITEM_ROWS
        planes = t_ref[:, first : first + size, :]
        if size % 16:
            planes = planes.astype(F32)
        planes = planes.reshape(SLABS * size, WIDE).astype(BF16)
        rows = 2 * len(group) * N
        low[place : place + rows, :] = jnp.dot(
            x_ref[...], planes, preferred_element_type=F32
        ).astype(BF16)
        first += size
        place += rows


def first_kernel(
    t_ref, x_ref, own_ref, own_kx_ref, far_ref, far_kx_ref, own_out, far_out, low
):
    transform_x(0, t_ref, (x_ref,), low)

    def store_far(lanes, values):
        far_out[:, lanes] = values.astype(BF16)

    def store_own(lanes, values):
        own_out[:, lanes] = values

    pick(low, far_ref, far_kx_ref, store_far)
    pick(low, own_ref, own_kx_ref, store_own)


def second_far_kernel(
    t_ref, x0_ref, x1_ref, far_ref, far_kx_ref, first_ref, far_out, low, block_out
):
    transform_x(1, t_ref, (x0_ref, x1_ref), low)
    rows = first_ref.shape[0]
    far_out[:rows, :] = first_ref[...]

    def store_far(lanes, values):
        far_out[rows:, lanes] = values.astype(BF16)

    pick(low, far_ref, far_kx_ref, store_far)
    spare = t_ref[:, :32, SPARE:].astype(F32).sum(axis=0)
    spare = spare[:16] + spare[16:]
    spare = spare + pltpu.roll(spare, 128 - NBLOCK, 1)
    block_out[...] = spare


def second_own_kernel(low, own_ref, own_kx_ref, own_out):
    def store_own(lanes, values):
        own_out[:, lanes] = values

    pick(low, own_ref, own_kx_ref, store_own)


FIRST, SECOND = (2 * sum(len(group) for group in chunk) for chunk in GROUPS)


def first_points(planes, own, far):
    return pl.pallas_call(
        first_kernel,
        out_shape=(
            jax.ShapeDtypeStruct((FIRST, G_DEV), F32),
            jax.ShapeDtypeStruct((FIRST, G_DEV), BF16),
        ),
        scratch_shapes=[pltpu.VMEM((FIRST * N, WIDE), BF16)],
        compiler_params=pltpu.CompilerParams(vmem_limit_bytes=16 << 20),
        cost_estimate=pl.CostEstimate(
            flops=100_000_000, bytes_accessed=100_000, transcendentals=0
        ),
        name="first_points",
    )(planes, x_table(FIRST // 2), *own, *far)


def second_far_points(planes, far, first):
    return pl.pallas_call(
        second_far_kernel,
        out_shape=(
            jax.ShapeDtypeStruct((FIRST + SECOND, G_DEV), BF16),
            jax.ShapeDtypeStruct((SECOND * N, WIDE), BF16),
            jax.ShapeDtypeStruct((16, 128), F32),
        ),
        compiler_params=pltpu.CompilerParams(vmem_limit_bytes=16 << 20),
        cost_estimate=pl.CostEstimate(
            flops=100_000_000, bytes_accessed=100_000, transcendentals=0
        ),
        name="second_far_points",
    )(planes, *(x_table(len(group)) for group in GROUPS[1]), *far, first)


def second_own_points(low, own):
    return pl.pallas_call(
        second_own_kernel,
        out_shape=jax.ShapeDtypeStruct((SECOND, G_DEV), F32),
        compiler_params=pltpu.CompilerParams(vmem_limit_bytes=16 << 20),
        cost_estimate=pl.CostEstimate(
            flops=2_400_000_000, bytes_accessed=1_300_000, transcendentals=0
        ),
        name="second_own_points",
    )(low, *own)


def split_kernel(own0_ref, own1_ref, far_ref, block_ref, out_ref):
    parts = [[], [], [], []]
    first, place = 0, 0
    for own_ref, chunk in zip((own0_ref, own1_ref), GROUPS):
        first = 0
        for group in chunk:
            size = len(group)
            own_r = own_ref[first : first + size, :]
            own_i = own_ref[first + size : first + 2 * size, :]
            far_r = far_ref[place : place + size, :].astype(F32)
            far_i = far_ref[place + size : place + 2 * size, :].astype(F32)
            parts[0].append(own_r + far_r)
            parts[1].append(own_i + far_i)
            parts[2].append(own_i - far_i)
            parts[3].append(far_r - own_r)
            first += 2 * size
            place += 2 * size
    pairs = jnp.concatenate(sum(parts, []), axis=0).astype(BF16)
    block = block_ref[...].astype(BF16)
    for band in range(16):
        out_ref[band, :32, :] = pairs[:, band * 128 : (band + 1) * 128]
        out_ref[band, 32:, :] = block


def split_pairs(own0, own1, far, block):
    return pl.pallas_call(
        split_kernel,
        out_shape=jax.ShapeDtypeStruct((16, 48, 128), BF16),
        compiler_params=pltpu.CompilerParams(vmem_limit_bytes=8 << 20),
        cost_estimate=pl.CostEstimate(
            flops=1_000_000, bytes_accessed=500_000, transcendentals=0
        ),
        name="split",
    )(own0, own1, far, block)


def block_kernel(v0, v1, v2, v3, c0, c1, c2, c3, lane_ref, row_ref, out_ref):
    waves = (v0, v1, v2, v3)
    waves_c = (c0, c1, c2, c3)
    for half in range(2):
        for item, (pair, slot) in enumerate(ITEM_LIST):
            product = waves[2 * pair + half][...] * waves_c[slot][...]
            sums = jnp.dot(product, lane_ref[...], preferred_element_type=F32) * row_ref[...]
            total = sums.sum(axis=0, keepdims=True)
            high = total.astype(BF16).astype(F32)
            index = half * len(ITEM_LIST) + item
            out_ref[index : index + 1, :] = high
            out_ref[16 + index : 17 + index, :] = total - high


def block_sums(v, c, lanes, rows):
    return pl.pallas_call(
        block_kernel,
        out_shape=jax.ShapeDtypeStruct((32, 128), F32),
        compiler_params=pltpu.CompilerParams(vmem_limit_bytes=4 << 20),
        cost_estimate=pl.CostEstimate(
            flops=10_000_000, bytes_accessed=100_000, transcendentals=0
        ),
        name="block",
    )(*v, *c, lanes, rows)


def sum_kernel(pairs_ref, weight_ref, column_ref, out_ref):
    pairs = 16 * 16
    block = pairs_ref[:, 32:, :].reshape(pairs, 128)
    total = None
    for part in range(2):
        left = pairs_ref[:, 16 * part : 16 * (part + 1), :].reshape(pairs, 128)
        columns = jnp.dot(block, column_ref[part], preferred_element_type=F32)
        right = (columns * weight_ref[...]).astype(BF16)
        term = lax.dot_general(
            left, right, (((0,), (0,)), ((), ())), preferred_element_type=F32
        )
        total = term if total is None else total + term
    out_ref[...] = total


def wave_rows(wave):
    return wave.reshape(X6, Y6, Y16, N).transpose(0, 2, 1, 3).reshape(X6 * Y16, Y6 * N)


def spread(cells, masks):
    arrived = [lax.ppermute(cells, COL, [(k, k ^ mask) for k in range(SLABS)]) for mask in masks]
    return sum(arrived, cells)


def cosine(phase):
    return jnp.cos((phase % N).astype(F32) * (2.0 * math.pi / N))


def per_device(
    valence_wave,
    conduction_wave,
    valence_index,
    occupied_energy,
    conduction_energy,
    frequency,
    gvec_cell,
    block_cell,
):
    col = lax.axis_index(COL)
    wave_v = wave_rows(valence_wave)
    wave_c = wave_rows(conduction_wave)
    twin = [[(i, i ^ mask) for i in range(4)] for mask in range(4)]
    ahead = [(i, (i + 1) % 4) for i in range(4)]
    behind = [(i, (i + 3) % 4) for i in range(4)]
    v = [wave_v, lax.ppermute(wave_v, VGROUP, twin[1])]
    c = [wave_c, lax.ppermute(wave_c, "z1", ahead)]

    spots = jnp.arange(128, dtype=jnp.int32)
    cells = jnp.where(spots % NBLOCK == col, block_cell[0], 0)
    cells = spread(cells, (1, 2, 3))
    cells = spread(cells, (4, 8, 12))

    mirror_of = [(k, SLABS - 1 - k) for k in range(SLABS)]
    far_cell = lax.ppermute(gvec_cell, COL, mirror_of).reshape(16, 128)
    planes0, far_cell, *passed = planes_of(0, v, c, through=(far_cell, *v, *c))
    sent0 = lax.all_to_all(planes0, COL, 0, 0, tiled=True)
    v.append(lax.ppermute(passed[0], VGROUP, twin[2]))
    v.append(lax.ppermute(passed[1], VGROUP, twin[2]))
    c.append(lax.ppermute(passed[3], "z1", ahead))
    c.append(lax.ppermute(passed[2], "z1", behind))

    far_cell = far_cell.reshape(G_DEV)
    far_x, far_y, far_z = far_cell // 576, far_cell // N % 6, far_cell % N
    own = ((gvec_cell % 576)[None], (gvec_cell // 576)[None])
    far = (((6 - far_y) * N + (N - far_z) % N)[None], ((N - far_x) % N)[None])

    block_x = cells // 576
    block_y = spots % NBLOCK * 6 + cells // N % 6
    block_z = cells % N
    group = spots // NBLOCK - 2
    quarter = N // 4
    lane = jnp.arange(Y6 * N, dtype=jnp.int32)[:, None]
    lanes = cosine(
        lane // N * 16 * block_y + lane % N * block_z + jnp.where(group % 2 == 1, quarter, 0)
    ).astype(BF16)
    row = jnp.arange(X6 * Y16, dtype=jnp.int32)[:, None]
    shift = jnp.where(group == 1, 3 * quarter, jnp.where(group == 2, quarter, 0))
    rows = cosine((row // Y16 + X6 * col) * block_x + row % Y16 * block_y + shift)
    scale = 1.0 / (N * math.sqrt(N))
    rows = jnp.where((group >= 0) & (group < 4), rows * scale, 0.0)
    block = block_sums(v, c, lanes, rows)
    (planes1,) = planes_of(1, v, c, block=(block,))
    sent1 = lax.all_to_all(planes1, COL, 0, 0, tiled=True)

    pair_v, pair_c = pair_table()
    occupied = jnp.arange(occupied_energy.shape[0], dtype=jnp.int32)
    valence_energy = jnp.sum(
        jnp.where(valence_index[:, None] == occupied[None, :], occupied_energy[None, :], 0.0),
        axis=1,
    )
    count_v, count_c = valence_index.shape[0], conduction_energy.shape[0]
    energy_v = jnp.sum(
        jnp.where(pair_v[:, None] == np.arange(count_v)[None], valence_energy[None], 0.0), axis=1
    )
    energy_c = jnp.sum(
        jnp.where(pair_c[:, None] == np.arange(count_c)[None], conduction_energy[None], 0.0),
        axis=1,
    )
    gap = (energy_c - energy_v)[:, None]
    omega = jnp.repeat(frequency, 2 * NBLOCK)[None]
    weight = -4.0 * gap / (gap * gap + omega * omega) * (1.0 / math.sqrt(count_v * count_c))

    own0, far0 = first_points(sent0, own, far)
    mirrored, low, columns = second_far_points(sent1, far, far0)
    mirrored = lax.ppermute(mirrored, COL, mirror_of)
    own1 = second_own_points(low, own)
    pairs = split_pairs(own0, own1, mirrored, columns)
    pairs = lax.all_to_all(pairs, BAND, 0, 0, tiled=True)
    return pl.pallas_call(
        sum_kernel,
        out_shape=jax.ShapeDtypeStruct((128, 128), F32),
        compiler_params=pltpu.CompilerParams(vmem_limit_bytes=4 << 20),
        name="pair_sum",
    )(pairs, weight, column_tables())


def solution(mesh):
    fine = Mesh(
        mesh.devices.reshape(4, 2, 2, 4, 2, 2), ("z1", "z0", "yl", "x", "yh", "co")
    )
    return jax.shard_map(
        per_device,
        mesh=fine,
        in_specs=(
            P(BAND, COL, None),
            P(BAND, COL, None),
            P(),
            P(),
            P(),
            P(),
            P(COL),
            P(COL),
        ),
        out_specs=P(COL + BAND, None),
        check_vma=False,
    )
```

time: 129 us -> 124 us (0.961)
  Pallas kernels: 32.1 us -> 24.8 us
  starting transfers between devices: 38.6 us -> 43.8 us
  waiting for transfers between devices: 49 us -> 44.8 us
  local copies, waits for them, and re-layouts: 2.83 us -> 5.03 us
    all_to_all x1, waiting for transfers between devices: 0.01 us -> 18.4 us  [per_device(): sent1 = lax.all_to_all(planes1, COL, 0, 0, tiled=True)]
    ppermute x1, waiting for transfers between devices: 8.49 us -> 0.01 us  [per_device(): c = [wave_c, lax.ppermute(wave_c, 'z1', ahead)]]
    ppermute x6, waiting for transfers between devices: 9.52 us -> 1.52 us  [spread(): lax.ppermute(cells, COL, [(k, k ^ mask) for k in range(SLABS)])]
    pallas_call x5, Pallas kernels: 29.7 us -> 22.3 us  [the longest x2 7.53 us: planes_of(): pl.pallas_call(functools.partial(plane_kernel, groups=groups, slots=(slot...]
    ppermute x1, waiting for transfers between devices: 4.37 us -> 0.4 us  [per_device(): mirrored = lax.ppermute(mirrored, COL, mirror_of)]
    ppermute x1, starting transfers between devices: 0.09 us -> 2.99 us  [per_device(): mirrored = lax.ppermute(mirrored, COL, mirror_of)]
    all_to_all x1, starting transfers between devices: 3.53 us -> 6.39 us  [per_device(): pairs = lax.all_to_all(pairs, BAND, 0, 0, tiled=True)]
    unnamed x26 -> x32, local copies, waits for them, and re-layouts: 0.07 us -> 2.31 us
  transfers between devices with their start and end apart: 17 -> 17, of which waited for: 8 -> 8; matrix products, arithmetic and copies ran while one was open for 4% -> 4% of each run, Pallas kernels for 15% -> 12%
where the time goes in v4:
time: 124 us; the launch traced here: 122 us
  waiting for transfers between devices  44.8 us (36%)
  starting transfers between devices  43.8 us (35%)
  Pallas kernels  24.8 us (20%)
  local copies, waits for them, and re-layouts  5.03 us (4%)
  other arithmetic  2.64 us (2%)
    all_to_all x1, waiting for transfers between devices, per_device(): sent1 = lax.all_to_all(planes1, COL, 0, 0, tiled=True)  18.4 us
    all_to_all x1, waiting for transfers between devices, per_device(): pairs = lax.all_to_all(pairs, BAND, 0, 0, tiled=True)  10.8 us
    ppermute x6, starting transfers between devices, spread(): lax.ppermute(cells, COL, [(k, k ^ mask) for k in range(SLABS)])  7.63 us
    pallas_call x2, Pallas kernels, planes_of(): pl.pallas_call(functools.partial(plane_kernel, groups=groups, slots=(slot...  7.53 us
    all_to_all x1, starting transfers between devices, per_device(): sent1 = lax.all_to_all(planes1, COL, 0, 0, tiled=True)  7.37 us
    all_to_all x1, starting transfers between devices, per_device(): sent0 = lax.all_to_all(planes0, COL, 0, 0, tiled=True)  7.01 us
    all_to_all x1, starting transfers between devices, per_device(): pairs = lax.all_to_all(pairs, BAND, 0, 0, tiled=True)  6.39 us
    pallas_call x1, Pallas kernels, second_far_points(): pl.pallas_call(second_far_kernel, out_shape=(jax.ShapeDtypeStruct((FIRST...  5.95 us
  transfers between devices with their start and end apart: 17, of which 8 were waited for; matrix products, arithmetic and copies ran while one was open for 4% of the time, Pallas kernels for 12%

profile of v4, /device:TPU:6, one launch (start us, length us, event | category | flops | bytes accessed | tf_op | source)
XLA Modules:
  0.0 122.3 jit_solution(16307392498654869815)
XLA Ops:
  0.8 2.7 %collective-permute-start.9 = (s32[128]{0:T(128)S(1)}, s32[128]{0:T(128)S(1)}, u32[]{:S(2)}, u32[]{:S(2)}) collective-permute-start(s32[128]{0:T(128)S(1)} %compare_select_fusion.5), channel_id=1, source_target_pairs={{0,3},{1,2},{2,1},{3,0},{4,7},{5,6},{6,5},{7,4},{8,11},{9,10},{10,... | collective-permute-start | bytes 1544 | tf_op jit(solution)/shard_map/ppermute | solution.py:436
  3.5 0.7 collective-permute-start.8
  4.3 1.1 reshape.339
  5.6 1.7 %collective-permute-start = (bf16[96,576]{1,0:T(8,128)(2,1)S(1)}, bf16[96,576]{1,0:T(8,128)(2,1)S(1)}, u32[]{:S(2)}, u32[]{:S(2)}) collective-permute-start(bf16[96,576]{1,0:T(8,128)(2,1)S(1)} %reshape.340.refs_0_.refs_8_.v0), channel_id=1, source_target_pairs={{0,16},{16,0},{32,48},{48,32},{1,17},{17,1},{33,49},{49,33},{2,18}... | collective-permute-start | bytes 331784 | tf_op jit(solution)/shard_map/ppermute | solution.py:460
  7.2 1.1 reshape.341
  8.6 3.3 %collective-permute-start.1 = (bf16[96,576]{1,0:T(8,128)(2,1)S(1)}, bf16[96,576]{1,0:T(8,128)(2,1)S(1)}, u32[]{:S(2)}, u32[]{:S(2)}) collective-permute-start(bf16[96,576]{1,0:T(8,128)(2,1)S(1)} %reshape.342.refs_2_.refs_10_.c0.refs_4_), channel_id=1, source_target_pairs={{0,64},{64,128},{128,192},{192,0},{1,65},{65,129},{129,193},{193,1... | collective-permute-start | bytes 331784 | tf_op jit(solution)/shard_map/ppermute | solution.py:461
  12.6 2.4 %collective-permute-start.11 = (s32[128]{0:T(128)S(1)}, s32[128]{0:T(128)S(1)}, u32[]{:S(2)}, u32[]{:S(2)}) collective-permute-start(s32[128]{0:T(128)S(1)} %add_add_fusion.1), channel_id=1, source_target_pairs={{0,8},{1,9},{2,10},{3,11},{4,12},{5,13},{6,14},{7,15},{8,0},{9,1},... | collective-permute-start | bytes 1544 | tf_op jit(solution)/shard_map/ppermute | solution.py:436
  15.0 1.2 collective-permute-start.10
  16.9 0.8 collective-permute-start.2
  17.7 0.9 collective-permute-done.10
  18.6 5.0 %collective-permute-done.2 = s32[2048]{0:T(1024)S(1)} collective-permute-done((s32[2048]{0:T(1024)S(1)}, s32[2048]{0:T(1024)S(1)}, u32[]{:S(2)}, u32[]{:S(2)}) %collective-permute-start.2) | collective-permute-done | bytes 8224 | tf_op jit(solution)/shard_map/ppermute | solution.py:469
  23.6 1.0 copy-done.1
  24.5 2.4 %planes.2 = (bf16[16,24,768]{2,1,0:T(8,128)(2,1)}, s32[16,128]{1,0:T(8,128)}, bf16[96,576]{1,0:T(8,128)(2,1)}, bf16[96,576]{1,0:T(8,128)(2,1)}, bf16[96,576]{1,0:T(8,128)(2,1)}, /*index=5*/bf16[96,576]{1,0:T(8,128)(2,1)}) custom-call(bf16[96,576]{1,0:T(8,128)(2,1)S(1)} %reshape.340.refs_0_.refs_8_.v0, ...), custom_call_target="tpu_custom_call" | custom-call | flops 50000000 | bytes 100000 | tf_op jit(solution)/shard_map/planes/pallas_call | solution.py:202
  26.9 7.0 %all-to-all-start = ((bf16[16,24,768]{2,1,0:T(8,128)(2,1)}), bf16[16,24,768]{2,1,0:T(8,128)(2,1)S(1)}, u32[]{:S(2)}, u32[]{:S(2)}) async-start(bf16[16,24,768]{2,1,0:T(8,128)(2,1)} %get-tuple-element.16), calls=%async_computation | async-start | bytes 1179648 | tf_op jit(solution)/shard_map/all_to_all | solution.py:471
  34.0 1.6 %fusion.3.lane_ref = bf16[576,128]{1,0:T(8,128)(2,1)S(1)} fusion(s32[128]{0:T(128)S(1)} %compare_select_fusion.4, s32[128]{0:T(128)S(1)} %get-tuple-element.41, s32[576]{0:T(1024)S(1)} %get-tuple-element.42, s32[128]{0:T(128)S(1)} %get-tuple-element.40, s32[576]{0:T(1024)S(1)} %get-tuple-element.43), kind=kLoop, calls=%fused_computation.4 | loop fusion | flops 958464 | bytes 153600 | tf_op jit(solution)/shard_map/convert_element_type | solution.py:490
  35.6 2.0 %collective-permute-start.3 = (bf16[96,576]{1,0:T(8,128)(2,1)}, bf16[96,576]{1,0:T(8,128)(2,1)S(1)}, u32[]{:S(2)}, u32[]{:S(2)}) collective-permute-start(bf16[96,576]{1,0:T(8,128)(2,1)} %get-tuple-element.19), channel_id=1, source_target_pairs={{0,32},{16,48},{32,0},{48,16},{1,33},{17,49},{33,1},{49,17},{2,34}... | collective-permute-start | bytes 331784 | tf_op jit(solution)/shard_map/ppermute | solution.py:472
  37.7 4.5 %collective-permute-start.5 = (bf16[96,576]{1,0:T(8,128)(2,1)}, bf16[96,576]{1,0:T(8,128)(2,1)S(1)}, u32[]{:S(2)}, u32[]{:S(2)}) collective-permute-start(bf16[96,576]{1,0:T(8,128)(2,1)} %get-tuple-element.21), channel_id=1, source_target_pairs={{0,64},{64,128},{128,192},{192,0},{1,65},{65,129},{129,193},{193,1... | collective-permute-start | bytes 331784 | tf_op jit(solution)/shard_map/ppermute | solution.py:474
  42.5 4.4 %collective-permute-done.4.v3.refs_3_ = bf16[96,576]{1,0:T(8,128)(2,1)S(1)} collective-permute-done((bf16[96,576]{1,0:T(8,128)(2,1)}, bf16[96,576]{1,0:T(8,128)(2,1)S(1)}, u32[]{:S(2)}, u32[]{:S(2)}) %collective-permute-start.4) | collective-permute-done | bytes 110624 | tf_op jit(solution)/shard_map/ppermute | solution.py:473
  46.9 4.3 %collective-permute-done.5.c2.refs_6_ = bf16[96,576]{1,0:T(8,128)(2,1)S(1)} collective-permute-done((bf16[96,576]{1,0:T(8,128)(2,1)}, bf16[96,576]{1,0:T(8,128)(2,1)S(1)}, u32[]{:S(2)}, u32[]{:S(2)}) %collective-permute-start.5) | collective-permute-done | bytes 110624 | tf_op jit(solution)/shard_map/ppermute | solution.py:474
  51.2 0.8 block.1.refs_12_
  52.0 5.1 %planes.3 = bf16[16,72,768]{2,1,0:T(8,128)(2,1)} custom-call(bf16[96,576]{1,0:T(8,128)(2,1)S(1)} %reshape.340.refs_0_.refs_8_.v0, bf16[96,576]{1,0:T(8,128)(2,1)S(1)} %collective-permute-done.refs_1_.refs_9_.v1, bf16[96,576]{1,0:T(8,128)(2,1)S(1)} %collective-permute-done.3.v2.refs_2_, bf16[96,576]{1,0:T(8,128)(2,1)S(1)} %collective-permute-done.4.v3.refs_3_, ...), custom_call_target="tpu_custom_call" | custom-call | flops 50000000 | bytes 100000 | tf_op jit(solution)/shard_map/planes/pallas_call | solution.py:202
  57.2 7.4 %all-to-all-start.1 = ((bf16[16,72,768]{2,1,0:T(8,128)(2,1)}), bf16[16,72,768]{2,1,0:T(8,128)(2,1)S(1)}, u32[]{:S(2)}, u32[]{:S(2)}) async-start(bf16[16,72,768]{2,1,0:T(8,128)(2,1)} %planes.3), calls=%async_computation.1 | async-start | bytes 3538944 | tf_op jit(solution)/shard_map/all_to_all | solution.py:498
  65.4 4.4 %first_points.1 = (f32[4,2048]{1,0:T(4,128)S(1)}, bf16[4,2048]{1,0:T(4,128)(2,1)S(1)}) custom-call(bf16[16,24,768]{2,1,0:T(8,128)(2,1)S(1)} %all-to-all-done.t_ref, bf16[384,384]{1,0:T(8,128)(2,1)S(1)} %copy-done.3, s32[1,2048]{1,0:T(1,128)S(1)} %bitcast.38, s32[1,2048]{1,0:T(1,128)S(1)} %bitcast.36, s32[1,2048]{1,0:T(1,128)S(1)} %get-tuple-element.39.far_ref, ...), custom_call_target="tpu_custom_call" | custom-call | flops 100000000 | bytes 100000 | tf_op jit(solution)/shard_map/first_points/pallas_call | solution.py:311
  69.8 18.4 %all-to-all-done.1.t_ref = bf16[16,72,768]{2,1,0:T(8,128)(2,1)S(1)} async-done(((bf16[16,72,768]{2,1,0:T(8,128)(2,1)}), bf16[16,72,768]{2,1,0:T(8,128)(2,1)S(1)}, u32[]{:S(2)}, u32[]{:S(2)}) %all-to-all-start.1) | async-done | bytes 1769504 | tf_op jit(solution)/shard_map/all_to_all | solution.py:498
  88.1 1.3 %copy-done.4 = bf16[768,768]{1,0:T(8,128)(2,1)S(1)} copy-done((bf16[768,768]{1,0:T(8,128)(2,1)S(1)}, bf16[768,768]{1,0:T(8,128)(2,1)}, u32[]{:S(2)}) %copy-start.4) | copy-done | bytes 1179672
  89.4 5.9 %second_far_points.1 = (bf16[16,2048]{1,0:T(8,128)(2,1)S(1)}, bf16[1152,768]{1,0:T(8,128)(2,1)S(1)}, f32[16,128]{1,0:T(8,128)S(1)}) custom-call(bf16[16,72,768]{2,1,0:T(8,128)(2,1)S(1)} %all-to-all-done.1.t_ref, bf16[768,768]{1,0:T(8,128)(2,1)S(1)} %copy-done.4, bf16[384,384]{1,0:T(8,128)(2,1)S(1)} %copy-done.3, s32[1,2048]{1,0:T(1,128)S(1)} %get-tuple-element.39.far_ref, ...), custom_call_target="tpu_custom_call" | custom-call | flops 100000000 | bytes 100000 | tf_op jit(solution)/shard_map/second_far_points/pallas_call | solution.py:327
  95.3 3.0 %collective-permute-start.13 = (bf16[16,2048]{1,0:T(8,128)(2,1)S(1)}, bf16[16,2048]{1,0:T(8,128)(2,1)S(1)}, u32[]{:S(2)}, u32[]{:S(2)}) collective-permute-start(bf16[16,2048]{1,0:T(8,128)(2,1)S(1)} %get-tuple-element.25), channel_id=1, source_target_pairs={{0,15},{1,14},{2,13},{3,12},{4,11},{5,10},{6,9},{7,8},{8,7},{9,6},... | collective-permute-start | bytes 196616 | tf_op jit(solution)/shard_map/ppermute | solution.py:520
  98.3 4.5 %second_own_points.1.own1_ref = f32[12,2048]{1,0:T(8,128)S(1)} custom-call(bf16[1152,768]{1,0:T(8,128)(2,1)S(1)} %get-tuple-element.24.low, s32[1,2048]{1,0:T(1,128)S(1)} %bitcast.39, s32[1,2048]{1,0:T(1,128)S(1)} %bitcast.37), custom_call_target="tpu_custom_call" | custom-call | flops 2400000000 | bytes 1300000 | tf_op jit(solution)/shard_map/second_own_points/pallas_call | solution.py:343
  103.2 0.8 split.1
  104.0 6.4 %all-to-all-start.2 = ((bf16[16,48,128]{2,1,0:T(8,128)(2,1)}), bf16[16,48,128]{2,1,0:T(8,128)(2,1)S(1)}, u32[]{:S(2)}, u32[]{:S(2)}) async-start(bf16[16,48,128]{2,1,0:T(8,128)(2,1)} %split.1), calls=%async_computation.2 | async-start | bytes 393216 | tf_op jit(solution)/shard_map/all_to_all | solution.py:523
  110.5 10.8 %all-to-all-done.2.pairs_ref = bf16[16,48,128]{2,1,0:T(8,128)(2,1)S(1)} async-done(((bf16[16,48,128]{2,1,0:T(8,128)(2,1)}), bf16[16,48,128]{2,1,0:T(8,128)(2,1)S(1)}, u32[]{:S(2)}, u32[]{:S(2)}) %all-to-all-start.2) | async-done | bytes 196640 | tf_op jit(solution)/shard_map/all_to_all | solution.py:523
  121.3 1.0 pair_sum.1
  (71 shorter events, 3.5 us)
Async XLA Ops:
  0.0 23.5 %copy-start = (bf16[576,1536]{1,0:T(8,128)(2,1)S(1)}, bf16[576,1536]{1,0:T(8,128)(2,1)}, u32[]{:S(2)}) copy-start(bf16[576,1536]{1,0:T(8,128)(2,1)} %constant.205.clone.refs_4_.refs_8_) | copy-start | bytes 5308420
  0.0 23.6 %copy-start.6 = (f32[2,16,768]{2,1,0:T(8,128)S(1)}, f32[2,16,768]{2,1,0:T(8,128)}, u32[]{:S(2)}) copy-start(f32[2,16,768]{2,1,0:T(8,128)} %constant.206.clone.refs_5_.refs_9_) | copy-start | bytes 294916
  0.0 16.8 %copy-start.10 = (s32[2048]{0:T(1024)S(1)}, s32[2048]{0:T(1024)}, u32[]{:S(2)}) copy-start(s32[2048]{0:T(1024)} %param.23) | copy-start | bytes 24580
  0.8 11.1 %collective-permute-start.9 = (s32[128]{0:T(128)S(1)}, s32[128]{0:T(128)S(1)}, u32[]{:S(2)}, u32[]{:S(2)}) collective-permute-start(s32[128]{0:T(128)S(1)} %compare_select_fusion.5), channel_id=1, source_target_pairs={{0,3},{1,2},{2,1},{3,0},{4,7},{5,6},{6,5},{7,4},{8,11},{9,10},{10,... | collective-permute-start | bytes 1544 | tf_op jit(solution)/shard_map/ppermute | solution.py:436
  3.5 8.4 %collective-permute-start.8 = (s32[128]{0:T(128)S(1)}, s32[128]{0:T(128)S(1)}, u32[]{:S(2)}, u32[]{:S(2)}) collective-permute-start(s32[128]{0:T(128)S(1)} %compare_select_fusion.5), channel_id=1, source_target_pairs={{0,2},{1,3},{2,0},{3,1},{4,6},{5,7},{6,4},{7,5},{8,10},{9,11},{10,... | collective-permute-start | bytes 1544 | tf_op jit(solution)/shard_map/ppermute | solution.py:436
  4.2 7.8 %collective-permute-start.7 = (s32[128]{0:T(128)S(1)}, s32[128]{0:T(128)S(1)}, u32[]{:S(2)}, u32[]{:S(2)}) collective-permute-start(s32[128]{0:T(128)S(1)} %compare_select_fusion.5), channel_id=1, source_target_pairs={{0,1},{1,0},{2,3},{3,2},{4,5},{5,4},{6,7},{7,6},{8,9},{9,8},{10,11... | collective-permute-start | bytes 1544 | tf_op jit(solution)/shard_map/ppermute | solution.py:436
  5.6 18.0 %collective-permute-start = (bf16[96,576]{1,0:T(8,128)(2,1)S(1)}, bf16[96,576]{1,0:T(8,128)(2,1)S(1)}, u32[]{:S(2)}, u32[]{:S(2)}) collective-permute-start(bf16[96,576]{1,0:T(8,128)(2,1)S(1)} %reshape.340.refs_0_.refs_8_.v0), channel_id=1, source_target_pairs={{0,16},{16,0},{32,48},{48,32},{1,17},{17,1},{33,49},{49,33},{2,18}... | collective-permute-start | bytes 331784 | tf_op jit(solution)/shard_map/ppermute | solution.py:460
  8.6 15.0 %collective-permute-start.1 = (bf16[96,576]{1,0:T(8,128)(2,1)S(1)}, bf16[96,576]{1,0:T(8,128)(2,1)S(1)}, u32[]{:S(2)}, u32[]{:S(2)}) collective-permute-start(bf16[96,576]{1,0:T(8,128)(2,1)S(1)} %reshape.342.refs_2_.refs_10_.c0.refs_4_), channel_id=1, source_target_pairs={{0,64},{64,128},{128,192},{192,0},{1,65},{65,129},{129,193},{193,1... | collective-permute-start | bytes 331784 | tf_op jit(solution)/shard_map/ppermute | solution.py:461
  12.0 4.8 %collective-permute-start.12 = (s32[128]{0:T(128)S(1)}, s32[128]{0:T(128)S(1)}, u32[]{:S(2)}, u32[]{:S(2)}) collective-permute-start(s32[128]{0:T(128)S(1)} %add_add_fusion.1), channel_id=1, source_target_pairs={{0,12},{1,13},{2,14},{3,15},{4,8},{5,9},{6,10},{7,11},{8,4},{9,5},... | collective-permute-start | bytes 1544 | tf_op jit(solution)/shard_map/ppermute | solution.py:436
  12.6 5.1 %collective-permute-start.11 = (s32[128]{0:T(128)S(1)}, s32[128]{0:T(128)S(1)}, u32[]{:S(2)}, u32[]{:S(2)}) collective-permute-start(s32[128]{0:T(128)S(1)} %add_add_fusion.1), channel_id=1, source_target_pairs={{0,8},{1,9},{2,10},{3,11},{4,12},{5,13},{6,14},{7,15},{8,0},{9,1},... | collective-permute-start | bytes 1544 | tf_op jit(solution)/shard_map/ppermute | solution.py:436
  15.0 3.5 %collective-permute-start.10 = (s32[128]{0:T(128)S(1)}, s32[128]{0:T(128)S(1)}, u32[]{:S(2)}, u32[]{:S(2)}) collective-permute-start(s32[128]{0:T(128)S(1)} %add_add_fusion.1), channel_id=1, source_target_pairs={{0,4},{1,5},{2,6},{3,7},{4,0},{5,1},{6,2},{7,3},{8,12},{9,13},{10,... | collective-permute-start | bytes 1544 | tf_op jit(solution)/shard_map/ppermute | solution.py:436
  16.9 6.7 %collective-permute-start.2 = (s32[2048]{0:T(1024)S(1)}, s32[2048]{0:T(1024)S(1)}, u32[]{:S(2)}, u32[]{:S(2)}) collective-permute-start(s32[2048]{0:T(1024)S(1)} %copy-done.10), channel_id=1, source_target_pairs={{0,15},{1,14},{2,13},{3,12},{4,11},{5,10},{6,9},{7,8},{8,7},{9,6},... | collective-permute-start | bytes 24584 | tf_op jit(solution)/shard_map/ppermute | solution.py:469
  26.9 25.0 %copy-start.2 = (bf16[384,384]{1,0:T(8,128)(2,1)S(1)}, bf16[384,384]{1,0:T(8,128)(2,1)}, u32[]{:S(2)}) copy-start(bf16[384,384]{1,0:T(8,128)(2,1)} %constant.207.clone.refs_6_.refs_11_) | copy-start | bytes 884740
  26.9 30.3 %all-to-all-start = ((bf16[16,24,768]{2,1,0:T(8,128)(2,1)}), bf16[16,24,768]{2,1,0:T(8,128)(2,1)S(1)}, u32[]{:S(2)}, u32[]{:S(2)}) async-start(bf16[16,24,768]{2,1,0:T(8,128)(2,1)} %get-tuple-element.16), calls=%async_computation | async-start | bytes 1179648 | tf_op jit(solution)/shard_map/all_to_all | solution.py:471
  34.0 18.0 %copy-start.5 = (bf16[768,768]{1,0:T(8,128)(2,1)S(1)}, bf16[768,768]{1,0:T(8,128)(2,1)}, u32[]{:S(2)}) copy-start(bf16[768,768]{1,0:T(8,128)(2,1)} %constant.208.clone.refs_10_) | copy-start | bytes 3538948
  35.6 6.9 %collective-permute-start.3 = (bf16[96,576]{1,0:T(8,128)(2,1)}, bf16[96,576]{1,0:T(8,128)(2,1)S(1)}, u32[]{:S(2)}, u32[]{:S(2)}) collective-permute-start(bf16[96,576]{1,0:T(8,128)(2,1)} %get-tuple-element.19), channel_id=1, source_target_pairs={{0,32},{16,48},{32,0},{48,16},{1,33},{17,49},{33,1},{49,17},{2,34}... | collective-permute-start | bytes 331784 | tf_op jit(solution)/shard_map/ppermute | solution.py:472
  37.6 9.3 %collective-permute-start.4 = (bf16[96,576]{1,0:T(8,128)(2,1)}, bf16[96,576]{1,0:T(8,128)(2,1)S(1)}, u32[]{:S(2)}, u32[]{:S(2)}) collective-permute-start(bf16[96,576]{1,0:T(8,128)(2,1)} %get-tuple-element.20), channel_id=1, source_target_pairs={{0,32},{16,48},{32,0},{48,16},{1,33},{17,49},{33,1},{49,17},{2,34}... | collective-permute-start | bytes 331784 | tf_op jit(solution)/shard_map/ppermute | solution.py:473
  37.7 13.5 %collective-permute-start.5 = (bf16[96,576]{1,0:T(8,128)(2,1)}, bf16[96,576]{1,0:T(8,128)(2,1)S(1)}, u32[]{:S(2)}, u32[]{:S(2)}) collective-permute-start(bf16[96,576]{1,0:T(8,128)(2,1)} %get-tuple-element.21), channel_id=1, source_target_pairs={{0,64},{64,128},{128,192},{192,0},{1,65},{65,129},{129,193},{193,1... | collective-permute-start | bytes 331784 | tf_op jit(solution)/shard_map/ppermute | solution.py:474
  42.2 9.0 %collective-permute-start.6 = (bf16[96,576]{1,0:T(8,128)(2,1)}, bf16[96,576]{1,0:T(8,128)(2,1)S(1)}, u32[]{:S(2)}, u32[]{:S(2)}) collective-permute-start(bf16[96,576]{1,0:T(8,128)(2,1)} %get-tuple-element.22), channel_id=1, source_target_pairs={{0,192},{64,0},{128,64},{192,128},{1,193},{65,1},{129,65},{193,129... | collective-permute-start | bytes 331784 | tf_op jit(solution)/shard_map/ppermute | solution.py:475
  57.1 7.5 %copy-start.15 = (f32[4]{0:T(128)S(1)}, f32[4]{0:T(128)}, u32[]{:S(2)}) copy-start(f32[4]{0:T(128)} %param.22) | copy-start | bytes 52
  57.1 7.6 %copy-start.9 = (f32[4096]{0:T(1024)S(1)}, f32[4096]{0:T(1024)}, u32[]{:S(2)}) copy-start(f32[4096]{0:T(1024)} %param.20) | copy-start | bytes 49156
  57.2 7.6 %copy-start.13 = (s32[16]{0:T(128)S(1)}, s32[16]{0:T(128)}, u32[]{:S(2)}) copy-start(s32[16]{0:T(128)} %param.19) | copy-start | bytes 196
  57.2 7.9 %copy-start.11 = (pred[256,16]{0,1:T(8,128)(4,1)S(1)}, pred[256,16]{0,1:T(8,128)(4,1)}, u32[]{:S(2)}) copy-start(pred[256,16]{0,1:T(8,128)(4,1)} %constant.209.clone) | copy-start | bytes 12292
  57.2 7.8 %copy-start.12 = (pred[256,16]{0,1:T(8,128)(4,1)S(1)}, pred[256,16]{0,1:T(8,128)(4,1)}, u32[]{:S(2)}) copy-start(pred[256,16]{0,1:T(8,128)(4,1)} %constant.210.clone) | copy-start | bytes 12292
  57.2 7.8 %copy-start.14 = (f32[16]{0:T(128)S(1)}, f32[16]{0:T(128)}, u32[]{:S(2)}) copy-start(f32[16]{0:T(128)} %param.21) | copy-start | bytes 196
  57.2 7.9 %copy-start.8 = (s32[16,128]{1,0:T(8,128)S(1)}, s32[16,128]{1,0:T(8,128)}, u32[]{:S(2)}) copy-start(s32[16,128]{1,0:T(8,128)} %get-tuple-element.17) | copy-start | bytes 24580
  57.2 8.1 %copy-start.3 = (bf16[384,384]{1,0:T(8,128)(2,1)S(1)}, bf16[384,384]{1,0:T(8,128)(2,1)}, u32[]{:S(2)}) copy-start(bf16[384,384]{1,0:T(8,128)(2,1)} %constant.211.clone.x_ref.x1_ref) | copy-start | bytes 884740
  57.2 30.9 %all-to-all-start.1 = ((bf16[16,72,768]{2,1,0:T(8,128)(2,1)}), bf16[16,72,768]{2,1,0:T(8,128)(2,1)S(1)}, u32[]{:S(2)}, u32[]{:S(2)}) async-start(bf16[16,72,768]{2,1,0:T(8,128)(2,1)} %planes.3), calls=%async_computation.1 | async-start | bytes 3538944 | tf_op jit(solution)/shard_map/all_to_all | solution.py:498
  88.1 1.3 %copy-start.4 = (bf16[768,768]{1,0:T(8,128)(2,1)S(1)}, bf16[768,768]{1,0:T(8,128)(2,1)}, u32[]{:S(2)}) copy-start(bf16[768,768]{1,0:T(8,128)(2,1)} %constant.212.clone.x0_ref) | copy-start | bytes 3538948
  95.3 7.9 %collective-permute-start.13 = (bf16[16,2048]{1,0:T(8,128)(2,1)S(1)}, bf16[16,2048]{1,0:T(8,128)(2,1)S(1)}, u32[]{:S(2)}, u32[]{:S(2)}) collective-permute-start(bf16[16,2048]{1,0:T(8,128)(2,1)S(1)} %get-tuple-element.25), channel_id=1, source_target_pairs={{0,15},{1,14},{2,13},{3,12},{4,11},{5,10},{6,9},{7,8},{8,7},{9,6},... | collective-permute-start | bytes 196616 | tf_op jit(solution)/shard_map/ppermute | solution.py:520
  98.3 23.0 %copy-start.7 = (bf16[2,128,128]{2,1,0:T(8,128)(2,1)S(1)}, bf16[2,128,128]{2,1,0:T(8,128)(2,1)}, u32[]{:S(2)}) copy-start(bf16[2,128,128]{2,1,0:T(8,128)(2,1)} %constant.213.clone.column_ref) | copy-start | bytes 196612
  104.0 17.4 %all-to-all-start.2 = ((bf16[16,48,128]{2,1,0:T(8,128)(2,1)}), bf16[16,48,128]{2,1,0:T(8,128)(2,1)S(1)}, u32[]{:S(2)}, u32[]{:S(2)}) async-start(bf16[16,48,128]{2,1,0:T(8,128)(2,1)} %split.1), calls=%async_computation.2 | async-start | bytes 393216 | tf_op jit(solution)/shard_map/all_to_all | solution.py:523
  (1 other events, 1.0 us)

commit v5 on v4

--- a/solution.py
+++ b/solution.py
@@ -22,19 +22,14 @@
 K7 = 7
 FLAT = K7 * N
 WIDE = 768
-GROUPS = (
-    (((0, 0), (0, 1)),),
-    (((1, 0), (1, 1), (0, 3), (1, 3)), ((0, 2), (1, 2))),
-)
-ITEM_LIST = [item for chunk in GROUPS for group in chunk for item in group]
+GROUPS = (((0, 1, 7),), ((2, 6, 3), (5, 4)))
+SLOTS = [slot for chunk in GROUPS for group in chunk for slot in group]
 SPARE = 640
 G_DEV = 2048
 NBLOCK = 16
 TILE = 512
 
-ITEM_ROWS = 2 * X6
-BAND = ("z1", "z0", "yl")
-VGROUP = ("z0", "yl")
+BAND = ("z", "yl")
 COL = ("x", "yh", "co")
 
 
@@ -69,6 +64,10 @@
     return table
 
 
+def slab_rows(items):
+    return -(-items * 2 * X6 // 8) * 8
+
+
 @functools.cache
 def row_table(items):
     table = np.zeros((SLABS, items, 2, X6, 2, items, X6, Y16))
@@ -79,7 +78,10 @@
             table[:, item, 0, x, 1, item, x] = -sine
             table[:, item, 1, x, 0, item, x] = sine
             table[:, item, 1, x, 1, item, x] = cosine
-    return bf16(table.reshape(SLABS * items * 2 * X6, 2 * items * X6 * Y16))
+    rows = items * 2 * X6
+    whole = np.zeros((SLABS, slab_rows(items), 2 * items * X6 * Y16))
+    whole[:, :rows] = table.reshape(SLABS, rows, -1)
+    return bf16(whole.reshape(SLABS * slab_rows(items), -1))
 
 
 @functools.cache
@@ -93,18 +95,21 @@
         table[0, item, :, :, item, 1] = -sine
         table[1, item, :, :, item, 0] = sine
         table[1, item, :, :, item, 1] = cosine
-    return bf16(table.reshape(2 * items * N, SLABS * items * 2 * X6))
+    rows = items * 2 * X6
+    whole = np.zeros((2 * items * N, SLABS, slab_rows(items)))
+    whole[:, :, :rows] = table.reshape(2 * items * N, SLABS, rows)
+    return bf16(whole.reshape(2 * items * N, -1))
 
 
 @functools.cache
 def pair_table():
     valence, conduction = [], []
     for band in range(16):
-        z1, group = divmod(band, 4)
+        z, yl = divmod(band, 2)
         for half in range(2):
-            for pair, slot in ITEM_LIST:
-                valence.append(z1 * 4 + (group ^ (2 * pair + half)))
-                conduction.append((z1 - slot) % 4 * 4 + group)
+            for slot in SLOTS:
+                valence.append(z * 2 + (yl ^ half))
+                conduction.append((z - slot) % 8 * 2 + yl)
     return np.array(valence), np.array(conduction)
 
 
@@ -125,15 +130,14 @@
 SLAB_CUTS = 4
 
 
-def plane_kernel(*refs, groups, slots, through):
+def plane_kernel(*refs, groups, place, through):
     refs = list(refs)
     take = lambda count: [refs.pop(0) for _ in range(count)]
-    waves = dict(zip(slots[0], take(len(slots[0]))))
-    waves_c = dict(zip(slots[1], take(len(slots[1]))))
-    lane_ref, twiddle_ref = take(2)
+    v0_ref, v1_ref = take(2)
+    c_refs = [take(len(group)) for group in groups]
+    lane_ref, twiddle_ref, extra_ref = take(3)
     row_refs = take(len(groups))
     kept = take(through)
-    block_refs = take(len(refs) - 4 - through - len(groups))
     (out_ref,) = take(1)
     kept_out = take(through)
     low_refs = take(len(groups))
@@ -147,12 +151,10 @@
     rows = X6 * Y16
     twiddle_c = twiddle_ref[0][None]
     twiddle_s = twiddle_ref[1][None]
-    for group, low_ref in zip(groups, low_refs):
-        for index, (pair, slot) in enumerate(group):
-            wave_c = waves_c[slot][...]
-            pairs = jnp.concatenate(
-                [waves[2 * pair][...] * wave_c, waves[2 * pair + 1][...] * wave_c], axis=0
-            )
+    for group, waves_c, low_ref in zip(groups, c_refs, low_refs):
+        for index, c_ref in enumerate(waves_c):
+            wave_c = c_ref[...]
+            pairs = jnp.concatenate([v0_ref[...] * wave_c, v1_ref[...] * wave_c], axis=0)
             moved = jnp.dot(pairs, lane_ref[...], preferred_element_type=F32)
             real = moved[:rows, :WIDE] - moved[rows:, WIDE:]
             imag = moved[:rows, WIDE:] + moved[rows:, :WIDE]
@@ -168,20 +170,21 @@
                 BF16
             )
     count = SLABS // SLAB_CUTS
+    extra = extra_ref[...]
     for part in range(SLAB_CUTS):
         slabs = slice(part * count, (part + 1) * count)
         first = 0
         for group, low_ref, row_ref in zip(groups, low_refs, row_refs):
-            size = len(group) * ITEM_ROWS
+            size = slab_rows(len(group))
             planes = jnp.dot(
                 row_ref[part * count * size : (part + 1) * count * size, :],
                 low_ref[...],
                 preferred_element_type=F32,
             ).reshape(count, size, WIDE)
             slab_ref[slabs, first : first + size, :] = planes.astype(BF16)
-            if first == 0 and block_refs:
-                spare = planes[:, :32, SPARE:] + block_refs[0][...][None]
-                slab_ref[slabs, :32, SPARE:] = spare.astype(BF16)
+            if first == place:
+                spare = planes[:, : extra.shape[0], SPARE:] + extra[None]
+                slab_ref[slabs, first : first + extra.shape[0], SPARE:] = spare.astype(BF16)
             first += size
         window = pl.ds(part * count, count)
         moves.append(
@@ -192,24 +195,23 @@
         move.wait()
 
 
-def planes_of(chunk, v, c, through=(), block=()):
+PLACE = slab_rows(len(GROUPS[1][0]))
+
+
+def planes_of(chunk, v, c, extra, through=()):
     groups = GROUPS[chunk]
-    items = [item for group in groups for item in group]
-    slots_v = sorted({2 * pair + half for pair, _ in items for half in range(2)})
-    slots_c = sorted({slot for _, slot in items})
-    rows = len(items) * ITEM_ROWS
+    slots = [slot for group in groups for slot in group]
+    rows = sum(slab_rows(len(group)) for group in groups)
     tables = [row_table(len(group)) for group in groups]
     return pl.pallas_call(
         functools.partial(
-            plane_kernel, groups=groups, slots=(slots_v, slots_c), through=len(through)
+            plane_kernel, groups=groups, place=chunk * PLACE, through=len(through)
         ),
         out_shape=[
             pltpu.HBM((SLABS, rows, WIDE), BF16),
             *(pltpu.HBM(x.shape, x.dtype) for x in through),
         ],
-        in_specs=[VMEM] * (len(slots_v) + len(slots_c) + 2 + len(tables))
-        + [ANY] * len(through)
-        + [VMEM] * len(block),
+        in_specs=[VMEM] * (2 + len(slots) + 3 + len(tables)) + [ANY] * len(through),
         out_specs=[HBM] * (1 + len(through)),
         scratch_shapes=[
             *(pltpu.VMEM((2 * len(group) * X6 * Y16, WIDE), BF16) for group in groups),
@@ -223,13 +225,13 @@
         ),
         name="planes",
     )(
-        *(v[slot] for slot in slots_v),
-        *(c[slot] for slot in slots_c),
+        *v,
+        *(c[slot] for slot in slots),
         lane_table(),
         twiddle_table(),
+        extra,
         *tables,
         *through,
-        *block,
     )
 
 
@@ -252,7 +254,7 @@
 def transform_x(chunk, t_ref, x_refs, low):
     first, place = 0, 0
     for group, x_ref in zip(GROUPS[chunk], x_refs):
-        size = len(group) * ITEM_ROWS
+        size = slab_rows(len(group))
         planes = t_ref[:, first : first + size, :]
         if size % 16:
             planes = planes.astype(F32)
@@ -291,8 +293,7 @@
         far_out[rows:, lanes] = values.astype(BF16)
 
     pick(low, far_ref, far_kx_ref, store_far)
-    spare = t_ref[:, :32, SPARE:].astype(F32).sum(axis=0)
-    spare = spare[:16] + spare[16:]
+    spare = t_ref[:, PLACE : PLACE + 16, SPARE:].astype(F32).sum(axis=0)
     spare = spare + pltpu.roll(spare, 128 - NBLOCK, 1)
     block_out[...] = spare
 
@@ -387,24 +388,28 @@
     )(own0, own1, far, block)
 
 
-def block_kernel(v0, v1, v2, v3, c0, c1, c2, c3, lane_ref, row_ref, out_ref):
-    waves = (v0, v1, v2, v3)
-    waves_c = (c0, c1, c2, c3)
+def block_kernel(*refs):
+    *waves, lane_ref, row_ref, out_ref = refs
+    waves_v, waves_c = waves[:2], waves[2:]
     for half in range(2):
-        for item, (pair, slot) in enumerate(ITEM_LIST):
-            product = waves[2 * pair + half][...] * waves_c[slot][...]
+        for item, slot in enumerate(SLOTS):
+            product = waves_v[half][...] * waves_c[slot][...]
             sums = jnp.dot(product, lane_ref[...], preferred_element_type=F32) * row_ref[...]
-            total = sums.sum(axis=0, keepdims=True)
-            high = total.astype(BF16).astype(F32)
-            index = half * len(ITEM_LIST) + item
-            out_ref[index : index + 1, :] = high
-            out_ref[16 + index : 17 + index, :] = total - high
+            index = half * len(SLOTS) + item
+            out_ref[index : index + 1, :] = sums.sum(axis=0, keepdims=True)
+    sums = out_ref[...]
+    sums = sums + pltpu.roll(sums, 128 - NBLOCK, 1)
+    high = sums.astype(BF16).astype(F32)
+    rest = pltpu.roll(sums - high, NBLOCK, 1)
+    lane = lax.broadcasted_iota(jnp.int32, sums.shape, 1)
+    sums = jnp.where(lane // NBLOCK % 2 == 0, high, rest)
+    out_ref[...] = jnp.where((lane >= 32) & (lane < 96), sums, 0.0)
 
 
 def block_sums(v, c, lanes, rows):
     return pl.pallas_call(
         block_kernel,
-        out_shape=jax.ShapeDtypeStruct((32, 128), F32),
+        out_shape=jax.ShapeDtypeStruct((16, 128), F32),
         compiler_params=pltpu.CompilerParams(vmem_limit_bytes=4 << 20),
         cost_estimate=pl.CostEstimate(
             flops=10_000_000, bytes_accessed=100_000, transcendentals=0
@@ -432,11 +437,6 @@
     return wave.reshape(X6, Y6, Y16, N).transpose(0, 2, 1, 3).reshape(X6 * Y16, Y6 * N)
 
 
-def spread(cells, masks):
-    arrived = [lax.ppermute(cells, COL, [(k, k ^ mask) for k in range(SLABS)]) for mask in masks]
-    return sum(arrived, cells)
-
-
 def cosine(phase):
     return jnp.cos((phase % N).astype(F32) * (2.0 * math.pi / N))
 
@@ -454,31 +454,30 @@
     col = lax.axis_index(COL)
     wave_v = wave_rows(valence_wave)
     wave_c = wave_rows(conduction_wave)
-    twin = [[(i, i ^ mask) for i in range(4)] for mask in range(4)]
-    ahead = [(i, (i + 1) % 4) for i in range(4)]
-    behind = [(i, (i + 3) % 4) for i in range(4)]
-    v = [wave_v, lax.ppermute(wave_v, VGROUP, twin[1])]
-    c = [wave_c, lax.ppermute(wave_c, "z1", ahead)]
-
-    spots = jnp.arange(128, dtype=jnp.int32)
-    cells = jnp.where(spots % NBLOCK == col, block_cell[0], 0)
-    cells = spread(cells, (1, 2, 3))
-    cells = spread(cells, (4, 8, 12))
+    ahead = [(i, (i + 1) % 8) for i in range(8)]
+    behind = [(i, (i + 7) % 8) for i in range(8)]
+    v = [wave_v, lax.ppermute(wave_v, "yl", [(0, 1), (1, 0)])]
+    c = [wave_c] + [None] * 7
+    for slot in (1, 2, 3, 4):
+        c[slot] = lax.ppermute(c[slot - 1], "z", ahead)
+        if slot < 4:
+            c[8 - slot] = lax.ppermute(c[(9 - slot) % 8], "z", behind)
 
     mirror_of = [(k, SLABS - 1 - k) for k in range(SLABS)]
     far_cell = lax.ppermute(gvec_cell, COL, mirror_of).reshape(16, 128)
-    planes0, far_cell, *passed = planes_of(0, v, c, through=(far_cell, *v, *c))
+    spots = jnp.arange(128, dtype=jnp.int32)
+    cell = jnp.where((spots % NBLOCK == col) & (spots >= 32), block_cell[0], 0)
+    marks = jnp.concatenate([jnp.stack([cell // 256, cell % 256]), jnp.zeros((6, 128), jnp.int32)])
+    planes0, far_cell = planes_of(0, v, c, marks.astype(F32), through=(far_cell,))
     sent0 = lax.all_to_all(planes0, COL, 0, 0, tiled=True)
-    v.append(lax.ppermute(passed[0], VGROUP, twin[2]))
-    v.append(lax.ppermute(passed[1], VGROUP, twin[2]))
-    c.append(lax.ppermute(passed[3], "z1", ahead))
-    c.append(lax.ppermute(passed[2], "z1", behind))
 
     far_cell = far_cell.reshape(G_DEV)
     far_x, far_y, far_z = far_cell // 576, far_cell // N % 6, far_cell % N
     own = ((gvec_cell % 576)[None], (gvec_cell // 576)[None])
     far = (((6 - far_y) * N + (N - far_z) % N)[None], ((N - far_x) % N)[None])
 
+    marks = sent0[:, :2, SPARE:].astype(F32).sum(axis=0)
+    cells = jnp.where(spots >= 32, (256.0 * marks[0] + marks[1]).astype(jnp.int32), 0)
     block_x = cells // 576
     block_y = spots % NBLOCK * 6 + cells // N % 6
     block_z = cells % N
@@ -494,7 +493,7 @@
     scale = 1.0 / (N * math.sqrt(N))
     rows = jnp.where((group >= 0) & (group < 4), rows * scale, 0.0)
     block = block_sums(v, c, lanes, rows)
-    (planes1,) = planes_of(1, v, c, block=(block,))
+    (planes1,) = planes_of(1, v, c, block)
     sent1 = lax.all_to_all(planes1, COL, 0, 0, tiled=True)
 
     pair_v, pair_c = pair_table()
@@ -531,7 +530,7 @@
 
 def solution(mesh):
     fine = Mesh(
-        mesh.devices.reshape(4, 2, 2, 4, 2, 2), ("z1", "z0", "yl", "x", "yh", "co")
+        mesh.devices.reshape(8, 2, 4, 2, 2), ("z", "yl", "x", "yh", "co")
     )
     return jax.shard_map(
         per_device,

time: 124 us -> 118 us (0.952)
  starting transfers between devices: 43.8 us -> 38.8 us
  waiting for transfers between devices: 44.8 us -> 41.6 us
  Pallas kernels: 24.8 us -> 27.3 us
    ppermute x12 -> x8, starting transfers between devices: 19.2 us -> 14.3 us  [the longest x3 10.5 us: per_device(): c[8 - slot] = lax.ppermute(c[(9 - slot) % 8], 'z', behind)]
    all_to_all x1, waiting for transfers between devices: 18.4 us -> 14.6 us  [per_device(): sent1 = lax.all_to_all(planes1, COL, 0, 0, tiled=True)]
    pallas_call x3, Pallas kernels: 8.29 us -> 10.7 us  [the longest x2 8.77 us: planes_of(): pl.pallas_call(functools.partial(plane_kernel, groups=groups, place=chunk...]
    all_to_all x1, waiting for transfers between devices: 0.01 us -> 2.18 us  [per_device(): sent0 = lax.all_to_all(planes0, COL, 0, 0, tiled=True)]
    ppermute x12 -> x8, waiting for transfers between devices: 10.2 us -> 8.46 us  [the longest x4 8.45 us: per_device(): c[slot] = lax.ppermute(c[slot - 1], 'z', ahead)]
    pallas_call x1, Pallas kernels: 4.39 us -> 6 us  [first_points(): pl.pallas_call(first_kernel, out_shape=(jax.ShapeDtypeStruct((FIRST, G_DE...]
  transfers between devices with their start and end apart: 17 -> 13, of which waited for: 8 -> 8; matrix products, arithmetic and copies ran while one was open for 4% -> 4% of each run, Pallas kernels for 12% -> 8%
where the time goes in v5:
time: 118 us; the launch traced here: 117 us
  waiting for transfers between devices  41.6 us (35%)
  starting transfers between devices  38.8 us (33%)
  Pallas kernels  27.3 us (23%)
  local copies, waits for them, and re-layouts  5.13 us (4%)
  other arithmetic  2.74 us (2%)
    all_to_all x1, waiting for transfers between devices, per_device(): sent1 = lax.all_to_all(planes1, COL, 0, 0, tiled=True)  14.6 us
    all_to_all x1, waiting for transfers between devices, per_device(): pairs = lax.all_to_all(pairs, BAND, 0, 0, tiled=True)  10.8 us
    ppermute x3, starting transfers between devices, per_device(): c[8 - slot] = lax.ppermute(c[(9 - slot) % 8], 'z', behind)  10.5 us
    pallas_call x2, Pallas kernels, planes_of(): pl.pallas_call(functools.partial(plane_kernel, groups=groups, place=chunk...  8.77 us
    ppermute x4, waiting for transfers between devices, per_device(): c[slot] = lax.ppermute(c[slot - 1], 'z', ahead)  8.45 us
    all_to_all x1, starting transfers between devices, per_device(): sent1 = lax.all_to_all(planes1, COL, 0, 0, tiled=True)  7.37 us
    all_to_all x1, starting transfers between devices, per_device(): sent0 = lax.all_to_all(planes0, COL, 0, 0, tiled=True)  6.88 us
    pallas_call x1, Pallas kernels, first_points(): pl.pallas_call(first_kernel, out_shape=(jax.ShapeDtypeStruct((FIRST, G_DE...  6 us
  transfers between devices with their start and end apart: 13, of which 8 were waited for; matrix products, arithmetic and copies ran while one was open for 4% of the time, Pallas kernels for 8%

profile of v5, /device:TPU:6, one launch (start us, length us, event | category | flops | bytes accessed | tf_op | source)
XLA Modules:
  0.0 116.6 jit_solution(5993746905594653828)
XLA Ops:
  0.0 1.2 %reshape.446 = bf16[6,6,16,96]{3,2,1,0:T(8,128)(2,1)S(1)} reshape(bf16[1,6,9216]{2,1,0:T(8,128)(2,1)} %param.18) | data formatting | bytes 221184 | tf_op jit(solution)/shard_map/reshape | solution.py:437
  1.5 2.0 %collective-permute-start.1 = (bf16[96,576]{1,0:T(8,128)(2,1)S(1)}, bf16[96,576]{1,0:T(8,128)(2,1)S(1)}, u32[]{:S(2)}, u32[]{:S(2)}) collective-permute-start(bf16[96,576]{1,0:T(8,128)(2,1)S(1)} %reshape.447.refs_2_), channel_id=1, source_target_pairs={{0,32},{32,64},{64,96},{96,128},{128,160},{160,192},{192,224},{224... | collective-permute-start | bytes 331784 | tf_op jit(solution)/shard_map/ppermute | solution.py:462
  3.5 4.0 %collective-permute-start.2 = (bf16[96,576]{1,0:T(8,128)(2,1)S(1)}, bf16[96,576]{1,0:T(8,128)(2,1)S(1)}, u32[]{:S(2)}, u32[]{:S(2)}) collective-permute-start(bf16[96,576]{1,0:T(8,128)(2,1)S(1)} %reshape.447.refs_2_), channel_id=1, source_target_pairs={{0,224},{32,0},{64,32},{96,64},{128,96},{160,128},{192,160},{224,1... | collective-permute-start | bytes 331784 | tf_op jit(solution)/shard_map/ppermute | solution.py:464
  7.5 1.1 reshape.444
  8.8 1.7 %collective-permute-start = (bf16[96,576]{1,0:T(8,128)(2,1)S(1)}, bf16[96,576]{1,0:T(8,128)(2,1)S(1)}, u32[]{:S(2)}, u32[]{:S(2)}) collective-permute-start(bf16[96,576]{1,0:T(8,128)(2,1)S(1)} %reshape.445.refs_0_), channel_id=1, source_target_pairs={{0,16},{16,0},{1,17},{17,1},{2,18},{18,2},{3,19},{19,3},{4,20},{20... | collective-permute-start | bytes 331784 | tf_op jit(solution)/shard_map/ppermute | solution.py:459
  10.5 1.7 %collective-permute-start.3 = (s32[2048]{0:T(1024)S(1)}, s32[2048]{0:T(1024)S(1)}, u32[]{:S(2)}, u32[]{:S(2)}) collective-permute-start(s32[2048]{0:T(1024)S(1)} %copy-done.11), channel_id=1, source_target_pairs={{0,15},{1,14},{2,13},{3,12},{4,11},{5,10},{6,9},{7,8},{8,7},{9,6},... | collective-permute-start | bytes 24584 | tf_op jit(solution)/shard_map/ppermute | solution.py:467
  13.0 4.2 %collective-permute-done.3 = s32[2048]{0:T(1024)S(1)} collective-permute-done((s32[2048]{0:T(1024)S(1)}, s32[2048]{0:T(1024)S(1)}, u32[]{:S(2)}, u32[]{:S(2)}) %collective-permute-start.3) | collective-permute-done | bytes 8224 | tf_op jit(solution)/shard_map/ppermute | solution.py:467
  17.2 1.1 copy-done.1
  18.3 3.3 %planes.2 = (bf16[16,40,768]{2,1,0:T(8,128)(2,1)}, s32[16,128]{1,0:T(8,128)}) custom-call(bf16[96,576]{1,0:T(8,128)(2,1)S(1)} %reshape.445.refs_0_, bf16[96,576]{1,0:T(8,128)(2,1)S(1)} %collective-permute-done.refs_1_, bf16[96,576]{1,0:T(8,128)(2,1)S(1)} %reshape.447.refs_2_, bf16[96,576]{1,0:T(8,128)(2,1)S(1)} %collective-permute-done.1.refs_3_, ...), custom_call_target="tpu_custom_call" | custom-call | flops 50000000 | bytes 100000 | tf_op jit(solution)/shard_map/planes/pallas_call | solution.py:206
  21.6 6.9 %all-to-all-start = ((bf16[16,40,768]{2,1,0:T(8,128)(2,1)}), bf16[16,40,768]{2,1,0:T(8,128)(2,1)S(1)}, u32[]{:S(2)}, u32[]{:S(2)}) async-start(bf16[16,40,768]{2,1,0:T(8,128)(2,1)} %get-tuple-element.12), calls=%async_computation | async-start | bytes 1966080 | tf_op jit(solution)/shard_map/all_to_all | solution.py:472
  28.7 3.2 %collective-permute-start.5 = (bf16[96,576]{1,0:T(8,128)(2,1)S(1)}, bf16[96,576]{1,0:T(8,128)(2,1)}, u32[]{:S(2)}, u32[]{:S(2)}) collective-permute-start(bf16[96,576]{1,0:T(8,128)(2,1)S(1)} %collective-permute-done.2.refs_4_.refs_9_), channel_id=1, source_target_pairs={{0,224},{32,0},{64,32},{96,64},{128,96},{160,128},{192,160},{224,1... | collective-permute-start | bytes 331784 | tf_op jit(solution)/shard_map/ppermute | solution.py:464
  31.9 3.3 %collective-permute-done.4.refs_4_.refs_2_ = bf16[96,576]{1,0:T(8,128)(2,1)S(1)} collective-permute-done((bf16[96,576]{1,0:T(8,128)(2,1)S(1)}, bf16[96,576]{1,0:T(8,128)(2,1)S(1)}, u32[]{:S(2)}, u32[]{:S(2)}) %collective-permute-start.4) | collective-permute-done | bytes 110624 | tf_op jit(solution)/shard_map/ppermute | solution.py:462
  35.3 3.3 %collective-permute-start.7 = (bf16[96,576]{1,0:T(8,128)(2,1)}, bf16[96,576]{1,0:T(8,128)(2,1)}, u32[]{:S(2)}, u32[]{:S(2)}) collective-permute-start(bf16[96,576]{1,0:T(8,128)(2,1)} %collective-permute-done.5.refs_8_.refs_3_), channel_id=1, source_target_pairs={{0,224},{32,0},{64,32},{96,64},{128,96},{160,128},{192,160},{224,1... | collective-permute-start | bytes 331784 | tf_op jit(solution)/shard_map/ppermute | solution.py:464
  38.6 2.9 %collective-permute-done.6.refs_5_.refs_4_ = bf16[96,576]{1,0:T(8,128)(2,1)} collective-permute-done((bf16[96,576]{1,0:T(8,128)(2,1)S(1)}, bf16[96,576]{1,0:T(8,128)(2,1)}, u32[]{:S(2)}, u32[]{:S(2)}) %collective-permute-start.6) | collective-permute-done | bytes 110624 | tf_op jit(solution)/shard_map/ppermute | solution.py:462
  41.4 2.2 %all-to-all-done.t_ref = bf16[16,40,768]{2,1,0:T(8,128)(2,1)S(1)} async-done(((bf16[16,40,768]{2,1,0:T(8,128)(2,1)}), bf16[16,40,768]{2,1,0:T(8,128)(2,1)S(1)}, u32[]{:S(2)}, u32[]{:S(2)}) %all-to-all-start) | async-done | bytes 983072 | tf_op jit(solution)/shard_map/all_to_all | solution.py:472
  43.7 1.6 %fusion.3.refs_10_ = bf16[576,128]{1,0:T(8,128)(2,1)S(1)} fusion(s32[128]{0:T(128)S(1)} %compare_select_fusion.4, s32[128]{0:T(128)S(1)} %get-tuple-element.33, s32[576]{0:T(1024)S(1)} %get-tuple-element.36, s32[128]{0:T(128)S(1)} %get-tuple-element.32, s32[576]{0:T(1024)S(1)} %get-tuple-element.37), kind=kLoop, calls=%fused_computation.4 | loop fusion | flops 958464 | bytes 153600 | tf_op jit(solution)/shard_map/convert_element_type | solution.py:489
  45.3 0.3 fusion.11.refs_11_
  45.6 2.2 %collective-permute-done.8.refs_6_ = bf16[96,576]{1,0:T(8,128)(2,1)} collective-permute-done((bf16[96,576]{1,0:T(8,128)(2,1)}, bf16[96,576]{1,0:T(8,128)(2,1)}, u32[]{:S(2)}, u32[]{:S(2)}) %collective-permute-start.8) | collective-permute-done | bytes 110624 | tf_op jit(solution)/shard_map/ppermute | solution.py:462
  47.8 2.0 %block.1.refs_9_ = f32[16,128]{1,0:T(8,128)S(1)} custom-call(bf16[96,576]{1,0:T(8,128)(2,1)S(1)} %reshape.445.refs_0_, bf16[96,576]{1,0:T(8,128)(2,1)S(1)} %collective-permute-done.refs_1_, bf16[96,576]{1,0:T(8,128)(2,1)S(1)} %reshape.447.refs_2_, bf16[96,576]{1,0:T(8,128)(2,1)S(1)} %collective-permute-done.1.refs_3_, ...), custom_call_target="tpu_custom_call" | custom-call | flops 10000000 | bytes 100000 | tf_op jit(solution)/shard_map/block/pallas_call | solution.py:410
  49.8 5.5 %planes.3 = bf16[16,64,768]{2,1,0:T(8,128)(2,1)} custom-call(bf16[96,576]{1,0:T(8,128)(2,1)S(1)} %reshape.445.refs_0_, bf16[96,576]{1,0:T(8,128)(2,1)S(1)} %collective-permute-done.refs_1_, bf16[96,576]{1,0:T(8,128)(2,1)S(1)} %collective-permute-done.4.refs_4_.refs_2_, bf16[96,576]{1,0:T(8,128)(2,1)} %collective-permute-done.5.refs_8_.refs_3_, ...), custom_call_target="tpu_custom_call" | custom-call | flops 50000000 | bytes 100000 | tf_op jit(solution)/shard_map/planes/pallas_call | solution.py:206
  55.4 7.4 %all-to-all-start.1 = ((bf16[16,64,768]{2,1,0:T(8,128)(2,1)}), bf16[16,64,768]{2,1,0:T(8,128)(2,1)S(1)}, u32[]{:S(2)}, u32[]{:S(2)}) async-start(bf16[16,64,768]{2,1,0:T(8,128)(2,1)} %planes.3), calls=%async_computation.1 | async-start | bytes 3145728 | tf_op jit(solution)/shard_map/all_to_all | solution.py:497
  63.5 6.0 %first_points.1 = (f32[6,2048]{1,0:T(8,128)S(1)}, bf16[6,2048]{1,0:T(8,128)(2,1)S(1)}) custom-call(bf16[16,40,768]{2,1,0:T(8,128)(2,1)S(1)} %all-to-all-done.t_ref, bf16[576,640]{1,0:T(8,128)(2,1)S(1)} %copy-done.3, s32[1,2048]{1,0:T(1,128)S(1)} %bitcast.43, s32[1,2048]{1,0:T(1,128)S(1)} %bitcast.41, s32[1,2048]{1,0:T(1,128)S(1)} %get-tuple-element.31.far_ref, ...), custom_call_target="tpu_custom_call" | custom-call | flops 100000000 | bytes 100000 | tf_op jit(solution)/shard_map/first_points/pallas_call | solution.py:312
  69.5 14.6 %all-to-all-done.1.t_ref = bf16[16,64,768]{2,1,0:T(8,128)(2,1)S(1)} async-done(((bf16[16,64,768]{2,1,0:T(8,128)(2,1)}), bf16[16,64,768]{2,1,0:T(8,128)(2,1)S(1)}, u32[]{:S(2)}, u32[]{:S(2)}) %all-to-all-start.1) | async-done | bytes 1572896 | tf_op jit(solution)/shard_map/all_to_all | solution.py:497
  84.2 1.0 copy-done.6
  85.1 5.0 %second_far_points.1 = (bf16[16,2048]{1,0:T(8,128)(2,1)S(1)}, bf16[960,768]{1,0:T(8,128)(2,1)S(1)}, f32[16,128]{1,0:T(8,128)S(1)}) custom-call(bf16[16,64,768]{2,1,0:T(8,128)(2,1)S(1)} %all-to-all-done.1.t_ref, bf16[576,640]{1,0:T(8,128)(2,1)S(1)} %copy-done.3, bf16[384,384]{1,0:T(8,128)(2,1)S(1)} %copy-done.6, s32[1,2048]{1,0:T(1,128)S(1)} %get-tuple-element.31.far_ref, ...), custom_call_target="tpu_custom_call" | custom-call | flops 100000000 | bytes 100000 | tf_op jit(solution)/shard_map/second_far_points/pallas_call | solution.py:328
  90.2 2.7 %collective-permute-start.9 = (bf16[16,2048]{1,0:T(8,128)(2,1)S(1)}, bf16[16,2048]{1,0:T(8,128)(2,1)S(1)}, u32[]{:S(2)}, u32[]{:S(2)}) collective-permute-start(bf16[16,2048]{1,0:T(8,128)(2,1)S(1)} %get-tuple-element.17), channel_id=1, source_target_pairs={{0,15},{1,14},{2,13},{3,12},{4,11},{5,10},{6,9},{7,8},{8,7},{9,6},... | collective-permute-start | bytes 196616 | tf_op jit(solution)/shard_map/ppermute | solution.py:519
  92.9 3.8 %second_own_points.1.own1_ref = f32[10,2048]{1,0:T(8,128)S(1)} custom-call(bf16[960,768]{1,0:T(8,128)(2,1)S(1)} %get-tuple-element.16.low, s32[1,2048]{1,0:T(1,128)S(1)} %bitcast.44, s32[1,2048]{1,0:T(1,128)S(1)} %bitcast.42), custom_call_target="tpu_custom_call" | custom-call | flops 2400000000 | bytes 1300000 | tf_op jit(solution)/shard_map/second_own_points/pallas_call | solution.py:344
  96.7 1.3 %collective-permute-done.9.far_ref = bf16[16,2048]{1,0:T(8,128)(2,1)S(1)} collective-permute-done((bf16[16,2048]{1,0:T(8,128)(2,1)S(1)}, bf16[16,2048]{1,0:T(8,128)(2,1)S(1)}, u32[]{:S(2)}, u32[]{:S(2)}) %collective-permute-start.9) | collective-permute-done | bytes 65568 | tf_op jit(solution)/shard_map/ppermute | solution.py:519
  98.0 0.8 split.1
  98.8 5.9 %all-to-all-start.2 = ((bf16[16,48,128]{2,1,0:T(8,128)(2,1)}), bf16[16,48,128]{2,1,0:T(8,128)(2,1)S(1)}, u32[]{:S(2)}, u32[]{:S(2)}) async-start(bf16[16,48,128]{2,1,0:T(8,128)(2,1)} %split.1), calls=%async_computation.2 | async-start | bytes 393216 | tf_op jit(solution)/shard_map/all_to_all | solution.py:522
  104.8 10.8 %all-to-all-done.2.pairs_ref = bf16[16,48,128]{2,1,0:T(8,128)(2,1)S(1)} async-done(((bf16[16,48,128]{2,1,0:T(8,128)(2,1)}), bf16[16,48,128]{2,1,0:T(8,128)(2,1)S(1)}, u32[]{:S(2)}, u32[]{:S(2)}) %all-to-all-start.2) | async-done | bytes 196640 | tf_op jit(solution)/shard_map/all_to_all | solution.py:522
  115.7 1.0 pair_sum.1
  (67 shorter events, 1.7 us)
Async XLA Ops:
  0.0 17.2 %copy-start = (bf16[576,1536]{1,0:T(8,128)(2,1)S(1)}, bf16[576,1536]{1,0:T(8,128)(2,1)}, u32[]{:S(2)}) copy-start(bf16[576,1536]{1,0:T(8,128)(2,1)} %constant.230.clone.refs_5_.refs_7_) | copy-start | bytes 5308420
  0.0 17.2 %copy-start.4 = (f32[2,16,768]{2,1,0:T(8,128)S(1)}, f32[2,16,768]{2,1,0:T(8,128)}, u32[]{:S(2)}) copy-start(f32[2,16,768]{2,1,0:T(8,128)} %constant.231.clone.refs_6_.refs_8_) | copy-start | bytes 294916
  0.0 10.4 %copy-start.11 = (s32[2048]{0:T(1024)S(1)}, s32[2048]{0:T(1024)}, u32[]{:S(2)}) copy-start(s32[2048]{0:T(1024)} %param.23) | copy-start | bytes 24580
  1.5 15.7 %collective-permute-start.1 = (bf16[96,576]{1,0:T(8,128)(2,1)S(1)}, bf16[96,576]{1,0:T(8,128)(2,1)S(1)}, u32[]{:S(2)}, u32[]{:S(2)}) collective-permute-start(bf16[96,576]{1,0:T(8,128)(2,1)S(1)} %reshape.447.refs_2_), channel_id=1, source_target_pairs={{0,32},{32,64},{64,96},{96,128},{128,160},{160,192},{192,224},{224... | collective-permute-start | bytes 331784 | tf_op jit(solution)/shard_map/ppermute | solution.py:462
  3.5 13.7 %collective-permute-start.2 = (bf16[96,576]{1,0:T(8,128)(2,1)S(1)}, bf16[96,576]{1,0:T(8,128)(2,1)S(1)}, u32[]{:S(2)}, u32[]{:S(2)}) collective-permute-start(bf16[96,576]{1,0:T(8,128)(2,1)S(1)} %reshape.447.refs_2_), channel_id=1, source_target_pairs={{0,224},{32,0},{64,32},{96,64},{128,96},{160,128},{192,160},{224,1... | collective-permute-start | bytes 331784 | tf_op jit(solution)/shard_map/ppermute | solution.py:464
  8.8 8.4 %collective-permute-start = (bf16[96,576]{1,0:T(8,128)(2,1)S(1)}, bf16[96,576]{1,0:T(8,128)(2,1)S(1)}, u32[]{:S(2)}, u32[]{:S(2)}) collective-permute-start(bf16[96,576]{1,0:T(8,128)(2,1)S(1)} %reshape.445.refs_0_), channel_id=1, source_target_pairs={{0,16},{16,0},{1,17},{17,1},{2,18},{18,2},{3,19},{19,3},{4,20},{20... | collective-permute-start | bytes 331784 | tf_op jit(solution)/shard_map/ppermute | solution.py:459
  10.5 6.7 %collective-permute-start.3 = (s32[2048]{0:T(1024)S(1)}, s32[2048]{0:T(1024)S(1)}, u32[]{:S(2)}, u32[]{:S(2)}) collective-permute-start(s32[2048]{0:T(1024)S(1)} %copy-done.11), channel_id=1, source_target_pairs={{0,15},{1,14},{2,13},{3,12},{4,11},{5,10},{6,9},{7,8},{8,7},{9,6},... | collective-permute-start | bytes 24584 | tf_op jit(solution)/shard_map/ppermute | solution.py:467
  17.2 1.1 copy-start.1
  21.6 22.0 %all-to-all-start = ((bf16[16,40,768]{2,1,0:T(8,128)(2,1)}), bf16[16,40,768]{2,1,0:T(8,128)(2,1)S(1)}, u32[]{:S(2)}, u32[]{:S(2)}) async-start(bf16[16,40,768]{2,1,0:T(8,128)(2,1)} %get-tuple-element.12), calls=%async_computation | async-start | bytes 1966080 | tf_op jit(solution)/shard_map/all_to_all | solution.py:472
  28.6 6.7 %collective-permute-start.4 = (bf16[96,576]{1,0:T(8,128)(2,1)S(1)}, bf16[96,576]{1,0:T(8,128)(2,1)S(1)}, u32[]{:S(2)}, u32[]{:S(2)}) collective-permute-start(bf16[96,576]{1,0:T(8,128)(2,1)S(1)} %collective-permute-done.1.refs_3_), channel_id=1, source_target_pairs={{0,32},{32,64},{64,96},{96,128},{128,160},{160,192},{192,224},{224... | collective-permute-start | bytes 331784 | tf_op jit(solution)/shard_map/ppermute | solution.py:462
  28.7 6.6 %collective-permute-start.5 = (bf16[96,576]{1,0:T(8,128)(2,1)S(1)}, bf16[96,576]{1,0:T(8,128)(2,1)}, u32[]{:S(2)}, u32[]{:S(2)}) collective-permute-start(bf16[96,576]{1,0:T(8,128)(2,1)S(1)} %collective-permute-done.2.refs_4_.refs_9_), channel_id=1, source_target_pairs={{0,224},{32,0},{64,32},{96,64},{128,96},{160,128},{192,160},{224,1... | collective-permute-start | bytes 331784 | tf_op jit(solution)/shard_map/ppermute | solution.py:464
  35.2 6.2 %collective-permute-start.6 = (bf16[96,576]{1,0:T(8,128)(2,1)S(1)}, bf16[96,576]{1,0:T(8,128)(2,1)}, u32[]{:S(2)}, u32[]{:S(2)}) collective-permute-start(bf16[96,576]{1,0:T(8,128)(2,1)S(1)} %collective-permute-done.4.refs_4_.refs_2_), channel_id=1, source_target_pairs={{0,32},{32,64},{64,96},{96,128},{128,160},{160,192},{192,224},{224... | collective-permute-start | bytes 331784 | tf_op jit(solution)/shard_map/ppermute | solution.py:462
  35.3 10.3 %collective-permute-start.7 = (bf16[96,576]{1,0:T(8,128)(2,1)}, bf16[96,576]{1,0:T(8,128)(2,1)}, u32[]{:S(2)}, u32[]{:S(2)}) collective-permute-start(bf16[96,576]{1,0:T(8,128)(2,1)} %collective-permute-done.5.refs_8_.refs_3_), channel_id=1, source_target_pairs={{0,224},{32,0},{64,32},{96,64},{128,96},{160,128},{192,160},{224,1... | collective-permute-start | bytes 331784 | tf_op jit(solution)/shard_map/ppermute | solution.py:464
  41.4 6.4 %collective-permute-start.8 = (bf16[96,576]{1,0:T(8,128)(2,1)}, bf16[96,576]{1,0:T(8,128)(2,1)}, u32[]{:S(2)}, u32[]{:S(2)}) collective-permute-start(bf16[96,576]{1,0:T(8,128)(2,1)} %collective-permute-done.6.refs_5_.refs_4_), channel_id=1, source_target_pairs={{0,32},{32,64},{64,96},{96,128},{128,160},{160,192},{192,224},{224... | collective-permute-start | bytes 331784 | tf_op jit(solution)/shard_map/ppermute | solution.py:462
  43.6 6.2 %copy-start.2 = (bf16[640,576]{1,0:T(8,128)(2,1)S(1)}, bf16[640,576]{1,0:T(8,128)(2,1)}, u32[]{:S(2)}) copy-start(bf16[640,576]{1,0:T(8,128)(2,1)} %constant.232.clone.refs_8_.refs_10_) | copy-start | bytes 2211844
  43.6 6.2 %copy-start.5 = (f32[2,16,768]{2,1,0:T(8,128)S(1)}, f32[2,16,768]{2,1,0:T(8,128)}, u32[]{:S(2)}) copy-start(f32[2,16,768]{2,1,0:T(8,128)} %constant.231.clone.refs_6_.refs_8_) | copy-start | bytes 294916
  43.6 6.2 %copy-start.7 = (bf16[384,384]{1,0:T(8,128)(2,1)S(1)}, bf16[384,384]{1,0:T(8,128)(2,1)}, u32[]{:S(2)}) copy-start(bf16[384,384]{1,0:T(8,128)(2,1)} %constant.233.clone.refs_11_) | copy-start | bytes 884740
  55.3 7.5 %copy-start.16 = (f32[4]{0:T(128)S(1)}, f32[4]{0:T(128)}, u32[]{:S(2)}) copy-start(f32[4]{0:T(128)} %param.22) | copy-start | bytes 52
  55.3 7.6 %copy-start.10 = (f32[4096]{0:T(1024)S(1)}, f32[4096]{0:T(1024)}, u32[]{:S(2)}) copy-start(f32[4096]{0:T(1024)} %param.20) | copy-start | bytes 49156
  55.3 7.6 %copy-start.14 = (s32[16]{0:T(128)S(1)}, s32[16]{0:T(128)}, u32[]{:S(2)}) copy-start(s32[16]{0:T(128)} %param.19) | copy-start | bytes 196
  55.3 7.8 %copy-start.12 = (pred[256,16]{0,1:T(8,128)(4,1)S(1)}, pred[256,16]{0,1:T(8,128)(4,1)}, u32[]{:S(2)}) copy-start(pred[256,16]{0,1:T(8,128)(4,1)} %constant.234.clone) | copy-start | bytes 12292
  55.4 7.8 %copy-start.13 = (pred[256,16]{0,1:T(8,128)(4,1)S(1)}, pred[256,16]{0,1:T(8,128)(4,1)}, u32[]{:S(2)}) copy-start(pred[256,16]{0,1:T(8,128)(4,1)} %constant.235.clone) | copy-start | bytes 12292
  55.4 7.8 %copy-start.15 = (f32[16]{0:T(128)S(1)}, f32[16]{0:T(128)}, u32[]{:S(2)}) copy-start(f32[16]{0:T(128)} %param.21) | copy-start | bytes 196
  55.4 7.9 %copy-start.9 = (s32[16,128]{1,0:T(8,128)S(1)}, s32[16,128]{1,0:T(8,128)}, u32[]{:S(2)}) copy-start(s32[16,128]{1,0:T(8,128)} %get-tuple-element.13) | copy-start | bytes 24580
  55.4 8.1 %copy-start.3 = (bf16[576,640]{1,0:T(8,128)(2,1)S(1)}, bf16[576,640]{1,0:T(8,128)(2,1)}, u32[]{:S(2)}) copy-start(bf16[576,640]{1,0:T(8,128)(2,1)} %constant.236.clone.x_ref.x0_ref) | copy-start | bytes 2211844
  55.4 28.8 %all-to-all-start.1 = ((bf16[16,64,768]{2,1,0:T(8,128)(2,1)}), bf16[16,64,768]{2,1,0:T(8,128)(2,1)S(1)}, u32[]{:S(2)}, u32[]{:S(2)}) async-start(bf16[16,64,768]{2,1,0:T(8,128)(2,1)} %planes.3), calls=%async_computation.1 | async-start | bytes 3145728 | tf_op jit(solution)/shard_map/all_to_all | solution.py:497
  84.2 1.0 copy-start.6
  90.2 7.8 %collective-permute-start.9 = (bf16[16,2048]{1,0:T(8,128)(2,1)S(1)}, bf16[16,2048]{1,0:T(8,128)(2,1)S(1)}, u32[]{:S(2)}, u32[]{:S(2)}) collective-permute-start(bf16[16,2048]{1,0:T(8,128)(2,1)S(1)} %get-tuple-element.17), channel_id=1, source_target_pairs={{0,15},{1,14},{2,13},{3,12},{4,11},{5,10},{6,9},{7,8},{8,7},{9,6},... | collective-permute-start | bytes 196616 | tf_op jit(solution)/shard_map/ppermute | solution.py:519
  92.9 22.7 %copy-start.8 = (bf16[2,128,128]{2,1,0:T(8,128)(2,1)S(1)}, bf16[2,128,128]{2,1,0:T(8,128)(2,1)}, u32[]{:S(2)}) copy-start(bf16[2,128,128]{2,1,0:T(8,128)(2,1)} %constant.238.clone.column_ref) | copy-start | bytes 196612
  98.8 16.8 %all-to-all-start.2 = ((bf16[16,48,128]{2,1,0:T(8,128)(2,1)}), bf16[16,48,128]{2,1,0:T(8,128)(2,1)S(1)}, u32[]{:S(2)}, u32[]{:S(2)}) async-start(bf16[16,48,128]{2,1,0:T(8,128)(2,1)} %split.1), calls=%async_computation.2 | async-start | bytes 393216 | tf_op jit(solution)/shard_map/all_to_all | solution.py:522

commit v6 on v5

v6 whole, which is shorter than its diff:
```python
import functools
import math

import jax
import jax.numpy as jnp
import ml_dtypes
import numpy as np
from jax import lax
from jax.experimental import pallas as pl
from jax.experimental.pallas import tpu as pltpu
from jax.sharding import Mesh
from jax.sharding import PartitionSpec as P

BF16 = jnp.bfloat16
F32 = jnp.float32

N = 96
SLABS = 16
X6 = 6
Y6 = 6
Y16 = 16
K7 = 7
FLAT = K7 * N
WIDE = 768
GROUPS = ((0, 1), (7, 2), (6, 3), (5, 4))
SLOTS = [slot for group in GROUPS for slot in group]
ITEMS = len(SLOTS)
SPARE = 640
G_DEV = 2048
NBLOCK = 16
TILE = 512
ROWS = ITEMS * 2 * X6

BAND = ("z", "yl")
COL = ("x", "yh", "co")


def unit(phase, period):
    angle = 2.0 * np.pi * (np.asarray(phase) % period) / period
    return np.cos(angle), -np.sin(angle)


def bf16(table):
    return np.asarray(table, np.float32).astype(ml_dtypes.bfloat16)


@functools.cache
def lane_table():
    y6, z = np.divmod(np.arange(Y6 * N), N)
    k7, kz = np.divmod(np.arange(FLAT), N)
    phase = 16 * y6[:, None] * k7[None, :] + z[:, None] * kz[None, :]
    cosine, sine = unit(phase, N)
    table = np.zeros((Y6 * N, 2 * WIDE))
    table[:, :FLAT] = cosine
    table[:, WIDE : WIDE + FLAT] = sine
    return bf16(table)


@functools.cache
def twiddle_table():
    k7 = np.arange(FLAT) // N
    cosine, sine = unit(np.arange(Y16)[:, None] * k7[None, :], N)
    table = np.zeros((2, Y16, WIDE), np.float32)
    table[0, :, :FLAT] = cosine / N
    table[1, :, :FLAT] = sine / N
    return table


@functools.cache
def row_table(items):
    table = np.zeros((SLABS, items, 2, X6, 2, items, X6, Y16))
    cosine, sine = unit(np.arange(SLABS)[:, None] * np.arange(Y16)[None, :], SLABS)
    for item in range(items):
        for x in range(X6):
            table[:, item, 0, x, 0, item, x] = cosine
            table[:, item, 0, x, 1, item, x] = -sine
            table[:, item, 1, x, 0, item, x] = sine
            table[:, item, 1, x, 1, item, x] = cosine
    return bf16(table.reshape(SLABS * items * 2 * X6, 2 * items * X6 * Y16))


@functools.cache
def x_table(items):
    table = np.zeros((2, items, N, SLABS, items, 2, X6))
    cosine, sine = unit(np.arange(N)[:, None] * np.arange(N)[None, :], N)
    cosine = (cosine * 0.5 / math.sqrt(N)).reshape(N, SLABS, X6)
    sine = (sine * 0.5 / math.sqrt(N)).reshape(N, SLABS, X6)
    for item in range(items):
        table[0, item, :, :, item, 0] = cosine
        table[0, item, :, :, item, 1] = -sine
        table[1, item, :, :, item, 0] = sine
        table[1, item, :, :, item, 1] = cosine
    return bf16(table.reshape(2 * items * N, SLABS * items * 2 * X6))


@functools.cache
def pair_table():
    valence, conduction = [], []
    for band in range(16):
        z, yl = divmod(band, 2)
        for half in range(2):
            for slot in SLOTS:
                valence.append(z * 2 + (yl ^ half))
                conduction.append((z - slot) % 8 * 2 + yl)
    return np.array(valence), np.array(conduction)


@functools.cache
def column_tables():
    tables = np.zeros((2, 128, 4, 2, NBLOCK))
    m = np.arange(NBLOCK)
    tables[0, 32 + m, :, 0, m] = 1.0
    tables[0, 64 + m, :, 1, m] = -1.0
    tables[1, 64 + m, :, 0, m] = 1.0
    tables[1, 32 + m, :, 1, m] = 1.0
    return bf16(tables.reshape(2, 128, 128))


VMEM = pl.BlockSpec(memory_space=pltpu.VMEM)
HBM = pl.BlockSpec(memory_space=pltpu.HBM)
ANY = pl.BlockSpec(memory_space=pl.ANY)
SLAB_CUTS = 4
PLANES_FLOPS = (600_000_000, 600_000_000, 600_000_000, 600_000_000)


def plane_kernel(*refs, items, first, through, chained, spare):
    refs = list(refs)
    take = lambda count: [refs.pop(0) for _ in range(count)]
    v0_ref, v1_ref = take(2)
    waves_c = take(items)
    lane_ref, twiddle_ref, row_ref = take(3)
    extra = take(spare)
    kept = take(through)
    take(chained)
    (out_ref,) = take(1)
    kept_out = take(through)
    low_ref, slab_ref, slab_sems, keep_sems = refs
    moves = [
        pltpu.make_async_copy(source, target, keep_sems.at[i])
        for i, (source, target) in enumerate(zip(kept, kept_out))
    ]
    for move in moves:
        move.start()
    rows = X6 * Y16
    twiddle_c = twiddle_ref[0][None]
    twiddle_s = twiddle_ref[1][None]
    for index, c_ref in enumerate(waves_c):
        wave_c = c_ref[...]
        pairs = jnp.concatenate([v0_ref[...] * wave_c, v1_ref[...] * wave_c], axis=0)
        moved = jnp.dot(pairs, lane_ref[...], preferred_element_type=F32)
        real = moved[:rows, :WIDE] - moved[rows:, WIDE:]
        imag = moved[:rows, WIDE:] + moved[rows:, :WIDE]
        real = real.reshape(X6, Y16, WIDE)
        imag = imag.reshape(X6, Y16, WIDE)
        turned_r = real * twiddle_c - imag * twiddle_s
        turned_i = real * twiddle_s + imag * twiddle_c
        low_ref[index * rows : (index + 1) * rows, :] = turned_r.reshape(rows, WIDE).astype(BF16)
        index += items
        low_ref[index * rows : (index + 1) * rows, :] = turned_i.reshape(rows, WIDE).astype(BF16)
    count = SLABS // SLAB_CUTS
    size = items * 2 * X6
    for part in range(SLAB_CUTS):
        slabs = slice(part * count, (part + 1) * count)
        planes = jnp.dot(
            row_ref[part * count * size : (part + 1) * count * size, :],
            low_ref[...],
            preferred_element_type=F32,
        ).reshape(count, size, WIDE)
        slab_ref[slabs] = planes.astype(BF16)
        if spare:
            block = extra[0][...]
            tail = planes[:, : block.shape[0], SPARE:] + block[None]
            slab_ref[slabs, : block.shape[0], SPARE:] = tail.astype(BF16)
        window = pl.ds(part * count, count)
        moves.append(
            pltpu.make_async_copy(
                slab_ref.at[window],
                out_ref.at[window, pl.ds(first, size)],
                slab_sems.at[part],
            )
        )
        moves[-1].start()
    for move in moves:
        move.wait()


def planes_of(group, v, c, extra=(), through=(), buffer=()):
    slots = GROUPS[group]
    items = len(slots)
    first = sum(len(before) for before in GROUPS[:group]) * 2 * X6
    inputs = (
        *v,
        *(c[slot] for slot in slots),
        lane_table(),
        twiddle_table(),
        row_table(items),
        *extra,
        *through,
        *buffer,
    )
    outside = len(through) + len(buffer)
    return pl.pallas_call(
        functools.partial(
            plane_kernel,
            items=items,
            first=first,
            through=len(through),
            chained=len(buffer),
            spare=len(extra),
        ),
        out_shape=[
            pltpu.HBM((SLABS, ROWS, WIDE), BF16),
            *(pltpu.HBM(x.shape, x.dtype) for x in through),
        ],
        in_specs=[VMEM] * (len(inputs) - outside) + [ANY] * len(through) + [HBM] * len(buffer),
        out_specs=[HBM] * (1 + len(through)),
        input_output_aliases={len(inputs) - 1: 0} if buffer else {},
        scratch_shapes=[
            pltpu.VMEM((2 * items * X6 * Y16, WIDE), BF16),
            pltpu.VMEM((SLABS, items * 2 * X6, WIDE), BF16),
            pltpu.SemaphoreType.DMA((SLAB_CUTS,)),
            pltpu.SemaphoreType.DMA((max(len(through), 1),)),
        ],
        compiler_params=pltpu.CompilerParams(vmem_limit_bytes=16 << 20),
        cost_estimate=pl.CostEstimate(
            flops=PLANES_FLOPS[group] * items, bytes_accessed=100_000, transcendentals=0
        ),
        name="planes",
    )(*inputs)


def pick(density_ref, flat_ref, kx_ref, store):
    rows = density_ref.shape[0]

    def body(step, carry):
        lanes = pl.ds(pl.multiple_of(step * TILE, TILE), TILE)
        spot = lax.broadcasted_iota(jnp.int32, (WIDE, TILE), 0)
        chosen = jnp.where(spot == flat_ref[:, lanes], 1.0, 0.0).astype(BF16)
        values = jnp.dot(density_ref[...], chosen, preferred_element_type=F32)
        kx = lax.broadcasted_iota(jnp.int32, (N, TILE), 0) == kx_ref[:, lanes]
        values = jnp.where(kx[None], values.reshape(rows // N, N, TILE), 0.0)
        store(lanes, values.sum(axis=1))
        return carry

    lax.fori_loop(0, G_DEV // TILE, body, 0)


X_ITEMS = 4


def transform_x(t_ref, x_ref, low):
    size = X_ITEMS * 2 * X6
    rows = X_ITEMS * N
    for item in range(0, ITEMS, X_ITEMS):
        planes = t_ref[:, item * 2 * X6 : item * 2 * X6 + size, :].reshape(SLABS * size, WIDE)
        for part in range(2):
            place = (part * ITEMS + item) * N
            low[place : place + rows, :] = jnp.dot(
                x_ref[part * rows : (part + 1) * rows, :], planes, preferred_element_type=F32
            ).astype(BF16)


PLACE = sum(len(group) for group in GROUPS[:-1]) * 2 * X6


def far_kernel(t_ref, x_ref, far_ref, far_kx_ref, far_out, low, block_out):
    transform_x(t_ref, x_ref, low)

    def store_far(lanes, values):
        far_out[:, lanes] = values.astype(BF16)

    pick(low, far_ref, far_kx_ref, store_far)
    spare = t_ref[:, PLACE : PLACE + 16, SPARE:].astype(F32).sum(axis=0)
    spare = spare + pltpu.roll(spare, 128 - NBLOCK, 1)
    block_out[...] = spare


def own_kernel(low, own_ref, own_kx_ref, own_out):
    def store_own(lanes, values):
        own_out[:, lanes] = values

    pick(low, own_ref, own_kx_ref, store_own)


def far_points(planes, far):
    return pl.pallas_call(
        far_kernel,
        out_shape=(
            jax.ShapeDtypeStruct((2 * ITEMS, G_DEV), BF16),
            jax.ShapeDtypeStruct((2 * ITEMS * N, WIDE), BF16),
            jax.ShapeDtypeStruct((16, 128), F32),
        ),
        compiler_params=pltpu.CompilerParams(vmem_limit_bytes=20 << 20),
        cost_estimate=pl.CostEstimate(
            flops=100_000_000, bytes_accessed=100_000, transcendentals=0
        ),
        name="far_points",
    )(planes, x_table(X_ITEMS), *far)


def own_points(low, own):
    return pl.pallas_call(
        own_kernel,
        out_shape=jax.ShapeDtypeStruct((2 * ITEMS, G_DEV), F32),
        compiler_params=pltpu.CompilerParams(vmem_limit_bytes=20 << 20),
        cost_estimate=pl.CostEstimate(
            flops=5_000_000_000, bytes_accessed=2_500_000, transcendentals=0
        ),
        name="own_points",
    )(low, *own)


def split_kernel(own_ref, far_ref, block_ref, out_ref):
    own_r, own_i = own_ref[:ITEMS, :], own_ref[ITEMS:, :]
    far_r = far_ref[:ITEMS, :].astype(F32)
    far_i = far_ref[ITEMS:, :].astype(F32)
    pairs = jnp.concatenate(
        [own_r + far_r, own_i + far_i, own_i - far_i, far_r - own_r], axis=0
    ).astype(BF16)
    block = block_ref[...].astype(BF16)
    for band in range(16):
        out_ref[band, :32, :] = pairs[:, band * 128 : (band + 1) * 128]
        out_ref[band, 32:, :] = block


def split_pairs(own, far, block):
    return pl.pallas_call(
        split_kernel,
        out_shape=jax.ShapeDtypeStruct((16, 48, 128), BF16),
        compiler_params=pltpu.CompilerParams(vmem_limit_bytes=8 << 20),
        cost_estimate=pl.CostEstimate(
            flops=1_000_000, bytes_accessed=500_000, transcendentals=0
        ),
        name="split",
    )(own, far, block)


def block_kernel(*refs):
    *waves, lane_ref, row_ref, out_ref = refs
    waves_v, waves_c = waves[:2], waves[2:]
    for half in range(2):
        for item, slot in enumerate(SLOTS):
            product = waves_v[half][...] * waves_c[slot][...]
            sums = jnp.dot(product, lane_ref[...], preferred_element_type=F32) * row_ref[...]
            index = half * len(SLOTS) + item
            out_ref[index : index + 1, :] = sums.sum(axis=0, keepdims=True)
    sums = out_ref[...]
    sums = sums + pltpu.roll(sums, 128 - NBLOCK, 1)
    high = sums.astype(BF16).astype(F32)
    rest = pltpu.roll(sums - high, NBLOCK, 1)
    lane = lax.broadcasted_iota(jnp.int32, sums.shape, 1)
    sums = jnp.where(lane // NBLOCK % 2 == 0, high, rest)
    out_ref[...] = jnp.where((lane >= 32) & (lane < 96), sums, 0.0)


def block_sums(v, c, lanes, rows):
    return pl.pallas_call(
        block_kernel,
        out_shape=jax.ShapeDtypeStruct((16, 128), F32),
        compiler_params=pltpu.CompilerParams(vmem_limit_bytes=4 << 20),
        cost_estimate=pl.CostEstimate(
            flops=10_000_000, bytes_accessed=100_000, transcendentals=0
        ),
        name="block",
    )(*v, *c, lanes, rows)


def sum_kernel(pairs_ref, weight_ref, column_ref, out_ref):
    pairs = 16 * 16
    block = pairs_ref[:, 32:, :].reshape(pairs, 128)
    total = None
    for part in range(2):
        left = pairs_ref[:, 16 * part : 16 * (part + 1), :].reshape(pairs, 128)
        columns = jnp.dot(block, column_ref[part], preferred_element_type=F32)
        right = (columns * weight_ref[...]).astype(BF16)
        term = lax.dot_general(
            left, right, (((0,), (0,)), ((), ())), preferred_element_type=F32
        )
        total = term if total is None else total + term
    out_ref[...] = total


def wave_rows(wave):
    return wave.reshape(X6, Y6, Y16, N).transpose(0, 2, 1, 3).reshape(X6 * Y16, Y6 * N)


def cosine(phase):
    return jnp.cos((phase % N).astype(F32) * (2.0 * math.pi / N))


def per_device(
    valence_wave,
    conduction_wave,
    valence_index,
    occupied_energy,
    conduction_energy,
    frequency,
    gvec_cell,
    block_cell,
):
    col = lax.axis_index(COL)
    wave_v = wave_rows(valence_wave)
    wave_c = wave_rows(conduction_wave)
    ahead = [(i, (i + 1) % 8) for i in range(8)]
    behind = [(i, (i + 7) % 8) for i in range(8)]
    v = [wave_v, lax.ppermute(wave_v, "yl", [(0, 1), (1, 0)])]
    c = [wave_c] + [None] * 7
    for slot in (1, 2, 3, 4):
        c[slot] = lax.ppermute(c[slot - 1], "z", ahead)
        if slot < 4:
            c[8 - slot] = lax.ppermute(c[(9 - slot) % 8], "z", behind)

    spots = jnp.arange(128, dtype=jnp.int32)
    cells = jnp.where(spots % NBLOCK == col, block_cell[0], 0)
    for mask in (1, 2):
        cells = cells + lax.ppermute(cells, COL, [(k, k ^ mask) for k in range(SLABS)])

    mirror_of = [(k, SLABS - 1 - k) for k in range(SLABS)]
    far_cell = lax.ppermute(gvec_cell, COL, mirror_of).reshape(16, 128)
    (planes,) = planes_of(0, v, c)
    planes, far_cell, cells = planes_of(
        1, v, c, through=(far_cell, cells[None]), buffer=(planes,)
    )
    far_cell = far_cell.reshape(G_DEV)
    far_x, far_y, far_z = far_cell // 576, far_cell // N % 6, far_cell % N
    own = ((gvec_cell % 576)[None], (gvec_cell // 576)[None])
    far = (((6 - far_y) * N + (N - far_z) % N)[None], ((N - far_x) % N)[None])

    cells = cells[0]
    arrived = [
        lax.ppermute(cells, COL, [(k, k ^ mask) for k in range(SLABS)]) for mask in (4, 8, 12)
    ]
    cells = sum(arrived, cells)
    block_x = cells // 576
    block_y = spots % NBLOCK * 6 + cells // N % 6
    block_z = cells % N
    group = spots // NBLOCK - 2
    quarter = N // 4
    lane = jnp.arange(Y6 * N, dtype=jnp.int32)[:, None]
    lanes = cosine(
        lane // N * 16 * block_y + lane % N * block_z + jnp.where(group % 2 == 1, quarter, 0)
    ).astype(BF16)
    row = jnp.arange(X6 * Y16, dtype=jnp.int32)[:, None]
    shift = jnp.where(group == 1, 3 * quarter, jnp.where(group == 2, quarter, 0))
    rows = cosine((row // Y16 + X6 * col) * block_x + row % Y16 * block_y + shift)
    scale = 1.0 / (N * math.sqrt(N))
    rows = jnp.where((group >= 0) & (group < 4), rows * scale, 0.0)
    block = block_sums(v, c, lanes, rows)

    (planes,) = planes_of(2, v, c, buffer=(planes,))
    (planes,) = planes_of(3, v, c, extra=(block,), buffer=(planes,))
    planes = lax.all_to_all(planes, COL, 0, 0, tiled=True)

    pair_v, pair_c = pair_table()
    occupied = jnp.arange(occupied_energy.shape[0], dtype=jnp.int32)
    valence_energy = jnp.sum(
        jnp.where(valence_index[:, None] == occupied[None, :], occupied_energy[None, :], 0.0),
        axis=1,
    )
    count_v, count_c = valence_index.shape[0], conduction_energy.shape[0]
    energy_v = jnp.sum(
        jnp.where(pair_v[:, None] == np.arange(count_v)[None], valence_energy[None], 0.0), axis=1
    )
    energy_c = jnp.sum(
        jnp.where(pair_c[:, None] == np.arange(count_c)[None], conduction_energy[None], 0.0),
        axis=1,
    )
    gap = (energy_c - energy_v)[:, None]
    omega = jnp.repeat(frequency, 2 * NBLOCK)[None]
    weight = -4.0 * gap / (gap * gap + omega * omega) * (1.0 / math.sqrt(count_v * count_c))

    mirrored, low, columns = far_points(planes, far)
    mirrored = lax.ppermute(mirrored, COL, mirror_of)
    pairs = split_pairs(own_points(low, own), mirrored, columns)
    pairs = lax.all_to_all(pairs, BAND, 0, 0, tiled=True)
    return pl.pallas_call(
        sum_kernel,
        out_shape=jax.ShapeDtypeStruct((128, 128), F32),
        compiler_params=pltpu.CompilerParams(vmem_limit_bytes=4 << 20),
        name="pair_sum",
    )(pairs, weight, column_tables())


def solution(mesh):
    fine = Mesh(
        mesh.devices.reshape(8, 2, 4, 2, 2), ("z", "yl", "x", "yh", "co")
    )
    return jax.shard_map(
        per_device,
        mesh=fine,
        in_specs=(
            P(BAND, COL, None),
            P(BAND, COL, None),
            P(),
            P(),
            P(),
            P(),
            P(COL),
            P(COL),
        ),
        out_specs=P(COL + BAND, None),
        check_vma=False,
    )
```

time: 118 us -> 124 us (1.051)
  other arithmetic: 2.74 us -> 6.57 us
  waiting for transfers between devices: 41.6 us -> 44.3 us
  Pallas kernels: 27.3 us -> 25.6 us
  local copies, waits for them, and re-layouts: 5.13 us -> 6.49 us
    all_to_all x2 -> x1, starting transfers between devices: 14.3 us -> 5.56 us  [per_device(): planes = lax.all_to_all(planes, COL, 0, 0, tiled=True)]
    all_to_all x2 -> x1, waiting for transfers between devices: 16.8 us -> 24.1 us  [per_device(): planes = lax.all_to_all(planes, COL, 0, 0, tiled=True)]
    ppermute x0 -> x5, starting transfers between devices: none -> 5.59 us  [per_device(): lax.ppermute(cells, COL, [(k, k ^ mask) for k in range(SLABS)])]
    ppermute x0 -> x5, waiting for transfers between devices: none -> 5.49 us  [per_device(): lax.ppermute(cells, COL, [(k, k ^ mask) for k in range(SLABS)])]
    ppermute x4, waiting for transfers between devices: 8.45 us -> 3.7 us  [per_device(): c[slot] = lax.ppermute(c[slot - 1], 'z', ahead)]
    ppermute x1, waiting for transfers between devices: 4.17 us -> 0.01 us  [per_device(): far_cell = lax.ppermute(gvec_cell, COL, mirror_of).reshape(16, 128)]
    ppermute x1, starting transfers between devices: 2.72 us -> 5.61 us  [per_device(): mirrored = lax.ppermute(mirrored, COL, mirror_of)]
    ppermute x1, waiting for transfers between devices: 1.34 us -> 0.01 us  [per_device(): mirrored = lax.ppermute(mirrored, COL, mirror_of)]
  transfers between devices with their start and end apart: 13 -> 17, of which waited for: 8 -> 5; matrix products, arithmetic and copies ran while one was open for 4% -> 8% of each run, Pallas kernels for 8% -> 10%
where the time goes in v6:
time: 124 us; the launch traced here: 123 us
  waiting for transfers between devices  44.3 us (36%)
  starting transfers between devices  39.5 us (32%)
  Pallas kernels  25.6 us (21%)
  other arithmetic  6.57 us (5%)
  local copies, waits for them, and re-layouts  6.49 us (5%)
    all_to_all x1, waiting for transfers between devices, per_device(): planes = lax.all_to_all(planes, COL, 0, 0, tiled=True)  24.1 us
    all_to_all x1, waiting for transfers between devices, per_device(): pairs = lax.all_to_all(pairs, BAND, 0, 0, tiled=True)  10.9 us
    ppermute x3, starting transfers between devices, per_device(): c[8 - slot] = lax.ppermute(c[(9 - slot) % 8], 'z', behind)  10.5 us
    pallas_call x4, Pallas kernels, planes_of(): pl.pallas_call(functools.partial(plane_kernel, items=items, first=first,...  9.45 us
    pallas_call x1, Pallas kernels, far_points(): pl.pallas_call(far_kernel, out_shape=(jax.ShapeDtypeStruct((2 * ITEMS, G_...  7.87 us
    all_to_all x1, starting transfers between devices, per_device(): pairs = lax.all_to_all(pairs, BAND, 0, 0, tiled=True)  5.87 us
    pallas_call x1, Pallas kernels, own_points(): pl.pallas_call(own_kernel, out_shape=jax.ShapeDtypeStruct((2 * ITEMS, G_D...  5.72 us
    ppermute x1, starting transfers between devices, per_device(): mirrored = lax.ppermute(mirrored, COL, mirror_of)  5.61 us
  transfers between devices with their start and end apart: 17, of which 5 were waited for; matrix products, arithmetic and copies ran while one was open for 8% of the time, Pallas kernels for 10%

profile of v6, /device:TPU:6, one launch (start us, length us, event | category | flops | bytes accessed | tf_op | source)
XLA Modules:
  0.0 123.4 jit_solution(5000796688389356876)
XLA Ops:
  0.0 1.2 reshape.341
  1.4 2.0 %collective-permute-start.4 = (bf16[96,576]{1,0:T(8,128)(2,1)S(1)}, bf16[96,576]{1,0:T(8,128)(2,1)S(1)}, u32[]{:S(2)}, u32[]{:S(2)}) collective-permute-start(bf16[96,576]{1,0:T(8,128)(2,1)S(1)} %reshape.342.refs_2_), channel_id=1, source_target_pairs={{0,32},{32,64},{64,96},{96,128},{128,160},{160,192},{192,224},{224... | collective-permute-start | bytes 331784 | tf_op jit(solution)/shard_map/ppermute | solution.py:409
  3.4 4.0 %collective-permute-start.1 = (bf16[96,576]{1,0:T(8,128)(2,1)S(1)}, bf16[96,576]{1,0:T(8,128)(2,1)S(1)}, u32[]{:S(2)}, u32[]{:S(2)}) collective-permute-start(bf16[96,576]{1,0:T(8,128)(2,1)S(1)} %reshape.342.refs_2_), channel_id=1, source_target_pairs={{0,224},{32,0},{64,32},{96,64},{128,96},{160,128},{192,160},{224,1... | collective-permute-start | bytes 331784 | tf_op jit(solution)/shard_map/ppermute | solution.py:411
  8.2 1.1 reshape.339
  9.5 1.7 %collective-permute-start = (bf16[96,576]{1,0:T(8,128)(2,1)S(1)}, bf16[96,576]{1,0:T(8,128)(2,1)S(1)}, u32[]{:S(2)}, u32[]{:S(2)}) collective-permute-start(bf16[96,576]{1,0:T(8,128)(2,1)S(1)} %reshape.340.refs_0_), channel_id=1, source_target_pairs={{0,16},{16,0},{1,17},{17,1},{2,18},{18,2},{3,19},{19,3},{4,20},{20... | collective-permute-start | bytes 331784 | tf_op jit(solution)/shard_map/ppermute | solution.py:406
  11.2 2.6 %collective-permute-start.8 = (s32[2048]{0:T(1024)}, s32[2048]{0:T(1024)S(1)}, u32[]{:S(2)}, u32[]{:S(2)}) collective-permute-start(s32[2048]{0:T(1024)} %param.21), channel_id=1, source_target_pairs={{0,15},{1,14},{2,13},{3,12},{4,11},{5,10},{6,9},{7,8},{8,7},{9,6},... | collective-permute-start | bytes 24584 | tf_op jit(solution)/shard_map/ppermute | solution.py:419
  14.6 4.4 %collective-permute-done.10 = s32[128]{0:T(128)S(1)} collective-permute-done((s32[128]{0:T(128)S(1)}, s32[128]{0:T(128)S(1)}, u32[]{:S(2)}, u32[]{:S(2)}) %collective-permute-start.10) | collective-permute-done | bytes 544 | tf_op jit(solution)/shard_map/ppermute | solution.py:416
  19.1 3.2 %collective-permute-start.2 = (bf16[96,576]{1,0:T(8,128)(2,1)S(1)}, bf16[96,576]{1,0:T(8,128)(2,1)S(1)}, u32[]{:S(2)}, u32[]{:S(2)}) collective-permute-start(bf16[96,576]{1,0:T(8,128)(2,1)S(1)} %collective-permute-done.1.refs_2_.refs_9_), channel_id=1, source_target_pairs={{0,224},{32,0},{64,32},{96,64},{128,96},{160,128},{192,160},{224,1... | collective-permute-start | bytes 331784 | tf_op jit(solution)/shard_map/ppermute | solution.py:411
  22.3 1.0 copy-done.1
  23.2 0.9 copy-done.2
  24.1 2.4 %planes.4.refs_9_ = bf16[16,96,768]{2,1,0:T(8,128)(2,1)} custom-call(bf16[96,576]{1,0:T(8,128)(2,1)S(1)} %reshape.340.refs_0_, bf16[96,576]{1,0:T(8,128)(2,1)S(1)} %collective-permute-done.refs_1_, bf16[96,576]{1,0:T(8,128)(2,1)S(1)} %reshape.342.refs_2_, bf16[96,576]{1,0:T(8,128)(2,1)S(1)} %collective-permute-done.4.refs_3_, bf16[576,1536]{1,0:T(8,128)(2,1)S(1)} %copy-done, ...), custom_call_target="tpu_custom_call" | custom-call | flops 1200000000 | bytes 100000 | tf_op jit(solution)/shard_map/planes/pallas_call | solution.py:202
  26.5 2.4 %planes.5 = (bf16[16,96,768]{2,1,0:T(8,128)(2,1)}, s32[16,128]{1,0:T(8,128)}, s32[1,128]{1,0:T(1,128)}) custom-call(bf16[96,576]{1,0:T(8,128)(2,1)S(1)} %reshape.340.refs_0_, bf16[96,576]{1,0:T(8,128)(2,1)S(1)} %collective-permute-done.refs_1_, bf16[96,576]{1,0:T(8,128)(2,1)S(1)} %collective-permute-done.1.refs_2_.refs_9_, ...), custom_call_target="tpu_custom_call", output_to_operand_aliasing={{0}: (9, {})} | custom-call | flops 1200000000 | bytes 100000 | tf_op jit(solution)/shard_map/planes/pallas_call | solution.py:202
  28.9 1.0 collective-permute-start.11
  29.9 3.3 %collective-permute-start.12 = (s32[128]{0:T(128)}, s32[128]{0:T(128)S(1)}, u32[]{:S(2)}, u32[]{:S(2)}) collective-permute-start(s32[128]{0:T(128)} %bitcast.50), channel_id=1, source_target_pairs={{0,8},{1,9},{2,10},{3,11},{4,12},{5,13},{6,14},{7,15},{8,0},{9,1},... | collective-permute-start | bytes 1544 | tf_op jit(solution)/shard_map/ppermute | solution.py:431
  33.7 3.2 %collective-permute-start.3 = (bf16[96,576]{1,0:T(8,128)(2,1)S(1)}, bf16[96,576]{1,0:T(8,128)(2,1)S(1)}, u32[]{:S(2)}, u32[]{:S(2)}) collective-permute-start(bf16[96,576]{1,0:T(8,128)(2,1)S(1)} %collective-permute-done.2.refs_8_.refs_2_), channel_id=1, source_target_pairs={{0,224},{32,0},{64,32},{96,64},{128,96},{160,128},{192,160},{224,1... | collective-permute-start | bytes 331784 | tf_op jit(solution)/shard_map/ppermute | solution.py:411
  36.9 1.1 collective-permute-done.13
  38.7 1.6 %fusion.3.refs_10_ = bf16[576,128]{1,0:T(8,128)(2,1)S(1)} fusion(s32[128]{0:T(128)S(1)} %compare_select_fusion.4, s32[128]{0:T(128)S(1)} %get-tuple-element.31, s32[576]{0:T(1024)S(1)} %get-tuple-element.32, s32[128]{0:T(128)S(1)} %get-tuple-element.30, s32[576]{0:T(1024)S(1)} %get-tuple-element.33), kind=kLoop, calls=%fused_computation.4 | loop fusion | flops 958464 | bytes 153600 | tf_op jit(solution)/shard_map/convert_element_type | solution.py:442
  40.7 2.4 %planes.6.refs_8_ = bf16[16,96,768]{2,1,0:T(8,128)(2,1)} custom-call(bf16[96,576]{1,0:T(8,128)(2,1)S(1)} %reshape.340.refs_0_, bf16[96,576]{1,0:T(8,128)(2,1)S(1)} %collective-permute-done.refs_1_, bf16[96,576]{1,0:T(8,128)(2,1)S(1)} %collective-permute-done.2.refs_8_.refs_2_, ...), custom_call_target="tpu_custom_call", output_to_operand_aliasing={{}: (7, {})} | custom-call | flops 1200000000 | bytes 100000 | tf_op jit(solution)/shard_map/planes/pallas_call | solution.py:202
  43.1 3.7 %collective-permute-done.7.refs_6_.refs_3_ = bf16[96,576]{1,0:T(8,128)(2,1)S(1)} collective-permute-done((bf16[96,576]{1,0:T(8,128)(2,1)S(1)}, bf16[96,576]{1,0:T(8,128)(2,1)S(1)}, u32[]{:S(2)}, u32[]{:S(2)}) %collective-permute-start.7) | collective-permute-done | bytes 110624 | tf_op jit(solution)/shard_map/ppermute | solution.py:409
  46.8 0.9 block.1.refs_7_
  47.7 2.4 %planes.7 = bf16[16,96,768]{2,1,0:T(8,128)(2,1)} custom-call(bf16[96,576]{1,0:T(8,128)(2,1)S(1)} %reshape.340.refs_0_, bf16[96,576]{1,0:T(8,128)(2,1)S(1)} %collective-permute-done.refs_1_, bf16[96,576]{1,0:T(8,128)(2,1)S(1)} %collective-permute-done.3.refs_7_.refs_2_, ...), custom_call_target="tpu_custom_call", output_to_operand_aliasing={{}: (8, {})} | custom-call | flops 1200000000 | bytes 100000 | tf_op jit(solution)/shard_map/planes/pallas_call | solution.py:202
  50.1 5.6 %all-to-all-start = ((bf16[16,96,768]{2,1,0:T(8,128)(2,1)}), bf16[16,96,768]{2,1,0:T(8,128)(2,1)S(1)}, u32[]{:S(2)}, u32[]{:S(2)}) async-start(bf16[16,96,768]{2,1,0:T(8,128)(2,1)} %planes.7), calls=%async_computation | async-start | bytes 4718592 | tf_op jit(solution)/shard_map/all_to_all | solution.py:452
  57.0 1.2 mul.173
  58.3 0.9 select_reduce_fusion
  59.2 1.3 %select_reduce_fusion.1 = (f32[256]{0:T(256)}, f32[256]{0:T(256)}) fusion(pred[256,16]{0,1:T(8,128)(4,1)} %constant.204.clone, f32[16]{0:T(128)S(1)} %select_reduce_fusion, pred[256,16]{0,1:T(8,128)(4,1)} %constant.205.clone, f32[16]{0:T(128)} %param.19), kind=kLoop, calls=%fused_computation.32 | loop fusion | flops 15872 | bytes 10368 | tf_op jit(solution)/shard_map/reduce_sum | solution.py:461
  61.4 24.1 %all-to-all-done.t_ref = bf16[16,96,768]{2,1,0:T(8,128)(2,1)S(1)} async-done(((bf16[16,96,768]{2,1,0:T(8,128)(2,1)}), bf16[16,96,768]{2,1,0:T(8,128)(2,1)S(1)}, u32[]{:S(2)}, u32[]{:S(2)}) %all-to-all-start) | async-done | bytes 2359328 | tf_op jit(solution)/shard_map/all_to_all | solution.py:452
  85.5 7.9 %far_points.1 = (bf16[16,2048]{1,0:T(8,128)(2,1)S(1)}, bf16[1536,768]{1,0:T(8,128)(2,1)S(1)}, f32[16,128]{1,0:T(8,128)S(1)}) custom-call(bf16[16,96,768]{2,1,0:T(8,128)(2,1)S(1)} %all-to-all-done.t_ref, bf16[768,768]{1,0:T(8,128)(2,1)S(1)} %copy-done.3, s32[1,2048]{1,0:T(1,128)S(1)} %get-tuple-element.29.far_ref, s32[1,2048]{1,0:T(1,128)S(1)} %get-tuple-element.28.far_kx_ref), custom_call_target="tpu_custom_call" | custom-call | flops 100000000 | bytes 100000 | tf_op jit(solution)/shard_map/far_points/pallas_call | solution.py:286
  93.3 5.6 %collective-permute-start.14 = (bf16[16,2048]{1,0:T(8,128)(2,1)S(1)}, bf16[16,2048]{1,0:T(8,128)(2,1)S(1)}, u32[]{:S(2)}, u32[]{:S(2)}) collective-permute-start(bf16[16,2048]{1,0:T(8,128)(2,1)S(1)} %get-tuple-element.15), channel_id=1, source_target_pairs={{0,15},{1,14},{2,13},{3,12},{4,11},{5,10},{6,9},{7,8},{8,7},{9,6},... | collective-permute-start | bytes 196616 | tf_op jit(solution)/shard_map/ppermute | solution.py:473
  99.0 5.7 %own_points.1.own_ref = f32[16,2048]{1,0:T(8,128)S(1)} custom-call(bf16[1536,768]{1,0:T(8,128)(2,1)S(1)} %get-tuple-element.14.low, s32[1,2048]{1,0:T(1,128)S(1)} %bitcast.43, s32[1,2048]{1,0:T(1,128)S(1)} %bitcast.42), custom_call_target="tpu_custom_call" | custom-call | flops 5000000000 | bytes 2500000 | tf_op jit(solution)/shard_map/own_points/pallas_call | solution.py:302
  105.4 5.9 %all-to-all-start.1 = ((bf16[16,48,128]{2,1,0:T(8,128)(2,1)}), bf16[16,48,128]{2,1,0:T(8,128)(2,1)S(1)}, u32[]{:S(2)}, u32[]{:S(2)}) async-start(bf16[16,48,128]{2,1,0:T(8,128)(2,1)} %split.1), calls=%async_computation.1 | async-start | bytes 393216 | tf_op jit(solution)/shard_map/all_to_all | solution.py:475
  111.5 10.9 %all-to-all-done.1.pairs_ref = bf16[16,48,128]{2,1,0:T(8,128)(2,1)S(1)} async-done(((bf16[16,48,128]{2,1,0:T(8,128)(2,1)}), bf16[16,48,128]{2,1,0:T(8,128)(2,1)S(1)}, u32[]{:S(2)}, u32[]{:S(2)}) %all-to-all-start.1) | async-done | bytes 196640 | tf_op jit(solution)/shard_map/all_to_all | solution.py:475
  122.4 1.0 pair_sum.1
  (65 shorter events, 5.9 us)
Async XLA Ops:
  0.0 22.3 %copy-start = (bf16[576,1536]{1,0:T(8,128)(2,1)S(1)}, bf16[576,1536]{1,0:T(8,128)(2,1)}, u32[]{:S(2)}) copy-start(bf16[576,1536]{1,0:T(8,128)(2,1)} %constant.201.clone.refs_4_) | copy-start | bytes 5308420
  1.4 17.6 %collective-permute-start.4 = (bf16[96,576]{1,0:T(8,128)(2,1)S(1)}, bf16[96,576]{1,0:T(8,128)(2,1)S(1)}, u32[]{:S(2)}, u32[]{:S(2)}) collective-permute-start(bf16[96,576]{1,0:T(8,128)(2,1)S(1)} %reshape.342.refs_2_), channel_id=1, source_target_pairs={{0,32},{32,64},{64,96},{96,128},{128,160},{160,192},{192,224},{224... | collective-permute-start | bytes 331784 | tf_op jit(solution)/shard_map/ppermute | solution.py:409
  3.4 15.6 %collective-permute-start.1 = (bf16[96,576]{1,0:T(8,128)(2,1)S(1)}, bf16[96,576]{1,0:T(8,128)(2,1)S(1)}, u32[]{:S(2)}, u32[]{:S(2)}) collective-permute-start(bf16[96,576]{1,0:T(8,128)(2,1)S(1)} %reshape.342.refs_2_), channel_id=1, source_target_pairs={{0,224},{32,0},{64,32},{96,64},{128,96},{160,128},{192,160},{224,1... | collective-permute-start | bytes 331784 | tf_op jit(solution)/shard_map/ppermute | solution.py:411
  8.1 5.7 %collective-permute-start.9 = (s32[128]{0:T(128)S(1)}, s32[128]{0:T(128)S(1)}, u32[]{:S(2)}, u32[]{:S(2)}) collective-permute-start(s32[128]{0:T(128)S(1)} %compare_select_fusion.5), channel_id=1, source_target_pairs={{0,1},{1,0},{2,3},{3,2},{4,5},{5,4},{6,7},{7,6},{8,9},{9,8},{10,11... | collective-permute-start | bytes 1544 | tf_op jit(solution)/shard_map/ppermute | solution.py:416
  9.5 12.7 %collective-permute-start = (bf16[96,576]{1,0:T(8,128)(2,1)S(1)}, bf16[96,576]{1,0:T(8,128)(2,1)S(1)}, u32[]{:S(2)}, u32[]{:S(2)}) collective-permute-start(bf16[96,576]{1,0:T(8,128)(2,1)S(1)} %reshape.340.refs_0_), channel_id=1, source_target_pairs={{0,16},{16,0},{1,17},{17,1},{2,18},{18,2},{3,19},{19,3},{4,20},{20... | collective-permute-start | bytes 331784 | tf_op jit(solution)/shard_map/ppermute | solution.py:406
  11.2 15.3 %collective-permute-start.8 = (s32[2048]{0:T(1024)}, s32[2048]{0:T(1024)S(1)}, u32[]{:S(2)}, u32[]{:S(2)}) collective-permute-start(s32[2048]{0:T(1024)} %param.21), channel_id=1, source_target_pairs={{0,15},{1,14},{2,13},{3,12},{4,11},{5,10},{6,9},{7,8},{8,7},{9,6},... | collective-permute-start | bytes 24584 | tf_op jit(solution)/shard_map/ppermute | solution.py:419
  13.9 5.1 %collective-permute-start.10 = (s32[128]{0:T(128)S(1)}, s32[128]{0:T(128)S(1)}, u32[]{:S(2)}, u32[]{:S(2)}) collective-permute-start(s32[128]{0:T(128)S(1)} %fusion.37), channel_id=1, source_target_pairs={{0,2},{1,3},{2,0},{3,1},{4,6},{5,7},{6,4},{7,5},{8,10},{9,11},{10,... | collective-permute-start | bytes 1544 | tf_op jit(solution)/shard_map/ppermute | solution.py:416
  19.0 7.5 %collective-permute-start.5 = (bf16[96,576]{1,0:T(8,128)(2,1)S(1)}, bf16[96,576]{1,0:T(8,128)(2,1)S(1)}, u32[]{:S(2)}, u32[]{:S(2)}) collective-permute-start(bf16[96,576]{1,0:T(8,128)(2,1)S(1)} %collective-permute-done.4.refs_3_), channel_id=1, source_target_pairs={{0,32},{32,64},{64,96},{96,128},{128,160},{160,192},{192,224},{224... | collective-permute-start | bytes 331784 | tf_op jit(solution)/shard_map/ppermute | solution.py:409
  19.1 14.6 %collective-permute-start.2 = (bf16[96,576]{1,0:T(8,128)(2,1)S(1)}, bf16[96,576]{1,0:T(8,128)(2,1)S(1)}, u32[]{:S(2)}, u32[]{:S(2)}) collective-permute-start(bf16[96,576]{1,0:T(8,128)(2,1)S(1)} %collective-permute-done.1.refs_2_.refs_9_), channel_id=1, source_target_pairs={{0,224},{32,0},{64,32},{96,64},{128,96},{160,128},{192,160},{224,1... | collective-permute-start | bytes 331784 | tf_op jit(solution)/shard_map/ppermute | solution.py:411
  22.3 1.0 copy-start.1
  23.2 0.9 copy-start.2
  28.9 8.0 %collective-permute-start.11 = (s32[128]{0:T(128)}, s32[128]{0:T(128)S(1)}, u32[]{:S(2)}, u32[]{:S(2)}) collective-permute-start(s32[128]{0:T(128)} %bitcast.49), channel_id=1, source_target_pairs={{0,4},{1,5},{2,6},{3,7},{4,0},{5,1},{6,2},{7,3},{8,12},{9,13},{10,... | collective-permute-start | bytes 1544 | tf_op jit(solution)/shard_map/ppermute | solution.py:431
  29.9 7.1 %collective-permute-start.12 = (s32[128]{0:T(128)}, s32[128]{0:T(128)S(1)}, u32[]{:S(2)}, u32[]{:S(2)}) collective-permute-start(s32[128]{0:T(128)} %bitcast.50), channel_id=1, source_target_pairs={{0,8},{1,9},{2,10},{3,11},{4,12},{5,13},{6,14},{7,15},{8,0},{9,1},... | collective-permute-start | bytes 1544 | tf_op jit(solution)/shard_map/ppermute | solution.py:431
  33.2 4.8 %collective-permute-start.13 = (s32[128]{0:T(128)}, s32[128]{0:T(128)S(1)}, u32[]{:S(2)}, u32[]{:S(2)}) collective-permute-start(s32[128]{0:T(128)} %bitcast.51), channel_id=1, source_target_pairs={{0,12},{1,13},{2,14},{3,15},{4,8},{5,9},{6,10},{7,11},{8,4},{9,5},... | collective-permute-start | bytes 1544 | tf_op jit(solution)/shard_map/ppermute | solution.py:431
  33.7 6.9 %collective-permute-start.6 = (bf16[96,576]{1,0:T(8,128)(2,1)S(1)}, bf16[96,576]{1,0:T(8,128)(2,1)S(1)}, u32[]{:S(2)}, u32[]{:S(2)}) collective-permute-start(bf16[96,576]{1,0:T(8,128)(2,1)S(1)} %collective-permute-done.5.refs_3_.refs_4_), channel_id=1, source_target_pairs={{0,32},{32,64},{64,96},{96,128},{128,160},{160,192},{192,224},{224... | collective-permute-start | bytes 331784 | tf_op jit(solution)/shard_map/ppermute | solution.py:409
  33.7 9.4 %collective-permute-start.3 = (bf16[96,576]{1,0:T(8,128)(2,1)S(1)}, bf16[96,576]{1,0:T(8,128)(2,1)S(1)}, u32[]{:S(2)}, u32[]{:S(2)}) collective-permute-start(bf16[96,576]{1,0:T(8,128)(2,1)S(1)} %collective-permute-done.2.refs_8_.refs_2_), channel_id=1, source_target_pairs={{0,224},{32,0},{64,32},{96,64},{128,96},{160,128},{192,160},{224,1... | collective-permute-start | bytes 331784 | tf_op jit(solution)/shard_map/ppermute | solution.py:411
  40.6 6.2 %collective-permute-start.7 = (bf16[96,576]{1,0:T(8,128)(2,1)S(1)}, bf16[96,576]{1,0:T(8,128)(2,1)S(1)}, u32[]{:S(2)}, u32[]{:S(2)}) collective-permute-start(bf16[96,576]{1,0:T(8,128)(2,1)S(1)} %collective-permute-done.6.refs_5_.refs_3_), channel_id=1, source_target_pairs={{0,32},{32,64},{64,96},{96,128},{128,160},{160,192},{192,224},{224... | collective-permute-start | bytes 331784 | tf_op jit(solution)/shard_map/ppermute | solution.py:409
  50.1 10.5 %copy-start.8 = (s32[2048]{0:T(1024)S(1)}, s32[2048]{0:T(1024)}, u32[]{:S(2)}) copy-start(s32[2048]{0:T(1024)} %param.21) | copy-start | bytes 24580
  50.1 11.1 %copy-start.7 = (s32[16,128]{1,0:T(8,128)S(1)}, s32[16,128]{1,0:T(8,128)}, u32[]{:S(2)}) copy-start(s32[16,128]{1,0:T(8,128)} %get-tuple-element.13) | copy-start | bytes 24580
  50.1 35.4 %copy-start.3 = (bf16[768,768]{1,0:T(8,128)(2,1)S(1)}, bf16[768,768]{1,0:T(8,128)(2,1)}, u32[]{:S(2)}) copy-start(bf16[768,768]{1,0:T(8,128)(2,1)} %constant.206.clone.x_ref) | copy-start | bytes 3538948
  50.1 35.4 %all-to-all-start = ((bf16[16,96,768]{2,1,0:T(8,128)(2,1)}), bf16[16,96,768]{2,1,0:T(8,128)(2,1)S(1)}, u32[]{:S(2)}, u32[]{:S(2)}) async-start(bf16[16,96,768]{2,1,0:T(8,128)(2,1)} %planes.7), calls=%async_computation | async-start | bytes 4718592 | tf_op jit(solution)/shard_map/all_to_all | solution.py:452
  85.5 13.5 %copy-start.5 = (s32[2048]{0:T(1024)S(1)}, s32[2048]{0:T(1024)}, u32[]{:S(2)}) copy-start(s32[2048]{0:T(1024)} %get-tuple-element.19) | copy-start | bytes 24580
  85.5 13.5 %copy-start.6 = (s32[2048]{0:T(1024)S(1)}, s32[2048]{0:T(1024)}, u32[]{:S(2)}) copy-start(s32[2048]{0:T(1024)} %get-tuple-element.20) | copy-start | bytes 24580
  93.3 11.4 %collective-permute-start.14 = (bf16[16,2048]{1,0:T(8,128)(2,1)S(1)}, bf16[16,2048]{1,0:T(8,128)(2,1)S(1)}, u32[]{:S(2)}, u32[]{:S(2)}) collective-permute-start(bf16[16,2048]{1,0:T(8,128)(2,1)S(1)} %get-tuple-element.15), channel_id=1, source_target_pairs={{0,15},{1,14},{2,13},{3,12},{4,11},{5,10},{6,9},{7,8},{8,7},{9,6},... | collective-permute-start | bytes 196616 | tf_op jit(solution)/shard_map/ppermute | solution.py:473
  99.0 12.3 %copy-start.9 = (f32[256]{0:T(256)S(1)}, f32[256]{0:T(256)}, u32[]{:S(2)}) copy-start(f32[256]{0:T(256)} %get-tuple-element.34) | copy-start | bytes 3076
  99.0 12.4 %copy-start.10 = (f32[256]{0:T(256)S(1)}, f32[256]{0:T(256)}, u32[]{:S(2)}) copy-start(f32[256]{0:T(256)} %get-tuple-element.35) | copy-start | bytes 3076
  99.0 12.4 %copy-start.11 = (f32[128]{0:T(128)S(1)}, f32[128]{0:T(128)}, u32[]{:S(2)}) copy-start(f32[128]{0:T(128)} %mul.173) | copy-start | bytes 1540
  99.0 23.4 %copy-start.4 = (bf16[2,128,128]{2,1,0:T(8,128)(2,1)S(1)}, bf16[2,128,128]{2,1,0:T(8,128)(2,1)}, u32[]{:S(2)}) copy-start(bf16[2,128,128]{2,1,0:T(8,128)(2,1)} %constant.207.clone.column_ref) | copy-start | bytes 196612
  105.4 17.0 %all-to-all-start.1 = ((bf16[16,48,128]{2,1,0:T(8,128)(2,1)}), bf16[16,48,128]{2,1,0:T(8,128)(2,1)S(1)}, u32[]{:S(2)}, u32[]{:S(2)}) async-start(bf16[16,48,128]{2,1,0:T(8,128)(2,1)} %split.1), calls=%async_computation.1 | async-start | bytes 393216 | tf_op jit(solution)/shard_map/all_to_all | solution.py:475

commit v7 on v5

--- a/solution.py
+++ b/solution.py
@@ -22,12 +22,15 @@
 K7 = 7
 FLAT = K7 * N
 WIDE = 768
-GROUPS = (((0, 1, 7),), ((2, 6, 3), (5, 4)))
-SLOTS = [slot for chunk in GROUPS for group in chunk for slot in group]
+GROUPS = ((0, 1), (7, 2), (6, 3), (5, 4))
+SLOTS = [slot for group in GROUPS for slot in group]
+ITEMS = len(SLOTS)
 SPARE = 640
 G_DEV = 2048
 NBLOCK = 16
 TILE = 512
+CHUNK_ROWS = (24, 72)
+X_GROUPS = ((2,), (4, 2))
 
 BAND = ("z", "yl")
 COL = ("x", "yh", "co")
@@ -64,10 +67,6 @@
     return table
 
 
-def slab_rows(items):
-    return -(-items * 2 * X6 // 8) * 8
-
-
 @functools.cache
 def row_table(items):
     table = np.zeros((SLABS, items, 2, X6, 2, items, X6, Y16))
@@ -78,10 +77,7 @@
             table[:, item, 0, x, 1, item, x] = -sine
             table[:, item, 1, x, 0, item, x] = sine
             table[:, item, 1, x, 1, item, x] = cosine
-    rows = items * 2 * X6
-    whole = np.zeros((SLABS, slab_rows(items), 2 * items * X6 * Y16))
-    whole[:, :rows] = table.reshape(SLABS, rows, -1)
-    return bf16(whole.reshape(SLABS * slab_rows(items), -1))
+    return bf16(table.reshape(SLABS * items * 2 * X6, 2 * items * X6 * Y16))
 
 
 @functools.cache
@@ -95,10 +91,7 @@
         table[0, item, :, :, item, 1] = -sine
         table[1, item, :, :, item, 0] = sine
         table[1, item, :, :, item, 1] = cosine
-    rows = items * 2 * X6
-    whole = np.zeros((2 * items * N, SLABS, slab_rows(items)))
-    whole[:, :, :rows] = table.reshape(2 * items * N, SLABS, rows)
-    return bf16(whole.reshape(2 * items * N, -1))
+    return bf16(table.reshape(2 * items * N, SLABS * items * 2 * X6))
 
 
 @functools.cache
@@ -128,20 +121,21 @@
 HBM = pl.BlockSpec(memory_space=pltpu.HBM)
 ANY = pl.BlockSpec(memory_space=pl.ANY)
 SLAB_CUTS = 4
-
-
-def plane_kernel(*refs, groups, place, through):
+PLANES_FLOPS = (30_000_000, 30_000_000, 30_000_000, 30_000_000)
+
+
+def plane_kernel(*refs, items, first, through, chained, marked):
     refs = list(refs)
     take = lambda count: [refs.pop(0) for _ in range(count)]
     v0_ref, v1_ref = take(2)
-    c_refs = [take(len(group)) for group in groups]
-    lane_ref, twiddle_ref, extra_ref = take(3)
-    row_refs = take(len(groups))
+    waves_c = take(items)
+    lane_ref, twiddle_ref, row_ref = take(3)
+    marks = take(marked)
     kept = take(through)
+    take(chained)
     (out_ref,) = take(1)
     kept_out = take(through)
-    low_refs = take(len(groups))
-    slab_ref, slab_sems, keep_sems = refs
+    low_ref, slab_ref, slab_sems, keep_sems = refs
     moves = [
         pltpu.make_async_copy(source, target, keep_sems.at[i])
         for i, (source, target) in enumerate(zip(kept, kept_out))
@@ -151,88 +145,89 @@
     rows = X6 * Y16
     twiddle_c = twiddle_ref[0][None]
     twiddle_s = twiddle_ref[1][None]
-    for group, waves_c, low_ref in zip(groups, c_refs, low_refs):
-        for index, c_ref in enumerate(waves_c):
-            wave_c = c_ref[...]
-            pairs = jnp.concatenate([v0_ref[...] * wave_c, v1_ref[...] * wave_c], axis=0)
-            moved = jnp.dot(pairs, lane_ref[...], preferred_element_type=F32)
-            real = moved[:rows, :WIDE] - moved[rows:, WIDE:]
-            imag = moved[:rows, WIDE:] + moved[rows:, :WIDE]
-            real = real.reshape(X6, Y16, WIDE)
-            imag = imag.reshape(X6, Y16, WIDE)
-            turned_r = real * twiddle_c - imag * twiddle_s
-            turned_i = real * twiddle_s + imag * twiddle_c
-            low_ref[index * rows : (index + 1) * rows, :] = turned_r.reshape(rows, WIDE).astype(
-                BF16
-            )
-            index += len(group)
-            low_ref[index * rows : (index + 1) * rows, :] = turned_i.reshape(rows, WIDE).astype(
-                BF16
-            )
+    for index, c_ref in enumerate(waves_c):
+        wave_c = c_ref[...]
+        pairs = jnp.concatenate([v0_ref[...] * wave_c, v1_ref[...] * wave_c], axis=0)
+        moved = jnp.dot(pairs, lane_ref[...], preferred_element_type=F32)
+        real = moved[:rows, :WIDE] - moved[rows:, WIDE:]
+        imag = moved[:rows, WIDE:] + moved[rows:, :WIDE]
+        real = real.reshape(X6, Y16, WIDE)
+        imag = imag.reshape(X6, Y16, WIDE)
+        turned_r = real * twiddle_c - imag * twiddle_s
+        turned_i = real * twiddle_s + imag * twiddle_c
+        low_ref[index * rows : (index + 1) * rows, :] = turned_r.reshape(rows, WIDE).astype(BF16)
+        index += items
+        low_ref[index * rows : (index + 1) * rows, :] = turned_i.reshape(rows, WIDE).astype(BF16)
     count = SLABS // SLAB_CUTS
-    extra = extra_ref[...]
+    size = items * 2 * X6
     for part in range(SLAB_CUTS):
         slabs = slice(part * count, (part + 1) * count)
-        first = 0
-        for group, low_ref, row_ref in zip(groups, low_refs, row_refs):
-            size = slab_rows(len(group))
-            planes = jnp.dot(
-                row_ref[part * count * size : (part + 1) * count * size, :],
-                low_ref[...],
-                preferred_element_type=F32,
-            ).reshape(count, size, WIDE)
-            slab_ref[slabs, first : first + size, :] = planes.astype(BF16)
-            if first == place:
-                spare = planes[:, : extra.shape[0], SPARE:] + extra[None]
-                slab_ref[slabs, first : first + extra.shape[0], SPARE:] = spare.astype(BF16)
-            first += size
+        planes = jnp.dot(
+            row_ref[part * count * size : (part + 1) * count * size, :],
+            low_ref[...],
+            preferred_element_type=F32,
+        ).reshape(count, size, WIDE)
+        slab_ref[slabs] = planes.astype(BF16)
+        if marks:
+            tail = planes[:, :8, SPARE:] + marks[0][...][None]
+            slab_ref[slabs, :8, SPARE:] = tail.astype(BF16)
         window = pl.ds(part * count, count)
         moves.append(
-            pltpu.make_async_copy(slab_ref.at[window], out_ref.at[window], slab_sems.at[part])
+            pltpu.make_async_copy(
+                slab_ref.at[window],
+                out_ref.at[window, pl.ds(first, size)],
+                slab_sems.at[part],
+            )
         )
         moves[-1].start()
     for move in moves:
         move.wait()
 
 
-PLACE = slab_rows(len(GROUPS[1][0]))
-
-
-def planes_of(chunk, v, c, extra, through=()):
-    groups = GROUPS[chunk]
-    slots = [slot for group in groups for slot in group]
-    rows = sum(slab_rows(len(group)) for group in groups)
-    tables = [row_table(len(group)) for group in groups]
+def planes_of(group, v, c, marks=(), through=(), buffer=()):
+    slots = GROUPS[group]
+    items = len(slots)
+    first = max(group - 1, 0) * items * 2 * X6
+    rows = CHUNK_ROWS[min(group, 1)]
+    inputs = (
+        *v,
+        *(c[slot] for slot in slots),
+        lane_table(),
+        twiddle_table(),
+        row_table(items),
+        *marks,
+        *through,
+        *buffer,
+    )
+    outside = len(through) + len(buffer)
     return pl.pallas_call(
         functools.partial(
-            plane_kernel, groups=groups, place=chunk * PLACE, through=len(through)
+            plane_kernel,
+            items=items,
+            first=first,
+            through=len(through),
+            chained=len(buffer),
+            marked=len(marks),
         ),
         out_shape=[
             pltpu.HBM((SLABS, rows, WIDE), BF16),
             *(pltpu.HBM(x.shape, x.dtype) for x in through),
         ],
-        in_specs=[VMEM] * (2 + len(slots) + 3 + len(tables)) + [ANY] * len(through),
+        in_specs=[VMEM] * (len(inputs) - outside) + [ANY] * len(through) + [HBM] * len(buffer),
         out_specs=[HBM] * (1 + len(through)),
+        input_output_aliases={len(inputs) - 1: 0} if buffer else {},
         scratch_shapes=[
-            *(pltpu.VMEM((2 * len(group) * X6 * Y16, WIDE), BF16) for group in groups),
-            pltpu.VMEM((SLABS, rows, WIDE), BF16),
+            pltpu.VMEM((2 * items * X6 * Y16, WIDE), BF16),
+            pltpu.VMEM((SLABS, items * 2 * X6, WIDE), BF16),
             pltpu.SemaphoreType.DMA((SLAB_CUTS,)),
             pltpu.SemaphoreType.DMA((max(len(through), 1),)),
         ],
         compiler_params=pltpu.CompilerParams(vmem_limit_bytes=16 << 20),
         cost_estimate=pl.CostEstimate(
-            flops=50_000_000, bytes_accessed=100_000, transcendentals=0
+            flops=PLANES_FLOPS[group] * items, bytes_accessed=100_000, transcendentals=0
         ),
         name="planes",
-    )(
-        *v,
-        *(c[slot] for slot in slots),
-        lane_table(),
-        twiddle_table(),
-        extra,
-        *tables,
-        *through,
-    )
+    )(*inputs)
 
 
 def pick(density_ref, flat_ref, kx_ref, store):
@@ -253,13 +248,13 @@
 
 def transform_x(chunk, t_ref, x_refs, low):
     first, place = 0, 0
-    for group, x_ref in zip(GROUPS[chunk], x_refs):
-        size = slab_rows(len(group))
+    for items, x_ref in zip(X_GROUPS[chunk], x_refs):
+        size = items * 2 * X6
         planes = t_ref[:, first : first + size, :]
         if size % 16:
             planes = planes.astype(F32)
         planes = planes.reshape(SLABS * size, WIDE).astype(BF16)
-        rows = 2 * len(group) * N
+        rows = 2 * items * N
         low[place : place + rows, :] = jnp.dot(
             x_ref[...], planes, preferred_element_type=F32
         ).astype(BF16)
@@ -293,7 +288,7 @@
         far_out[rows:, lanes] = values.astype(BF16)
 
     pick(low, far_ref, far_kx_ref, store_far)
-    spare = t_ref[:, PLACE : PLACE + 16, SPARE:].astype(F32).sum(axis=0)
+    spare = t_ref[:, :16, SPARE:].astype(F32).sum(axis=0)
     spare = spare + pltpu.roll(spare, 128 - NBLOCK, 1)
     block_out[...] = spare
 
@@ -305,7 +300,7 @@
     pick(low, own_ref, own_kx_ref, store_own)
 
 
-FIRST, SECOND = (2 * sum(len(group) for group in chunk) for chunk in GROUPS)
+FIRST, SECOND = (2 * sum(chunk) for chunk in X_GROUPS)
 
 
 def first_points(planes, own, far):
@@ -337,7 +332,7 @@
             flops=100_000_000, bytes_accessed=100_000, transcendentals=0
         ),
         name="second_far_points",
-    )(planes, *(x_table(len(group)) for group in GROUPS[1]), *far, first)
+    )(planes, *(x_table(items) for items in X_GROUPS[1]), *far, first)
 
 
 def second_own_points(low, own):
@@ -355,10 +350,9 @@
 def split_kernel(own0_ref, own1_ref, far_ref, block_ref, out_ref):
     parts = [[], [], [], []]
     first, place = 0, 0
-    for own_ref, chunk in zip((own0_ref, own1_ref), GROUPS):
+    for own_ref, chunk in zip((own0_ref, own1_ref), X_GROUPS):
         first = 0
-        for group in chunk:
-            size = len(group)
+        for size in chunk:
             own_r = own_ref[first : first + size, :]
             own_i = own_ref[first + size : first + 2 * size, :]
             far_r = far_ref[place : place + size, :].astype(F32)
@@ -388,34 +382,78 @@
     )(own0, own1, far, block)
 
 
+def phase_cosine(phase):
+    turns = jnp.floor((phase + 0.5) * (1.0 / N))
+    return jnp.cos((phase - N * turns) * (2.0 * math.pi / N))
+
+
 def block_kernel(*refs):
-    *waves, lane_ref, row_ref, out_ref = refs
+    waves, refs = refs[:2 + len(SLOTS)], refs[2 + len(SLOTS) :]
+    info_ref, marks_hbm, _, out_hbm, marks_ref, tail_ref, sums_ref, sems = refs
     waves_v, waves_c = waves[:2], waves[2:]
+    tail = (slice(None), pl.ds(0, 16), pl.ds(SPARE, 128))
+    fetch = pltpu.make_async_copy(out_hbm.at[tail], tail_ref, sems.at[0])
+    fetch.start()
+    place = marks_hbm.at[:, pl.ds(0, 8), pl.ds(SPARE, 128)]
+    marks_in = pltpu.make_async_copy(place, marks_ref, sems.at[1])
+    marks_in.start()
+    info = info_ref[...]
+    marks_in.wait()
+    marks = marks_ref[...].astype(F32).sum(axis=0)
+    used = info[3:4] != 0.0
+    cell = jnp.where(used, 256.0 * marks[0:1] + marks[1:2], 0.0)
+    block_x = jnp.floor((cell + 0.5) * (1.0 / 576.0))
+    cell = cell - 576.0 * block_x
+    block_y = jnp.floor((cell + 0.5) * (1.0 / N))
+    block_z = cell - N * block_y
+    block_y = block_y + info[0:1]
+    lane = lax.broadcasted_iota(jnp.int32, (Y6 * N, 128), 0).astype(F32)
+    y6 = jnp.floor((lane + 0.5) * (1.0 / N))
+    lanes = phase_cosine(16.0 * y6 * block_y + (lane - N * y6) * block_z + info[1:2]).astype(BF16)
+    row = lax.broadcasted_iota(jnp.int32, (X6 * Y16, 128), 0).astype(F32)
+    x = jnp.floor((row + 0.5) * (1.0 / Y16))
+    rows = phase_cosine((x + info[4:5]) * block_x + (row - Y16 * x) * block_y + info[2:3])
+    rows = rows * info[3:4]
     for half in range(2):
         for item, slot in enumerate(SLOTS):
             product = waves_v[half][...] * waves_c[slot][...]
-            sums = jnp.dot(product, lane_ref[...], preferred_element_type=F32) * row_ref[...]
+            sums = jnp.dot(product, lanes, preferred_element_type=F32) * rows
             index = half * len(SLOTS) + item
-            out_ref[index : index + 1, :] = sums.sum(axis=0, keepdims=True)
-    sums = out_ref[...]
+            sums_ref[index : index + 1, :] = sums.sum(axis=0, keepdims=True)
+    sums = sums_ref[...]
     sums = sums + pltpu.roll(sums, 128 - NBLOCK, 1)
     high = sums.astype(BF16).astype(F32)
     rest = pltpu.roll(sums - high, NBLOCK, 1)
-    lane = lax.broadcasted_iota(jnp.int32, sums.shape, 1)
-    sums = jnp.where(lane // NBLOCK % 2 == 0, high, rest)
-    out_ref[...] = jnp.where((lane >= 32) & (lane < 96), sums, 0.0)
-
-
-def block_sums(v, c, lanes, rows):
+    spot = lax.broadcasted_iota(jnp.int32, sums.shape, 1)
+    sums = jnp.where(spot // NBLOCK % 2 == 0, high, rest)
+    fetch.wait()
+    tails = tail_ref[...].astype(F32)
+    tail_ref[...] = jnp.where((spot >= 32) & (spot < 96), sums, tails).astype(BF16)
+    store = pltpu.make_async_copy(tail_ref, out_hbm.at[tail], sems.at[2])
+    store.start()
+    store.wait()
+
+
+def with_block_sums(v, c, info, arrived, planes):
+    inputs = (*v, *c, info, arrived, planes)
     return pl.pallas_call(
         block_kernel,
-        out_shape=jax.ShapeDtypeStruct((16, 128), F32),
-        compiler_params=pltpu.CompilerParams(vmem_limit_bytes=4 << 20),
+        out_shape=pltpu.HBM(planes.shape, planes.dtype),
+        in_specs=[VMEM] * (len(inputs) - 2) + [ANY, HBM],
+        out_specs=HBM,
+        input_output_aliases={len(inputs) - 1: 0},
+        scratch_shapes=[
+            pltpu.VMEM((SLABS, 8, 128), BF16),
+            pltpu.VMEM((SLABS, 16, 128), BF16),
+            pltpu.VMEM((16, 128), F32),
+            pltpu.SemaphoreType.DMA((3,)),
+        ],
+        compiler_params=pltpu.CompilerParams(vmem_limit_bytes=6 << 20),
         cost_estimate=pl.CostEstimate(
             flops=10_000_000, bytes_accessed=100_000, transcendentals=0
         ),
         name="block",
-    )(*v, *c, lanes, rows)
+    )(*inputs)
 
 
 def sum_kernel(pairs_ref, weight_ref, column_ref, out_ref):
@@ -435,10 +473,6 @@
 
 def wave_rows(wave):
     return wave.reshape(X6, Y6, Y16, N).transpose(0, 2, 1, 3).reshape(X6 * Y16, Y6 * N)
-
-
-def cosine(phase):
-    return jnp.cos((phase % N).astype(F32) * (2.0 * math.pi / N))
 
 
 def per_device(
@@ -468,33 +502,27 @@
     spots = jnp.arange(128, dtype=jnp.int32)
     cell = jnp.where((spots % NBLOCK == col) & (spots >= 32), block_cell[0], 0)
     marks = jnp.concatenate([jnp.stack([cell // 256, cell % 256]), jnp.zeros((6, 128), jnp.int32)])
-    planes0, far_cell = planes_of(0, v, c, marks.astype(F32), through=(far_cell,))
+    planes0, far_cell = planes_of(0, v, c, marks=(marks.astype(F32),), through=(far_cell,))
     sent0 = lax.all_to_all(planes0, COL, 0, 0, tiled=True)
+    (planes1,) = planes_of(1, v, c)
+    (planes1,) = planes_of(2, v, c, buffer=(planes1,))
+    (planes1,) = planes_of(3, v, c, buffer=(planes1,))
+
+    group = np.arange(128) // NBLOCK - 2
+    used = (group >= 0) & (group < 4)
+    info = np.zeros((8, 128), np.float32)
+    info[0] = np.arange(128) % NBLOCK * 6
+    info[1] = np.where(group % 2 == 1, N // 4, 0)
+    info[2] = np.where(group == 1, 3 * N // 4, np.where(group == 2, N // 4, 0))
+    info[3] = np.where(used, 1.0 / (N * math.sqrt(N)), 0.0)
+    info = info + jnp.where(np.arange(8)[:, None] == 4, (X6 * col).astype(F32), 0.0)
+    planes1 = with_block_sums(v, c, info, sent0, planes1)
+    sent1 = lax.all_to_all(planes1, COL, 0, 0, tiled=True)
 
     far_cell = far_cell.reshape(G_DEV)
     far_x, far_y, far_z = far_cell // 576, far_cell // N % 6, far_cell % N
     own = ((gvec_cell % 576)[None], (gvec_cell // 576)[None])
     far = (((6 - far_y) * N + (N - far_z) % N)[None], ((N - far_x) % N)[None])
-
-    marks = sent0[:, :2, SPARE:].astype(F32).sum(axis=0)
-    cells = jnp.where(spots >= 32, (256.0 * marks[0] + marks[1]).astype(jnp.int32), 0)
-    block_x = cells // 576
-    block_y = spots % NBLOCK * 6 + cells // N % 6
-    block_z = cells % N
-    group = spots // NBLOCK - 2
-    quarter = N // 4
-    lane = jnp.arange(Y6 * N, dtype=jnp.int32)[:, None]
-    lanes = cosine(
-        lane // N * 16 * block_y + lane % N * block_z + jnp.where(group % 2 == 1, quarter, 0)
-    ).astype(BF16)
-    row = jnp.arange(X6 * Y16, dtype=jnp.int32)[:, None]
-    shift = jnp.where(group == 1, 3 * quarter, jnp.where(group == 2, quarter, 0))
-    rows = cosine((row // Y16 + X6 * col) * block_x + row % Y16 * block_y + shift)
-    scale = 1.0 / (N * math.sqrt(N))
-    rows = jnp.where((group >= 0) & (group < 4), rows * scale, 0.0)
-    block = block_sums(v, c, lanes, rows)
-    (planes1,) = planes_of(1, v, c, block)
-    sent1 = lax.all_to_all(planes1, COL, 0, 0, tiled=True)
 
     pair_v, pair_c = pair_table()
     occupied = jnp.arange(occupied_energy.shape[0], dtype=jnp.int32)

time: 118 us -> 118 us (level)
  local copies, waits for them, and re-layouts: 5.13 us -> 9.27 us
  waiting for transfers between devices: 41.6 us -> 38.3 us
  Pallas kernels: 27.3 us -> 30.6 us
  starting transfers between devices: 38.8 us -> 36.2 us
  other arithmetic: 2.74 us -> 0.81 us
    ppermute x4, waiting for transfers between devices: 8.45 us -> 1.25 us  [per_device(): c[slot] = lax.ppermute(c[slot - 1], 'z', ahead)]
    unnamed x34 -> x46, local copies, waits for them, and re-layouts: 2.18 us -> 6.32 us
    all_to_all x1, waiting for transfers between devices: 14.6 us -> 18.4 us  [per_device(): sent1 = lax.all_to_all(planes1, COL, 0, 0, tiled=True)]
    pallas_call x3 -> x5, Pallas kernels: 10.7 us -> 14.1 us  [the longest x4 10.4 us: planes_of(): pl.pallas_call(functools.partial(plane_kernel, items=items, first=first,...]
    ppermute x3, waiting for transfers between devices: 0.01 us -> 3.34 us  [per_device(): c[8 - slot] = lax.ppermute(c[(9 - slot) % 8], 'z', behind)]
    all_to_all x1, waiting for transfers between devices: 2.18 us -> 0.01 us  [per_device(): sent0 = lax.all_to_all(planes0, COL, 0, 0, tiled=True)]
    all_to_all x1, starting transfers between devices: 5.86 us -> 4.21 us  [per_device(): pairs = lax.all_to_all(pairs, BAND, 0, 0, tiled=True)]
    pallas_call x1, Pallas kernels: 6 us -> 4.39 us  [first_points(): pl.pallas_call(first_kernel, out_shape=(jax.ShapeDtypeStruct((FIRST, G_DE...]
  transfers between devices with their start and end apart: 13 -> 13, of which waited for: 8 -> 6; matrix products, arithmetic and copies ran while one was open for 4% -> 2% of each run, Pallas kernels for 8% -> 17%
where the time goes in v7:
time: 118 us; the launch traced here: 116 us
  waiting for transfers between devices  38.3 us (32%)
  starting transfers between devices  36.2 us (31%)
  Pallas kernels  30.6 us (26%)
  local copies, waits for them, and re-layouts  9.27 us (8%)
    all_to_all x1, waiting for transfers between devices, per_device(): sent1 = lax.all_to_all(planes1, COL, 0, 0, tiled=True)  18.4 us
    all_to_all x1, waiting for transfers between devices, per_device(): pairs = lax.all_to_all(pairs, BAND, 0, 0, tiled=True)  10.8 us
    pallas_call x4, Pallas kernels, planes_of(): pl.pallas_call(functools.partial(plane_kernel, items=items, first=first,...  10.4 us
    ppermute x3, starting transfers between devices, per_device(): c[8 - slot] = lax.ppermute(c[(9 - slot) % 8], 'z', behind)  9.2 us
    all_to_all x1, starting transfers between devices, per_device(): sent1 = lax.all_to_all(planes1, COL, 0, 0, tiled=True)  7.37 us
    all_to_all x1, starting transfers between devices, per_device(): sent0 = lax.all_to_all(planes0, COL, 0, 0, tiled=True)  6.88 us
    unnamed x46, local copies, waits for them, and re-layouts  6.32 us
    pallas_call x1, Pallas kernels, second_far_points(): pl.pallas_call(second_far_kernel, out_shape=(jax.ShapeDtypeStruct((FIRST...  5.9 us
  transfers between devices with their start and end apart: 13, of which 6 were waited for; matrix products, arithmetic and copies ran while one was open for 2% of the time, Pallas kernels for 17%

profile of v7, /device:TPU:6, one launch (start us, length us, event | category | flops | bytes accessed | tf_op | source)
XLA Modules:
  0.0 116.1 jit_solution(5820645181387875741)
XLA Ops:
  0.0 1.2 %reshape.316 = bf16[6,6,16,96]{3,2,1,0:T(8,128)(2,1)S(1)} reshape(bf16[1,6,9216]{2,1,0:T(8,128)(2,1)} %param.19) | data formatting | bytes 221184 | tf_op jit(solution)/shard_map/reshape | solution.py:475
  1.5 2.0 %collective-permute-start.1 = (bf16[96,576]{1,0:T(8,128)(2,1)S(1)}, bf16[96,576]{1,0:T(8,128)(2,1)}, u32[]{:S(2)}, u32[]{:S(2)}) collective-permute-start(bf16[96,576]{1,0:T(8,128)(2,1)S(1)} %reshape.317.refs_2_), channel_id=1, source_target_pairs={{0,32},{32,64},{64,96},{96,128},{128,160},{160,192},{192,224},{224... | collective-permute-start | bytes 331784 | tf_op jit(solution)/shard_map/ppermute | solution.py:496
  3.5 4.0 %collective-permute-start.6 = (bf16[96,576]{1,0:T(8,128)(2,1)S(1)}, bf16[96,576]{1,0:T(8,128)(2,1)S(1)}, u32[]{:S(2)}, u32[]{:S(2)}) collective-permute-start(bf16[96,576]{1,0:T(8,128)(2,1)S(1)} %reshape.317.refs_2_), channel_id=1, source_target_pairs={{0,224},{32,0},{64,32},{96,64},{128,96},{160,128},{192,160},{224,1... | collective-permute-start | bytes 331784 | tf_op jit(solution)/shard_map/ppermute | solution.py:498
  7.5 1.1 reshape.314
  8.8 1.7 %collective-permute-start = (bf16[96,576]{1,0:T(8,128)(2,1)S(1)}, bf16[96,576]{1,0:T(8,128)(2,1)S(1)}, u32[]{:S(2)}, u32[]{:S(2)}) collective-permute-start(bf16[96,576]{1,0:T(8,128)(2,1)S(1)} %reshape.315.refs_0_), channel_id=1, source_target_pairs={{0,16},{16,0},{1,17},{17,1},{2,18},{18,2},{3,19},{19,3},{4,20},{20... | collective-permute-start | bytes 331784 | tf_op jit(solution)/shard_map/ppermute | solution.py:493
  10.5 1.7 %collective-permute-start.2 = (s32[2048]{0:T(1024)S(1)}, s32[2048]{0:T(1024)S(1)}, u32[]{:S(2)}, u32[]{:S(2)}) collective-permute-start(s32[2048]{0:T(1024)S(1)} %copy-done.15), channel_id=1, source_target_pairs={{0,15},{1,14},{2,13},{3,12},{4,11},{5,10},{6,9},{7,8},{8,7},{9,6},... | collective-permute-start | bytes 24584 | tf_op jit(solution)/shard_map/ppermute | solution.py:501
  13.1 4.1 %collective-permute-done.2 = s32[2048]{0:T(1024)S(1)} collective-permute-done((s32[2048]{0:T(1024)S(1)}, s32[2048]{0:T(1024)S(1)}, u32[]{:S(2)}, u32[]{:S(2)}) %collective-permute-start.2) | collective-permute-done | bytes 8224 | tf_op jit(solution)/shard_map/ppermute | solution.py:501
  17.2 1.0 copy-done.1
  18.1 3.3 %planes.4 = (bf16[16,24,768]{2,1,0:T(8,128)(2,1)}, s32[16,128]{1,0:T(8,128)}) custom-call(bf16[96,576]{1,0:T(8,128)(2,1)S(1)} %reshape.315.refs_0_, bf16[96,576]{1,0:T(8,128)(2,1)S(1)} %collective-permute-done.refs_1_, bf16[96,576]{1,0:T(8,128)(2,1)S(1)} %reshape.317.refs_2_, bf16[96,576]{1,0:T(8,128)(2,1)} %collective-permute-done.1.refs_3_, ...), custom_call_target="tpu_custom_call" | custom-call | flops 60000000 | bytes 100000 | tf_op jit(solution)/shard_map/planes/pallas_call | solution.py:203
  21.4 6.9 %all-to-all-start = ((bf16[16,24,768]{2,1,0:T(8,128)(2,1)}), bf16[16,24,768]{2,1,0:T(8,128)(2,1)S(1)}, u32[]{:S(2)}, u32[]{:S(2)}) async-start(bf16[16,24,768]{2,1,0:T(8,128)(2,1)} %get-tuple-element.12), calls=%async_computation | async-start | bytes 1179648 | tf_op jit(solution)/shard_map/all_to_all | solution.py:506
  28.3 2.0 %collective-permute-start.7 = (bf16[96,576]{1,0:T(8,128)(2,1)S(1)}, bf16[96,576]{1,0:T(8,128)(2,1)S(1)}, u32[]{:S(2)}, u32[]{:S(2)}) collective-permute-start(bf16[96,576]{1,0:T(8,128)(2,1)S(1)} %collective-permute-done.6.refs_2_.refs_9_), channel_id=1, source_target_pairs={{0,224},{32,0},{64,32},{96,64},{128,96},{160,128},{192,160},{224,1... | collective-permute-start | bytes 331784 | tf_op jit(solution)/shard_map/ppermute | solution.py:498
  30.4 3.3 %collective-permute-done.7.refs_2_.refs_8_ = bf16[96,576]{1,0:T(8,128)(2,1)S(1)} collective-permute-done((bf16[96,576]{1,0:T(8,128)(2,1)S(1)}, bf16[96,576]{1,0:T(8,128)(2,1)S(1)}, u32[]{:S(2)}, u32[]{:S(2)}) %collective-permute-start.7) | collective-permute-done | bytes 110624 | tf_op jit(solution)/shard_map/ppermute | solution.py:498
  33.8 3.2 %collective-permute-start.8 = (bf16[96,576]{1,0:T(8,128)(2,1)S(1)}, bf16[96,576]{1,0:T(8,128)(2,1)S(1)}, u32[]{:S(2)}, u32[]{:S(2)}) collective-permute-start(bf16[96,576]{1,0:T(8,128)(2,1)S(1)} %collective-permute-done.7.refs_2_.refs_8_), channel_id=1, source_target_pairs={{0,224},{32,0},{64,32},{96,64},{128,96},{160,128},{192,160},{224,1... | collective-permute-start | bytes 331784 | tf_op jit(solution)/shard_map/ppermute | solution.py:498
  37.0 2.4 %planes.5.refs_7_ = bf16[16,72,768]{2,1,0:T(8,128)(2,1)} custom-call(bf16[96,576]{1,0:T(8,128)(2,1)S(1)} %reshape.315.refs_0_, bf16[96,576]{1,0:T(8,128)(2,1)S(1)} %collective-permute-done.refs_1_, bf16[96,576]{1,0:T(8,128)(2,1)S(1)} %collective-permute-done.6.refs_2_.refs_9_, bf16[96,576]{1,0:T(8,128)(2,1)S(1)} %collective-permute-done.3.refs_3_.refs_4_, ...), custom_call_target="tpu_custom_call" | custom-call | flops 60000000 | bytes 100000 | tf_op jit(solution)/shard_map/planes/pallas_call | solution.py:203
  39.4 2.4 %planes.6.refs_7_ = bf16[16,72,768]{2,1,0:T(8,128)(2,1)} custom-call(bf16[96,576]{1,0:T(8,128)(2,1)S(1)} %reshape.315.refs_0_, bf16[96,576]{1,0:T(8,128)(2,1)S(1)} %collective-permute-done.refs_1_, bf16[96,576]{1,0:T(8,128)(2,1)S(1)} %collective-permute-done.7.refs_2_.refs_8_, ...), custom_call_target="tpu_custom_call", output_to_operand_aliasing={{}: (7, {})} | custom-call | flops 60000000 | bytes 100000 | tf_op jit(solution)/shard_map/planes/pallas_call | solution.py:203
  41.8 1.2 %collective-permute-done.5.refs_3_.refs_6_ = bf16[96,576]{1,0:T(8,128)(2,1)S(1)} collective-permute-done((bf16[96,576]{1,0:T(8,128)(2,1)S(1)}, bf16[96,576]{1,0:T(8,128)(2,1)S(1)}, u32[]{:S(2)}, u32[]{:S(2)}) %collective-permute-start.5) | collective-permute-done | bytes 110624 | tf_op jit(solution)/shard_map/ppermute | solution.py:496
  43.0 2.4 %planes.7.refs_12_ = bf16[16,72,768]{2,1,0:T(8,128)(2,1)} custom-call(bf16[96,576]{1,0:T(8,128)(2,1)S(1)} %reshape.315.refs_0_, bf16[96,576]{1,0:T(8,128)(2,1)S(1)} %collective-permute-done.refs_1_, bf16[96,576]{1,0:T(8,128)(2,1)S(1)} %collective-permute-done.8.refs_2_.refs_7_, ...), custom_call_target="tpu_custom_call", output_to_operand_aliasing={{}: (7, {})} | custom-call | flops 60000000 | bytes 100000 | tf_op jit(solution)/shard_map/planes/pallas_call | solution.py:203
  46.7 0.9 copy-done.7
  47.6 0.9 copy-done.9
  48.5 0.9 copy-done.11
  49.4 3.7 %block.1 = bf16[16,72,768]{2,1,0:T(8,128)(2,1)} custom-call(bf16[96,576]{1,0:T(8,128)(2,1)S(1)} %reshape.315.refs_0_, bf16[96,576]{1,0:T(8,128)(2,1)S(1)} %collective-permute-done.refs_1_, bf16[96,576]{1,0:T(8,128)(2,1)S(1)} %reshape.317.refs_2_, bf16[96,576]{1,0:T(8,128)(2,1)} %collective-permute-done.1.refs_3_, ...), custom_call_target="tpu_custom_call", output_to_operand_aliasing={{}: (12, {})} | custom-call | flops 10000000 | bytes 100000 | tf_op jit(solution)/shard_map/block/pallas_call | solution.py:439
  53.3 7.4 %all-to-all-start.1 = ((bf16[16,72,768]{2,1,0:T(8,128)(2,1)}), bf16[16,72,768]{2,1,0:T(8,128)(2,1)S(1)}, u32[]{:S(2)}, u32[]{:S(2)}) async-start(bf16[16,72,768]{2,1,0:T(8,128)(2,1)} %block.1), calls=%async_computation.1 | async-start | bytes 3538944 | tf_op jit(solution)/shard_map/all_to_all | solution.py:520
  61.4 4.4 %first_points.1 = (f32[4,2048]{1,0:T(4,128)S(1)}, bf16[4,2048]{1,0:T(4,128)(2,1)S(1)}) custom-call(bf16[16,24,768]{2,1,0:T(8,128)(2,1)S(1)} %all-to-all-done.t_ref.refs_11_, bf16[384,384]{1,0:T(8,128)(2,1)S(1)} %copy-done.4, s32[1,2048]{1,0:T(1,128)S(1)} %bitcast.39, s32[1,2048]{1,0:T(1,128)S(1)} %bitcast.37, s32[1,2048]{1,0:T(1,128)S(1)} %get-tuple-element.29.far_ref, ...), custom_call_target="tpu_custom_call" | custom-call | flops 100000000 | bytes 100000 | tf_op jit(solution)/shard_map/first_points/pallas_call | solution.py:307
  65.8 18.4 %all-to-all-done.1.t_ref = bf16[16,72,768]{2,1,0:T(8,128)(2,1)S(1)} async-done(((bf16[16,72,768]{2,1,0:T(8,128)(2,1)}), bf16[16,72,768]{2,1,0:T(8,128)(2,1)S(1)}, u32[]{:S(2)}, u32[]{:S(2)}) %all-to-all-start.1) | async-done | bytes 1769504 | tf_op jit(solution)/shard_map/all_to_all | solution.py:520
  84.1 1.3 %copy-done.5 = bf16[768,768]{1,0:T(8,128)(2,1)S(1)} copy-done((bf16[768,768]{1,0:T(8,128)(2,1)S(1)}, bf16[768,768]{1,0:T(8,128)(2,1)}, u32[]{:S(2)}) %copy-start.5) | copy-done | bytes 1179672
  85.4 5.9 %second_far_points.1 = (bf16[16,2048]{1,0:T(8,128)(2,1)S(1)}, bf16[1152,768]{1,0:T(8,128)(2,1)S(1)}, f32[16,128]{1,0:T(8,128)S(1)}) custom-call(bf16[16,72,768]{2,1,0:T(8,128)(2,1)S(1)} %all-to-all-done.1.t_ref, bf16[768,768]{1,0:T(8,128)(2,1)S(1)} %copy-done.5, bf16[384,384]{1,0:T(8,128)(2,1)S(1)} %copy-done.4, s32[1,2048]{1,0:T(1,128)S(1)} %get-tuple-element.29.far_ref, ...), custom_call_target="tpu_custom_call" | custom-call | flops 100000000 | bytes 100000 | tf_op jit(solution)/shard_map/second_far_points/pallas_call | solution.py:323
  91.3 3.0 %collective-permute-start.9 = (bf16[16,2048]{1,0:T(8,128)(2,1)S(1)}, bf16[16,2048]{1,0:T(8,128)(2,1)S(1)}, u32[]{:S(2)}, u32[]{:S(2)}) collective-permute-start(bf16[16,2048]{1,0:T(8,128)(2,1)S(1)} %get-tuple-element.17), channel_id=1, source_target_pairs={{0,15},{1,14},{2,13},{3,12},{4,11},{5,10},{6,9},{7,8},{8,7},{9,6},... | collective-permute-start | bytes 196616 | tf_op jit(solution)/shard_map/ppermute | solution.py:547
  94.3 4.4 %second_own_points.1.own1_ref = f32[12,2048]{1,0:T(8,128)S(1)} custom-call(bf16[1152,768]{1,0:T(8,128)(2,1)S(1)} %get-tuple-element.16.low, s32[1,2048]{1,0:T(1,128)S(1)} %bitcast.40, s32[1,2048]{1,0:T(1,128)S(1)} %bitcast.38), custom_call_target="tpu_custom_call" | custom-call | flops 2400000000 | bytes 1300000 | tf_op jit(solution)/shard_map/second_own_points/pallas_call | solution.py:339
  99.2 0.8 split.1
  99.9 4.2 %all-to-all-start.2 = ((bf16[16,48,128]{2,1,0:T(8,128)(2,1)}), bf16[16,48,128]{2,1,0:T(8,128)(2,1)S(1)}, u32[]{:S(2)}, u32[]{:S(2)}) async-start(bf16[16,48,128]{2,1,0:T(8,128)(2,1)} %split.1), calls=%async_computation.2 | async-start | bytes 393216 | tf_op jit(solution)/shard_map/all_to_all | solution.py:550
  104.3 10.8 %all-to-all-done.2.pairs_ref = bf16[16,48,128]{2,1,0:T(8,128)(2,1)S(1)} async-done(((bf16[16,48,128]{2,1,0:T(8,128)(2,1)}), bf16[16,48,128]{2,1,0:T(8,128)(2,1)S(1)}, u32[]{:S(2)}, u32[]{:S(2)}) %all-to-all-start.2) | async-done | bytes 196640 | tf_op jit(solution)/shard_map/all_to_all | solution.py:550
  115.1 1.0 pair_sum.1
  (73 shorter events, 3.5 us)
Async XLA Ops:
  0.0 17.1 %copy-start = (bf16[576,1536]{1,0:T(8,128)(2,1)S(1)}, bf16[576,1536]{1,0:T(8,128)(2,1)}, u32[]{:S(2)}) copy-start(bf16[576,1536]{1,0:T(8,128)(2,1)} %constant.133.clone.refs_4_) | copy-start | bytes 5308420
  0.0 17.2 %copy-start.3 = (f32[2,16,768]{2,1,0:T(8,128)S(1)}, f32[2,16,768]{2,1,0:T(8,128)}, u32[]{:S(2)}) copy-start(f32[2,16,768]{2,1,0:T(8,128)} %constant.134.clone.refs_5_) | copy-start | bytes 294916
  0.0 10.4 %copy-start.15 = (s32[2048]{0:T(1024)S(1)}, s32[2048]{0:T(1024)}, u32[]{:S(2)}) copy-start(s32[2048]{0:T(1024)} %param.24) | copy-start | bytes 24580
  1.5 11.4 %collective-permute-start.1 = (bf16[96,576]{1,0:T(8,128)(2,1)S(1)}, bf16[96,576]{1,0:T(8,128)(2,1)}, u32[]{:S(2)}, u32[]{:S(2)}) collective-permute-start(bf16[96,576]{1,0:T(8,128)(2,1)S(1)} %reshape.317.refs_2_), channel_id=1, source_target_pairs={{0,32},{32,64},{64,96},{96,128},{128,160},{160,192},{192,224},{224... | collective-permute-start | bytes 331784 | tf_op jit(solution)/shard_map/ppermute | solution.py:496
  3.5 24.9 %collective-permute-start.6 = (bf16[96,576]{1,0:T(8,128)(2,1)S(1)}, bf16[96,576]{1,0:T(8,128)(2,1)S(1)}, u32[]{:S(2)}, u32[]{:S(2)}) collective-permute-start(bf16[96,576]{1,0:T(8,128)(2,1)S(1)} %reshape.317.refs_2_), channel_id=1, source_target_pairs={{0,224},{32,0},{64,32},{96,64},{128,96},{160,128},{192,160},{224,1... | collective-permute-start | bytes 331784 | tf_op jit(solution)/shard_map/ppermute | solution.py:498
  8.8 8.4 %collective-permute-start = (bf16[96,576]{1,0:T(8,128)(2,1)S(1)}, bf16[96,576]{1,0:T(8,128)(2,1)S(1)}, u32[]{:S(2)}, u32[]{:S(2)}) collective-permute-start(bf16[96,576]{1,0:T(8,128)(2,1)S(1)} %reshape.315.refs_0_), channel_id=1, source_target_pairs={{0,16},{16,0},{1,17},{17,1},{2,18},{18,2},{3,19},{19,3},{4,20},{20... | collective-permute-start | bytes 331784 | tf_op jit(solution)/shard_map/ppermute | solution.py:493
  10.5 6.7 %collective-permute-start.2 = (s32[2048]{0:T(1024)S(1)}, s32[2048]{0:T(1024)S(1)}, u32[]{:S(2)}, u32[]{:S(2)}) collective-permute-start(s32[2048]{0:T(1024)S(1)} %copy-done.15), channel_id=1, source_target_pairs={{0,15},{1,14},{2,13},{3,12},{4,11},{5,10},{6,9},{7,8},{8,7},{9,6},... | collective-permute-start | bytes 24584 | tf_op jit(solution)/shard_map/ppermute | solution.py:501
  12.9 17.4 %collective-permute-start.3 = (bf16[96,576]{1,0:T(8,128)(2,1)}, bf16[96,576]{1,0:T(8,128)(2,1)S(1)}, u32[]{:S(2)}, u32[]{:S(2)}) collective-permute-start(bf16[96,576]{1,0:T(8,128)(2,1)} %collective-permute-done.1.refs_3_), channel_id=1, source_target_pairs={{0,32},{32,64},{64,96},{96,128},{128,160},{160,192},{192,224},{224... | collective-permute-start | bytes 331784 | tf_op jit(solution)/shard_map/ppermute | solution.py:496
  17.2 1.0 copy-start.1
  18.1 12.3 %copy-start.22 = (pred[8,1]{0,1:T(4,128)(4,1)S(1)}, pred[8,1]{0,1:T(4,128)(4,1)}, u32[]{:S(2)}) copy-start(pred[8,1]{0,1:T(4,128)(4,1)} %constant.136.clone) | copy-start | bytes 28
  18.1 18.8 %copy-start.16 = (f32[8,128]{1,0:T(8,128)S(1)}, f32[8,128]{1,0:T(8,128)}, u32[]{:S(2)}) copy-start(f32[8,128]{1,0:T(8,128)} %constant.137.clone) | copy-start | bytes 12292
  18.1 18.9 %copy-start.2 = (bf16[384,384]{1,0:T(8,128)(2,1)S(1)}, bf16[384,384]{1,0:T(8,128)(2,1)}, u32[]{:S(2)}) copy-start(bf16[384,384]{1,0:T(8,128)(2,1)} %constant.135.clone.refs_6_) | copy-start | bytes 884740
  21.4 25.3 %all-to-all-start = ((bf16[16,24,768]{2,1,0:T(8,128)(2,1)}), bf16[16,24,768]{2,1,0:T(8,128)(2,1)S(1)}, u32[]{:S(2)}, u32[]{:S(2)}) async-start(bf16[16,24,768]{2,1,0:T(8,128)(2,1)} %get-tuple-element.12), calls=%async_computation | async-start | bytes 1179648 | tf_op jit(solution)/shard_map/all_to_all | solution.py:506
  28.3 5.5 %collective-permute-start.7 = (bf16[96,576]{1,0:T(8,128)(2,1)S(1)}, bf16[96,576]{1,0:T(8,128)(2,1)S(1)}, u32[]{:S(2)}, u32[]{:S(2)}) collective-permute-start(bf16[96,576]{1,0:T(8,128)(2,1)S(1)} %collective-permute-done.6.refs_2_.refs_9_), channel_id=1, source_target_pairs={{0,224},{32,0},{64,32},{96,64},{128,96},{160,128},{192,160},{224,1... | collective-permute-start | bytes 331784 | tf_op jit(solution)/shard_map/ppermute | solution.py:498
  30.3 6.6 %collective-permute-start.4 = (bf16[96,576]{1,0:T(8,128)(2,1)S(1)}, bf16[96,576]{1,0:T(8,128)(2,1)S(1)}, u32[]{:S(2)}, u32[]{:S(2)}) collective-permute-start(bf16[96,576]{1,0:T(8,128)(2,1)S(1)} %collective-permute-done.3.refs_3_.refs_4_), channel_id=1, source_target_pairs={{0,32},{32,64},{64,96},{96,128},{128,160},{160,192},{192,224},{224... | collective-permute-start | bytes 331784 | tf_op jit(solution)/shard_map/ppermute | solution.py:496
  33.8 8.0 %collective-permute-start.8 = (bf16[96,576]{1,0:T(8,128)(2,1)S(1)}, bf16[96,576]{1,0:T(8,128)(2,1)S(1)}, u32[]{:S(2)}, u32[]{:S(2)}) collective-permute-start(bf16[96,576]{1,0:T(8,128)(2,1)S(1)} %collective-permute-done.7.refs_2_.refs_8_), channel_id=1, source_target_pairs={{0,224},{32,0},{64,32},{96,64},{128,96},{160,128},{192,160},{224,1... | collective-permute-start | bytes 331784 | tf_op jit(solution)/shard_map/ppermute | solution.py:498
  36.9 2.5 %copy-start.6 = (bf16[96,576]{1,0:T(8,128)(2,1)}, bf16[96,576]{1,0:T(8,128)(2,1)S(1)}, u32[]{:S(2)}) copy-start(bf16[96,576]{1,0:T(8,128)(2,1)S(1)} %collective-permute-done.4.refs_3_.refs_5_) | copy-start | bytes 331780
  36.9 6.1 %collective-permute-start.5 = (bf16[96,576]{1,0:T(8,128)(2,1)S(1)}, bf16[96,576]{1,0:T(8,128)(2,1)S(1)}, u32[]{:S(2)}, u32[]{:S(2)}) collective-permute-start(bf16[96,576]{1,0:T(8,128)(2,1)S(1)} %collective-permute-done.4.refs_3_.refs_5_), channel_id=1, source_target_pairs={{0,32},{32,64},{64,96},{96,128},{128,160},{160,192},{192,224},{224... | collective-permute-start | bytes 331784 | tf_op jit(solution)/shard_map/ppermute | solution.py:496
  46.7 0.9 copy-start.7
  53.2 7.5 %copy-start.21 = (f32[4]{0:T(128)S(1)}, f32[4]{0:T(128)}, u32[]{:S(2)}) copy-start(f32[4]{0:T(128)} %param.23) | copy-start | bytes 52
  53.2 7.6 %copy-start.14 = (f32[4096]{0:T(1024)S(1)}, f32[4096]{0:T(1024)}, u32[]{:S(2)}) copy-start(f32[4096]{0:T(1024)} %param.21) | copy-start | bytes 49156
  53.2 7.6 %copy-start.19 = (s32[16]{0:T(128)S(1)}, s32[16]{0:T(128)}, u32[]{:S(2)}) copy-start(s32[16]{0:T(128)} %param.20) | copy-start | bytes 196
  53.2 7.8 %copy-start.17 = (pred[256,16]{0,1:T(8,128)(4,1)S(1)}, pred[256,16]{0,1:T(8,128)(4,1)}, u32[]{:S(2)}) copy-start(pred[256,16]{0,1:T(8,128)(4,1)} %constant.138.clone) | copy-start | bytes 12292
  53.2 7.8 %copy-start.18 = (pred[256,16]{0,1:T(8,128)(4,1)S(1)}, pred[256,16]{0,1:T(8,128)(4,1)}, u32[]{:S(2)}) copy-start(pred[256,16]{0,1:T(8,128)(4,1)} %constant.139.clone) | copy-start | bytes 12292
  53.2 7.8 %copy-start.20 = (f32[16]{0:T(128)S(1)}, f32[16]{0:T(128)}, u32[]{:S(2)}) copy-start(f32[16]{0:T(128)} %param.22) | copy-start | bytes 196
  53.2 7.9 %copy-start.13 = (s32[16,128]{1,0:T(8,128)S(1)}, s32[16,128]{1,0:T(8,128)}, u32[]{:S(2)}) copy-start(s32[16,128]{1,0:T(8,128)} %get-tuple-element.13) | copy-start | bytes 24580
  53.2 8.1 %copy-start.4 = (bf16[384,384]{1,0:T(8,128)(2,1)S(1)}, bf16[384,384]{1,0:T(8,128)(2,1)}, u32[]{:S(2)}) copy-start(bf16[384,384]{1,0:T(8,128)(2,1)} %constant.140.clone.x_ref.x1_ref) | copy-start | bytes 884740
  53.3 30.9 %all-to-all-start.1 = ((bf16[16,72,768]{2,1,0:T(8,128)(2,1)}), bf16[16,72,768]{2,1,0:T(8,128)(2,1)S(1)}, u32[]{:S(2)}, u32[]{:S(2)}) async-start(bf16[16,72,768]{2,1,0:T(8,128)(2,1)} %block.1), calls=%async_computation.1 | async-start | bytes 3538944 | tf_op jit(solution)/shard_map/all_to_all | solution.py:520
  84.1 1.3 %copy-start.5 = (bf16[768,768]{1,0:T(8,128)(2,1)S(1)}, bf16[768,768]{1,0:T(8,128)(2,1)}, u32[]{:S(2)}) copy-start(bf16[768,768]{1,0:T(8,128)(2,1)} %constant.141.clone.x0_ref) | copy-start | bytes 3538948
  91.3 7.8 %collective-permute-start.9 = (bf16[16,2048]{1,0:T(8,128)(2,1)S(1)}, bf16[16,2048]{1,0:T(8,128)(2,1)S(1)}, u32[]{:S(2)}, u32[]{:S(2)}) collective-permute-start(bf16[16,2048]{1,0:T(8,128)(2,1)S(1)} %get-tuple-element.17), channel_id=1, source_target_pairs={{0,15},{1,14},{2,13},{3,12},{4,11},{5,10},{6,9},{7,8},{8,7},{9,6},... | collective-permute-start | bytes 196616 | tf_op jit(solution)/shard_map/ppermute | solution.py:547
  94.3 20.8 %copy-start.12 = (bf16[2,128,128]{2,1,0:T(8,128)(2,1)S(1)}, bf16[2,128,128]{2,1,0:T(8,128)(2,1)}, u32[]{:S(2)}) copy-start(bf16[2,128,128]{2,1,0:T(8,128)(2,1)} %constant.142.clone.column_ref) | copy-start | bytes 196612
  99.9 15.2 %all-to-all-start.2 = ((bf16[16,48,128]{2,1,0:T(8,128)(2,1)}), bf16[16,48,128]{2,1,0:T(8,128)(2,1)S(1)}, u32[]{:S(2)}, u32[]{:S(2)}) async-start(bf16[16,48,128]{2,1,0:T(8,128)(2,1)} %split.1), calls=%async_computation.2 | async-start | bytes 393216 | tf_op jit(solution)/shard_map/all_to_all | solution.py:550
  (4 other events, 3.1 us)

commit v8 on v7

--- a/solution.py
+++ b/solution.py
@@ -22,7 +22,7 @@
 K7 = 7
 FLAT = K7 * N
 WIDE = 768
-GROUPS = ((0, 1), (7, 2), (6, 3), (5, 4))
+GROUPS = ((0, 1), (6, 2), (7, 3), (5, 4))
 SLOTS = [slot for group in GROUPS for slot in group]
 ITEMS = len(SLOTS)
 SPARE = 640
@@ -30,7 +30,7 @@
 NBLOCK = 16
 TILE = 512
 CHUNK_ROWS = (24, 72)
-X_GROUPS = ((2,), (4, 2))
+X_GROUPS = ((2,), (2, 2, 2))
 
 BAND = ("z", "yl")
 COL = ("x", "yh", "co")
@@ -121,6 +121,12 @@
 HBM = pl.BlockSpec(memory_space=pltpu.HBM)
 ANY = pl.BlockSpec(memory_space=pl.ANY)
 SLAB_CUTS = 4
+
+
+def in_hbm(x):
+    return pltpu.with_memory_space_constraint(x, pltpu.HBM)
+
+
 PLANES_FLOPS = (30_000_000, 30_000_000, 30_000_000, 30_000_000)
 
 
@@ -184,7 +190,7 @@
         move.wait()
 
 
-def planes_of(group, v, c, marks=(), through=(), buffer=()):
+def planes_of(group, v, c, marks=(), through=(), after=(), buffer=()):
     slots = GROUPS[group]
     items = len(slots)
     first = max(group - 1, 0) * items * 2 * X6
@@ -197,23 +203,26 @@
         row_table(items),
         *marks,
         *through,
+        *after,
         *buffer,
     )
-    outside = len(through) + len(buffer)
+    outside = len(through) + len(after) + len(buffer)
     return pl.pallas_call(
         functools.partial(
             plane_kernel,
             items=items,
             first=first,
             through=len(through),
-            chained=len(buffer),
+            chained=len(after) + len(buffer),
             marked=len(marks),
         ),
         out_shape=[
             pltpu.HBM((SLABS, rows, WIDE), BF16),
             *(pltpu.HBM(x.shape, x.dtype) for x in through),
         ],
-        in_specs=[VMEM] * (len(inputs) - outside) + [ANY] * len(through) + [HBM] * len(buffer),
+        in_specs=[VMEM] * (len(inputs) - outside)
+        + [ANY] * (len(through) + len(after))
+        + [HBM] * len(buffer),
         out_specs=[HBM] * (1 + len(through)),
         input_output_aliases={len(inputs) - 1: 0} if buffer else {},
         scratch_shapes=[
@@ -243,7 +252,7 @@
         store(lanes, values.sum(axis=1))
         return carry
 
-    lax.fori_loop(0, G_DEV // TILE, body, 0)
+    lax.fori_loop(0, G_DEV // TILE, body, 0, unroll=True)
 
 
 def transform_x(chunk, t_ref, x_refs, low):
@@ -278,9 +287,9 @@
 
 
 def second_far_kernel(
-    t_ref, x0_ref, x1_ref, far_ref, far_kx_ref, first_ref, far_out, low, block_out
+    t_ref, x_ref, far_ref, far_kx_ref, first_ref, far_out, low, block_out
 ):
-    transform_x(1, t_ref, (x0_ref, x1_ref), low)
+    transform_x(1, t_ref, (x_ref,) * len(X_GROUPS[1]), low)
     rows = first_ref.shape[0]
     far_out[:rows, :] = first_ref[...]
 
@@ -332,7 +341,7 @@
             flops=100_000_000, bytes_accessed=100_000, transcendentals=0
         ),
         name="second_far_points",
-    )(planes, *(x_table(items) for items in X_GROUPS[1]), *far, first)
+    )(planes, x_table(X_GROUPS[1][0]), *far, first)
 
 
 def second_own_points(low, own):
@@ -384,19 +393,31 @@
 
 def phase_cosine(phase):
     turns = jnp.floor((phase + 0.5) * (1.0 / N))
-    return jnp.cos((phase - N * turns) * (2.0 * math.pi / N))
+    rest = phase - N * turns
+    angle = (N // 4 - jnp.minimum(rest, N - rest)) * (2.0 * math.pi / N)
+    square = angle * angle
+    series = -1.0 / 39916800.0
+    for factor in (1.0 / 362880.0, -1.0 / 5040.0, 1.0 / 120.0, -1.0 / 6.0, 1.0):
+        series = series * square + factor
+    return angle * series
 
 
 def block_kernel(*refs):
-    waves, refs = refs[:2 + len(SLOTS)], refs[2 + len(SLOTS) :]
-    info_ref, marks_hbm, _, out_hbm, marks_ref, tail_ref, sums_ref, sems = refs
-    waves_v, waves_c = waves[:2], waves[2:]
+    waves_hbm, refs = refs[: 2 + len(SLOTS)], refs[2 + len(SLOTS) :]
+    info_ref, marks_hbm, _, out_hbm, *refs = refs
+    waves_ref, product_ref, marks_ref, tail_ref, sums_ref, wave_sems, sems = refs
+    waves_in = [
+        pltpu.make_async_copy(wave, waves_ref.at[i], wave_sems.at[i])
+        for i, wave in enumerate(waves_hbm)
+    ]
+    place = marks_hbm.at[:, pl.ds(0, 8), pl.ds(SPARE, 128)]
+    marks_in = pltpu.make_async_copy(place, marks_ref, sems.at[1])
+    marks_in.start()
+    for move in waves_in:
+        move.start()
     tail = (slice(None), pl.ds(0, 16), pl.ds(SPARE, 128))
     fetch = pltpu.make_async_copy(out_hbm.at[tail], tail_ref, sems.at[0])
     fetch.start()
-    place = marks_hbm.at[:, pl.ds(0, 8), pl.ds(SPARE, 128)]
-    marks_in = pltpu.make_async_copy(place, marks_ref, sems.at[1])
-    marks_in.start()
     info = info_ref[...]
     marks_in.wait()
     marks = marks_ref[...].astype(F32).sum(axis=0)
@@ -410,16 +431,21 @@
     lane = lax.broadcasted_iota(jnp.int32, (Y6 * N, 128), 0).astype(F32)
     y6 = jnp.floor((lane + 0.5) * (1.0 / N))
     lanes = phase_cosine(16.0 * y6 * block_y + (lane - N * y6) * block_z + info[1:2]).astype(BF16)
-    row = lax.broadcasted_iota(jnp.int32, (X6 * Y16, 128), 0).astype(F32)
+    rows = X6 * Y16
+    row = lax.broadcasted_iota(jnp.int32, (rows, 128), 0).astype(F32)
     x = jnp.floor((row + 0.5) * (1.0 / Y16))
-    rows = phase_cosine((x + info[4:5]) * block_x + (row - Y16 * x) * block_y + info[2:3])
-    rows = rows * info[3:4]
+    turned = phase_cosine((x + info[4:5]) * block_x + (row - Y16 * x) * block_y + info[2:3])
+    turned = turned * info[3:4]
+    for move in waves_in:
+        move.wait()
     for half in range(2):
         for item, slot in enumerate(SLOTS):
-            product = waves_v[half][...] * waves_c[slot][...]
-            sums = jnp.dot(product, lanes, preferred_element_type=F32) * rows
             index = half * len(SLOTS) + item
-            sums_ref[index : index + 1, :] = sums.sum(axis=0, keepdims=True)
+            product_ref[index * rows : (index + 1) * rows, :] = (
+                waves_ref[half] * waves_ref[2 + slot]
+            )
+    sums = jnp.dot(product_ref[...], lanes, preferred_element_type=F32)
+    sums_ref[...] = (sums.reshape(2 * ITEMS, rows, 128) * turned[None]).sum(axis=1)
     sums = sums_ref[...]
     sums = sums + pltpu.roll(sums, 128 - NBLOCK, 1)
     high = sums.astype(BF16).astype(F32)
@@ -435,20 +461,24 @@
 
 
 def with_block_sums(v, c, info, arrived, planes):
-    inputs = (*v, *c, info, arrived, planes)
+    waves = [in_hbm(wave) for wave in (*v, *c)]
+    inputs = (*waves, info, arrived, planes)
     return pl.pallas_call(
         block_kernel,
         out_shape=pltpu.HBM(planes.shape, planes.dtype),
-        in_specs=[VMEM] * (len(inputs) - 2) + [ANY, HBM],
+        in_specs=[HBM] * len(waves) + [VMEM, ANY, HBM],
         out_specs=HBM,
         input_output_aliases={len(inputs) - 1: 0},
         scratch_shapes=[
+            pltpu.VMEM((len(waves), X6 * Y16, Y6 * N), BF16),
+            pltpu.VMEM((2 * ITEMS * X6 * Y16, Y6 * N), BF16),
             pltpu.VMEM((SLABS, 8, 128), BF16),
             pltpu.VMEM((SLABS, 16, 128), BF16),
-            pltpu.VMEM((16, 128), F32),
+            pltpu.VMEM((2 * ITEMS, 128), F32),
+            pltpu.SemaphoreType.DMA((len(waves),)),
             pltpu.SemaphoreType.DMA((3,)),
         ],
-        compiler_params=pltpu.CompilerParams(vmem_limit_bytes=6 << 20),
+        compiler_params=pltpu.CompilerParams(vmem_limit_bytes=10 << 20),
         cost_estimate=pl.CostEstimate(
             flops=10_000_000, bytes_accessed=100_000, transcendentals=0
         ),
@@ -502,7 +532,9 @@
     spots = jnp.arange(128, dtype=jnp.int32)
     cell = jnp.where((spots % NBLOCK == col) & (spots >= 32), block_cell[0], 0)
     marks = jnp.concatenate([jnp.stack([cell // 256, cell % 256]), jnp.zeros((6, 128), jnp.int32)])
-    planes0, far_cell = planes_of(0, v, c, marks=(marks.astype(F32),), through=(far_cell,))
+    planes0, far_cell = planes_of(
+        0, v, c, marks=(marks.astype(F32),), through=(far_cell,), after=(c[7],)
+    )
     sent0 = lax.all_to_all(planes0, COL, 0, 0, tiled=True)
     (planes1,) = planes_of(1, v, c)
     (planes1,) = planes_of(2, v, c, buffer=(planes1,))

time: 118 us -> 112 us (0.949)
  Pallas kernels: 30.6 us -> 26.3 us
  local copies, waits for them, and re-layouts: 9.27 us -> 5.37 us
  waiting for transfers between devices: 38.3 us -> 39.9 us
    unnamed x46 -> x52, local copies, waits for them, and re-layouts: 6.32 us -> 2.42 us
    ppermute x3, starting transfers between devices: 9.2 us -> 12.9 us  [per_device(): c[8 - slot] = lax.ppermute(c[(9 - slot) % 8], 'z', behind)]
    ppermute x4, starting transfers between devices: 2.16 us -> 0.01 us  [per_device(): c[slot] = lax.ppermute(c[slot - 1], 'z', ahead)]
  transfers between devices with their start and end apart: 13 -> 13, of which waited for: 6 -> 7; matrix products, arithmetic and copies ran while one was open for 2% -> 2% of each run, Pallas kernels for 17% -> 15%
where the time goes in v8:
time: 112 us; the launch traced here: 111 us
  waiting for transfers between devices  39.9 us (36%)
  starting transfers between devices  37.1 us (33%)
  Pallas kernels  26.3 us (23%)
  local copies, waits for them, and re-layouts  5.37 us (5%)
    all_to_all x1, waiting for transfers between devices, per_device(): sent1 = lax.all_to_all(planes1, COL, 0, 0, tiled=True)  19.5 us
    ppermute x3, starting transfers between devices, per_device(): c[8 - slot] = lax.ppermute(c[(9 - slot) % 8], 'z', behind)  12.9 us
    all_to_all x1, waiting for transfers between devices, per_device(): pairs = lax.all_to_all(pairs, BAND, 0, 0, tiled=True)  11.3 us
    pallas_call x4, Pallas kernels, planes_of(): pl.pallas_call(functools.partial(plane_kernel, items=items, first=first,...  9.45 us
    all_to_all x1, starting transfers between devices, per_device(): sent1 = lax.all_to_all(planes1, COL, 0, 0, tiled=True)  7.37 us
    all_to_all x1, starting transfers between devices, per_device(): sent0 = lax.all_to_all(planes0, COL, 0, 0, tiled=True)  6.87 us
    pallas_call x1, Pallas kernels, second_far_points(): pl.pallas_call(second_far_kernel, out_shape=(jax.ShapeDtypeStruct((FIRST...  4.88 us
    pallas_call x1, Pallas kernels, second_own_points(): pl.pallas_call(second_own_kernel, out_shape=jax.ShapeDtypeStruct((SECOND,...  3.99 us
  transfers between devices with their start and end apart: 13, of which 7 were waited for; matrix products, arithmetic and copies ran while one was open for 2% of the time, Pallas kernels for 15%

profile of v8, /device:TPU:6, one launch (start us, length us, event | category | flops | bytes accessed | tf_op | source)
XLA Modules:
  0.0 110.5 jit_solution(8534799175294590294)
XLA Ops:
  0.0 1.2 %reshape.316 = bf16[6,6,16,96]{3,2,1,0:T(8,128)(2,1)S(1)} reshape(bf16[1,6,9216]{2,1,0:T(8,128)(2,1)} %param.18) | data formatting | bytes 221184 | tf_op jit(solution)/shard_map/reshape | solution.py:505
  1.5 5.9 %collective-permute-start.3 = (bf16[96,576]{1,0:T(8,128)(2,1)S(1)}, bf16[96,576]{1,0:T(8,128)(2,1)S(1)}, u32[]{:S(2)}, u32[]{:S(2)}) collective-permute-start(bf16[96,576]{1,0:T(8,128)(2,1)S(1)} %reshape.317.refs_2_), channel_id=1, source_target_pairs={{0,224},{32,0},{64,32},{96,64},{128,96},{160,128},{192,160},{224,1... | collective-permute-start | bytes 331784 | tf_op jit(solution)/shard_map/ppermute | solution.py:528
  7.4 1.1 reshape.314
  8.7 1.7 %collective-permute-start = (bf16[96,576]{1,0:T(8,128)(2,1)S(1)}, bf16[96,576]{1,0:T(8,128)(2,1)S(1)}, u32[]{:S(2)}, u32[]{:S(2)}) collective-permute-start(bf16[96,576]{1,0:T(8,128)(2,1)S(1)} %reshape.315.refs_0_), channel_id=1, source_target_pairs={{0,16},{16,0},{1,17},{17,1},{2,18},{18,2},{3,19},{19,3},{4,20},{20... | collective-permute-start | bytes 331784 | tf_op jit(solution)/shard_map/ppermute | solution.py:523
  10.4 1.7 %collective-permute-start.2 = (s32[2048]{0:T(1024)S(1)}, s32[2048]{0:T(1024)S(1)}, u32[]{:S(2)}, u32[]{:S(2)}) collective-permute-start(s32[2048]{0:T(1024)S(1)} %copy-done.18), channel_id=1, source_target_pairs={{0,15},{1,14},{2,13},{3,12},{4,11},{5,10},{6,9},{7,8},{8,7},{9,6},... | collective-permute-start | bytes 24584 | tf_op jit(solution)/shard_map/ppermute | solution.py:531
  12.8 0.7 collective-permute-done.1.refs_3_
  13.6 3.5 %collective-permute-done.2 = s32[2048]{0:T(1024)S(1)} collective-permute-done((s32[2048]{0:T(1024)S(1)}, s32[2048]{0:T(1024)S(1)}, u32[]{:S(2)}, u32[]{:S(2)}) %collective-permute-start.2) | collective-permute-done | bytes 8224 | tf_op jit(solution)/shard_map/ppermute | solution.py:531
  17.1 1.0 copy-done.1
  18.2 2.4 %planes.4 = (bf16[16,24,768]{2,1,0:T(8,128)(2,1)}, s32[16,128]{1,0:T(8,128)}) custom-call(bf16[96,576]{1,0:T(8,128)(2,1)S(1)} %reshape.315.refs_0_, bf16[96,576]{1,0:T(8,128)(2,1)S(1)} %collective-permute-done.refs_1_, bf16[96,576]{1,0:T(8,128)(2,1)S(1)} %reshape.317.refs_2_, bf16[96,576]{1,0:T(8,128)(2,1)S(1)} %collective-permute-done.1.refs_3_, ...), custom_call_target="tpu_custom_call" | custom-call | flops 60000000 | bytes 100000 | tf_op jit(solution)/shard_map/planes/pallas_call | solution.py:210
  20.6 6.9 %all-to-all-start = ((bf16[16,24,768]{2,1,0:T(8,128)(2,1)}), bf16[16,24,768]{2,1,0:T(8,128)(2,1)S(1)}, u32[]{:S(2)}, u32[]{:S(2)}) async-start(bf16[16,24,768]{2,1,0:T(8,128)(2,1)} %get-tuple-element.12), calls=%async_computation | async-start | bytes 1179648 | tf_op jit(solution)/shard_map/all_to_all | solution.py:538
  27.4 3.2 %collective-permute-start.7 = (bf16[96,576]{1,0:T(8,128)(2,1)S(1)}, bf16[96,576]{1,0:T(8,128)(2,1)S(1)}, u32[]{:S(2)}, u32[]{:S(2)}) collective-permute-start(bf16[96,576]{1,0:T(8,128)(2,1)S(1)} %collective-permute-done.3.refs_9_.refs_2_), channel_id=1, source_target_pairs={{0,224},{32,0},{64,32},{96,64},{128,96},{160,128},{192,160},{224,1... | collective-permute-start | bytes 331784 | tf_op jit(solution)/shard_map/ppermute | solution.py:528
  30.7 2.9 %collective-permute-done.7.refs_2_.refs_8_ = bf16[96,576]{1,0:T(8,128)(2,1)S(1)} collective-permute-done((bf16[96,576]{1,0:T(8,128)(2,1)S(1)}, bf16[96,576]{1,0:T(8,128)(2,1)S(1)}, u32[]{:S(2)}, u32[]{:S(2)}) %collective-permute-start.7) | collective-permute-done | bytes 110624 | tf_op jit(solution)/shard_map/ppermute | solution.py:528
  33.6 3.7 %collective-permute-start.8 = (bf16[96,576]{1,0:T(8,128)(2,1)S(1)}, bf16[96,576]{1,0:T(8,128)(2,1)S(1)}, u32[]{:S(2)}, u32[]{:S(2)}) collective-permute-start(bf16[96,576]{1,0:T(8,128)(2,1)S(1)} %collective-permute-done.7.refs_2_.refs_8_), channel_id=1, source_target_pairs={{0,224},{32,0},{64,32},{96,64},{128,96},{160,128},{192,160},{224,1... | collective-permute-start | bytes 331784 | tf_op jit(solution)/shard_map/ppermute | solution.py:528
  37.4 2.4 %planes.5.refs_7_ = bf16[16,72,768]{2,1,0:T(8,128)(2,1)} custom-call(bf16[96,576]{1,0:T(8,128)(2,1)S(1)} %reshape.315.refs_0_, bf16[96,576]{1,0:T(8,128)(2,1)S(1)} %collective-permute-done.refs_1_, bf16[96,576]{1,0:T(8,128)(2,1)S(1)} %collective-permute-done.7.refs_2_.refs_8_, bf16[96,576]{1,0:T(8,128)(2,1)S(1)} %collective-permute-done.4.refs_3_.refs_4_, ...), custom_call_target="tpu_custom_call" | custom-call | flops 60000000 | bytes 100000 | tf_op jit(solution)/shard_map/planes/pallas_call | solution.py:210
  39.8 2.4 %planes.6.refs_7_ = bf16[16,72,768]{2,1,0:T(8,128)(2,1)} custom-call(bf16[96,576]{1,0:T(8,128)(2,1)S(1)} %reshape.315.refs_0_, bf16[96,576]{1,0:T(8,128)(2,1)S(1)} %collective-permute-done.refs_1_, bf16[96,576]{1,0:T(8,128)(2,1)S(1)} %collective-permute-done.3.refs_9_.refs_2_, ...), custom_call_target="tpu_custom_call", output_to_operand_aliasing={{}: (7, {})} | custom-call | flops 60000000 | bytes 100000 | tf_op jit(solution)/shard_map/planes/pallas_call | solution.py:210
  42.2 1.2 %collective-permute-done.6.refs_3_.refs_6_ = bf16[96,576]{1,0:T(8,128)(2,1)S(1)} collective-permute-done((bf16[96,576]{1,0:T(8,128)(2,1)S(1)}, bf16[96,576]{1,0:T(8,128)(2,1)S(1)}, u32[]{:S(2)}, u32[]{:S(2)}) %collective-permute-start.6) | collective-permute-done | bytes 110624 | tf_op jit(solution)/shard_map/ppermute | solution.py:526
  43.4 2.3 %planes.7.refs_12_ = bf16[16,72,768]{2,1,0:T(8,128)(2,1)} custom-call(bf16[96,576]{1,0:T(8,128)(2,1)S(1)} %reshape.315.refs_0_, bf16[96,576]{1,0:T(8,128)(2,1)S(1)} %collective-permute-done.refs_1_, bf16[96,576]{1,0:T(8,128)(2,1)S(1)} %collective-permute-done.8.refs_2_.refs_7_, ...), custom_call_target="tpu_custom_call", output_to_operand_aliasing={{}: (7, {})} | custom-call | flops 60000000 | bytes 100000 | tf_op jit(solution)/shard_map/planes/pallas_call | solution.py:210
  45.7 0.6 copy-done.13
  46.4 0.7 copy-done.14
  47.0 3.0 %block.1 = bf16[16,72,768]{2,1,0:T(8,128)(2,1)} custom-call(bf16[96,576]{1,0:T(8,128)(2,1)} %copy-done.3, bf16[96,576]{1,0:T(8,128)(2,1)} %copy-done.4, bf16[96,576]{1,0:T(8,128)(2,1)} %copy-done.7, bf16[96,576]{1,0:T(8,128)(2,1)} %copy-done.9, bf16[96,576]{1,0:T(8,128)(2,1)} %copy-done.10, ...), custom_call_target="tpu_custom_call", output_to_operand_aliasing={{}: (12, {})} | custom-call | flops 10000000 | bytes 100000 | tf_op jit(solution)/shard_map/block/pallas_call | solution.py:466
  50.1 7.4 %all-to-all-start.1 = ((bf16[16,72,768]{2,1,0:T(8,128)(2,1)}), bf16[16,72,768]{2,1,0:T(8,128)(2,1)S(1)}, u32[]{:S(2)}, u32[]{:S(2)}) async-start(bf16[16,72,768]{2,1,0:T(8,128)(2,1)} %block.1), calls=%async_computation.1 | async-start | bytes 3538944 | tf_op jit(solution)/shard_map/all_to_all | solution.py:552
  57.6 0.2 select_reduce_fusion
  58.2 3.3 %first_points.1 = (f32[4,2048]{1,0:T(4,128)S(1)}, bf16[4,2048]{1,0:T(4,128)(2,1)S(1)}) custom-call(bf16[16,24,768]{2,1,0:T(8,128)(2,1)S(1)} %all-to-all-done.t_ref.refs_11_, bf16[384,384]{1,0:T(8,128)(2,1)S(1)} %copy-done.6, s32[1,2048]{1,0:T(1,128)S(1)} %bitcast.39, s32[1,2048]{1,0:T(1,128)S(1)} %bitcast.37, s32[1,2048]{1,0:T(1,128)S(1)} %get-tuple-element.29.far_ref, ...), custom_call_target="tpu_custom_call" | custom-call | flops 100000000 | bytes 100000 | tf_op jit(solution)/shard_map/first_points/pallas_call | solution.py:316
  61.5 19.5 %all-to-all-done.1.t_ref = bf16[16,72,768]{2,1,0:T(8,128)(2,1)S(1)} async-done(((bf16[16,72,768]{2,1,0:T(8,128)(2,1)}), bf16[16,72,768]{2,1,0:T(8,128)(2,1)S(1)}, u32[]{:S(2)}, u32[]{:S(2)}) %all-to-all-start.1) | async-done | bytes 1769504 | tf_op jit(solution)/shard_map/all_to_all | solution.py:552
  81.0 4.9 %second_far_points.1 = (bf16[16,2048]{1,0:T(8,128)(2,1)S(1)}, bf16[1152,768]{1,0:T(8,128)(2,1)S(1)}, f32[16,128]{1,0:T(8,128)S(1)}) custom-call(bf16[16,72,768]{2,1,0:T(8,128)(2,1)S(1)} %all-to-all-done.1.t_ref, bf16[384,384]{1,0:T(8,128)(2,1)S(1)} %copy-done.6, s32[1,2048]{1,0:T(1,128)S(1)} %get-tuple-element.29.far_ref, ...), custom_call_target="tpu_custom_call" | custom-call | flops 100000000 | bytes 100000 | tf_op jit(solution)/shard_map/second_far_points/pallas_call | solution.py:332
  85.9 3.0 %collective-permute-start.9 = (bf16[16,2048]{1,0:T(8,128)(2,1)S(1)}, bf16[16,2048]{1,0:T(8,128)(2,1)S(1)}, u32[]{:S(2)}, u32[]{:S(2)}) collective-permute-start(bf16[16,2048]{1,0:T(8,128)(2,1)S(1)} %get-tuple-element.17), channel_id=1, source_target_pairs={{0,15},{1,14},{2,13},{3,12},{4,11},{5,10},{6,9},{7,8},{8,7},{9,6},... | collective-permute-start | bytes 196616 | tf_op jit(solution)/shard_map/ppermute | solution.py:579
  88.9 4.0 %second_own_points.1.own1_ref = f32[12,2048]{1,0:T(8,128)S(1)} custom-call(bf16[1152,768]{1,0:T(8,128)(2,1)S(1)} %get-tuple-element.16.low, s32[1,2048]{1,0:T(1,128)S(1)} %bitcast.40, s32[1,2048]{1,0:T(1,128)S(1)} %bitcast.38), custom_call_target="tpu_custom_call" | custom-call | flops 2400000000 | bytes 1300000 | tf_op jit(solution)/shard_map/second_own_points/pallas_call | solution.py:348
  92.9 0.9 collective-permute-done.9.far_ref
  93.8 0.8 split.1
  94.6 3.5 %all-to-all-start.2 = ((bf16[16,48,128]{2,1,0:T(8,128)(2,1)}), bf16[16,48,128]{2,1,0:T(8,128)(2,1)S(1)}, u32[]{:S(2)}, u32[]{:S(2)}) async-start(bf16[16,48,128]{2,1,0:T(8,128)(2,1)} %split.1), calls=%async_computation.2 | async-start | bytes 393216 | tf_op jit(solution)/shard_map/all_to_all | solution.py:582
  98.2 11.3 %all-to-all-done.2.pairs_ref = bf16[16,48,128]{2,1,0:T(8,128)(2,1)S(1)} async-done(((bf16[16,48,128]{2,1,0:T(8,128)(2,1)}), bf16[16,48,128]{2,1,0:T(8,128)(2,1)S(1)}, u32[]{:S(2)}, u32[]{:S(2)}) %all-to-all-start.2) | async-done | bytes 196640 | tf_op jit(solution)/shard_map/all_to_all | solution.py:582
  109.5 1.0 pair_sum.1
  (79 shorter events, 1.4 us)
Async XLA Ops:
  0.0 17.1 %copy-start = (bf16[576,1536]{1,0:T(8,128)(2,1)S(1)}, bf16[576,1536]{1,0:T(8,128)(2,1)}, u32[]{:S(2)}) copy-start(bf16[576,1536]{1,0:T(8,128)(2,1)} %constant.131.clone.refs_4_) | copy-start | bytes 5308420
  0.0 17.1 %copy-start.5 = (f32[2,16,768]{2,1,0:T(8,128)S(1)}, f32[2,16,768]{2,1,0:T(8,128)}, u32[]{:S(2)}) copy-start(f32[2,16,768]{2,1,0:T(8,128)} %constant.132.clone.refs_5_) | copy-start | bytes 294916
  0.0 10.4 %copy-start.18 = (s32[2048]{0:T(1024)S(1)}, s32[2048]{0:T(1024)}, u32[]{:S(2)}) copy-start(s32[2048]{0:T(1024)} %param.23) | copy-start | bytes 24580
  1.5 19.1 %copy-start.7 = (bf16[96,576]{1,0:T(8,128)(2,1)}, bf16[96,576]{1,0:T(8,128)(2,1)S(1)}, u32[]{:S(2)}) copy-start(bf16[96,576]{1,0:T(8,128)(2,1)S(1)} %reshape.317.refs_2_) | copy-start | bytes 331780
  1.5 15.6 %collective-permute-start.3 = (bf16[96,576]{1,0:T(8,128)(2,1)S(1)}, bf16[96,576]{1,0:T(8,128)(2,1)S(1)}, u32[]{:S(2)}, u32[]{:S(2)}) collective-permute-start(bf16[96,576]{1,0:T(8,128)(2,1)S(1)} %reshape.317.refs_2_), channel_id=1, source_target_pairs={{0,224},{32,0},{64,32},{96,64},{128,96},{160,128},{192,160},{224,1... | collective-permute-start | bytes 331784 | tf_op jit(solution)/shard_map/ppermute | solution.py:528
  7.4 6.1 %collective-permute-start.1 = (bf16[96,576]{1,0:T(8,128)(2,1)S(1)}, bf16[96,576]{1,0:T(8,128)(2,1)S(1)}, u32[]{:S(2)}, u32[]{:S(2)}) collective-permute-start(bf16[96,576]{1,0:T(8,128)(2,1)S(1)} %reshape.317.refs_2_), channel_id=1, source_target_pairs={{0,32},{32,64},{64,96},{96,128},{128,160},{160,192},{192,224},{224... | collective-permute-start | bytes 331784 | tf_op jit(solution)/shard_map/ppermute | solution.py:526
  8.7 34.6 %copy-start.3 = (bf16[96,576]{1,0:T(8,128)(2,1)}, bf16[96,576]{1,0:T(8,128)(2,1)S(1)}, u32[]{:S(2)}) copy-start(bf16[96,576]{1,0:T(8,128)(2,1)S(1)} %reshape.315.refs_0_) | copy-start | bytes 331780
  8.7 8.4 %collective-permute-start = (bf16[96,576]{1,0:T(8,128)(2,1)S(1)}, bf16[96,576]{1,0:T(8,128)(2,1)S(1)}, u32[]{:S(2)}, u32[]{:S(2)}) collective-permute-start(bf16[96,576]{1,0:T(8,128)(2,1)S(1)} %reshape.315.refs_0_), channel_id=1, source_target_pairs={{0,16},{16,0},{1,17},{17,1},{2,18},{18,2},{3,19},{19,3},{4,20},{20... | collective-permute-start | bytes 331784 | tf_op jit(solution)/shard_map/ppermute | solution.py:523
  10.4 6.7 %collective-permute-start.2 = (s32[2048]{0:T(1024)S(1)}, s32[2048]{0:T(1024)S(1)}, u32[]{:S(2)}, u32[]{:S(2)}) collective-permute-start(s32[2048]{0:T(1024)S(1)} %copy-done.18), channel_id=1, source_target_pairs={{0,15},{1,14},{2,13},{3,12},{4,11},{5,10},{6,9},{7,8},{8,7},{9,6},... | collective-permute-start | bytes 24584 | tf_op jit(solution)/shard_map/ppermute | solution.py:531
  13.5 17.2 %collective-permute-start.4 = (bf16[96,576]{1,0:T(8,128)(2,1)S(1)}, bf16[96,576]{1,0:T(8,128)(2,1)S(1)}, u32[]{:S(2)}, u32[]{:S(2)}) collective-permute-start(bf16[96,576]{1,0:T(8,128)(2,1)S(1)} %collective-permute-done.1.refs_3_), channel_id=1, source_target_pairs={{0,32},{32,64},{64,96},{96,128},{128,160},{160,192},{192,224},{224... | collective-permute-start | bytes 331784 | tf_op jit(solution)/shard_map/ppermute | solution.py:526
  17.1 26.3 %copy-start.4 = (bf16[96,576]{1,0:T(8,128)(2,1)}, bf16[96,576]{1,0:T(8,128)(2,1)S(1)}, u32[]{:S(2)}) copy-start(bf16[96,576]{1,0:T(8,128)(2,1)S(1)} %collective-permute-done.refs_1_) | copy-start | bytes 331780
  17.1 22.6 %copy-start.8 = (bf16[96,576]{1,0:T(8,128)(2,1)}, bf16[96,576]{1,0:T(8,128)(2,1)S(1)}, u32[]{:S(2)}) copy-start(bf16[96,576]{1,0:T(8,128)(2,1)S(1)} %collective-permute-done.3.refs_9_.refs_2_) | copy-start | bytes 331780
  18.2 12.5 %copy-start.25 = (pred[8,1]{0,1:T(4,128)(4,1)S(1)}, pred[8,1]{0,1:T(4,128)(4,1)}, u32[]{:S(2)}) copy-start(pred[8,1]{0,1:T(4,128)(4,1)} %constant.134.clone) | copy-start | bytes 28
  18.2 19.1 %copy-start.19 = (f32[8,128]{1,0:T(8,128)S(1)}, f32[8,128]{1,0:T(8,128)}, u32[]{:S(2)}) copy-start(f32[8,128]{1,0:T(8,128)} %constant.135.clone) | copy-start | bytes 12292
  18.2 19.2 %copy-start.2 = (bf16[384,384]{1,0:T(8,128)(2,1)S(1)}, bf16[384,384]{1,0:T(8,128)(2,1)}, u32[]{:S(2)}) copy-start(bf16[384,384]{1,0:T(8,128)(2,1)} %constant.133.clone.refs_6_) | copy-start | bytes 884740
  20.6 26.5 %all-to-all-start = ((bf16[16,24,768]{2,1,0:T(8,128)(2,1)}), bf16[16,24,768]{2,1,0:T(8,128)(2,1)S(1)}, u32[]{:S(2)}, u32[]{:S(2)}) async-start(bf16[16,24,768]{2,1,0:T(8,128)(2,1)} %get-tuple-element.12), calls=%async_computation | async-start | bytes 1179648 | tf_op jit(solution)/shard_map/all_to_all | solution.py:538
  27.4 6.1 %collective-permute-start.7 = (bf16[96,576]{1,0:T(8,128)(2,1)S(1)}, bf16[96,576]{1,0:T(8,128)(2,1)S(1)}, u32[]{:S(2)}, u32[]{:S(2)}) collective-permute-start(bf16[96,576]{1,0:T(8,128)(2,1)S(1)} %collective-permute-done.3.refs_9_.refs_2_), channel_id=1, source_target_pairs={{0,224},{32,0},{64,32},{96,64},{128,96},{160,128},{192,160},{224,1... | collective-permute-start | bytes 331784 | tf_op jit(solution)/shard_map/ppermute | solution.py:528
  30.7 9.1 %copy-start.10 = (bf16[96,576]{1,0:T(8,128)(2,1)}, bf16[96,576]{1,0:T(8,128)(2,1)S(1)}, u32[]{:S(2)}) copy-start(bf16[96,576]{1,0:T(8,128)(2,1)S(1)} %collective-permute-done.4.refs_3_.refs_4_) | copy-start | bytes 331780
  30.7 6.6 %collective-permute-start.5 = (bf16[96,576]{1,0:T(8,128)(2,1)S(1)}, bf16[96,576]{1,0:T(8,128)(2,1)S(1)}, u32[]{:S(2)}, u32[]{:S(2)}) collective-permute-start(bf16[96,576]{1,0:T(8,128)(2,1)S(1)} %collective-permute-done.4.refs_3_.refs_4_), channel_id=1, source_target_pairs={{0,32},{32,64},{64,96},{96,128},{128,160},{160,192},{192,224},{224... | collective-permute-start | bytes 331784 | tf_op jit(solution)/shard_map/ppermute | solution.py:526
  33.6 8.6 %collective-permute-start.8 = (bf16[96,576]{1,0:T(8,128)(2,1)S(1)}, bf16[96,576]{1,0:T(8,128)(2,1)S(1)}, u32[]{:S(2)}, u32[]{:S(2)}) collective-permute-start(bf16[96,576]{1,0:T(8,128)(2,1)S(1)} %collective-permute-done.7.refs_2_.refs_8_), channel_id=1, source_target_pairs={{0,224},{32,0},{64,32},{96,64},{128,96},{160,128},{192,160},{224,1... | collective-permute-start | bytes 331784 | tf_op jit(solution)/shard_map/ppermute | solution.py:528
  37.3 6.1 %collective-permute-start.6 = (bf16[96,576]{1,0:T(8,128)(2,1)S(1)}, bf16[96,576]{1,0:T(8,128)(2,1)S(1)}, u32[]{:S(2)}, u32[]{:S(2)}) collective-permute-start(bf16[96,576]{1,0:T(8,128)(2,1)S(1)} %collective-permute-done.5.refs_3_.refs_5_), channel_id=1, source_target_pairs={{0,32},{32,64},{64,96},{96,128},{128,160},{160,192},{192,224},{224... | collective-permute-start | bytes 331784 | tf_op jit(solution)/shard_map/ppermute | solution.py:526
  50.0 7.6 %copy-start.17 = (f32[4096]{0:T(1024)S(1)}, f32[4096]{0:T(1024)}, u32[]{:S(2)}) copy-start(f32[4096]{0:T(1024)} %param.20) | copy-start | bytes 49156
  50.0 7.6 %copy-start.22 = (s32[16]{0:T(128)S(1)}, s32[16]{0:T(128)}, u32[]{:S(2)}) copy-start(s32[16]{0:T(128)} %param.19) | copy-start | bytes 196
  50.0 7.8 %copy-start.20 = (pred[256,16]{0,1:T(8,128)(4,1)S(1)}, pred[256,16]{0,1:T(8,128)(4,1)}, u32[]{:S(2)}) copy-start(pred[256,16]{0,1:T(8,128)(4,1)} %constant.136.clone) | copy-start | bytes 12292
  50.0 7.8 %copy-start.21 = (pred[256,16]{0,1:T(8,128)(4,1)S(1)}, pred[256,16]{0,1:T(8,128)(4,1)}, u32[]{:S(2)}) copy-start(pred[256,16]{0,1:T(8,128)(4,1)} %constant.137.clone) | copy-start | bytes 12292
  50.1 7.8 %copy-start.23 = (f32[16]{0:T(128)S(1)}, f32[16]{0:T(128)}, u32[]{:S(2)}) copy-start(f32[16]{0:T(128)} %param.21) | copy-start | bytes 196
  50.1 7.9 %copy-start.16 = (s32[16,128]{1,0:T(8,128)S(1)}, s32[16,128]{1,0:T(8,128)}, u32[]{:S(2)}) copy-start(s32[16,128]{1,0:T(8,128)} %get-tuple-element.13) | copy-start | bytes 24580
  50.1 8.1 %copy-start.6 = (bf16[384,384]{1,0:T(8,128)(2,1)S(1)}, bf16[384,384]{1,0:T(8,128)(2,1)}, u32[]{:S(2)}) copy-start(bf16[384,384]{1,0:T(8,128)(2,1)} %constant.138.clone.x_ref) | copy-start | bytes 884740
  50.1 30.9 %all-to-all-start.1 = ((bf16[16,72,768]{2,1,0:T(8,128)(2,1)}), bf16[16,72,768]{2,1,0:T(8,128)(2,1)S(1)}, u32[]{:S(2)}, u32[]{:S(2)}) async-start(bf16[16,72,768]{2,1,0:T(8,128)(2,1)} %block.1), calls=%async_computation.1 | async-start | bytes 3538944 | tf_op jit(solution)/shard_map/all_to_all | solution.py:552
  85.9 7.9 %collective-permute-start.9 = (bf16[16,2048]{1,0:T(8,128)(2,1)S(1)}, bf16[16,2048]{1,0:T(8,128)(2,1)S(1)}, u32[]{:S(2)}, u32[]{:S(2)}) collective-permute-start(bf16[16,2048]{1,0:T(8,128)(2,1)S(1)} %get-tuple-element.17), channel_id=1, source_target_pairs={{0,15},{1,14},{2,13},{3,12},{4,11},{5,10},{6,9},{7,8},{8,7},{9,6},... | collective-permute-start | bytes 196616 | tf_op jit(solution)/shard_map/ppermute | solution.py:579
  88.9 20.6 %copy-start.15 = (bf16[2,128,128]{2,1,0:T(8,128)(2,1)S(1)}, bf16[2,128,128]{2,1,0:T(8,128)(2,1)}, u32[]{:S(2)}) copy-start(bf16[2,128,128]{2,1,0:T(8,128)(2,1)} %constant.139.clone.column_ref) | copy-start | bytes 196612
  94.6 15.0 %all-to-all-start.2 = ((bf16[16,48,128]{2,1,0:T(8,128)(2,1)}), bf16[16,48,128]{2,1,0:T(8,128)(2,1)S(1)}, u32[]{:S(2)}, u32[]{:S(2)}) async-start(bf16[16,48,128]{2,1,0:T(8,128)(2,1)} %split.1), calls=%async_computation.2 | async-start | bytes 393216 | tf_op jit(solution)/shard_map/all_to_all | solution.py:582
  (7 other events, 25.5 us)

commit v9 on v8

--- a/solution.py
+++ b/solution.py
@@ -130,18 +130,28 @@
 PLANES_FLOPS = (30_000_000, 30_000_000, 30_000_000, 30_000_000)
 
 
-def plane_kernel(*refs, items, first, through, chained, marked):
+def whole_wave(arrived, slot):
+    if slot == 4:
+        half = X6 * Y16 // 2
+        return jnp.concatenate([arrived[4][:half, :], arrived[8][half:, :]], axis=0)
+    return arrived[slot][...]
+
+
+def plane_kernel(*refs, slots, items, first, through, chained, marked):
     refs = list(refs)
     take = lambda count: [refs.pop(0) for _ in range(count)]
     v0_ref, v1_ref = take(2)
-    waves_c = take(items)
-    lane_ref, twiddle_ref, row_ref = take(3)
+    waves_c = take(len(slots))
+    lane_ref, twiddle_ref = take(2)
     marks = take(marked)
+    (row_hbm,) = take(1)
     kept = take(through)
     take(chained)
     (out_ref,) = take(1)
     kept_out = take(through)
-    low_ref, slab_ref, slab_sems, keep_sems = refs
+    low_ref, slab_ref, row_ref, slab_sems, keep_sems, row_sem = refs
+    row_in = pltpu.make_async_copy(row_hbm, row_ref, row_sem)
+    row_in.start()
     moves = [
         pltpu.make_async_copy(source, target, keep_sems.at[i])
         for i, (source, target) in enumerate(zip(kept, kept_out))
@@ -151,8 +161,9 @@
     rows = X6 * Y16
     twiddle_c = twiddle_ref[0][None]
     twiddle_s = twiddle_ref[1][None]
-    for index, c_ref in enumerate(waves_c):
-        wave_c = c_ref[...]
+    arrived = dict(zip(slots, waves_c))
+    for index, slot in enumerate(slots[:items]):
+        wave_c = whole_wave(arrived, slot)
         pairs = jnp.concatenate([v0_ref[...] * wave_c, v1_ref[...] * wave_c], axis=0)
         moved = jnp.dot(pairs, lane_ref[...], preferred_element_type=F32)
         real = moved[:rows, :WIDE] - moved[rows:, WIDE:]
@@ -164,6 +175,7 @@
         low_ref[index * rows : (index + 1) * rows, :] = turned_r.reshape(rows, WIDE).astype(BF16)
         index += items
         low_ref[index * rows : (index + 1) * rows, :] = turned_i.reshape(rows, WIDE).astype(BF16)
+    row_in.wait()
     count = SLABS // SLAB_CUTS
     size = items * 2 * X6
     for part in range(SLAB_CUTS):
@@ -193,6 +205,7 @@
 def planes_of(group, v, c, marks=(), through=(), after=(), buffer=()):
     slots = GROUPS[group]
     items = len(slots)
+    slots = slots + (8,) if 4 in slots else slots
     first = max(group - 1, 0) * items * 2 * X6
     rows = CHUNK_ROWS[min(group, 1)]
     inputs = (
@@ -200,8 +213,8 @@
         *(c[slot] for slot in slots),
         lane_table(),
         twiddle_table(),
-        row_table(items),
         *marks,
+        in_hbm(jnp.asarray(row_table(items))),
         *through,
         *after,
         *buffer,
@@ -210,6 +223,7 @@
     return pl.pallas_call(
         functools.partial(
             plane_kernel,
+            slots=slots,
             items=items,
             first=first,
             through=len(through),
@@ -228,8 +242,10 @@
         scratch_shapes=[
             pltpu.VMEM((2 * items * X6 * Y16, WIDE), BF16),
             pltpu.VMEM((SLABS, items * 2 * X6, WIDE), BF16),
+            pltpu.VMEM((SLABS * items * 2 * X6, 2 * items * X6 * Y16), BF16),
             pltpu.SemaphoreType.DMA((SLAB_CUTS,)),
             pltpu.SemaphoreType.DMA((max(len(through), 1),)),
+            pltpu.SemaphoreType.DMA,
         ],
         compiler_params=pltpu.CompilerParams(vmem_limit_bytes=16 << 20),
         cost_estimate=pl.CostEstimate(
@@ -403,7 +419,7 @@
 
 
 def block_kernel(*refs):
-    waves_hbm, refs = refs[: 2 + len(SLOTS)], refs[2 + len(SLOTS) :]
+    waves_hbm, refs = refs[:11], refs[11:]
     info_ref, marks_hbm, _, out_hbm, *refs = refs
     waves_ref, product_ref, marks_ref, tail_ref, sums_ref, wave_sems, sems = refs
     waves_in = [
@@ -438,11 +454,12 @@
     turned = turned * info[3:4]
     for move in waves_in:
         move.wait()
+    arrived = {slot: waves_ref.at[2 + slot] for slot in range(9)}
     for half in range(2):
         for item, slot in enumerate(SLOTS):
             index = half * len(SLOTS) + item
-            product_ref[index * rows : (index + 1) * rows, :] = (
-                waves_ref[half] * waves_ref[2 + slot]
+            product_ref[index * rows : (index + 1) * rows, :] = waves_ref[half] * whole_wave(
+                arrived, slot
             )
     sums = jnp.dot(product_ref[...], lanes, preferred_element_type=F32)
     sums_ref[...] = (sums.reshape(2 * ITEMS, rows, 128) * turned[None]).sum(axis=1)
@@ -521,11 +538,12 @@
     ahead = [(i, (i + 1) % 8) for i in range(8)]
     behind = [(i, (i + 7) % 8) for i in range(8)]
     v = [wave_v, lax.ppermute(wave_v, "yl", [(0, 1), (1, 0)])]
-    c = [wave_c] + [None] * 7
+    c = [wave_c] + [None] * 8
     for slot in (1, 2, 3, 4):
         c[slot] = lax.ppermute(c[slot - 1], "z", ahead)
         if slot < 4:
             c[8 - slot] = lax.ppermute(c[(9 - slot) % 8], "z", behind)
+    c[8] = lax.ppermute(c[5], "z", behind)
 
     mirror_of = [(k, SLABS - 1 - k) for k in range(SLABS)]
     far_cell = lax.ppermute(gvec_cell, COL, mirror_of).reshape(16, 128)

time: 112 us -> 115 us (1.027)
  waiting for transfers between devices: 39.9 us -> 35.2 us
  starting transfers between devices: 37.1 us -> 41.6 us
  Pallas kernels: 26.3 us -> 30.7 us
  local copies, waits for them, and re-layouts: 5.37 us -> 3.71 us
    pallas_call x4, Pallas kernels: 9.45 us -> 13.8 us  [planes_of(): pl.pallas_call(functools.partial(plane_kernel, slots=slots, items=items,...]
    ppermute x0 -> x1, starting transfers between devices: none -> 3.69 us  [per_device(): c[8] = lax.ppermute(c[5], 'z', behind)]
    ppermute x1, waiting for transfers between devices: 3.51 us -> 1.11 us  [per_device(): far_cell = lax.ppermute(gvec_cell, COL, mirror_of).reshape(16, 128)]
    ppermute x4, waiting for transfers between devices: 1.86 us -> 0.01 us  [per_device(): c[slot] = lax.ppermute(c[slot - 1], 'z', ahead)]
    unnamed x52 -> x50, local copies, waits for them, and re-layouts: 2.42 us -> 0.76 us
    all_to_all x1, starting transfers between devices: 3.52 us -> 4.92 us  [per_device(): pairs = lax.all_to_all(pairs, BAND, 0, 0, tiled=True)]
  transfers between devices with their start and end apart: 13 -> 14, of which waited for: 7 -> 5; matrix products, arithmetic and copies ran while one was open for 2% -> 2% of each run, Pallas kernels for 15% -> 19%
where the time goes in v9:
time: 115 us; the launch traced here: 113 us
  starting transfers between devices  41.6 us (36%)
  waiting for transfers between devices  35.2 us (31%)
  Pallas kernels  30.7 us (27%)
  local copies, waits for them, and re-layouts  3.71 us (3%)
  between operations  1.16 us (1%)
    all_to_all x1, waiting for transfers between devices, per_device(): sent1 = lax.all_to_all(planes1, COL, 0, 0, tiled=True)  19.5 us
    pallas_call x4, Pallas kernels, planes_of(): pl.pallas_call(functools.partial(plane_kernel, slots=slots, items=items,...  13.8 us
    ppermute x3, starting transfers between devices, per_device(): c[8 - slot] = lax.ppermute(c[(9 - slot) % 8], 'z', behind)  12.3 us
    all_to_all x1, waiting for transfers between devices, per_device(): pairs = lax.all_to_all(pairs, BAND, 0, 0, tiled=True)  10.8 us
    all_to_all x1, starting transfers between devices, per_device(): sent1 = lax.all_to_all(planes1, COL, 0, 0, tiled=True)  7.37 us
    all_to_all x1, starting transfers between devices, per_device(): sent0 = lax.all_to_all(planes0, COL, 0, 0, tiled=True)  6.88 us
    all_to_all x1, starting transfers between devices, per_device(): pairs = lax.all_to_all(pairs, BAND, 0, 0, tiled=True)  4.92 us
    pallas_call x1, Pallas kernels, second_far_points(): pl.pallas_call(second_far_kernel, out_shape=(jax.ShapeDtypeStruct((FIRST...  4.88 us
  transfers between devices with their start and end apart: 14, of which 5 were waited for; matrix products, arithmetic and copies ran while one was open for 2% of the time, Pallas kernels for 19%

profile of v9, /device:TPU:6, one launch (start us, length us, event | category | flops | bytes accessed | tf_op | source)
XLA Modules:
  0.0 113.2 jit_solution(4047004271404551013)
XLA Ops:
  0.0 1.2 %reshape.316 = bf16[6,6,16,96]{3,2,1,0:T(8,128)(2,1)S(1)} reshape(bf16[1,6,9216]{2,1,0:T(8,128)(2,1)} %param.18) | data formatting | bytes 221184 | tf_op jit(solution)/shard_map/reshape | solution.py:522
  1.3 0.1 reshape.317.refs_2_
  1.5 5.9 %collective-permute-start.3 = (bf16[96,576]{1,0:T(8,128)(2,1)S(1)}, bf16[96,576]{1,0:T(8,128)(2,1)S(1)}, u32[]{:S(2)}, u32[]{:S(2)}) collective-permute-start(bf16[96,576]{1,0:T(8,128)(2,1)S(1)} %reshape.317.refs_2_), channel_id=1, source_target_pairs={{0,224},{32,0},{64,32},{96,64},{128,96},{160,128},{192,160},{224,1... | collective-permute-start | bytes 331784 | tf_op jit(solution)/shard_map/ppermute | solution.py:545
  7.4 1.1 reshape.314
  8.6 0.1 reshape.315.refs_0_
  8.7 1.7 %collective-permute-start = (bf16[96,576]{1,0:T(8,128)(2,1)S(1)}, bf16[96,576]{1,0:T(8,128)(2,1)S(1)}, u32[]{:S(2)}, u32[]{:S(2)}) collective-permute-start(bf16[96,576]{1,0:T(8,128)(2,1)S(1)} %reshape.315.refs_0_), channel_id=1, source_target_pairs={{0,16},{16,0},{1,17},{17,1},{2,18},{18,2},{3,19},{19,3},{4,20},{20... | collective-permute-start | bytes 331784 | tf_op jit(solution)/shard_map/ppermute | solution.py:540
  10.4 1.7 %collective-permute-start.2 = (s32[2048]{0:T(1024)S(1)}, s32[2048]{0:T(1024)S(1)}, u32[]{:S(2)}, u32[]{:S(2)}) collective-permute-start(s32[2048]{0:T(1024)S(1)} %copy-done.17), channel_id=1, source_target_pairs={{0,15},{1,14},{2,13},{3,12},{4,11},{5,10},{6,9},{7,8},{8,7},{9,6},... | collective-permute-start | bytes 24584 | tf_op jit(solution)/shard_map/ppermute | solution.py:549
  12.9 3.0 %collective-permute-start.7 = (bf16[96,576]{1,0:T(8,128)(2,1)S(1)}, bf16[96,576]{1,0:T(8,128)(2,1)S(1)}, u32[]{:S(2)}, u32[]{:S(2)}) collective-permute-start(bf16[96,576]{1,0:T(8,128)(2,1)S(1)} %collective-permute-done.3.refs_9_.refs_2_), channel_id=1, source_target_pairs={{0,224},{32,0},{64,32},{96,64},{128,96},{160,128},{192,160},{224,1... | collective-permute-start | bytes 331784 | tf_op jit(solution)/shard_map/ppermute | solution.py:545
  16.0 1.1 collective-permute-done.2
  17.1 3.5 %planes.4 = (bf16[16,24,768]{2,1,0:T(8,128)(2,1)}, s32[16,128]{1,0:T(8,128)}) custom-call(bf16[96,576]{1,0:T(8,128)(2,1)S(1)} %reshape.315.refs_0_, bf16[96,576]{1,0:T(8,128)(2,1)S(1)} %collective-permute-done.refs_1_, bf16[96,576]{1,0:T(8,128)(2,1)S(1)} %reshape.317.refs_2_, bf16[96,576]{1,0:T(8,128)(2,1)S(1)} %collective-permute-done.1.refs_3_, ...), custom_call_target="tpu_custom_call" | custom-call | flops 60000000 | bytes 100000 | tf_op jit(solution)/shard_map/planes/pallas_call | solution.py:223
  20.6 6.9 %all-to-all-start = ((bf16[16,24,768]{2,1,0:T(8,128)(2,1)}), bf16[16,24,768]{2,1,0:T(8,128)(2,1)S(1)}, u32[]{:S(2)}, u32[]{:S(2)}) async-start(bf16[16,24,768]{2,1,0:T(8,128)(2,1)} %get-tuple-element.12), calls=%async_computation | async-start | bytes 1179648 | tf_op jit(solution)/shard_map/all_to_all | solution.py:556
  27.6 3.3 %collective-permute-start.8 = (bf16[96,576]{1,0:T(8,128)(2,1)S(1)}, bf16[96,576]{1,0:T(8,128)(2,1)S(1)}, u32[]{:S(2)}, u32[]{:S(2)}) collective-permute-start(bf16[96,576]{1,0:T(8,128)(2,1)S(1)} %collective-permute-done.7.refs_2_.refs_8_), channel_id=1, source_target_pairs={{0,224},{32,0},{64,32},{96,64},{128,96},{160,128},{192,160},{224,1... | collective-permute-start | bytes 331784 | tf_op jit(solution)/shard_map/ppermute | solution.py:545
  31.0 2.9 %collective-permute-done.8.refs_2_.refs_7_ = bf16[96,576]{1,0:T(8,128)(2,1)S(1)} collective-permute-done((bf16[96,576]{1,0:T(8,128)(2,1)S(1)}, bf16[96,576]{1,0:T(8,128)(2,1)S(1)}, u32[]{:S(2)}, u32[]{:S(2)}) %collective-permute-start.8) | collective-permute-done | bytes 110624 | tf_op jit(solution)/shard_map/ppermute | solution.py:545
  33.8 3.7 %collective-permute-start.9 = (bf16[96,576]{1,0:T(8,128)(2,1)S(1)}, bf16[96,576]{1,0:T(8,128)(2,1)S(1)}, u32[]{:S(2)}, u32[]{:S(2)}) collective-permute-start(bf16[96,576]{1,0:T(8,128)(2,1)S(1)} %collective-permute-done.8.refs_2_.refs_7_), channel_id=1, source_target_pairs={{0,224},{32,0},{64,32},{96,64},{128,96},{160,128},{192,160},{224,1... | collective-permute-start | bytes 331784 | tf_op jit(solution)/shard_map/ppermute | solution.py:546
  37.6 3.4 %planes.5.refs_7_ = bf16[16,72,768]{2,1,0:T(8,128)(2,1)} custom-call(bf16[96,576]{1,0:T(8,128)(2,1)S(1)} %reshape.315.refs_0_, bf16[96,576]{1,0:T(8,128)(2,1)S(1)} %collective-permute-done.refs_1_, bf16[96,576]{1,0:T(8,128)(2,1)S(1)} %collective-permute-done.7.refs_2_.refs_8_, bf16[96,576]{1,0:T(8,128)(2,1)S(1)} %collective-permute-done.4.refs_3_.refs_4_, ...), custom_call_target="tpu_custom_call" | custom-call | flops 60000000 | bytes 100000 | tf_op jit(solution)/shard_map/planes/pallas_call | solution.py:223
  41.1 3.4 %planes.6.refs_8_ = bf16[16,72,768]{2,1,0:T(8,128)(2,1)} custom-call(bf16[96,576]{1,0:T(8,128)(2,1)S(1)} %reshape.315.refs_0_, bf16[96,576]{1,0:T(8,128)(2,1)S(1)} %collective-permute-done.refs_1_, bf16[96,576]{1,0:T(8,128)(2,1)S(1)} %collective-permute-done.3.refs_9_.refs_2_, ...), custom_call_target="tpu_custom_call", output_to_operand_aliasing={{}: (7, {})} | custom-call | flops 60000000 | bytes 100000 | tf_op jit(solution)/shard_map/planes/pallas_call | solution.py:223
  44.6 3.4 %planes.7.refs_13_ = bf16[16,72,768]{2,1,0:T(8,128)(2,1)} custom-call(bf16[96,576]{1,0:T(8,128)(2,1)S(1)} %reshape.315.refs_0_, bf16[96,576]{1,0:T(8,128)(2,1)S(1)} %collective-permute-done.refs_1_, bf16[96,576]{1,0:T(8,128)(2,1)S(1)} %collective-permute-done.8.refs_2_.refs_7_, ...), custom_call_target="tpu_custom_call", output_to_operand_aliasing={{}: (8, {})} | custom-call | flops 60000000 | bytes 100000 | tf_op jit(solution)/shard_map/planes/pallas_call | solution.py:223
  48.1 0.6 copy-done.13
  48.7 3.0 %block.1 = bf16[16,72,768]{2,1,0:T(8,128)(2,1)} custom-call(bf16[96,576]{1,0:T(8,128)(2,1)} %copy-done.1, bf16[96,576]{1,0:T(8,128)(2,1)} %copy-done.2, bf16[96,576]{1,0:T(8,128)(2,1)} %copy-done.5, bf16[96,576]{1,0:T(8,128)(2,1)} %copy-done.7, bf16[96,576]{1,0:T(8,128)(2,1)} %copy-done.9, ...), custom_call_target="tpu_custom_call", output_to_operand_aliasing={{}: (13, {})} | custom-call | flops 10000000 | bytes 100000 | tf_op jit(solution)/shard_map/block/pallas_call | solution.py:483
  51.8 7.4 %all-to-all-start.1 = ((bf16[16,72,768]{2,1,0:T(8,128)(2,1)}), bf16[16,72,768]{2,1,0:T(8,128)(2,1)S(1)}, u32[]{:S(2)}, u32[]{:S(2)}) async-start(bf16[16,72,768]{2,1,0:T(8,128)(2,1)} %block.1), calls=%async_computation.1 | async-start | bytes 3538944 | tf_op jit(solution)/shard_map/all_to_all | solution.py:570
  59.4 0.2 select_reduce_fusion
  59.8 0.2 and_select_fusion
  60.0 3.3 %first_points.1 = (f32[4,2048]{1,0:T(4,128)S(1)}, bf16[4,2048]{1,0:T(4,128)(2,1)S(1)}) custom-call(bf16[16,24,768]{2,1,0:T(8,128)(2,1)S(1)} %all-to-all-done.t_ref.refs_12_, bf16[384,384]{1,0:T(8,128)(2,1)S(1)} %copy-done.4, s32[1,2048]{1,0:T(1,128)S(1)} %bitcast.39, s32[1,2048]{1,0:T(1,128)S(1)} %bitcast.37, s32[1,2048]{1,0:T(1,128)S(1)} %get-tuple-element.29.far_ref, ...), custom_call_target="tpu_custom_call" | custom-call | flops 100000000 | bytes 100000 | tf_op jit(solution)/shard_map/first_points/pallas_call | solution.py:332
  63.3 19.5 %all-to-all-done.1.t_ref = bf16[16,72,768]{2,1,0:T(8,128)(2,1)S(1)} async-done(((bf16[16,72,768]{2,1,0:T(8,128)(2,1)}), bf16[16,72,768]{2,1,0:T(8,128)(2,1)S(1)}, u32[]{:S(2)}, u32[]{:S(2)}) %all-to-all-start.1) | async-done | bytes 1769504 | tf_op jit(solution)/shard_map/all_to_all | solution.py:570
  82.7 4.9 %second_far_points.1 = (bf16[16,2048]{1,0:T(8,128)(2,1)S(1)}, bf16[1152,768]{1,0:T(8,128)(2,1)S(1)}, f32[16,128]{1,0:T(8,128)S(1)}) custom-call(bf16[16,72,768]{2,1,0:T(8,128)(2,1)S(1)} %all-to-all-done.1.t_ref, bf16[384,384]{1,0:T(8,128)(2,1)S(1)} %copy-done.4, s32[1,2048]{1,0:T(1,128)S(1)} %get-tuple-element.29.far_ref, ...), custom_call_target="tpu_custom_call" | custom-call | flops 100000000 | bytes 100000 | tf_op jit(solution)/shard_map/second_far_points/pallas_call | solution.py:348
  87.6 3.0 %collective-permute-start.10 = (bf16[16,2048]{1,0:T(8,128)(2,1)S(1)}, bf16[16,2048]{1,0:T(8,128)(2,1)S(1)}, u32[]{:S(2)}, u32[]{:S(2)}) collective-permute-start(bf16[16,2048]{1,0:T(8,128)(2,1)S(1)} %get-tuple-element.17), channel_id=1, source_target_pairs={{0,15},{1,14},{2,13},{3,12},{4,11},{5,10},{6,9},{7,8},{8,7},{9,6},... | collective-permute-start | bytes 196616 | tf_op jit(solution)/shard_map/ppermute | solution.py:597
  90.7 4.0 %second_own_points.1.own1_ref = f32[12,2048]{1,0:T(8,128)S(1)} custom-call(bf16[1152,768]{1,0:T(8,128)(2,1)S(1)} %get-tuple-element.16.low, s32[1,2048]{1,0:T(1,128)S(1)} %bitcast.40, s32[1,2048]{1,0:T(1,128)S(1)} %bitcast.38), custom_call_target="tpu_custom_call" | custom-call | flops 2400000000 | bytes 1300000 | tf_op jit(solution)/shard_map/second_own_points/pallas_call | solution.py:364
  94.7 0.9 collective-permute-done.10.far_ref
  95.5 0.8 split.1
  96.3 4.9 %all-to-all-start.2 = ((bf16[16,48,128]{2,1,0:T(8,128)(2,1)}), bf16[16,48,128]{2,1,0:T(8,128)(2,1)S(1)}, u32[]{:S(2)}, u32[]{:S(2)}) async-start(bf16[16,48,128]{2,1,0:T(8,128)(2,1)} %split.1), calls=%async_computation.2 | async-start | bytes 393216 | tf_op jit(solution)/shard_map/all_to_all | solution.py:600
  101.4 10.8 %all-to-all-done.2.pairs_ref = bf16[16,48,128]{2,1,0:T(8,128)(2,1)S(1)} async-done(((bf16[16,48,128]{2,1,0:T(8,128)(2,1)}), bf16[16,48,128]{2,1,0:T(8,128)(2,1)S(1)}, u32[]{:S(2)}, u32[]{:S(2)}) %all-to-all-start.2) | async-done | bytes 196640 | tf_op jit(solution)/shard_map/all_to_all | solution.py:600
  112.2 1.0 pair_sum.1
  (79 shorter events, 1.0 us)
Async XLA Ops:
  0.0 17.1 %copy-start = (bf16[576,1536]{1,0:T(8,128)(2,1)S(1)}, bf16[576,1536]{1,0:T(8,128)(2,1)}, u32[]{:S(2)}) copy-start(bf16[576,1536]{1,0:T(8,128)(2,1)} %constant.132.clone.refs_4_.refs_5_) | copy-start | bytes 5308420
  0.0 17.1 %copy-start.3 = (f32[2,16,768]{2,1,0:T(8,128)S(1)}, f32[2,16,768]{2,1,0:T(8,128)}, u32[]{:S(2)}) copy-start(f32[2,16,768]{2,1,0:T(8,128)} %constant.133.clone.refs_5_.refs_6_) | copy-start | bytes 294916
  0.0 10.4 %copy-start.17 = (s32[2048]{0:T(1024)S(1)}, s32[2048]{0:T(1024)}, u32[]{:S(2)}) copy-start(s32[2048]{0:T(1024)} %param.23) | copy-start | bytes 24580
  1.5 19.2 %copy-start.5 = (bf16[96,576]{1,0:T(8,128)(2,1)}, bf16[96,576]{1,0:T(8,128)(2,1)S(1)}, u32[]{:S(2)}) copy-start(bf16[96,576]{1,0:T(8,128)(2,1)S(1)} %reshape.317.refs_2_) | copy-start | bytes 331780
  1.5 11.4 %collective-permute-start.3 = (bf16[96,576]{1,0:T(8,128)(2,1)S(1)}, bf16[96,576]{1,0:T(8,128)(2,1)S(1)}, u32[]{:S(2)}, u32[]{:S(2)}) collective-permute-start(bf16[96,576]{1,0:T(8,128)(2,1)S(1)} %reshape.317.refs_2_), channel_id=1, source_target_pairs={{0,224},{32,0},{64,32},{96,64},{128,96},{160,128},{192,160},{224,1... | collective-permute-start | bytes 331784 | tf_op jit(solution)/shard_map/ppermute | solution.py:545
  7.4 8.5 %collective-permute-start.1 = (bf16[96,576]{1,0:T(8,128)(2,1)S(1)}, bf16[96,576]{1,0:T(8,128)(2,1)S(1)}, u32[]{:S(2)}, u32[]{:S(2)}) collective-permute-start(bf16[96,576]{1,0:T(8,128)(2,1)S(1)} %reshape.317.refs_2_), channel_id=1, source_target_pairs={{0,32},{32,64},{64,96},{96,128},{128,160},{160,192},{192,224},{224... | collective-permute-start | bytes 331784 | tf_op jit(solution)/shard_map/ppermute | solution.py:543
  8.7 35.9 %copy-start.1 = (bf16[96,576]{1,0:T(8,128)(2,1)}, bf16[96,576]{1,0:T(8,128)(2,1)S(1)}, u32[]{:S(2)}) copy-start(bf16[96,576]{1,0:T(8,128)(2,1)S(1)} %reshape.315.refs_0_) | copy-start | bytes 331780
  8.7 8.4 %collective-permute-start = (bf16[96,576]{1,0:T(8,128)(2,1)S(1)}, bf16[96,576]{1,0:T(8,128)(2,1)S(1)}, u32[]{:S(2)}, u32[]{:S(2)}) collective-permute-start(bf16[96,576]{1,0:T(8,128)(2,1)S(1)} %reshape.315.refs_0_), channel_id=1, source_target_pairs={{0,16},{16,0},{1,17},{17,1},{2,18},{18,2},{3,19},{19,3},{4,20},{20... | collective-permute-start | bytes 331784 | tf_op jit(solution)/shard_map/ppermute | solution.py:540
  10.4 6.7 %collective-permute-start.2 = (s32[2048]{0:T(1024)S(1)}, s32[2048]{0:T(1024)S(1)}, u32[]{:S(2)}, u32[]{:S(2)}) collective-permute-start(s32[2048]{0:T(1024)S(1)} %copy-done.17), channel_id=1, source_target_pairs={{0,15},{1,14},{2,13},{3,12},{4,11},{5,10},{6,9},{7,8},{8,7},{9,6},... | collective-permute-start | bytes 24584 | tf_op jit(solution)/shard_map/ppermute | solution.py:549
  12.8 28.2 %copy-start.6 = (bf16[96,576]{1,0:T(8,128)(2,1)}, bf16[96,576]{1,0:T(8,128)(2,1)S(1)}, u32[]{:S(2)}) copy-start(bf16[96,576]{1,0:T(8,128)(2,1)S(1)} %collective-permute-done.3.refs_9_.refs_2_) | copy-start | bytes 331780
  12.9 14.8 %collective-permute-start.7 = (bf16[96,576]{1,0:T(8,128)(2,1)S(1)}, bf16[96,576]{1,0:T(8,128)(2,1)S(1)}, u32[]{:S(2)}, u32[]{:S(2)}) collective-permute-start(bf16[96,576]{1,0:T(8,128)(2,1)S(1)} %collective-permute-done.3.refs_9_.refs_2_), channel_id=1, source_target_pairs={{0,224},{32,0},{64,32},{96,64},{128,96},{160,128},{192,160},{224,1... | collective-permute-start | bytes 331784 | tf_op jit(solution)/shard_map/ppermute | solution.py:545
  15.9 11.6 %collective-permute-start.4 = (bf16[96,576]{1,0:T(8,128)(2,1)S(1)}, bf16[96,576]{1,0:T(8,128)(2,1)S(1)}, u32[]{:S(2)}, u32[]{:S(2)}) collective-permute-start(bf16[96,576]{1,0:T(8,128)(2,1)S(1)} %collective-permute-done.1.refs_3_), channel_id=1, source_target_pairs={{0,32},{32,64},{64,96},{96,128},{128,160},{160,192},{192,224},{224... | collective-permute-start | bytes 331784 | tf_op jit(solution)/shard_map/ppermute | solution.py:543
  17.1 27.5 %copy-start.2 = (bf16[96,576]{1,0:T(8,128)(2,1)}, bf16[96,576]{1,0:T(8,128)(2,1)S(1)}, u32[]{:S(2)}) copy-start(bf16[96,576]{1,0:T(8,128)(2,1)S(1)} %collective-permute-done.refs_1_) | copy-start | bytes 331780
  17.1 13.9 %copy-start.24 = (pred[8,1]{0,1:T(4,128)(4,1)S(1)}, pred[8,1]{0,1:T(4,128)(4,1)}, u32[]{:S(2)}) copy-start(pred[8,1]{0,1:T(4,128)(4,1)} %constant.134.clone) | copy-start | bytes 28
  17.1 20.4 %copy-start.18 = (f32[8,128]{1,0:T(8,128)S(1)}, f32[8,128]{1,0:T(8,128)}, u32[]{:S(2)}) copy-start(f32[8,128]{1,0:T(8,128)} %constant.135.clone) | copy-start | bytes 12292
  20.6 28.1 %all-to-all-start = ((bf16[16,24,768]{2,1,0:T(8,128)(2,1)}), bf16[16,24,768]{2,1,0:T(8,128)(2,1)S(1)}, u32[]{:S(2)}, u32[]{:S(2)}) async-start(bf16[16,24,768]{2,1,0:T(8,128)(2,1)} %get-tuple-element.12), calls=%async_computation | async-start | bytes 1179648 | tf_op jit(solution)/shard_map/all_to_all | solution.py:556
  27.5 13.6 %copy-start.9 = (bf16[96,576]{1,0:T(8,128)(2,1)}, bf16[96,576]{1,0:T(8,128)(2,1)S(1)}, u32[]{:S(2)}) copy-start(bf16[96,576]{1,0:T(8,128)(2,1)S(1)} %collective-permute-done.4.refs_3_.refs_4_) | copy-start | bytes 331780
  27.5 10.0 %collective-permute-start.5 = (bf16[96,576]{1,0:T(8,128)(2,1)S(1)}, bf16[96,576]{1,0:T(8,128)(2,1)S(1)}, u32[]{:S(2)}, u32[]{:S(2)}) collective-permute-start(bf16[96,576]{1,0:T(8,128)(2,1)S(1)} %collective-permute-done.4.refs_3_.refs_4_), channel_id=1, source_target_pairs={{0,32},{32,64},{64,96},{96,128},{128,160},{160,192},{192,224},{224... | collective-permute-start | bytes 331784 | tf_op jit(solution)/shard_map/ppermute | solution.py:543
  27.6 13.5 %copy-start.8 = (bf16[96,576]{1,0:T(8,128)(2,1)}, bf16[96,576]{1,0:T(8,128)(2,1)S(1)}, u32[]{:S(2)}) copy-start(bf16[96,576]{1,0:T(8,128)(2,1)S(1)} %collective-permute-done.7.refs_2_.refs_8_) | copy-start | bytes 331780
  27.6 6.2 %collective-permute-start.8 = (bf16[96,576]{1,0:T(8,128)(2,1)S(1)}, bf16[96,576]{1,0:T(8,128)(2,1)S(1)}, u32[]{:S(2)}, u32[]{:S(2)}) collective-permute-start(bf16[96,576]{1,0:T(8,128)(2,1)S(1)} %collective-permute-done.7.refs_2_.refs_8_), channel_id=1, source_target_pairs={{0,224},{32,0},{64,32},{96,64},{128,96},{160,128},{192,160},{224,1... | collective-permute-start | bytes 331784 | tf_op jit(solution)/shard_map/ppermute | solution.py:545
  33.8 10.8 %copy-start.11 = (bf16[96,576]{1,0:T(8,128)(2,1)}, bf16[96,576]{1,0:T(8,128)(2,1)S(1)}, u32[]{:S(2)}) copy-start(bf16[96,576]{1,0:T(8,128)(2,1)S(1)} %collective-permute-done.8.refs_2_.refs_7_) | copy-start | bytes 331780
  33.8 10.7 %collective-permute-start.9 = (bf16[96,576]{1,0:T(8,128)(2,1)S(1)}, bf16[96,576]{1,0:T(8,128)(2,1)S(1)}, u32[]{:S(2)}, u32[]{:S(2)}) collective-permute-start(bf16[96,576]{1,0:T(8,128)(2,1)S(1)} %collective-permute-done.8.refs_2_.refs_7_), channel_id=1, source_target_pairs={{0,224},{32,0},{64,32},{96,64},{128,96},{160,128},{192,160},{224,1... | collective-permute-start | bytes 331784 | tf_op jit(solution)/shard_map/ppermute | solution.py:546
  37.5 7.0 %collective-permute-start.6 = (bf16[96,576]{1,0:T(8,128)(2,1)S(1)}, bf16[96,576]{1,0:T(8,128)(2,1)S(1)}, u32[]{:S(2)}, u32[]{:S(2)}) collective-permute-start(bf16[96,576]{1,0:T(8,128)(2,1)S(1)} %collective-permute-done.5.refs_3_.refs_5_), channel_id=1, source_target_pairs={{0,32},{32,64},{64,96},{96,128},{128,160},{160,192},{192,224},{224... | collective-permute-start | bytes 331784 | tf_op jit(solution)/shard_map/ppermute | solution.py:543
  51.8 7.8 %copy-start.19 = (pred[256,16]{0,1:T(8,128)(4,1)S(1)}, pred[256,16]{0,1:T(8,128)(4,1)}, u32[]{:S(2)}) copy-start(pred[256,16]{0,1:T(8,128)(4,1)} %constant.136.clone) | copy-start | bytes 12292
  51.8 7.8 %copy-start.20 = (pred[256,16]{0,1:T(8,128)(4,1)S(1)}, pred[256,16]{0,1:T(8,128)(4,1)}, u32[]{:S(2)}) copy-start(pred[256,16]{0,1:T(8,128)(4,1)} %constant.137.clone) | copy-start | bytes 12292
  51.8 7.8 %copy-start.22 = (f32[16]{0:T(128)S(1)}, f32[16]{0:T(128)}, u32[]{:S(2)}) copy-start(f32[16]{0:T(128)} %param.21) | copy-start | bytes 196
  51.8 7.9 %copy-start.15 = (s32[16,128]{1,0:T(8,128)S(1)}, s32[16,128]{1,0:T(8,128)}, u32[]{:S(2)}) copy-start(s32[16,128]{1,0:T(8,128)} %get-tuple-element.13) | copy-start | bytes 24580
  51.8 8.1 %copy-start.4 = (bf16[384,384]{1,0:T(8,128)(2,1)S(1)}, bf16[384,384]{1,0:T(8,128)(2,1)}, u32[]{:S(2)}) copy-start(bf16[384,384]{1,0:T(8,128)(2,1)} %constant.138.clone.x_ref) | copy-start | bytes 884740
  51.8 30.9 %all-to-all-start.1 = ((bf16[16,72,768]{2,1,0:T(8,128)(2,1)}), bf16[16,72,768]{2,1,0:T(8,128)(2,1)S(1)}, u32[]{:S(2)}, u32[]{:S(2)}) async-start(bf16[16,72,768]{2,1,0:T(8,128)(2,1)} %block.1), calls=%async_computation.1 | async-start | bytes 3538944 | tf_op jit(solution)/shard_map/all_to_all | solution.py:570
  87.6 7.9 %collective-permute-start.10 = (bf16[16,2048]{1,0:T(8,128)(2,1)S(1)}, bf16[16,2048]{1,0:T(8,128)(2,1)S(1)}, u32[]{:S(2)}, u32[]{:S(2)}) collective-permute-start(bf16[16,2048]{1,0:T(8,128)(2,1)S(1)} %get-tuple-element.17), channel_id=1, source_target_pairs={{0,15},{1,14},{2,13},{3,12},{4,11},{5,10},{6,9},{7,8},{8,7},{9,6},... | collective-permute-start | bytes 196616 | tf_op jit(solution)/shard_map/ppermute | solution.py:597
  90.7 21.6 %copy-start.14 = (bf16[2,128,128]{2,1,0:T(8,128)(2,1)S(1)}, bf16[2,128,128]{2,1,0:T(8,128)(2,1)}, u32[]{:S(2)}) copy-start(bf16[2,128,128]{2,1,0:T(8,128)(2,1)} %constant.139.clone.column_ref) | copy-start | bytes 196612
  96.3 15.9 %all-to-all-start.2 = ((bf16[16,48,128]{2,1,0:T(8,128)(2,1)}), bf16[16,48,128]{2,1,0:T(8,128)(2,1)S(1)}, u32[]{:S(2)}, u32[]{:S(2)}) async-start(bf16[16,48,128]{2,1,0:T(8,128)(2,1)} %split.1), calls=%async_computation.2 | async-start | bytes 393216 | tf_op jit(solution)/shard_map/all_to_all | solution.py:600
  (7 other events, 35.2 us)

commit v10 on v8

--- a/solution.py
+++ b/solution.py
@@ -22,15 +22,15 @@
 K7 = 7
 FLAT = K7 * N
 WIDE = 768
-GROUPS = ((0, 1), (6, 2), (7, 3), (5, 4))
+GROUPS = ((0, 1), (7, 2), (6, 3), (5, 4))
 SLOTS = [slot for group in GROUPS for slot in group]
 ITEMS = len(SLOTS)
 SPARE = 640
 G_DEV = 2048
 NBLOCK = 16
 TILE = 512
-CHUNK_ROWS = (24, 72)
-X_GROUPS = ((2,), (2, 2, 2))
+ROWS = 48
+X_GROUPS = ((2, 2), (2, 2))
 
 BAND = ("z", "yl")
 COL = ("x", "yh", "co")
@@ -193,8 +193,7 @@
 def planes_of(group, v, c, marks=(), through=(), after=(), buffer=()):
     slots = GROUPS[group]
     items = len(slots)
-    first = max(group - 1, 0) * items * 2 * X6
-    rows = CHUNK_ROWS[min(group, 1)]
+    first = group % 2 * items * 2 * X6
     inputs = (
         *v,
         *(c[slot] for slot in slots),
@@ -217,7 +216,7 @@
             marked=len(marks),
         ),
         out_shape=[
-            pltpu.HBM((SLABS, rows, WIDE), BF16),
+            pltpu.HBM((SLABS, ROWS, WIDE), BF16),
             *(pltpu.HBM(x.shape, x.dtype) for x in through),
         ],
         in_specs=[VMEM] * (len(inputs) - outside)
@@ -274,7 +273,7 @@
 def first_kernel(
     t_ref, x_ref, own_ref, own_kx_ref, far_ref, far_kx_ref, own_out, far_out, low
 ):
-    transform_x(0, t_ref, (x_ref,), low)
+    transform_x(0, t_ref, (x_ref,) * len(X_GROUPS[0]), low)
 
     def store_far(lanes, values):
         far_out[:, lanes] = values.astype(BF16)
@@ -325,7 +324,7 @@
             flops=100_000_000, bytes_accessed=100_000, transcendentals=0
         ),
         name="first_points",
-    )(planes, x_table(FIRST // 2), *own, *far)
+    )(planes, x_table(X_GROUPS[0][0]), *own, *far)
 
 
 def second_far_points(planes, far, first):
@@ -532,12 +531,10 @@
     spots = jnp.arange(128, dtype=jnp.int32)
     cell = jnp.where((spots % NBLOCK == col) & (spots >= 32), block_cell[0], 0)
     marks = jnp.concatenate([jnp.stack([cell // 256, cell % 256]), jnp.zeros((6, 128), jnp.int32)])
-    planes0, far_cell = planes_of(
-        0, v, c, marks=(marks.astype(F32),), through=(far_cell,), after=(c[7],)
-    )
+    (planes0,) = planes_of(0, v, c, marks=(marks.astype(F32),))
+    planes0, far_cell = planes_of(1, v, c, through=(far_cell,), buffer=(planes0,))
     sent0 = lax.all_to_all(planes0, COL, 0, 0, tiled=True)
-    (planes1,) = planes_of(1, v, c)
-    (planes1,) = planes_of(2, v, c, buffer=(planes1,))
+    (planes1,) = planes_of(2, v, c)
     (planes1,) = planes_of(3, v, c, buffer=(planes1,))
 
     group = np.arange(128) // NBLOCK - 2

time: 112 us -> 105 us (0.938)
  waiting for transfers between devices: 39.9 us -> 33.8 us
  starting transfers between devices: 37.1 us -> 35 us
    all_to_all x1, waiting for transfers between devices: 19.5 us -> 10.8 us  [per_device(): sent1 = lax.all_to_all(planes1, COL, 0, 0, tiled=True)]
    ppermute x3, starting transfers between devices: 12.9 us -> 5.79 us  [per_device(): c[8 - slot] = lax.ppermute(c[(9 - slot) % 8], 'z', behind)]
    ppermute x4, starting transfers between devices: 0.01 us -> 4.39 us  [per_device(): c[slot] = lax.ppermute(c[slot - 1], 'z', ahead)]
    ppermute x1, waiting for transfers between devices: 3.51 us -> 0.04 us  [per_device(): far_cell = lax.ppermute(gvec_cell, COL, mirror_of).reshape(16, 128)]
    ppermute x4, waiting for transfers between devices: 1.86 us -> 5.15 us  [per_device(): c[slot] = lax.ppermute(c[slot - 1], 'z', ahead)]
    pallas_call x1, Pallas kernels: 3.25 us -> 6.11 us  [first_points(): pl.pallas_call(first_kernel, out_shape=(jax.ShapeDtypeStruct((FIRST, G_DE...]
    ppermute x1, waiting for transfers between devices: 0.86 us -> 2.88 us  [per_device(): mirrored = lax.ppermute(mirrored, COL, mirror_of)]
    all_to_all x1, starting transfers between devices: 3.52 us -> 5.37 us  [per_device(): pairs = lax.all_to_all(pairs, BAND, 0, 0, tiled=True)]
where the time goes in v10:
time: 105 us; the launch traced here: 103 us
  starting transfers between devices  35 us (33%)
  waiting for transfers between devices  33.8 us (32%)
  Pallas kernels  26.4 us (25%)
  local copies, waits for them, and re-layouts  6.2 us (6%)
  between operations  1.06 us (1%)
    all_to_all x1, waiting for transfers between devices, per_device(): sent1 = lax.all_to_all(planes1, COL, 0, 0, tiled=True)  10.8 us
    all_to_all x1, waiting for transfers between devices, per_device(): pairs = lax.all_to_all(pairs, BAND, 0, 0, tiled=True)  10.8 us
    pallas_call x4, Pallas kernels, planes_of(): pl.pallas_call(functools.partial(plane_kernel, items=items, first=first,...  9.44 us
    all_to_all x1, starting transfers between devices, per_device(): sent1 = lax.all_to_all(planes1, COL, 0, 0, tiled=True)  7.32 us
    all_to_all x1, starting transfers between devices, per_device(): sent0 = lax.all_to_all(planes0, COL, 0, 0, tiled=True)  6.33 us
    pallas_call x1, Pallas kernels, first_points(): pl.pallas_call(first_kernel, out_shape=(jax.ShapeDtypeStruct((FIRST, G_DE...  6.11 us
    ppermute x3, starting transfers between devices, per_device(): c[8 - slot] = lax.ppermute(c[(9 - slot) % 8], 'z', behind)  5.79 us
    all_to_all x1, starting transfers between devices, per_device(): pairs = lax.all_to_all(pairs, BAND, 0, 0, tiled=True)  5.37 us
  transfers between devices with their start and end apart: 13, of which 7 were waited for; matrix products, arithmetic and copies ran while one was open for 2% of the time, Pallas kernels for 15%

profile of v10, /device:TPU:6, one launch (start us, length us, event | category | flops | bytes accessed | tf_op | source)
XLA Modules:
  0.0 103.3 jit_solution(8570228645588478208)
XLA Ops:
  0.0 1.2 %reshape.316 = bf16[6,6,16,96]{3,2,1,0:T(8,128)(2,1)S(1)} reshape(bf16[1,6,9216]{2,1,0:T(8,128)(2,1)} %param.18) | data formatting | bytes 221184 | tf_op jit(solution)/shard_map/reshape | solution.py:504
  1.5 2.0 %collective-permute-start.2 = (bf16[96,576]{1,0:T(8,128)(2,1)S(1)}, bf16[96,576]{1,0:T(8,128)(2,1)S(1)}, u32[]{:S(2)}, u32[]{:S(2)}) collective-permute-start(bf16[96,576]{1,0:T(8,128)(2,1)S(1)} %reshape.317.refs_2_), channel_id=1, source_target_pairs={{0,32},{32,64},{64,96},{96,128},{128,160},{160,192},{192,224},{224... | collective-permute-start | bytes 331784 | tf_op jit(solution)/shard_map/ppermute | solution.py:525
  3.5 4.0 %collective-permute-start.1 = (bf16[96,576]{1,0:T(8,128)(2,1)S(1)}, bf16[96,576]{1,0:T(8,128)(2,1)S(1)}, u32[]{:S(2)}, u32[]{:S(2)}) collective-permute-start(bf16[96,576]{1,0:T(8,128)(2,1)S(1)} %reshape.317.refs_2_), channel_id=1, source_target_pairs={{0,224},{32,0},{64,32},{96,64},{128,96},{160,128},{192,160},{224,1... | collective-permute-start | bytes 331784 | tf_op jit(solution)/shard_map/ppermute | solution.py:527
  7.5 1.1 %reshape.314 = bf16[6,6,16,96]{3,2,1,0:T(8,128)(2,1)S(1)} reshape(bf16[1,6,9216]{2,1,0:T(8,128)(2,1)} %param.17) | data formatting | bytes 221184 | tf_op jit(solution)/shard_map/reshape | solution.py:504
  8.8 1.7 %collective-permute-start = (bf16[96,576]{1,0:T(8,128)(2,1)S(1)}, bf16[96,576]{1,0:T(8,128)(2,1)S(1)}, u32[]{:S(2)}, u32[]{:S(2)}) collective-permute-start(bf16[96,576]{1,0:T(8,128)(2,1)S(1)} %reshape.315.refs_0_), channel_id=1, source_target_pairs={{0,16},{16,0},{1,17},{17,1},{2,18},{18,2},{3,19},{19,3},{4,20},{20... | collective-permute-start | bytes 331784 | tf_op jit(solution)/shard_map/ppermute | solution.py:522
  10.5 1.7 %collective-permute-start.4 = (s32[2048]{0:T(1024)S(1)}, s32[2048]{0:T(1024)S(1)}, u32[]{:S(2)}, u32[]{:S(2)}) collective-permute-start(s32[2048]{0:T(1024)S(1)} %copy-done.19), channel_id=1, source_target_pairs={{0,15},{1,14},{2,13},{3,12},{4,11},{5,10},{6,9},{7,8},{8,7},{9,6},... | collective-permute-start | bytes 24584 | tf_op jit(solution)/shard_map/ppermute | solution.py:530
  13.1 0.7 collective-permute-done.refs_1_
  13.8 1.0 copy-done.1
  14.7 2.3 %planes.4.refs_8_ = bf16[16,48,768]{2,1,0:T(8,128)(2,1)} custom-call(bf16[96,576]{1,0:T(8,128)(2,1)S(1)} %reshape.315.refs_0_, bf16[96,576]{1,0:T(8,128)(2,1)S(1)} %collective-permute-done.refs_1_, bf16[96,576]{1,0:T(8,128)(2,1)S(1)} %reshape.317.refs_2_, bf16[96,576]{1,0:T(8,128)(2,1)S(1)} %collective-permute-done.2.refs_3_, bf16[576,1536]{1,0:T(8,128)(2,1)S(1)} %copy-done, ...), custom_call_target="tpu_custom_call" | custom-call | flops 60000000 | bytes 100000 | tf_op jit(solution)/shard_map/planes/pallas_call | solution.py:209
  17.2 3.0 %collective-permute-done.3.refs_3_.refs_4_ = bf16[96,576]{1,0:T(8,128)(2,1)S(1)} collective-permute-done((bf16[96,576]{1,0:T(8,128)(2,1)S(1)}, bf16[96,576]{1,0:T(8,128)(2,1)S(1)}, u32[]{:S(2)}, u32[]{:S(2)}) %collective-permute-start.3) | collective-permute-done | bytes 110624 | tf_op jit(solution)/shard_map/ppermute | solution.py:525
  20.2 2.3 %planes.5 = (bf16[16,48,768]{2,1,0:T(8,128)(2,1)}, s32[16,128]{1,0:T(8,128)}) custom-call(bf16[96,576]{1,0:T(8,128)(2,1)S(1)} %reshape.315.refs_0_, bf16[96,576]{1,0:T(8,128)(2,1)S(1)} %collective-permute-done.refs_1_, bf16[96,576]{1,0:T(8,128)(2,1)S(1)} %collective-permute-done.1.refs_2_.refs_9_, ...), custom_call_target="tpu_custom_call", output_to_operand_aliasing={{0}: (8, {})} | custom-call | flops 60000000 | bytes 100000 | tf_op jit(solution)/shard_map/planes/pallas_call | solution.py:209
  22.6 6.3 %all-to-all-start = ((bf16[16,48,768]{2,1,0:T(8,128)(2,1)}), bf16[16,48,768]{2,1,0:T(8,128)(2,1)S(1)}, u32[]{:S(2)}, u32[]{:S(2)}) async-start(bf16[16,48,768]{2,1,0:T(8,128)(2,1)} %get-tuple-element.12), calls=%async_computation | async-start | bytes 2359296 | tf_op jit(solution)/shard_map/all_to_all | solution.py:536
  29.5 1.8 %collective-permute-start.5 = (bf16[96,576]{1,0:T(8,128)(2,1)}, bf16[96,576]{1,0:T(8,128)(2,1)S(1)}, u32[]{:S(2)}, u32[]{:S(2)}) collective-permute-start(bf16[96,576]{1,0:T(8,128)(2,1)} %copy-done.13), channel_id=1, source_target_pairs={{0,32},{32,64},{64,96},{96,128},{128,160},{160,192},{192,224},{224... | collective-permute-start | bytes 331784 | tf_op jit(solution)/shard_map/ppermute | solution.py:525
  31.5 3.3 %collective-permute-done.7.refs_2_.refs_8_ = bf16[96,576]{1,0:T(8,128)(2,1)S(1)} collective-permute-done((bf16[96,576]{1,0:T(8,128)(2,1)}, bf16[96,576]{1,0:T(8,128)(2,1)S(1)}, u32[]{:S(2)}, u32[]{:S(2)}) %collective-permute-start.7) | collective-permute-done | bytes 110624 | tf_op jit(solution)/shard_map/ppermute | solution.py:527
  34.8 1.5 %collective-permute-start.8 = (bf16[96,576]{1,0:T(8,128)(2,1)S(1)}, bf16[96,576]{1,0:T(8,128)(2,1)S(1)}, u32[]{:S(2)}, u32[]{:S(2)}) collective-permute-start(bf16[96,576]{1,0:T(8,128)(2,1)S(1)} %collective-permute-done.7.refs_2_.refs_8_), channel_id=1, source_target_pairs={{0,224},{32,0},{64,32},{96,64},{128,96},{160,128},{192,160},{224,1... | collective-permute-start | bytes 331784 | tf_op jit(solution)/shard_map/ppermute | solution.py:527
  37.0 0.9 copy-done.6
  37.9 2.4 %planes.6.refs_7_ = bf16[16,48,768]{2,1,0:T(8,128)(2,1)} custom-call(bf16[96,576]{1,0:T(8,128)(2,1)S(1)} %reshape.315.refs_0_, bf16[96,576]{1,0:T(8,128)(2,1)S(1)} %collective-permute-done.refs_1_, bf16[96,576]{1,0:T(8,128)(2,1)S(1)} %collective-permute-done.7.refs_2_.refs_8_, bf16[96,576]{1,0:T(8,128)(2,1)S(1)} %collective-permute-done.5.refs_3_.refs_5_, ...), custom_call_target="tpu_custom_call" | custom-call | flops 60000000 | bytes 100000 | tf_op jit(solution)/shard_map/planes/pallas_call | solution.py:209
  40.3 2.2 %collective-permute-done.6.refs_3_.refs_6_ = bf16[96,576]{1,0:T(8,128)(2,1)S(1)} collective-permute-done((bf16[96,576]{1,0:T(8,128)(2,1)S(1)}, bf16[96,576]{1,0:T(8,128)(2,1)S(1)}, u32[]{:S(2)}, u32[]{:S(2)}) %collective-permute-start.6) | collective-permute-done | bytes 110624 | tf_op jit(solution)/shard_map/ppermute | solution.py:525
  42.4 2.4 %planes.7.refs_12_ = bf16[16,48,768]{2,1,0:T(8,128)(2,1)} custom-call(bf16[96,576]{1,0:T(8,128)(2,1)S(1)} %reshape.315.refs_0_, bf16[96,576]{1,0:T(8,128)(2,1)S(1)} %collective-permute-done.refs_1_, bf16[96,576]{1,0:T(8,128)(2,1)S(1)} %collective-permute-done.8.refs_2_.refs_7_, ...), custom_call_target="tpu_custom_call", output_to_operand_aliasing={{}: (7, {})} | custom-call | flops 60000000 | bytes 100000 | tf_op jit(solution)/shard_map/planes/pallas_call | solution.py:209
  45.5 0.6 copy-done.11
  46.1 3.0 %block.1 = bf16[16,48,768]{2,1,0:T(8,128)(2,1)} custom-call(bf16[96,576]{1,0:T(8,128)(2,1)} %copy-done.3, bf16[96,576]{1,0:T(8,128)(2,1)} %copy-done.4, bf16[96,576]{1,0:T(8,128)(2,1)} %copy-done.8, bf16[96,576]{1,0:T(8,128)(2,1)} %copy-done.9, bf16[96,576]{1,0:T(8,128)(2,1)} %copy-done.13, ...), custom_call_target="tpu_custom_call", output_to_operand_aliasing={{}: (12, {})} | custom-call | flops 10000000 | bytes 100000 | tf_op jit(solution)/shard_map/block/pallas_call | solution.py:465
  49.1 7.3 %all-to-all-start.1 = ((bf16[16,48,768]{2,1,0:T(8,128)(2,1)}), bf16[16,48,768]{2,1,0:T(8,128)(2,1)S(1)}, u32[]{:S(2)}, u32[]{:S(2)}) async-start(bf16[16,48,768]{2,1,0:T(8,128)(2,1)} %block.1), calls=%async_computation.1 | async-start | bytes 2359296 | tf_op jit(solution)/shard_map/all_to_all | solution.py:549
  56.7 6.1 %first_points.1 = (f32[8,2048]{1,0:T(8,128)S(1)}, bf16[8,2048]{1,0:T(8,128)(2,1)S(1)}) custom-call(bf16[16,48,768]{2,1,0:T(8,128)(2,1)S(1)} %all-to-all-done.t_ref.refs_11_, bf16[384,384]{1,0:T(8,128)(2,1)S(1)} %copy-done.7, s32[1,2048]{1,0:T(1,128)S(1)} %bitcast.39, s32[1,2048]{1,0:T(1,128)S(1)} %bitcast.37, s32[1,2048]{1,0:T(1,128)S(1)} %get-tuple-element.29.far_ref, ...), custom_call_target="tpu_custom_call" | custom-call | flops 100000000 | bytes 100000 | tf_op jit(solution)/shard_map/first_points/pallas_call | solution.py:315
  62.8 10.8 %all-to-all-done.1.t_ref = bf16[16,48,768]{2,1,0:T(8,128)(2,1)S(1)} async-done(((bf16[16,48,768]{2,1,0:T(8,128)(2,1)}), bf16[16,48,768]{2,1,0:T(8,128)(2,1)S(1)}, u32[]{:S(2)}, u32[]{:S(2)}) %all-to-all-start.1) | async-done | bytes 1179680 | tf_op jit(solution)/shard_map/all_to_all | solution.py:549
  73.6 3.4 %second_far_points.1 = (bf16[16,2048]{1,0:T(8,128)(2,1)S(1)}, bf16[768,768]{1,0:T(8,128)(2,1)S(1)}, f32[16,128]{1,0:T(8,128)S(1)}) custom-call(bf16[16,48,768]{2,1,0:T(8,128)(2,1)S(1)} %all-to-all-done.1.t_ref, bf16[384,384]{1,0:T(8,128)(2,1)S(1)} %copy-done.7, s32[1,2048]{1,0:T(1,128)S(1)} %get-tuple-element.29.far_ref, ...), custom_call_target="tpu_custom_call" | custom-call | flops 100000000 | bytes 100000 | tf_op jit(solution)/shard_map/second_far_points/pallas_call | solution.py:331
  77.0 2.5 %collective-permute-start.9 = (bf16[16,2048]{1,0:T(8,128)(2,1)S(1)}, bf16[16,2048]{1,0:T(8,128)(2,1)S(1)}, u32[]{:S(2)}, u32[]{:S(2)}) collective-permute-start(bf16[16,2048]{1,0:T(8,128)(2,1)S(1)} %get-tuple-element.17), channel_id=1, source_target_pairs={{0,15},{1,14},{2,13},{3,12},{4,11},{5,10},{6,9},{7,8},{8,7},{9,6},... | collective-permute-start | bytes 196616 | tf_op jit(solution)/shard_map/ppermute | solution.py:576
  79.5 2.8 %second_own_points.1.own1_ref = f32[8,2048]{1,0:T(8,128)S(1)} custom-call(bf16[768,768]{1,0:T(8,128)(2,1)S(1)} %get-tuple-element.16.low, s32[1,2048]{1,0:T(1,128)S(1)} %bitcast.40, s32[1,2048]{1,0:T(1,128)S(1)} %bitcast.38), custom_call_target="tpu_custom_call" | custom-call | flops 2400000000 | bytes 1300000 | tf_op jit(solution)/shard_map/second_own_points/pallas_call | solution.py:347
  82.3 2.9 %collective-permute-done.9.far_ref = bf16[16,2048]{1,0:T(8,128)(2,1)S(1)} collective-permute-done((bf16[16,2048]{1,0:T(8,128)(2,1)S(1)}, bf16[16,2048]{1,0:T(8,128)(2,1)S(1)}, u32[]{:S(2)}, u32[]{:S(2)}) %collective-permute-start.9) | collective-permute-done | bytes 65568 | tf_op jit(solution)/shard_map/ppermute | solution.py:576
  85.2 0.8 split.1
  86.0 5.4 %all-to-all-start.2 = ((bf16[16,48,128]{2,1,0:T(8,128)(2,1)}), bf16[16,48,128]{2,1,0:T(8,128)(2,1)S(1)}, u32[]{:S(2)}, u32[]{:S(2)}) async-start(bf16[16,48,128]{2,1,0:T(8,128)(2,1)} %split.1), calls=%async_computation.2 | async-start | bytes 393216 | tf_op jit(solution)/shard_map/all_to_all | solution.py:579
  91.5 10.8 %all-to-all-done.2.pairs_ref = bf16[16,48,128]{2,1,0:T(8,128)(2,1)S(1)} async-done(((bf16[16,48,128]{2,1,0:T(8,128)(2,1)}), bf16[16,48,128]{2,1,0:T(8,128)(2,1)S(1)}, u32[]{:S(2)}, u32[]{:S(2)}) %all-to-all-start.2) | async-done | bytes 196640 | tf_op jit(solution)/shard_map/all_to_all | solution.py:579
  102.3 1.0 pair_sum.1
  (81 shorter events, 3.2 us)
Async XLA Ops:
  0.0 13.8 %copy-start = (bf16[576,1536]{1,0:T(8,128)(2,1)S(1)}, bf16[576,1536]{1,0:T(8,128)(2,1)}, u32[]{:S(2)}) copy-start(bf16[576,1536]{1,0:T(8,128)(2,1)} %constant.131.clone.refs_4_) | copy-start | bytes 5308420
  0.0 13.8 %copy-start.5 = (f32[2,16,768]{2,1,0:T(8,128)S(1)}, f32[2,16,768]{2,1,0:T(8,128)}, u32[]{:S(2)}) copy-start(f32[2,16,768]{2,1,0:T(8,128)} %constant.132.clone.refs_5_) | copy-start | bytes 294916
  0.0 10.5 %copy-start.19 = (s32[2048]{0:T(1024)S(1)}, s32[2048]{0:T(1024)}, u32[]{:S(2)}) copy-start(s32[2048]{0:T(1024)} %param.23) | copy-start | bytes 24580
  1.5 15.6 %copy-start.8 = (bf16[96,576]{1,0:T(8,128)(2,1)}, bf16[96,576]{1,0:T(8,128)(2,1)S(1)}, u32[]{:S(2)}) copy-start(bf16[96,576]{1,0:T(8,128)(2,1)S(1)} %reshape.317.refs_2_) | copy-start | bytes 331780
  1.5 11.5 %collective-permute-start.2 = (bf16[96,576]{1,0:T(8,128)(2,1)S(1)}, bf16[96,576]{1,0:T(8,128)(2,1)S(1)}, u32[]{:S(2)}, u32[]{:S(2)}) collective-permute-start(bf16[96,576]{1,0:T(8,128)(2,1)S(1)} %reshape.317.refs_2_), channel_id=1, source_target_pairs={{0,32},{32,64},{64,96},{96,128},{128,160},{160,192},{192,224},{224... | collective-permute-start | bytes 331784 | tf_op jit(solution)/shard_map/ppermute | solution.py:525
  3.5 13.7 %collective-permute-start.1 = (bf16[96,576]{1,0:T(8,128)(2,1)S(1)}, bf16[96,576]{1,0:T(8,128)(2,1)S(1)}, u32[]{:S(2)}, u32[]{:S(2)}) collective-permute-start(bf16[96,576]{1,0:T(8,128)(2,1)S(1)} %reshape.317.refs_2_), channel_id=1, source_target_pairs={{0,224},{32,0},{64,32},{96,64},{128,96},{160,128},{192,160},{224,1... | collective-permute-start | bytes 331784 | tf_op jit(solution)/shard_map/ppermute | solution.py:527
  8.8 33.6 %copy-start.3 = (bf16[96,576]{1,0:T(8,128)(2,1)}, bf16[96,576]{1,0:T(8,128)(2,1)S(1)}, u32[]{:S(2)}) copy-start(bf16[96,576]{1,0:T(8,128)(2,1)S(1)} %reshape.315.refs_0_) | copy-start | bytes 331780
  8.8 5.0 %collective-permute-start = (bf16[96,576]{1,0:T(8,128)(2,1)S(1)}, bf16[96,576]{1,0:T(8,128)(2,1)S(1)}, u32[]{:S(2)}, u32[]{:S(2)}) collective-permute-start(bf16[96,576]{1,0:T(8,128)(2,1)S(1)} %reshape.315.refs_0_), channel_id=1, source_target_pairs={{0,16},{16,0},{1,17},{17,1},{2,18},{18,2},{3,19},{19,3},{4,20},{20... | collective-permute-start | bytes 331784 | tf_op jit(solution)/shard_map/ppermute | solution.py:522
  10.5 6.7 %collective-permute-start.4 = (s32[2048]{0:T(1024)S(1)}, s32[2048]{0:T(1024)S(1)}, u32[]{:S(2)}, u32[]{:S(2)}) collective-permute-start(s32[2048]{0:T(1024)S(1)} %copy-done.19), channel_id=1, source_target_pairs={{0,15},{1,14},{2,13},{3,12},{4,11},{5,10},{6,9},{7,8},{8,7},{9,6},... | collective-permute-start | bytes 24584 | tf_op jit(solution)/shard_map/ppermute | solution.py:530
  12.9 7.2 %collective-permute-start.3 = (bf16[96,576]{1,0:T(8,128)(2,1)S(1)}, bf16[96,576]{1,0:T(8,128)(2,1)S(1)}, u32[]{:S(2)}, u32[]{:S(2)}) collective-permute-start(bf16[96,576]{1,0:T(8,128)(2,1)S(1)} %collective-permute-done.2.refs_3_), channel_id=1, source_target_pairs={{0,32},{32,64},{64,96},{96,128},{128,160},{160,192},{192,224},{224... | collective-permute-start | bytes 331784 | tf_op jit(solution)/shard_map/ppermute | solution.py:525
  14.7 27.7 %copy-start.4 = (bf16[96,576]{1,0:T(8,128)(2,1)}, bf16[96,576]{1,0:T(8,128)(2,1)S(1)}, u32[]{:S(2)}) copy-start(bf16[96,576]{1,0:T(8,128)(2,1)S(1)} %collective-permute-done.refs_1_) | copy-start | bytes 331780
  14.7 5.4 %copy-start.2 = (bf16[384,384]{1,0:T(8,128)(2,1)S(1)}, bf16[384,384]{1,0:T(8,128)(2,1)}, u32[]{:S(2)}) copy-start(bf16[384,384]{1,0:T(8,128)(2,1)} %constant.133.clone.refs_6_) | copy-start | bytes 884740
  17.2 5.5 %copy-start.12 = (bf16[96,576]{1,0:T(8,128)(2,1)}, bf16[96,576]{1,0:T(8,128)(2,1)S(1)}, u32[]{:S(2)}) copy-start(bf16[96,576]{1,0:T(8,128)(2,1)S(1)} %collective-permute-done.1.refs_2_.refs_9_) | copy-start | bytes 331780
  22.5 6.5 %copy-start.25 = (f32[4]{0:T(128)S(1)}, f32[4]{0:T(128)}, u32[]{:S(2)}) copy-start(f32[4]{0:T(128)} %param.22) | copy-start | bytes 52
  22.5 6.6 %copy-start.26 = (pred[8,1]{0,1:T(4,128)(4,1)S(1)}, pred[8,1]{0,1:T(4,128)(4,1)}, u32[]{:S(2)}) copy-start(pred[8,1]{0,1:T(4,128)(4,1)} %constant.134.clone) | copy-start | bytes 28
  22.5 6.6 %copy-start.20 = (f32[8,128]{1,0:T(8,128)S(1)}, f32[8,128]{1,0:T(8,128)}, u32[]{:S(2)}) copy-start(f32[8,128]{1,0:T(8,128)} %constant.135.clone) | copy-start | bytes 12292
  22.6 8.7 %copy-start.18 = (f32[4096]{0:T(1024)S(1)}, f32[4096]{0:T(1024)}, u32[]{:S(2)}) copy-start(f32[4096]{0:T(1024)} %param.20) | copy-start | bytes 49156
  22.6 8.7 %copy-start.23 = (s32[16]{0:T(128)S(1)}, s32[16]{0:T(128)}, u32[]{:S(2)}) copy-start(s32[16]{0:T(128)} %param.19) | copy-start | bytes 196
  22.6 14.3 %copy-start.21 = (pred[256,16]{0,1:T(8,128)(4,1)S(1)}, pred[256,16]{0,1:T(8,128)(4,1)}, u32[]{:S(2)}) copy-start(pred[256,16]{0,1:T(8,128)(4,1)} %constant.136.clone) | copy-start | bytes 12292
  22.6 14.3 %copy-start.22 = (pred[256,16]{0,1:T(8,128)(4,1)S(1)}, pred[256,16]{0,1:T(8,128)(4,1)}, u32[]{:S(2)}) copy-start(pred[256,16]{0,1:T(8,128)(4,1)} %constant.137.clone) | copy-start | bytes 12292
  22.6 14.3 %copy-start.24 = (f32[16]{0:T(128)S(1)}, f32[16]{0:T(128)}, u32[]{:S(2)}) copy-start(f32[16]{0:T(128)} %param.21) | copy-start | bytes 196
  22.6 23.5 %all-to-all-start = ((bf16[16,48,768]{2,1,0:T(8,128)(2,1)}), bf16[16,48,768]{2,1,0:T(8,128)(2,1)S(1)}, u32[]{:S(2)}, u32[]{:S(2)}) async-start(bf16[16,48,768]{2,1,0:T(8,128)(2,1)} %get-tuple-element.12), calls=%async_computation | async-start | bytes 2359296 | tf_op jit(solution)/shard_map/all_to_all | solution.py:536
  29.2 5.6 %collective-permute-start.7 = (bf16[96,576]{1,0:T(8,128)(2,1)}, bf16[96,576]{1,0:T(8,128)(2,1)S(1)}, u32[]{:S(2)}, u32[]{:S(2)}) collective-permute-start(bf16[96,576]{1,0:T(8,128)(2,1)} %copy-done.12), channel_id=1, source_target_pairs={{0,224},{32,0},{64,32},{96,64},{128,96},{160,128},{192,160},{224,1... | collective-permute-start | bytes 331784 | tf_op jit(solution)/shard_map/ppermute | solution.py:527
  29.5 6.8 %collective-permute-start.5 = (bf16[96,576]{1,0:T(8,128)(2,1)}, bf16[96,576]{1,0:T(8,128)(2,1)S(1)}, u32[]{:S(2)}, u32[]{:S(2)}) collective-permute-start(bf16[96,576]{1,0:T(8,128)(2,1)} %copy-done.13), channel_id=1, source_target_pairs={{0,32},{32,64},{64,96},{96,128},{128,160},{160,192},{192,224},{224... | collective-permute-start | bytes 331784 | tf_op jit(solution)/shard_map/ppermute | solution.py:525
  34.8 5.4 %collective-permute-start.8 = (bf16[96,576]{1,0:T(8,128)(2,1)S(1)}, bf16[96,576]{1,0:T(8,128)(2,1)S(1)}, u32[]{:S(2)}, u32[]{:S(2)}) collective-permute-start(bf16[96,576]{1,0:T(8,128)(2,1)S(1)} %collective-permute-done.7.refs_2_.refs_8_), channel_id=1, source_target_pairs={{0,224},{32,0},{64,32},{96,64},{128,96},{160,128},{192,160},{224,1... | collective-permute-start | bytes 331784 | tf_op jit(solution)/shard_map/ppermute | solution.py:527
  36.3 6.1 %collective-permute-start.6 = (bf16[96,576]{1,0:T(8,128)(2,1)S(1)}, bf16[96,576]{1,0:T(8,128)(2,1)S(1)}, u32[]{:S(2)}, u32[]{:S(2)}) collective-permute-start(bf16[96,576]{1,0:T(8,128)(2,1)S(1)} %collective-permute-done.5.refs_3_.refs_5_), channel_id=1, source_target_pairs={{0,32},{32,64},{64,96},{96,128},{128,160},{160,192},{192,224},{224... | collective-permute-start | bytes 331784 | tf_op jit(solution)/shard_map/ppermute | solution.py:525
  49.1 7.4 %copy-start.17 = (s32[16,128]{1,0:T(8,128)S(1)}, s32[16,128]{1,0:T(8,128)}, u32[]{:S(2)}) copy-start(s32[16,128]{1,0:T(8,128)} %get-tuple-element.13) | copy-start | bytes 24580
  49.1 7.6 %copy-start.7 = (bf16[384,384]{1,0:T(8,128)(2,1)S(1)}, bf16[384,384]{1,0:T(8,128)(2,1)}, u32[]{:S(2)}) copy-start(bf16[384,384]{1,0:T(8,128)(2,1)} %constant.138.clone.x_ref) | copy-start | bytes 884740
  49.1 24.5 %all-to-all-start.1 = ((bf16[16,48,768]{2,1,0:T(8,128)(2,1)}), bf16[16,48,768]{2,1,0:T(8,128)(2,1)S(1)}, u32[]{:S(2)}, u32[]{:S(2)}) async-start(bf16[16,48,768]{2,1,0:T(8,128)(2,1)} %block.1), calls=%async_computation.1 | async-start | bytes 2359296 | tf_op jit(solution)/shard_map/all_to_all | solution.py:549
  77.0 8.1 %collective-permute-start.9 = (bf16[16,2048]{1,0:T(8,128)(2,1)S(1)}, bf16[16,2048]{1,0:T(8,128)(2,1)S(1)}, u32[]{:S(2)}, u32[]{:S(2)}) collective-permute-start(bf16[16,2048]{1,0:T(8,128)(2,1)S(1)} %get-tuple-element.17), channel_id=1, source_target_pairs={{0,15},{1,14},{2,13},{3,12},{4,11},{5,10},{6,9},{7,8},{8,7},{9,6},... | collective-permute-start | bytes 196616 | tf_op jit(solution)/shard_map/ppermute | solution.py:576
  79.5 22.8 %copy-start.16 = (bf16[2,128,128]{2,1,0:T(8,128)(2,1)S(1)}, bf16[2,128,128]{2,1,0:T(8,128)(2,1)}, u32[]{:S(2)}) copy-start(bf16[2,128,128]{2,1,0:T(8,128)(2,1)} %constant.139.clone.column_ref) | copy-start | bytes 196612
  86.0 16.3 %all-to-all-start.2 = ((bf16[16,48,128]{2,1,0:T(8,128)(2,1)}), bf16[16,48,128]{2,1,0:T(8,128)(2,1)S(1)}, u32[]{:S(2)}, u32[]{:S(2)}) async-start(bf16[16,48,128]{2,1,0:T(8,128)(2,1)} %split.1), calls=%async_computation.2 | async-start | bytes 393216 | tf_op jit(solution)/shard_map/all_to_all | solution.py:579
  (8 other events, 19.1 us)

commit v11 on v10

--- a/solution.py
+++ b/solution.py
@@ -130,17 +130,17 @@
 PLANES_FLOPS = (30_000_000, 30_000_000, 30_000_000, 30_000_000)
 
 
-def plane_kernel(*refs, items, first, through, chained, marked):
+def plane_kernel(*refs, items, first, through, chained, marked, passing):
     refs = list(refs)
     take = lambda count: [refs.pop(0) for _ in range(count)]
     v0_ref, v1_ref = take(2)
     waves_c = take(items)
     lane_ref, twiddle_ref, row_ref = take(3)
     marks = take(marked)
-    kept = take(through)
+    kept = waves_c if passing else take(through)
     take(chained)
     (out_ref,) = take(1)
-    kept_out = take(through)
+    kept_out = take(len(kept))
     low_ref, slab_ref, slab_sems, keep_sems = refs
     moves = [
         pltpu.make_async_copy(source, target, keep_sems.at[i])
@@ -190,9 +190,10 @@
         move.wait()
 
 
-def planes_of(group, v, c, marks=(), through=(), after=(), buffer=()):
+def planes_of(group, v, c, marks=(), through=(), after=(), buffer=(), passing=False):
     slots = GROUPS[group]
     items = len(slots)
+    outputs = [c[slot] for slot in slots] if passing else through
     first = group % 2 * items * 2 * X6
     inputs = (
         *v,
@@ -214,21 +215,22 @@
             through=len(through),
             chained=len(after) + len(buffer),
             marked=len(marks),
+            passing=passing,
         ),
         out_shape=[
             pltpu.HBM((SLABS, ROWS, WIDE), BF16),
-            *(pltpu.HBM(x.shape, x.dtype) for x in through),
+            *(pltpu.HBM(x.shape, x.dtype) for x in outputs),
         ],
         in_specs=[VMEM] * (len(inputs) - outside)
         + [ANY] * (len(through) + len(after))
         + [HBM] * len(buffer),
-        out_specs=[HBM] * (1 + len(through)),
+        out_specs=[HBM] * (1 + len(outputs)),
         input_output_aliases={len(inputs) - 1: 0} if buffer else {},
         scratch_shapes=[
             pltpu.VMEM((2 * items * X6 * Y16, WIDE), BF16),
             pltpu.VMEM((SLABS, items * 2 * X6, WIDE), BF16),
             pltpu.SemaphoreType.DMA((SLAB_CUTS,)),
-            pltpu.SemaphoreType.DMA((max(len(through), 1),)),
+            pltpu.SemaphoreType.DMA((max(len(outputs), 1),)),
         ],
         compiler_params=pltpu.CompilerParams(vmem_limit_bytes=16 << 20),
         cost_estimate=pl.CostEstimate(
@@ -535,7 +537,10 @@
     planes0, far_cell = planes_of(1, v, c, through=(far_cell,), buffer=(planes0,))
     sent0 = lax.all_to_all(planes0, COL, 0, 0, tiled=True)
     (planes1,) = planes_of(2, v, c)
-    (planes1,) = planes_of(3, v, c, buffer=(planes1,))
+    last = GROUPS[3]
+    planes1, *passed = planes_of(3, v, c, buffer=(planes1,), passing=True)
+    for slot, wave in zip(last, passed):
+        c[slot] = wave
 
     group = np.arange(128) // NBLOCK - 2
     used = (group >= 0) & (group < 4)

time: 105 us -> 104 us (level)
  waiting for transfers between devices: 33.8 us -> 35.1 us
  local copies, waits for them, and re-layouts: 6.2 us -> 4.92 us
  starting transfers between devices: 35 us -> 33.8 us
    unnamed x54 -> x50, local copies, waits for them, and re-layouts: 3.26 us -> 1.97 us
    all_to_all x1, waiting for transfers between devices: 0.04 us -> 1.33 us  [per_device(): sent0 = lax.all_to_all(planes0, COL, 0, 0, tiled=True)]
    all_to_all x1, starting transfers between devices: 7.32 us -> 6.04 us  [per_device(): sent1 = lax.all_to_all(planes1, COL, 0, 0, tiled=True)]
  transfers between devices with their start and end apart: 13 -> 13, of which waited for: 7 -> 8; matrix products, arithmetic and copies ran while one was open for 2% -> 2% of each run, Pallas kernels for 15% -> 16%
where the time goes in v11:
time: 104 us; the launch traced here: 102 us
  waiting for transfers between devices  35.1 us (34%)
  starting transfers between devices  33.8 us (32%)
  Pallas kernels  26.4 us (25%)
  local copies, waits for them, and re-layouts  4.92 us (5%)
  between operations  1.05 us (1%)
    all_to_all x1, waiting for transfers between devices, per_device(): sent1 = lax.all_to_all(planes1, COL, 0, 0, tiled=True)  10.8 us
    all_to_all x1, waiting for transfers between devices, per_device(): pairs = lax.all_to_all(pairs, BAND, 0, 0, tiled=True)  10.8 us
    pallas_call x4, Pallas kernels, planes_of(): pl.pallas_call(functools.partial(plane_kernel, items=items, first=first,...  9.46 us
    all_to_all x1, starting transfers between devices, per_device(): sent0 = lax.all_to_all(planes0, COL, 0, 0, tiled=True)  6.33 us
    pallas_call x1, Pallas kernels, first_points(): pl.pallas_call(first_kernel, out_shape=(jax.ShapeDtypeStruct((FIRST, G_DE...  6.11 us
    all_to_all x1, starting transfers between devices, per_device(): sent1 = lax.all_to_all(planes1, COL, 0, 0, tiled=True)  6.04 us
    ppermute x3, starting transfers between devices, per_device(): c[8 - slot] = lax.ppermute(c[(9 - slot) % 8], 'z', behind)  5.8 us
    all_to_all x1, starting transfers between devices, per_device(): pairs = lax.all_to_all(pairs, BAND, 0, 0, tiled=True)  5.37 us
  transfers between devices with their start and end apart: 13, of which 8 were waited for; matrix products, arithmetic and copies ran while one was open for 2% of the time, Pallas kernels for 16%

profile of v11, /device:TPU:6, one launch (start us, length us, event | category | flops | bytes accessed | tf_op | source)
XLA Modules:
  0.0 102.0 jit_solution(16674089855586030645)
XLA Ops:
  0.0 1.2 %reshape.316 = bf16[6,6,16,96]{3,2,1,0:T(8,128)(2,1)S(1)} reshape(bf16[1,6,9216]{2,1,0:T(8,128)(2,1)} %param.18) | data formatting | bytes 221184 | tf_op jit(solution)/shard_map/reshape | solution.py:506
  1.5 2.0 %collective-permute-start.2 = (bf16[96,576]{1,0:T(8,128)(2,1)S(1)}, bf16[96,576]{1,0:T(8,128)(2,1)S(1)}, u32[]{:S(2)}, u32[]{:S(2)}) collective-permute-start(bf16[96,576]{1,0:T(8,128)(2,1)S(1)} %reshape.317.refs_2_), channel_id=1, source_target_pairs={{0,32},{32,64},{64,96},{96,128},{128,160},{160,192},{192,224},{224... | collective-permute-start | bytes 331784 | tf_op jit(solution)/shard_map/ppermute | solution.py:527
  3.5 4.0 %collective-permute-start.1 = (bf16[96,576]{1,0:T(8,128)(2,1)S(1)}, bf16[96,576]{1,0:T(8,128)(2,1)S(1)}, u32[]{:S(2)}, u32[]{:S(2)}) collective-permute-start(bf16[96,576]{1,0:T(8,128)(2,1)S(1)} %reshape.317.refs_2_), channel_id=1, source_target_pairs={{0,224},{32,0},{64,32},{96,64},{128,96},{160,128},{192,160},{224,1... | collective-permute-start | bytes 331784 | tf_op jit(solution)/shard_map/ppermute | solution.py:529
  7.5 1.1 %reshape.314 = bf16[6,6,16,96]{3,2,1,0:T(8,128)(2,1)S(1)} reshape(bf16[1,6,9216]{2,1,0:T(8,128)(2,1)} %param.17) | data formatting | bytes 221184 | tf_op jit(solution)/shard_map/reshape | solution.py:506
  8.8 1.7 %collective-permute-start = (bf16[96,576]{1,0:T(8,128)(2,1)S(1)}, bf16[96,576]{1,0:T(8,128)(2,1)S(1)}, u32[]{:S(2)}, u32[]{:S(2)}) collective-permute-start(bf16[96,576]{1,0:T(8,128)(2,1)S(1)} %reshape.315.refs_0_), channel_id=1, source_target_pairs={{0,16},{16,0},{1,17},{17,1},{2,18},{18,2},{3,19},{19,3},{4,20},{20... | collective-permute-start | bytes 331784 | tf_op jit(solution)/shard_map/ppermute | solution.py:524
  10.5 1.7 %collective-permute-start.4 = (s32[2048]{0:T(1024)S(1)}, s32[2048]{0:T(1024)S(1)}, u32[]{:S(2)}, u32[]{:S(2)}) collective-permute-start(s32[2048]{0:T(1024)S(1)} %copy-done.17), channel_id=1, source_target_pairs={{0,15},{1,14},{2,13},{3,12},{4,11},{5,10},{6,9},{7,8},{8,7},{9,6},... | collective-permute-start | bytes 24584 | tf_op jit(solution)/shard_map/ppermute | solution.py:532
  13.1 0.7 collective-permute-done.refs_1_
  13.8 1.0 copy-done.1
  14.7 2.4 %planes.4.refs_8_ = bf16[16,48,768]{2,1,0:T(8,128)(2,1)} custom-call(bf16[96,576]{1,0:T(8,128)(2,1)S(1)} %reshape.315.refs_0_, bf16[96,576]{1,0:T(8,128)(2,1)S(1)} %collective-permute-done.refs_1_, bf16[96,576]{1,0:T(8,128)(2,1)S(1)} %reshape.317.refs_2_, bf16[96,576]{1,0:T(8,128)(2,1)S(1)} %collective-permute-done.2.refs_3_, bf16[576,1536]{1,0:T(8,128)(2,1)S(1)} %copy-done, ...), custom_call_target="tpu_custom_call" | custom-call | flops 60000000 | bytes 100000 | tf_op jit(solution)/shard_map/planes/pallas_call | solution.py:210
  17.2 3.0 %collective-permute-done.3.refs_3_.refs_4_ = bf16[96,576]{1,0:T(8,128)(2,1)S(1)} collective-permute-done((bf16[96,576]{1,0:T(8,128)(2,1)S(1)}, bf16[96,576]{1,0:T(8,128)(2,1)S(1)}, u32[]{:S(2)}, u32[]{:S(2)}) %collective-permute-start.3) | collective-permute-done | bytes 110624 | tf_op jit(solution)/shard_map/ppermute | solution.py:527
  20.2 2.4 %planes.5 = (bf16[16,48,768]{2,1,0:T(8,128)(2,1)}, s32[16,128]{1,0:T(8,128)}) custom-call(bf16[96,576]{1,0:T(8,128)(2,1)S(1)} %reshape.315.refs_0_, bf16[96,576]{1,0:T(8,128)(2,1)S(1)} %collective-permute-done.refs_1_, bf16[96,576]{1,0:T(8,128)(2,1)S(1)} %collective-permute-done.1.refs_2_.refs_9_, ...), custom_call_target="tpu_custom_call", output_to_operand_aliasing={{0}: (8, {})} | custom-call | flops 60000000 | bytes 100000 | tf_op jit(solution)/shard_map/planes/pallas_call | solution.py:210
  22.7 6.3 %all-to-all-start = ((bf16[16,48,768]{2,1,0:T(8,128)(2,1)}), bf16[16,48,768]{2,1,0:T(8,128)(2,1)S(1)}, u32[]{:S(2)}, u32[]{:S(2)}) async-start(bf16[16,48,768]{2,1,0:T(8,128)(2,1)} %get-tuple-element.15), calls=%async_computation | async-start | bytes 2359296 | tf_op jit(solution)/shard_map/all_to_all | solution.py:538
  29.5 1.8 %collective-permute-start.5 = (bf16[96,576]{1,0:T(8,128)(2,1)}, bf16[96,576]{1,0:T(8,128)(2,1)S(1)}, u32[]{:S(2)}, u32[]{:S(2)}) collective-permute-start(bf16[96,576]{1,0:T(8,128)(2,1)} %copy-done.11), channel_id=1, source_target_pairs={{0,32},{32,64},{64,96},{96,128},{128,160},{160,192},{192,224},{224... | collective-permute-start | bytes 331784 | tf_op jit(solution)/shard_map/ppermute | solution.py:527
  31.5 3.3 %collective-permute-done.6.refs_2_.refs_8_ = bf16[96,576]{1,0:T(8,128)(2,1)S(1)} collective-permute-done((bf16[96,576]{1,0:T(8,128)(2,1)}, bf16[96,576]{1,0:T(8,128)(2,1)S(1)}, u32[]{:S(2)}, u32[]{:S(2)}) %collective-permute-start.6) | collective-permute-done | bytes 110624 | tf_op jit(solution)/shard_map/ppermute | solution.py:529
  34.9 1.5 %collective-permute-start.7 = (bf16[96,576]{1,0:T(8,128)(2,1)S(1)}, bf16[96,576]{1,0:T(8,128)(2,1)S(1)}, u32[]{:S(2)}, u32[]{:S(2)}) collective-permute-start(bf16[96,576]{1,0:T(8,128)(2,1)S(1)} %collective-permute-done.6.refs_2_.refs_8_), channel_id=1, source_target_pairs={{0,224},{32,0},{64,32},{96,64},{128,96},{160,128},{192,160},{224,1... | collective-permute-start | bytes 331784 | tf_op jit(solution)/shard_map/ppermute | solution.py:529
  37.0 0.9 copy-done.6
  37.9 2.4 %planes.6.refs_7_ = bf16[16,48,768]{2,1,0:T(8,128)(2,1)} custom-call(bf16[96,576]{1,0:T(8,128)(2,1)S(1)} %reshape.315.refs_0_, bf16[96,576]{1,0:T(8,128)(2,1)S(1)} %collective-permute-done.refs_1_, bf16[96,576]{1,0:T(8,128)(2,1)S(1)} %collective-permute-done.6.refs_2_.refs_8_, bf16[96,576]{1,0:T(8,128)(2,1)S(1)} %collective-permute-done.5.refs_3_.refs_5_, ...), custom_call_target="tpu_custom_call" | custom-call | flops 60000000 | bytes 100000 | tf_op jit(solution)/shard_map/planes/pallas_call | solution.py:210
  40.3 2.2 %collective-permute-done.8.refs_3_ = bf16[96,576]{1,0:T(8,128)(2,1)S(1)} collective-permute-done((bf16[96,576]{1,0:T(8,128)(2,1)S(1)}, bf16[96,576]{1,0:T(8,128)(2,1)S(1)}, u32[]{:S(2)}, u32[]{:S(2)}) %collective-permute-start.8) | collective-permute-done | bytes 110624 | tf_op jit(solution)/shard_map/ppermute | solution.py:527
  42.5 2.4 %planes.7 = (bf16[16,48,768]{2,1,0:T(8,128)(2,1)}, bf16[96,576]{1,0:T(8,128)(2,1)}, bf16[96,576]{1,0:T(8,128)(2,1)}) custom-call(bf16[96,576]{1,0:T(8,128)(2,1)S(1)} %reshape.315.refs_0_, bf16[96,576]{1,0:T(8,128)(2,1)S(1)} %collective-permute-done.refs_1_, bf16[96,576]{1,0:T(8,128)(2,1)S(1)} %collective-permute-done.7.refs_2_, ...), custom_call_target="tpu_custom_call", output_to_operand_aliasing={{0}: (7, {})} | custom-call | flops 60000000 | bytes 100000 | tf_op jit(solution)/shard_map/planes/pallas_call | solution.py:210
  44.8 1.3 %all-to-all-done.t_ref.refs_11_ = bf16[16,48,768]{2,1,0:T(8,128)(2,1)S(1)} async-done(((bf16[16,48,768]{2,1,0:T(8,128)(2,1)}), bf16[16,48,768]{2,1,0:T(8,128)(2,1)S(1)}, u32[]{:S(2)}, u32[]{:S(2)}) %all-to-all-start) | async-done | bytes 1179680 | tf_op jit(solution)/shard_map/all_to_all | solution.py:538
  46.2 3.0 %block.1 = bf16[16,48,768]{2,1,0:T(8,128)(2,1)} custom-call(bf16[96,576]{1,0:T(8,128)(2,1)} %copy-done.3, bf16[96,576]{1,0:T(8,128)(2,1)} %copy-done.4, bf16[96,576]{1,0:T(8,128)(2,1)} %copy-done.8, bf16[96,576]{1,0:T(8,128)(2,1)} %copy-done.9, bf16[96,576]{1,0:T(8,128)(2,1)} %copy-done.11, ...), custom_call_target="tpu_custom_call", output_to_operand_aliasing={{}: (12, {})} | custom-call | flops 10000000 | bytes 100000 | tf_op jit(solution)/shard_map/block/pallas_call | solution.py:467
  49.2 6.0 %all-to-all-start.1 = ((bf16[16,48,768]{2,1,0:T(8,128)(2,1)}), bf16[16,48,768]{2,1,0:T(8,128)(2,1)S(1)}, u32[]{:S(2)}, u32[]{:S(2)}) async-start(bf16[16,48,768]{2,1,0:T(8,128)(2,1)} %block.1), calls=%async_computation.1 | async-start | bytes 2359296 | tf_op jit(solution)/shard_map/all_to_all | solution.py:554
  55.4 6.1 %first_points.1 = (f32[8,2048]{1,0:T(8,128)S(1)}, bf16[8,2048]{1,0:T(8,128)(2,1)S(1)}) custom-call(bf16[16,48,768]{2,1,0:T(8,128)(2,1)S(1)} %all-to-all-done.t_ref.refs_11_, bf16[384,384]{1,0:T(8,128)(2,1)S(1)} %copy-done.7, s32[1,2048]{1,0:T(1,128)S(1)} %bitcast.39, s32[1,2048]{1,0:T(1,128)S(1)} %bitcast.37, s32[1,2048]{1,0:T(1,128)S(1)} %get-tuple-element.35.far_ref, ...), custom_call_target="tpu_custom_call" | custom-call | flops 100000000 | bytes 100000 | tf_op jit(solution)/shard_map/first_points/pallas_call | solution.py:317
  61.6 10.8 %all-to-all-done.1.t_ref = bf16[16,48,768]{2,1,0:T(8,128)(2,1)S(1)} async-done(((bf16[16,48,768]{2,1,0:T(8,128)(2,1)}), bf16[16,48,768]{2,1,0:T(8,128)(2,1)S(1)}, u32[]{:S(2)}, u32[]{:S(2)}) %all-to-all-start.1) | async-done | bytes 1179680 | tf_op jit(solution)/shard_map/all_to_all | solution.py:554
  72.4 3.4 %second_far_points.1 = (bf16[16,2048]{1,0:T(8,128)(2,1)S(1)}, bf16[768,768]{1,0:T(8,128)(2,1)S(1)}, f32[16,128]{1,0:T(8,128)S(1)}) custom-call(bf16[16,48,768]{2,1,0:T(8,128)(2,1)S(1)} %all-to-all-done.1.t_ref, bf16[384,384]{1,0:T(8,128)(2,1)S(1)} %copy-done.7, s32[1,2048]{1,0:T(1,128)S(1)} %get-tuple-element.35.far_ref, ...), custom_call_target="tpu_custom_call" | custom-call | flops 100000000 | bytes 100000 | tf_op jit(solution)/shard_map/second_far_points/pallas_call | solution.py:333
  75.8 2.5 %collective-permute-start.9 = (bf16[16,2048]{1,0:T(8,128)(2,1)S(1)}, bf16[16,2048]{1,0:T(8,128)(2,1)S(1)}, u32[]{:S(2)}, u32[]{:S(2)}) collective-permute-start(bf16[16,2048]{1,0:T(8,128)(2,1)S(1)} %get-tuple-element.23), channel_id=1, source_target_pairs={{0,15},{1,14},{2,13},{3,12},{4,11},{5,10},{6,9},{7,8},{8,7},{9,6},... | collective-permute-start | bytes 196616 | tf_op jit(solution)/shard_map/ppermute | solution.py:581
  78.3 2.7 %second_own_points.1.own1_ref = f32[8,2048]{1,0:T(8,128)S(1)} custom-call(bf16[768,768]{1,0:T(8,128)(2,1)S(1)} %get-tuple-element.22.low, s32[1,2048]{1,0:T(1,128)S(1)} %bitcast.40, s32[1,2048]{1,0:T(1,128)S(1)} %bitcast.38), custom_call_target="tpu_custom_call" | custom-call | flops 2400000000 | bytes 1300000 | tf_op jit(solution)/shard_map/second_own_points/pallas_call | solution.py:349
  81.0 2.9 %collective-permute-done.9.far_ref = bf16[16,2048]{1,0:T(8,128)(2,1)S(1)} collective-permute-done((bf16[16,2048]{1,0:T(8,128)(2,1)S(1)}, bf16[16,2048]{1,0:T(8,128)(2,1)S(1)}, u32[]{:S(2)}, u32[]{:S(2)}) %collective-permute-start.9) | collective-permute-done | bytes 65568 | tf_op jit(solution)/shard_map/ppermute | solution.py:581
  83.9 0.8 split.1
  84.7 5.4 %all-to-all-start.2 = ((bf16[16,48,128]{2,1,0:T(8,128)(2,1)}), bf16[16,48,128]{2,1,0:T(8,128)(2,1)S(1)}, u32[]{:S(2)}, u32[]{:S(2)}) async-start(bf16[16,48,128]{2,1,0:T(8,128)(2,1)} %split.1), calls=%async_computation.2 | async-start | bytes 393216 | tf_op jit(solution)/shard_map/all_to_all | solution.py:584
  90.2 10.8 %all-to-all-done.2.pairs_ref = bf16[16,48,128]{2,1,0:T(8,128)(2,1)S(1)} async-done(((bf16[16,48,128]{2,1,0:T(8,128)(2,1)}), bf16[16,48,128]{2,1,0:T(8,128)(2,1)S(1)}, u32[]{:S(2)}, u32[]{:S(2)}) %all-to-all-start.2) | async-done | bytes 196640 | tf_op jit(solution)/shard_map/all_to_all | solution.py:584
  101.1 1.0 pair_sum.1
  (77 shorter events, 2.5 us)
Async XLA Ops:
  0.0 13.8 %copy-start = (bf16[576,1536]{1,0:T(8,128)(2,1)S(1)}, bf16[576,1536]{1,0:T(8,128)(2,1)}, u32[]{:S(2)}) copy-start(bf16[576,1536]{1,0:T(8,128)(2,1)} %constant.131.clone.refs_4_) | copy-start | bytes 5308420
  0.0 13.8 %copy-start.5 = (f32[2,16,768]{2,1,0:T(8,128)S(1)}, f32[2,16,768]{2,1,0:T(8,128)}, u32[]{:S(2)}) copy-start(f32[2,16,768]{2,1,0:T(8,128)} %constant.132.clone.refs_5_) | copy-start | bytes 294916
  0.0 10.5 %copy-start.17 = (s32[2048]{0:T(1024)S(1)}, s32[2048]{0:T(1024)}, u32[]{:S(2)}) copy-start(s32[2048]{0:T(1024)} %param.23) | copy-start | bytes 24580
  1.5 15.7 %copy-start.8 = (bf16[96,576]{1,0:T(8,128)(2,1)}, bf16[96,576]{1,0:T(8,128)(2,1)S(1)}, u32[]{:S(2)}) copy-start(bf16[96,576]{1,0:T(8,128)(2,1)S(1)} %reshape.317.refs_2_) | copy-start | bytes 331780
  1.5 11.5 %collective-permute-start.2 = (bf16[96,576]{1,0:T(8,128)(2,1)S(1)}, bf16[96,576]{1,0:T(8,128)(2,1)S(1)}, u32[]{:S(2)}, u32[]{:S(2)}) collective-permute-start(bf16[96,576]{1,0:T(8,128)(2,1)S(1)} %reshape.317.refs_2_), channel_id=1, source_target_pairs={{0,32},{32,64},{64,96},{96,128},{128,160},{160,192},{192,224},{224... | collective-permute-start | bytes 331784 | tf_op jit(solution)/shard_map/ppermute | solution.py:527
  3.5 13.7 %collective-permute-start.1 = (bf16[96,576]{1,0:T(8,128)(2,1)S(1)}, bf16[96,576]{1,0:T(8,128)(2,1)S(1)}, u32[]{:S(2)}, u32[]{:S(2)}) collective-permute-start(bf16[96,576]{1,0:T(8,128)(2,1)S(1)} %reshape.317.refs_2_), channel_id=1, source_target_pairs={{0,224},{32,0},{64,32},{96,64},{128,96},{160,128},{192,160},{224,1... | collective-permute-start | bytes 331784 | tf_op jit(solution)/shard_map/ppermute | solution.py:529
  8.8 33.7 %copy-start.3 = (bf16[96,576]{1,0:T(8,128)(2,1)}, bf16[96,576]{1,0:T(8,128)(2,1)S(1)}, u32[]{:S(2)}) copy-start(bf16[96,576]{1,0:T(8,128)(2,1)S(1)} %reshape.315.refs_0_) | copy-start | bytes 331780
  8.8 5.0 %collective-permute-start = (bf16[96,576]{1,0:T(8,128)(2,1)S(1)}, bf16[96,576]{1,0:T(8,128)(2,1)S(1)}, u32[]{:S(2)}, u32[]{:S(2)}) collective-permute-start(bf16[96,576]{1,0:T(8,128)(2,1)S(1)} %reshape.315.refs_0_), channel_id=1, source_target_pairs={{0,16},{16,0},{1,17},{17,1},{2,18},{18,2},{3,19},{19,3},{4,20},{20... | collective-permute-start | bytes 331784 | tf_op jit(solution)/shard_map/ppermute | solution.py:524
  10.5 6.7 %collective-permute-start.4 = (s32[2048]{0:T(1024)S(1)}, s32[2048]{0:T(1024)S(1)}, u32[]{:S(2)}, u32[]{:S(2)}) collective-permute-start(s32[2048]{0:T(1024)S(1)} %copy-done.17), channel_id=1, source_target_pairs={{0,15},{1,14},{2,13},{3,12},{4,11},{5,10},{6,9},{7,8},{8,7},{9,6},... | collective-permute-start | bytes 24584 | tf_op jit(solution)/shard_map/ppermute | solution.py:532
  12.9 7.2 %collective-permute-start.3 = (bf16[96,576]{1,0:T(8,128)(2,1)S(1)}, bf16[96,576]{1,0:T(8,128)(2,1)S(1)}, u32[]{:S(2)}, u32[]{:S(2)}) collective-permute-start(bf16[96,576]{1,0:T(8,128)(2,1)S(1)} %collective-permute-done.2.refs_3_), channel_id=1, source_target_pairs={{0,32},{32,64},{64,96},{96,128},{128,160},{160,192},{192,224},{224... | collective-permute-start | bytes 331784 | tf_op jit(solution)/shard_map/ppermute | solution.py:527
  14.7 27.7 %copy-start.4 = (bf16[96,576]{1,0:T(8,128)(2,1)}, bf16[96,576]{1,0:T(8,128)(2,1)S(1)}, u32[]{:S(2)}) copy-start(bf16[96,576]{1,0:T(8,128)(2,1)S(1)} %collective-permute-done.refs_1_) | copy-start | bytes 331780
  14.7 5.4 %copy-start.2 = (bf16[384,384]{1,0:T(8,128)(2,1)S(1)}, bf16[384,384]{1,0:T(8,128)(2,1)}, u32[]{:S(2)}) copy-start(bf16[384,384]{1,0:T(8,128)(2,1)} %constant.133.clone.refs_6_) | copy-start | bytes 884740
  17.2 5.5 %copy-start.10 = (bf16[96,576]{1,0:T(8,128)(2,1)}, bf16[96,576]{1,0:T(8,128)(2,1)S(1)}, u32[]{:S(2)}) copy-start(bf16[96,576]{1,0:T(8,128)(2,1)S(1)} %collective-permute-done.1.refs_2_.refs_9_) | copy-start | bytes 331780
  22.5 6.5 %copy-start.23 = (f32[4]{0:T(128)S(1)}, f32[4]{0:T(128)}, u32[]{:S(2)}) copy-start(f32[4]{0:T(128)} %param.22) | copy-start | bytes 52
  22.5 6.6 %copy-start.24 = (pred[8,1]{0,1:T(4,128)(4,1)S(1)}, pred[8,1]{0,1:T(4,128)(4,1)}, u32[]{:S(2)}) copy-start(pred[8,1]{0,1:T(4,128)(4,1)} %constant.134.clone) | copy-start | bytes 28
  22.6 6.6 %copy-start.18 = (f32[8,128]{1,0:T(8,128)S(1)}, f32[8,128]{1,0:T(8,128)}, u32[]{:S(2)}) copy-start(f32[8,128]{1,0:T(8,128)} %constant.135.clone) | copy-start | bytes 12292
  22.6 8.7 %copy-start.16 = (f32[4096]{0:T(1024)S(1)}, f32[4096]{0:T(1024)}, u32[]{:S(2)}) copy-start(f32[4096]{0:T(1024)} %param.20) | copy-start | bytes 49156
  22.6 8.7 %copy-start.21 = (s32[16]{0:T(128)S(1)}, s32[16]{0:T(128)}, u32[]{:S(2)}) copy-start(s32[16]{0:T(128)} %param.19) | copy-start | bytes 196
  22.6 14.3 %copy-start.19 = (pred[256,16]{0,1:T(8,128)(4,1)S(1)}, pred[256,16]{0,1:T(8,128)(4,1)}, u32[]{:S(2)}) copy-start(pred[256,16]{0,1:T(8,128)(4,1)} %constant.136.clone) | copy-start | bytes 12292
  22.6 14.3 %copy-start.20 = (pred[256,16]{0,1:T(8,128)(4,1)S(1)}, pred[256,16]{0,1:T(8,128)(4,1)}, u32[]{:S(2)}) copy-start(pred[256,16]{0,1:T(8,128)(4,1)} %constant.137.clone) | copy-start | bytes 12292
  22.6 14.3 %copy-start.22 = (f32[16]{0:T(128)S(1)}, f32[16]{0:T(128)}, u32[]{:S(2)}) copy-start(f32[16]{0:T(128)} %param.21) | copy-start | bytes 196
  22.7 23.5 %all-to-all-start = ((bf16[16,48,768]{2,1,0:T(8,128)(2,1)}), bf16[16,48,768]{2,1,0:T(8,128)(2,1)S(1)}, u32[]{:S(2)}, u32[]{:S(2)}) async-start(bf16[16,48,768]{2,1,0:T(8,128)(2,1)} %get-tuple-element.15), calls=%async_computation | async-start | bytes 2359296 | tf_op jit(solution)/shard_map/all_to_all | solution.py:538
  29.2 5.6 %collective-permute-start.6 = (bf16[96,576]{1,0:T(8,128)(2,1)}, bf16[96,576]{1,0:T(8,128)(2,1)S(1)}, u32[]{:S(2)}, u32[]{:S(2)}) collective-permute-start(bf16[96,576]{1,0:T(8,128)(2,1)} %copy-done.10), channel_id=1, source_target_pairs={{0,224},{32,0},{64,32},{96,64},{128,96},{160,128},{192,160},{224,1... | collective-permute-start | bytes 331784 | tf_op jit(solution)/shard_map/ppermute | solution.py:529
  29.5 6.8 %collective-permute-start.5 = (bf16[96,576]{1,0:T(8,128)(2,1)}, bf16[96,576]{1,0:T(8,128)(2,1)S(1)}, u32[]{:S(2)}, u32[]{:S(2)}) collective-permute-start(bf16[96,576]{1,0:T(8,128)(2,1)} %copy-done.11), channel_id=1, source_target_pairs={{0,32},{32,64},{64,96},{96,128},{128,160},{160,192},{192,224},{224... | collective-permute-start | bytes 331784 | tf_op jit(solution)/shard_map/ppermute | solution.py:527
  34.9 5.4 %collective-permute-start.7 = (bf16[96,576]{1,0:T(8,128)(2,1)S(1)}, bf16[96,576]{1,0:T(8,128)(2,1)S(1)}, u32[]{:S(2)}, u32[]{:S(2)}) collective-permute-start(bf16[96,576]{1,0:T(8,128)(2,1)S(1)} %collective-permute-done.6.refs_2_.refs_8_), channel_id=1, source_target_pairs={{0,224},{32,0},{64,32},{96,64},{128,96},{160,128},{192,160},{224,1... | collective-permute-start | bytes 331784 | tf_op jit(solution)/shard_map/ppermute | solution.py:529
  36.4 6.1 %collective-permute-start.8 = (bf16[96,576]{1,0:T(8,128)(2,1)S(1)}, bf16[96,576]{1,0:T(8,128)(2,1)S(1)}, u32[]{:S(2)}, u32[]{:S(2)}) collective-permute-start(bf16[96,576]{1,0:T(8,128)(2,1)S(1)} %collective-permute-done.5.refs_3_.refs_5_), channel_id=1, source_target_pairs={{0,32},{32,64},{64,96},{96,128},{128,160},{160,192},{192,224},{224... | collective-permute-start | bytes 331784 | tf_op jit(solution)/shard_map/ppermute | solution.py:527
  49.1 6.1 %copy-start.15 = (s32[16,128]{1,0:T(8,128)S(1)}, s32[16,128]{1,0:T(8,128)}, u32[]{:S(2)}) copy-start(s32[16,128]{1,0:T(8,128)} %get-tuple-element.16) | copy-start | bytes 24580
  49.1 6.3 %copy-start.7 = (bf16[384,384]{1,0:T(8,128)(2,1)S(1)}, bf16[384,384]{1,0:T(8,128)(2,1)}, u32[]{:S(2)}) copy-start(bf16[384,384]{1,0:T(8,128)(2,1)} %constant.138.clone.x_ref) | copy-start | bytes 884740
  49.2 23.2 %all-to-all-start.1 = ((bf16[16,48,768]{2,1,0:T(8,128)(2,1)}), bf16[16,48,768]{2,1,0:T(8,128)(2,1)S(1)}, u32[]{:S(2)}, u32[]{:S(2)}) async-start(bf16[16,48,768]{2,1,0:T(8,128)(2,1)} %block.1), calls=%async_computation.1 | async-start | bytes 2359296 | tf_op jit(solution)/shard_map/all_to_all | solution.py:554
  75.8 8.1 %collective-permute-start.9 = (bf16[16,2048]{1,0:T(8,128)(2,1)S(1)}, bf16[16,2048]{1,0:T(8,128)(2,1)S(1)}, u32[]{:S(2)}, u32[]{:S(2)}) collective-permute-start(bf16[16,2048]{1,0:T(8,128)(2,1)S(1)} %get-tuple-element.23), channel_id=1, source_target_pairs={{0,15},{1,14},{2,13},{3,12},{4,11},{5,10},{6,9},{7,8},{8,7},{9,6},... | collective-permute-start | bytes 196616 | tf_op jit(solution)/shard_map/ppermute | solution.py:581
  78.3 22.8 %copy-start.14 = (bf16[2,128,128]{2,1,0:T(8,128)(2,1)S(1)}, bf16[2,128,128]{2,1,0:T(8,128)(2,1)}, u32[]{:S(2)}) copy-start(bf16[2,128,128]{2,1,0:T(8,128)(2,1)} %constant.139.clone.column_ref) | copy-start | bytes 196612
  84.7 16.4 %all-to-all-start.2 = ((bf16[16,48,128]{2,1,0:T(8,128)(2,1)}), bf16[16,48,128]{2,1,0:T(8,128)(2,1)S(1)}, u32[]{:S(2)}, u32[]{:S(2)}) async-start(bf16[16,48,128]{2,1,0:T(8,128)(2,1)} %split.1), calls=%async_computation.2 | async-start | bytes 393216 | tf_op jit(solution)/shard_map/all_to_all | solution.py:584
  (6 other events, 17.8 us)

commit v12 on v11

--- a/solution.py
+++ b/solution.py
@@ -240,6 +240,28 @@
     )(*inputs)
 
 
+def marks_kernel(cell_ref, out_ref):
+    cell = cell_ref[...].astype(F32)
+    high = jnp.floor((cell + 0.5) * (1.0 / 256.0))
+    row = lax.broadcasted_iota(jnp.int32, (8, 128), 0)
+    out_ref[...] = jnp.where(row == 0, high, jnp.where(row == 1, cell - 256.0 * high, 0.0))
+
+
+def block_marks(cell):
+    return pl.pallas_call(
+        marks_kernel,
+        out_shape=jax.ShapeDtypeStruct((8, 128), F32),
+        compiler_params=pltpu.CompilerParams(vmem_limit_bytes=1 << 20),
+        cost_estimate=pl.CostEstimate(
+            flops=MARKS_FLOPS, bytes_accessed=10_000, transcendentals=0
+        ),
+        name="marks",
+    )(cell[None])
+
+
+MARKS_FLOPS = 150_000_000
+
+
 def pick(density_ref, flat_ref, kx_ref, store):
     rows = density_ref.shape[0]
 
@@ -531,9 +553,8 @@
     mirror_of = [(k, SLABS - 1 - k) for k in range(SLABS)]
     far_cell = lax.ppermute(gvec_cell, COL, mirror_of).reshape(16, 128)
     spots = jnp.arange(128, dtype=jnp.int32)
-    cell = jnp.where((spots % NBLOCK == col) & (spots >= 32), block_cell[0], 0)
-    marks = jnp.concatenate([jnp.stack([cell // 256, cell % 256]), jnp.zeros((6, 128), jnp.int32)])
-    (planes0,) = planes_of(0, v, c, marks=(marks.astype(F32),))
+    marks = block_marks(jnp.where((spots % NBLOCK == col) & (spots >= 32), block_cell[0], 0))
+    (planes0,) = planes_of(0, v, c, marks=(marks,))
     planes0, far_cell = planes_of(1, v, c, through=(far_cell,), buffer=(planes0,))
     sent0 = lax.all_to_all(planes0, COL, 0, 0, tiled=True)
     (planes1,) = planes_of(2, v, c)

time: 104 us -> 103 us (level)
  local copies, waits for them, and re-layouts: 4.92 us -> 3.75 us
  transfers between devices with their start and end apart: 13 -> 13, of which waited for: 8 -> 9; matrix products, arithmetic and copies ran while one was open for 2% -> 2% of each run, Pallas kernels for 16% -> 16%
where the time goes in v12:
time: 103 us; the launch traced here: 102 us
  waiting for transfers between devices  36.1 us (35%)
  starting transfers between devices  33.9 us (33%)
  Pallas kernels  26.5 us (26%)
  local copies, waits for them, and re-layouts  3.75 us (4%)
  between operations  1.08 us (1%)
    all_to_all x1, waiting for transfers between devices, per_device(): sent1 = lax.all_to_all(planes1, COL, 0, 0, tiled=True)  10.8 us
    all_to_all x1, waiting for transfers between devices, per_device(): pairs = lax.all_to_all(pairs, BAND, 0, 0, tiled=True)  10.8 us
    pallas_call x4, Pallas kernels, planes_of(): pl.pallas_call(functools.partial(plane_kernel, items=items, first=first,...  9.48 us
    all_to_all x1, starting transfers between devices, per_device(): sent0 = lax.all_to_all(planes0, COL, 0, 0, tiled=True)  6.46 us
    pallas_call x1, Pallas kernels, first_points(): pl.pallas_call(first_kernel, out_shape=(jax.ShapeDtypeStruct((FIRST, G_DE...  6.11 us
    all_to_all x1, starting transfers between devices, per_device(): sent1 = lax.all_to_all(planes1, COL, 0, 0, tiled=True)  6.04 us
    ppermute x3, starting transfers between devices, per_device(): c[8 - slot] = lax.ppermute(c[(9 - slot) % 8], 'z', behind)  5.77 us
    all_to_all x1, starting transfers between devices, per_device(): pairs = lax.all_to_all(pairs, BAND, 0, 0, tiled=True)  5.37 us
  transfers between devices with their start and end apart: 13, of which 9 were waited for; matrix products, arithmetic and copies ran while one was open for 2% of the time, Pallas kernels for 16%

profile of v12, /device:TPU:6, one launch (start us, length us, event | category | flops | bytes accessed | tf_op | source)
XLA Modules:
  0.0 102.0 jit_solution(10739489727104252189)
XLA Ops:
  0.0 1.1 %reshape.251 = bf16[6,6,16,96]{3,2,1,0:T(8,128)(2,1)S(1)} reshape(bf16[1,6,9216]{2,1,0:T(8,128)(2,1)} %param.18) | data formatting | bytes 221184 | tf_op jit(solution)/shard_map/reshape | solution.py:528
  1.4 2.0 %collective-permute-start.2 = (bf16[96,576]{1,0:T(8,128)(2,1)S(1)}, bf16[96,576]{1,0:T(8,128)(2,1)S(1)}, u32[]{:S(2)}, u32[]{:S(2)}) collective-permute-start(bf16[96,576]{1,0:T(8,128)(2,1)S(1)} %reshape.252.refs_2_), channel_id=1, source_target_pairs={{0,32},{32,64},{64,96},{96,128},{128,160},{160,192},{192,224},{224... | collective-permute-start | bytes 331784 | tf_op jit(solution)/shard_map/ppermute | solution.py:549
  3.4 4.0 %collective-permute-start.1 = (bf16[96,576]{1,0:T(8,128)(2,1)S(1)}, bf16[96,576]{1,0:T(8,128)(2,1)S(1)}, u32[]{:S(2)}, u32[]{:S(2)}) collective-permute-start(bf16[96,576]{1,0:T(8,128)(2,1)S(1)} %reshape.252.refs_2_), channel_id=1, source_target_pairs={{0,224},{32,0},{64,32},{96,64},{128,96},{160,128},{192,160},{224,1... | collective-permute-start | bytes 331784 | tf_op jit(solution)/shard_map/ppermute | solution.py:551
  7.4 1.1 %reshape.249 = bf16[6,6,16,96]{3,2,1,0:T(8,128)(2,1)S(1)} reshape(bf16[1,6,9216]{2,1,0:T(8,128)(2,1)} %param.17) | data formatting | bytes 221184 | tf_op jit(solution)/shard_map/reshape | solution.py:528
  8.7 1.7 %collective-permute-start = (bf16[96,576]{1,0:T(8,128)(2,1)S(1)}, bf16[96,576]{1,0:T(8,128)(2,1)S(1)}, u32[]{:S(2)}, u32[]{:S(2)}) collective-permute-start(bf16[96,576]{1,0:T(8,128)(2,1)S(1)} %reshape.250.refs_0_), channel_id=1, source_target_pairs={{0,16},{16,0},{1,17},{17,1},{2,18},{18,2},{3,19},{19,3},{4,20},{20... | collective-permute-start | bytes 331784 | tf_op jit(solution)/shard_map/ppermute | solution.py:546
  10.4 1.7 %collective-permute-start.4 = (s32[2048]{0:T(1024)S(1)}, s32[2048]{0:T(1024)S(1)}, u32[]{:S(2)}, u32[]{:S(2)}) collective-permute-start(s32[2048]{0:T(1024)S(1)} %copy-done.16), channel_id=1, source_target_pairs={{0,15},{1,14},{2,13},{3,12},{4,11},{5,10},{6,9},{7,8},{8,7},{9,6},... | collective-permute-start | bytes 24584 | tf_op jit(solution)/shard_map/ppermute | solution.py:554
  12.9 0.8 collective-permute-done.refs_1_
  13.7 2.4 %planes.4.refs_8_ = bf16[16,48,768]{2,1,0:T(8,128)(2,1)} custom-call(bf16[96,576]{1,0:T(8,128)(2,1)S(1)} %reshape.250.refs_0_, bf16[96,576]{1,0:T(8,128)(2,1)S(1)} %collective-permute-done.refs_1_, bf16[96,576]{1,0:T(8,128)(2,1)S(1)} %reshape.252.refs_2_, bf16[96,576]{1,0:T(8,128)(2,1)S(1)} %collective-permute-done.2.refs_3_, bf16[576,1536]{1,0:T(8,128)(2,1)S(1)} %copy-done, ...), custom_call_target="tpu_custom_call" | custom-call | flops 60000000 | bytes 100000 | tf_op jit(solution)/shard_map/planes/pallas_call | solution.py:210
  16.1 1.0 collective-permute-done.4
  17.1 2.9 %collective-permute-done.3.refs_3_.refs_4_ = bf16[96,576]{1,0:T(8,128)(2,1)S(1)} collective-permute-done((bf16[96,576]{1,0:T(8,128)(2,1)S(1)}, bf16[96,576]{1,0:T(8,128)(2,1)S(1)}, u32[]{:S(2)}, u32[]{:S(2)}) %collective-permute-start.3) | collective-permute-done | bytes 110624 | tf_op jit(solution)/shard_map/ppermute | solution.py:549
  20.0 2.4 %planes.5 = (bf16[16,48,768]{2,1,0:T(8,128)(2,1)}, s32[16,128]{1,0:T(8,128)}) custom-call(bf16[96,576]{1,0:T(8,128)(2,1)S(1)} %reshape.250.refs_0_, bf16[96,576]{1,0:T(8,128)(2,1)S(1)} %collective-permute-done.refs_1_, bf16[96,576]{1,0:T(8,128)(2,1)S(1)} %collective-permute-done.1.refs_2_.refs_9_, ...), custom_call_target="tpu_custom_call", output_to_operand_aliasing={{0}: (8, {})} | custom-call | flops 60000000 | bytes 100000 | tf_op jit(solution)/shard_map/planes/pallas_call | solution.py:210
  22.5 6.5 %all-to-all-start = ((bf16[16,48,768]{2,1,0:T(8,128)(2,1)}), bf16[16,48,768]{2,1,0:T(8,128)(2,1)S(1)}, u32[]{:S(2)}, u32[]{:S(2)}) async-start(bf16[16,48,768]{2,1,0:T(8,128)(2,1)} %get-tuple-element.15), calls=%async_computation | async-start | bytes 2359296 | tf_op jit(solution)/shard_map/all_to_all | solution.py:559
  29.4 1.8 %collective-permute-start.5 = (bf16[96,576]{1,0:T(8,128)(2,1)}, bf16[96,576]{1,0:T(8,128)(2,1)S(1)}, u32[]{:S(2)}, u32[]{:S(2)}) collective-permute-start(bf16[96,576]{1,0:T(8,128)(2,1)} %copy-done.10), channel_id=1, source_target_pairs={{0,32},{32,64},{64,96},{96,128},{128,160},{160,192},{192,224},{224... | collective-permute-start | bytes 331784 | tf_op jit(solution)/shard_map/ppermute | solution.py:549
  31.5 3.3 %collective-permute-done.6.refs_2_.refs_8_ = bf16[96,576]{1,0:T(8,128)(2,1)S(1)} collective-permute-done((bf16[96,576]{1,0:T(8,128)(2,1)}, bf16[96,576]{1,0:T(8,128)(2,1)S(1)}, u32[]{:S(2)}, u32[]{:S(2)}) %collective-permute-start.6) | collective-permute-done | bytes 110624 | tf_op jit(solution)/shard_map/ppermute | solution.py:551
  34.8 1.5 %collective-permute-start.7 = (bf16[96,576]{1,0:T(8,128)(2,1)S(1)}, bf16[96,576]{1,0:T(8,128)(2,1)S(1)}, u32[]{:S(2)}, u32[]{:S(2)}) collective-permute-start(bf16[96,576]{1,0:T(8,128)(2,1)S(1)} %collective-permute-done.6.refs_2_.refs_8_), channel_id=1, source_target_pairs={{0,224},{32,0},{64,32},{96,64},{128,96},{160,128},{192,160},{224,1... | collective-permute-start | bytes 331784 | tf_op jit(solution)/shard_map/ppermute | solution.py:551
  36.9 0.9 copy-done.5
  37.8 2.4 %planes.6.refs_7_ = bf16[16,48,768]{2,1,0:T(8,128)(2,1)} custom-call(bf16[96,576]{1,0:T(8,128)(2,1)S(1)} %reshape.250.refs_0_, bf16[96,576]{1,0:T(8,128)(2,1)S(1)} %collective-permute-done.refs_1_, bf16[96,576]{1,0:T(8,128)(2,1)S(1)} %collective-permute-done.6.refs_2_.refs_8_, bf16[96,576]{1,0:T(8,128)(2,1)S(1)} %collective-permute-done.5.refs_3_.refs_5_, ...), custom_call_target="tpu_custom_call" | custom-call | flops 60000000 | bytes 100000 | tf_op jit(solution)/shard_map/planes/pallas_call | solution.py:210
  40.2 2.2 %collective-permute-done.8.refs_3_ = bf16[96,576]{1,0:T(8,128)(2,1)S(1)} collective-permute-done((bf16[96,576]{1,0:T(8,128)(2,1)S(1)}, bf16[96,576]{1,0:T(8,128)(2,1)S(1)}, u32[]{:S(2)}, u32[]{:S(2)}) %collective-permute-start.8) | collective-permute-done | bytes 110624 | tf_op jit(solution)/shard_map/ppermute | solution.py:549
  42.4 2.4 %planes.7 = (bf16[16,48,768]{2,1,0:T(8,128)(2,1)}, bf16[96,576]{1,0:T(8,128)(2,1)}, bf16[96,576]{1,0:T(8,128)(2,1)}) custom-call(bf16[96,576]{1,0:T(8,128)(2,1)S(1)} %reshape.250.refs_0_, bf16[96,576]{1,0:T(8,128)(2,1)S(1)} %collective-permute-done.refs_1_, bf16[96,576]{1,0:T(8,128)(2,1)S(1)} %collective-permute-done.7.refs_2_, ...), custom_call_target="tpu_custom_call", output_to_operand_aliasing={{0}: (7, {})} | custom-call | flops 60000000 | bytes 100000 | tf_op jit(solution)/shard_map/planes/pallas_call | solution.py:210
  44.8 1.3 %all-to-all-done.t_ref.refs_11_ = bf16[16,48,768]{2,1,0:T(8,128)(2,1)S(1)} async-done(((bf16[16,48,768]{2,1,0:T(8,128)(2,1)}), bf16[16,48,768]{2,1,0:T(8,128)(2,1)S(1)}, u32[]{:S(2)}, u32[]{:S(2)}) %all-to-all-start) | async-done | bytes 1179680 | tf_op jit(solution)/shard_map/all_to_all | solution.py:559
  46.1 3.0 %block.1 = bf16[16,48,768]{2,1,0:T(8,128)(2,1)} custom-call(bf16[96,576]{1,0:T(8,128)(2,1)} %copy-done.2, bf16[96,576]{1,0:T(8,128)(2,1)} %copy-done.3, bf16[96,576]{1,0:T(8,128)(2,1)} %copy-done.7, bf16[96,576]{1,0:T(8,128)(2,1)} %copy-done.8, bf16[96,576]{1,0:T(8,128)(2,1)} %copy-done.10, ...), custom_call_target="tpu_custom_call", output_to_operand_aliasing={{}: (12, {})} | custom-call | flops 10000000 | bytes 100000 | tf_op jit(solution)/shard_map/block/pallas_call | solution.py:489
  49.1 6.0 %all-to-all-start.1 = ((bf16[16,48,768]{2,1,0:T(8,128)(2,1)}), bf16[16,48,768]{2,1,0:T(8,128)(2,1)S(1)}, u32[]{:S(2)}, u32[]{:S(2)}) async-start(bf16[16,48,768]{2,1,0:T(8,128)(2,1)} %block.1), calls=%async_computation.1 | async-start | bytes 2359296 | tf_op jit(solution)/shard_map/all_to_all | solution.py:575
  55.4 6.1 %first_points.1 = (f32[8,2048]{1,0:T(8,128)S(1)}, bf16[8,2048]{1,0:T(8,128)(2,1)S(1)}) custom-call(bf16[16,48,768]{2,1,0:T(8,128)(2,1)S(1)} %all-to-all-done.t_ref.refs_11_, bf16[384,384]{1,0:T(8,128)(2,1)S(1)} %copy-done.6, s32[1,2048]{1,0:T(1,128)S(1)} %bitcast.39, s32[1,2048]{1,0:T(1,128)S(1)} %bitcast.37, s32[1,2048]{1,0:T(1,128)S(1)} %get-tuple-element.35.far_ref, ...), custom_call_target="tpu_custom_call" | custom-call | flops 100000000 | bytes 100000 | tf_op jit(solution)/shard_map/first_points/pallas_call | solution.py:339
  61.5 10.8 %all-to-all-done.1.t_ref = bf16[16,48,768]{2,1,0:T(8,128)(2,1)S(1)} async-done(((bf16[16,48,768]{2,1,0:T(8,128)(2,1)}), bf16[16,48,768]{2,1,0:T(8,128)(2,1)S(1)}, u32[]{:S(2)}, u32[]{:S(2)}) %all-to-all-start.1) | async-done | bytes 1179680 | tf_op jit(solution)/shard_map/all_to_all | solution.py:575
  72.3 3.4 %second_far_points.1 = (bf16[16,2048]{1,0:T(8,128)(2,1)S(1)}, bf16[768,768]{1,0:T(8,128)(2,1)S(1)}, f32[16,128]{1,0:T(8,128)S(1)}) custom-call(bf16[16,48,768]{2,1,0:T(8,128)(2,1)S(1)} %all-to-all-done.1.t_ref, bf16[384,384]{1,0:T(8,128)(2,1)S(1)} %copy-done.6, s32[1,2048]{1,0:T(1,128)S(1)} %get-tuple-element.35.far_ref, ...), custom_call_target="tpu_custom_call" | custom-call | flops 100000000 | bytes 100000 | tf_op jit(solution)/shard_map/second_far_points/pallas_call | solution.py:355
  75.7 2.5 %collective-permute-start.9 = (bf16[16,2048]{1,0:T(8,128)(2,1)S(1)}, bf16[16,2048]{1,0:T(8,128)(2,1)S(1)}, u32[]{:S(2)}, u32[]{:S(2)}) collective-permute-start(bf16[16,2048]{1,0:T(8,128)(2,1)S(1)} %get-tuple-element.23), channel_id=1, source_target_pairs={{0,15},{1,14},{2,13},{3,12},{4,11},{5,10},{6,9},{7,8},{8,7},{9,6},... | collective-permute-start | bytes 196616 | tf_op jit(solution)/shard_map/ppermute | solution.py:602
  78.2 2.7 %second_own_points.1.own1_ref = f32[8,2048]{1,0:T(8,128)S(1)} custom-call(bf16[768,768]{1,0:T(8,128)(2,1)S(1)} %get-tuple-element.22.low, s32[1,2048]{1,0:T(1,128)S(1)} %bitcast.40, s32[1,2048]{1,0:T(1,128)S(1)} %bitcast.38), custom_call_target="tpu_custom_call" | custom-call | flops 2400000000 | bytes 1300000 | tf_op jit(solution)/shard_map/second_own_points/pallas_call | solution.py:371
  81.0 2.9 %collective-permute-done.9.far_ref = bf16[16,2048]{1,0:T(8,128)(2,1)S(1)} collective-permute-done((bf16[16,2048]{1,0:T(8,128)(2,1)S(1)}, bf16[16,2048]{1,0:T(8,128)(2,1)S(1)}, u32[]{:S(2)}, u32[]{:S(2)}) %collective-permute-start.9) | collective-permute-done | bytes 65568 | tf_op jit(solution)/shard_map/ppermute | solution.py:602
  83.9 0.8 split.1
  84.6 5.4 %all-to-all-start.2 = ((bf16[16,48,128]{2,1,0:T(8,128)(2,1)}), bf16[16,48,128]{2,1,0:T(8,128)(2,1)S(1)}, u32[]{:S(2)}, u32[]{:S(2)}) async-start(bf16[16,48,128]{2,1,0:T(8,128)(2,1)} %split.1), calls=%async_computation.2 | async-start | bytes 393216 | tf_op jit(solution)/shard_map/all_to_all | solution.py:605
  90.2 10.8 %all-to-all-done.2.pairs_ref = bf16[16,48,128]{2,1,0:T(8,128)(2,1)S(1)} async-done(((bf16[16,48,128]{2,1,0:T(8,128)(2,1)}), bf16[16,48,128]{2,1,0:T(8,128)(2,1)S(1)}, u32[]{:S(2)}, u32[]{:S(2)}) %all-to-all-start.2) | async-done | bytes 196640 | tf_op jit(solution)/shard_map/all_to_all | solution.py:605
  101.0 1.0 pair_sum.1
  (73 shorter events, 2.3 us)
Async XLA Ops:
  0.0 10.4 %copy-start.16 = (s32[2048]{0:T(1024)S(1)}, s32[2048]{0:T(1024)}, u32[]{:S(2)}) copy-start(s32[2048]{0:T(1024)} %param.23) | copy-start | bytes 24580
  1.1 12.6 %copy-start = (bf16[576,1536]{1,0:T(8,128)(2,1)S(1)}, bf16[576,1536]{1,0:T(8,128)(2,1)}, u32[]{:S(2)}) copy-start(bf16[576,1536]{1,0:T(8,128)(2,1)} %constant.108.clone.refs_4_) | copy-start | bytes 5308420
  1.1 12.6 %copy-start.1 = (bf16[384,384]{1,0:T(8,128)(2,1)S(1)}, bf16[384,384]{1,0:T(8,128)(2,1)}, u32[]{:S(2)}) copy-start(bf16[384,384]{1,0:T(8,128)(2,1)} %constant.110.clone.refs_6_) | copy-start | bytes 884740
  1.1 12.5 %copy-start.4 = (f32[2,16,768]{2,1,0:T(8,128)S(1)}, f32[2,16,768]{2,1,0:T(8,128)}, u32[]{:S(2)}) copy-start(f32[2,16,768]{2,1,0:T(8,128)} %constant.109.clone.refs_5_) | copy-start | bytes 294916
  1.4 14.7 %copy-start.7 = (bf16[96,576]{1,0:T(8,128)(2,1)}, bf16[96,576]{1,0:T(8,128)(2,1)S(1)}, u32[]{:S(2)}) copy-start(bf16[96,576]{1,0:T(8,128)(2,1)S(1)} %reshape.252.refs_2_) | copy-start | bytes 331780
  1.4 11.4 %collective-permute-start.2 = (bf16[96,576]{1,0:T(8,128)(2,1)S(1)}, bf16[96,576]{1,0:T(8,128)(2,1)S(1)}, u32[]{:S(2)}, u32[]{:S(2)}) collective-permute-start(bf16[96,576]{1,0:T(8,128)(2,1)S(1)} %reshape.252.refs_2_), channel_id=1, source_target_pairs={{0,32},{32,64},{64,96},{96,128},{128,160},{160,192},{192,224},{224... | collective-permute-start | bytes 331784 | tf_op jit(solution)/shard_map/ppermute | solution.py:549
  3.4 13.7 %collective-permute-start.1 = (bf16[96,576]{1,0:T(8,128)(2,1)S(1)}, bf16[96,576]{1,0:T(8,128)(2,1)S(1)}, u32[]{:S(2)}, u32[]{:S(2)}) collective-permute-start(bf16[96,576]{1,0:T(8,128)(2,1)S(1)} %reshape.252.refs_2_), channel_id=1, source_target_pairs={{0,224},{32,0},{64,32},{96,64},{128,96},{160,128},{192,160},{224,1... | collective-permute-start | bytes 331784 | tf_op jit(solution)/shard_map/ppermute | solution.py:551
  8.7 33.7 %copy-start.2 = (bf16[96,576]{1,0:T(8,128)(2,1)}, bf16[96,576]{1,0:T(8,128)(2,1)S(1)}, u32[]{:S(2)}) copy-start(bf16[96,576]{1,0:T(8,128)(2,1)S(1)} %reshape.250.refs_0_) | copy-start | bytes 331780
  8.7 5.0 %collective-permute-start = (bf16[96,576]{1,0:T(8,128)(2,1)S(1)}, bf16[96,576]{1,0:T(8,128)(2,1)S(1)}, u32[]{:S(2)}, u32[]{:S(2)}) collective-permute-start(bf16[96,576]{1,0:T(8,128)(2,1)S(1)} %reshape.250.refs_0_), channel_id=1, source_target_pairs={{0,16},{16,0},{1,17},{17,1},{2,18},{18,2},{3,19},{19,3},{4,20},{20... | collective-permute-start | bytes 331784 | tf_op jit(solution)/shard_map/ppermute | solution.py:546
  10.4 6.7 %collective-permute-start.4 = (s32[2048]{0:T(1024)S(1)}, s32[2048]{0:T(1024)S(1)}, u32[]{:S(2)}, u32[]{:S(2)}) collective-permute-start(s32[2048]{0:T(1024)S(1)} %copy-done.16), channel_id=1, source_target_pairs={{0,15},{1,14},{2,13},{3,12},{4,11},{5,10},{6,9},{7,8},{8,7},{9,6},... | collective-permute-start | bytes 24584 | tf_op jit(solution)/shard_map/ppermute | solution.py:554
  12.7 7.2 %collective-permute-start.3 = (bf16[96,576]{1,0:T(8,128)(2,1)S(1)}, bf16[96,576]{1,0:T(8,128)(2,1)S(1)}, u32[]{:S(2)}, u32[]{:S(2)}) collective-permute-start(bf16[96,576]{1,0:T(8,128)(2,1)S(1)} %collective-permute-done.2.refs_3_), channel_id=1, source_target_pairs={{0,32},{32,64},{64,96},{96,128},{128,160},{160,192},{192,224},{224... | collective-permute-start | bytes 331784 | tf_op jit(solution)/shard_map/ppermute | solution.py:549
  13.7 28.7 %copy-start.3 = (bf16[96,576]{1,0:T(8,128)(2,1)}, bf16[96,576]{1,0:T(8,128)(2,1)S(1)}, u32[]{:S(2)}) copy-start(bf16[96,576]{1,0:T(8,128)(2,1)S(1)} %collective-permute-done.refs_1_) | copy-start | bytes 331780
  22.4 6.6 %copy-start.22 = (f32[4]{0:T(128)S(1)}, f32[4]{0:T(128)}, u32[]{:S(2)}) copy-start(f32[4]{0:T(128)} %param.22) | copy-start | bytes 52
  22.4 6.7 %copy-start.23 = (pred[8,1]{0,1:T(4,128)(4,1)S(1)}, pred[8,1]{0,1:T(4,128)(4,1)}, u32[]{:S(2)}) copy-start(pred[8,1]{0,1:T(4,128)(4,1)} %constant.111.clone) | copy-start | bytes 28
  22.4 6.7 %copy-start.17 = (f32[8,128]{1,0:T(8,128)S(1)}, f32[8,128]{1,0:T(8,128)}, u32[]{:S(2)}) copy-start(f32[8,128]{1,0:T(8,128)} %constant.112.clone) | copy-start | bytes 12292
  22.4 8.8 %copy-start.15 = (f32[4096]{0:T(1024)S(1)}, f32[4096]{0:T(1024)}, u32[]{:S(2)}) copy-start(f32[4096]{0:T(1024)} %param.20) | copy-start | bytes 49156
  22.4 8.8 %copy-start.20 = (s32[16]{0:T(128)S(1)}, s32[16]{0:T(128)}, u32[]{:S(2)}) copy-start(s32[16]{0:T(128)} %param.19) | copy-start | bytes 196
  22.4 14.4 %copy-start.18 = (pred[256,16]{0,1:T(8,128)(4,1)S(1)}, pred[256,16]{0,1:T(8,128)(4,1)}, u32[]{:S(2)}) copy-start(pred[256,16]{0,1:T(8,128)(4,1)} %constant.113.clone) | copy-start | bytes 12292
  22.4 14.4 %copy-start.19 = (pred[256,16]{0,1:T(8,128)(4,1)S(1)}, pred[256,16]{0,1:T(8,128)(4,1)}, u32[]{:S(2)}) copy-start(pred[256,16]{0,1:T(8,128)(4,1)} %constant.114.clone) | copy-start | bytes 12292
  22.4 14.4 %copy-start.21 = (f32[16]{0:T(128)S(1)}, f32[16]{0:T(128)}, u32[]{:S(2)}) copy-start(f32[16]{0:T(128)} %param.21) | copy-start | bytes 196
  22.5 23.6 %all-to-all-start = ((bf16[16,48,768]{2,1,0:T(8,128)(2,1)}), bf16[16,48,768]{2,1,0:T(8,128)(2,1)S(1)}, u32[]{:S(2)}, u32[]{:S(2)}) async-start(bf16[16,48,768]{2,1,0:T(8,128)(2,1)} %get-tuple-element.15), calls=%async_computation | async-start | bytes 2359296 | tf_op jit(solution)/shard_map/all_to_all | solution.py:559
  29.2 5.6 %collective-permute-start.6 = (bf16[96,576]{1,0:T(8,128)(2,1)}, bf16[96,576]{1,0:T(8,128)(2,1)S(1)}, u32[]{:S(2)}, u32[]{:S(2)}) collective-permute-start(bf16[96,576]{1,0:T(8,128)(2,1)} %copy-done.9), channel_id=1, source_target_pairs={{0,224},{32,0},{64,32},{96,64},{128,96},{160,128},{192,160},{224,1... | collective-permute-start | bytes 331784 | tf_op jit(solution)/shard_map/ppermute | solution.py:551
  29.4 6.9 %collective-permute-start.5 = (bf16[96,576]{1,0:T(8,128)(2,1)}, bf16[96,576]{1,0:T(8,128)(2,1)S(1)}, u32[]{:S(2)}, u32[]{:S(2)}) collective-permute-start(bf16[96,576]{1,0:T(8,128)(2,1)} %copy-done.10), channel_id=1, source_target_pairs={{0,32},{32,64},{64,96},{96,128},{128,160},{160,192},{192,224},{224... | collective-permute-start | bytes 331784 | tf_op jit(solution)/shard_map/ppermute | solution.py:549
  34.8 5.4 %copy-start.11 = (bf16[96,576]{1,0:T(8,128)(2,1)}, bf16[96,576]{1,0:T(8,128)(2,1)S(1)}, u32[]{:S(2)}) copy-start(bf16[96,576]{1,0:T(8,128)(2,1)S(1)} %collective-permute-done.6.refs_2_.refs_8_) | copy-start | bytes 331780
  34.8 5.4 %collective-permute-start.7 = (bf16[96,576]{1,0:T(8,128)(2,1)S(1)}, bf16[96,576]{1,0:T(8,128)(2,1)S(1)}, u32[]{:S(2)}, u32[]{:S(2)}) collective-permute-start(bf16[96,576]{1,0:T(8,128)(2,1)S(1)} %collective-permute-done.6.refs_2_.refs_8_), channel_id=1, source_target_pairs={{0,224},{32,0},{64,32},{96,64},{128,96},{160,128},{192,160},{224,1... | collective-permute-start | bytes 331784 | tf_op jit(solution)/shard_map/ppermute | solution.py:551
  36.3 6.1 %collective-permute-start.8 = (bf16[96,576]{1,0:T(8,128)(2,1)S(1)}, bf16[96,576]{1,0:T(8,128)(2,1)S(1)}, u32[]{:S(2)}, u32[]{:S(2)}) collective-permute-start(bf16[96,576]{1,0:T(8,128)(2,1)S(1)} %collective-permute-done.5.refs_3_.refs_5_), channel_id=1, source_target_pairs={{0,32},{32,64},{64,96},{96,128},{128,160},{160,192},{192,224},{224... | collective-permute-start | bytes 331784 | tf_op jit(solution)/shard_map/ppermute | solution.py:549
  49.1 6.1 %copy-start.14 = (s32[16,128]{1,0:T(8,128)S(1)}, s32[16,128]{1,0:T(8,128)}, u32[]{:S(2)}) copy-start(s32[16,128]{1,0:T(8,128)} %get-tuple-element.16) | copy-start | bytes 24580
  49.1 6.3 %copy-start.6 = (bf16[384,384]{1,0:T(8,128)(2,1)S(1)}, bf16[384,384]{1,0:T(8,128)(2,1)}, u32[]{:S(2)}) copy-start(bf16[384,384]{1,0:T(8,128)(2,1)} %constant.115.clone.x_ref) | copy-start | bytes 884740
  49.1 23.2 %all-to-all-start.1 = ((bf16[16,48,768]{2,1,0:T(8,128)(2,1)}), bf16[16,48,768]{2,1,0:T(8,128)(2,1)S(1)}, u32[]{:S(2)}, u32[]{:S(2)}) async-start(bf16[16,48,768]{2,1,0:T(8,128)(2,1)} %block.1), calls=%async_computation.1 | async-start | bytes 2359296 | tf_op jit(solution)/shard_map/all_to_all | solution.py:575
  75.7 8.1 %collective-permute-start.9 = (bf16[16,2048]{1,0:T(8,128)(2,1)S(1)}, bf16[16,2048]{1,0:T(8,128)(2,1)S(1)}, u32[]{:S(2)}, u32[]{:S(2)}) collective-permute-start(bf16[16,2048]{1,0:T(8,128)(2,1)S(1)} %get-tuple-element.23), channel_id=1, source_target_pairs={{0,15},{1,14},{2,13},{3,12},{4,11},{5,10},{6,9},{7,8},{8,7},{9,6},... | collective-permute-start | bytes 196616 | tf_op jit(solution)/shard_map/ppermute | solution.py:602
  78.2 22.8 %copy-start.13 = (bf16[2,128,128]{2,1,0:T(8,128)(2,1)S(1)}, bf16[2,128,128]{2,1,0:T(8,128)(2,1)}, u32[]{:S(2)}) copy-start(bf16[2,128,128]{2,1,0:T(8,128)(2,1)} %constant.116.clone.column_ref) | copy-start | bytes 196612
  84.6 16.4 %all-to-all-start.2 = ((bf16[16,48,128]{2,1,0:T(8,128)(2,1)}), bf16[16,48,128]{2,1,0:T(8,128)(2,1)S(1)}, u32[]{:S(2)}, u32[]{:S(2)}) async-start(bf16[16,48,128]{2,1,0:T(8,128)(2,1)} %split.1), calls=%async_computation.2 | async-start | bytes 393216 | tf_op jit(solution)/shard_map/all_to_all | solution.py:605
  (5 other events, 15.8 us)

commit v13 on v12

--- a/solution.py
+++ b/solution.py
@@ -28,7 +28,7 @@
 SPARE = 640
 G_DEV = 2048
 NBLOCK = 16
-TILE = 512
+TILE = 1024
 ROWS = 48
 X_GROUPS = ((2, 2), (2, 2))
 

time: 103 us -> 104 us (level)
  no operation moved by 1% of the time
where the time goes in v13:
time: 104 us; the launch traced here: 102 us
  waiting for transfers between devices  36 us (35%)
  starting transfers between devices  33.9 us (33%)
  Pallas kernels  26.5 us (25%)
  local copies, waits for them, and re-layouts  3.75 us (4%)
  between operations  1.08 us (1%)
    all_to_all x1, waiting for transfers between devices, per_device(): sent1 = lax.all_to_all(planes1, COL, 0, 0, tiled=True)  10.8 us
    all_to_all x1, waiting for transfers between devices, per_device(): pairs = lax.all_to_all(pairs, BAND, 0, 0, tiled=True)  10.8 us
    pallas_call x4, Pallas kernels, planes_of(): pl.pallas_call(functools.partial(plane_kernel, items=items, first=first,...  9.48 us
    all_to_all x1, starting transfers between devices, per_device(): sent0 = lax.all_to_all(planes0, COL, 0, 0, tiled=True)  6.46 us
    pallas_call x1, Pallas kernels, first_points(): pl.pallas_call(first_kernel, out_shape=(jax.ShapeDtypeStruct((FIRST, G_DE...  6.11 us
    all_to_all x1, starting transfers between devices, per_device(): sent1 = lax.all_to_all(planes1, COL, 0, 0, tiled=True)  6.04 us
    ppermute x3, starting transfers between devices, per_device(): c[8 - slot] = lax.ppermute(c[(9 - slot) % 8], 'z', behind)  5.77 us
    all_to_all x1, starting transfers between devices, per_device(): pairs = lax.all_to_all(pairs, BAND, 0, 0, tiled=True)  5.37 us
  transfers between devices with their start and end apart: 13, of which 9 were waited for; matrix products, arithmetic and copies ran while one was open for 2% of the time, Pallas kernels for 16%

profile of v13, /device:TPU:6, one launch (start us, length us, event | category | flops | bytes accessed | tf_op | source)
XLA Modules:
  0.0 102.0 jit_solution(13061091167438973773)
XLA Ops:
  0.0 1.1 %reshape.251 = bf16[6,6,16,96]{3,2,1,0:T(8,128)(2,1)S(1)} reshape(bf16[1,6,9216]{2,1,0:T(8,128)(2,1)} %param.18) | data formatting | bytes 221184 | tf_op jit(solution)/shard_map/reshape | solution.py:528
  1.4 2.0 %collective-permute-start.2 = (bf16[96,576]{1,0:T(8,128)(2,1)S(1)}, bf16[96,576]{1,0:T(8,128)(2,1)S(1)}, u32[]{:S(2)}, u32[]{:S(2)}) collective-permute-start(bf16[96,576]{1,0:T(8,128)(2,1)S(1)} %reshape.252.refs_2_), channel_id=1, source_target_pairs={{0,32},{32,64},{64,96},{96,128},{128,160},{160,192},{192,224},{224... | collective-permute-start | bytes 331784 | tf_op jit(solution)/shard_map/ppermute | solution.py:549
  3.4 4.0 %collective-permute-start.1 = (bf16[96,576]{1,0:T(8,128)(2,1)S(1)}, bf16[96,576]{1,0:T(8,128)(2,1)S(1)}, u32[]{:S(2)}, u32[]{:S(2)}) collective-permute-start(bf16[96,576]{1,0:T(8,128)(2,1)S(1)} %reshape.252.refs_2_), channel_id=1, source_target_pairs={{0,224},{32,0},{64,32},{96,64},{128,96},{160,128},{192,160},{224,1... | collective-permute-start | bytes 331784 | tf_op jit(solution)/shard_map/ppermute | solution.py:551
  7.4 1.1 %reshape.249 = bf16[6,6,16,96]{3,2,1,0:T(8,128)(2,1)S(1)} reshape(bf16[1,6,9216]{2,1,0:T(8,128)(2,1)} %param.17) | data formatting | bytes 221184 | tf_op jit(solution)/shard_map/reshape | solution.py:528
  8.7 1.7 %collective-permute-start = (bf16[96,576]{1,0:T(8,128)(2,1)S(1)}, bf16[96,576]{1,0:T(8,128)(2,1)S(1)}, u32[]{:S(2)}, u32[]{:S(2)}) collective-permute-start(bf16[96,576]{1,0:T(8,128)(2,1)S(1)} %reshape.250.refs_0_), channel_id=1, source_target_pairs={{0,16},{16,0},{1,17},{17,1},{2,18},{18,2},{3,19},{19,3},{4,20},{20... | collective-permute-start | bytes 331784 | tf_op jit(solution)/shard_map/ppermute | solution.py:546
  10.4 1.7 %collective-permute-start.4 = (s32[2048]{0:T(1024)S(1)}, s32[2048]{0:T(1024)S(1)}, u32[]{:S(2)}, u32[]{:S(2)}) collective-permute-start(s32[2048]{0:T(1024)S(1)} %copy-done.16), channel_id=1, source_target_pairs={{0,15},{1,14},{2,13},{3,12},{4,11},{5,10},{6,9},{7,8},{8,7},{9,6},... | collective-permute-start | bytes 24584 | tf_op jit(solution)/shard_map/ppermute | solution.py:554
  12.9 0.8 collective-permute-done.refs_1_
  13.7 2.4 %planes.4.refs_8_ = bf16[16,48,768]{2,1,0:T(8,128)(2,1)} custom-call(bf16[96,576]{1,0:T(8,128)(2,1)S(1)} %reshape.250.refs_0_, bf16[96,576]{1,0:T(8,128)(2,1)S(1)} %collective-permute-done.refs_1_, bf16[96,576]{1,0:T(8,128)(2,1)S(1)} %reshape.252.refs_2_, bf16[96,576]{1,0:T(8,128)(2,1)S(1)} %collective-permute-done.2.refs_3_, bf16[576,1536]{1,0:T(8,128)(2,1)S(1)} %copy-done, ...), custom_call_target="tpu_custom_call" | custom-call | flops 60000000 | bytes 100000 | tf_op jit(solution)/shard_map/planes/pallas_call | solution.py:210
  16.1 1.0 collective-permute-done.4
  17.1 2.9 %collective-permute-done.3.refs_3_.refs_4_ = bf16[96,576]{1,0:T(8,128)(2,1)S(1)} collective-permute-done((bf16[96,576]{1,0:T(8,128)(2,1)S(1)}, bf16[96,576]{1,0:T(8,128)(2,1)S(1)}, u32[]{:S(2)}, u32[]{:S(2)}) %collective-permute-start.3) | collective-permute-done | bytes 110624 | tf_op jit(solution)/shard_map/ppermute | solution.py:549
  20.0 2.4 %planes.5 = (bf16[16,48,768]{2,1,0:T(8,128)(2,1)}, s32[16,128]{1,0:T(8,128)}) custom-call(bf16[96,576]{1,0:T(8,128)(2,1)S(1)} %reshape.250.refs_0_, bf16[96,576]{1,0:T(8,128)(2,1)S(1)} %collective-permute-done.refs_1_, bf16[96,576]{1,0:T(8,128)(2,1)S(1)} %collective-permute-done.1.refs_2_.refs_9_, ...), custom_call_target="tpu_custom_call", output_to_operand_aliasing={{0}: (8, {})} | custom-call | flops 60000000 | bytes 100000 | tf_op jit(solution)/shard_map/planes/pallas_call | solution.py:210
  22.5 6.5 %all-to-all-start = ((bf16[16,48,768]{2,1,0:T(8,128)(2,1)}), bf16[16,48,768]{2,1,0:T(8,128)(2,1)S(1)}, u32[]{:S(2)}, u32[]{:S(2)}) async-start(bf16[16,48,768]{2,1,0:T(8,128)(2,1)} %get-tuple-element.15), calls=%async_computation | async-start | bytes 2359296 | tf_op jit(solution)/shard_map/all_to_all | solution.py:559
  29.4 1.8 %collective-permute-start.5 = (bf16[96,576]{1,0:T(8,128)(2,1)}, bf16[96,576]{1,0:T(8,128)(2,1)S(1)}, u32[]{:S(2)}, u32[]{:S(2)}) collective-permute-start(bf16[96,576]{1,0:T(8,128)(2,1)} %copy-done.10), channel_id=1, source_target_pairs={{0,32},{32,64},{64,96},{96,128},{128,160},{160,192},{192,224},{224... | collective-permute-start | bytes 331784 | tf_op jit(solution)/shard_map/ppermute | solution.py:549
  31.5 3.3 %collective-permute-done.6.refs_2_.refs_8_ = bf16[96,576]{1,0:T(8,128)(2,1)S(1)} collective-permute-done((bf16[96,576]{1,0:T(8,128)(2,1)}, bf16[96,576]{1,0:T(8,128)(2,1)S(1)}, u32[]{:S(2)}, u32[]{:S(2)}) %collective-permute-start.6) | collective-permute-done | bytes 110624 | tf_op jit(solution)/shard_map/ppermute | solution.py:551
  34.8 1.5 %collective-permute-start.7 = (bf16[96,576]{1,0:T(8,128)(2,1)S(1)}, bf16[96,576]{1,0:T(8,128)(2,1)S(1)}, u32[]{:S(2)}, u32[]{:S(2)}) collective-permute-start(bf16[96,576]{1,0:T(8,128)(2,1)S(1)} %collective-permute-done.6.refs_2_.refs_8_), channel_id=1, source_target_pairs={{0,224},{32,0},{64,32},{96,64},{128,96},{160,128},{192,160},{224,1... | collective-permute-start | bytes 331784 | tf_op jit(solution)/shard_map/ppermute | solution.py:551
  36.9 0.9 copy-done.5
  37.8 2.4 %planes.6.refs_7_ = bf16[16,48,768]{2,1,0:T(8,128)(2,1)} custom-call(bf16[96,576]{1,0:T(8,128)(2,1)S(1)} %reshape.250.refs_0_, bf16[96,576]{1,0:T(8,128)(2,1)S(1)} %collective-permute-done.refs_1_, bf16[96,576]{1,0:T(8,128)(2,1)S(1)} %collective-permute-done.6.refs_2_.refs_8_, bf16[96,576]{1,0:T(8,128)(2,1)S(1)} %collective-permute-done.5.refs_3_.refs_5_, ...), custom_call_target="tpu_custom_call" | custom-call | flops 60000000 | bytes 100000 | tf_op jit(solution)/shard_map/planes/pallas_call | solution.py:210
  40.2 2.2 %collective-permute-done.8.refs_3_ = bf16[96,576]{1,0:T(8,128)(2,1)S(1)} collective-permute-done((bf16[96,576]{1,0:T(8,128)(2,1)S(1)}, bf16[96,576]{1,0:T(8,128)(2,1)S(1)}, u32[]{:S(2)}, u32[]{:S(2)}) %collective-permute-start.8) | collective-permute-done | bytes 110624 | tf_op jit(solution)/shard_map/ppermute | solution.py:549
  42.4 2.4 %planes.7 = (bf16[16,48,768]{2,1,0:T(8,128)(2,1)}, bf16[96,576]{1,0:T(8,128)(2,1)}, bf16[96,576]{1,0:T(8,128)(2,1)}) custom-call(bf16[96,576]{1,0:T(8,128)(2,1)S(1)} %reshape.250.refs_0_, bf16[96,576]{1,0:T(8,128)(2,1)S(1)} %collective-permute-done.refs_1_, bf16[96,576]{1,0:T(8,128)(2,1)S(1)} %collective-permute-done.7.refs_2_, ...), custom_call_target="tpu_custom_call", output_to_operand_aliasing={{0}: (7, {})} | custom-call | flops 60000000 | bytes 100000 | tf_op jit(solution)/shard_map/planes/pallas_call | solution.py:210
  44.8 1.3 %all-to-all-done.t_ref.refs_11_ = bf16[16,48,768]{2,1,0:T(8,128)(2,1)S(1)} async-done(((bf16[16,48,768]{2,1,0:T(8,128)(2,1)}), bf16[16,48,768]{2,1,0:T(8,128)(2,1)S(1)}, u32[]{:S(2)}, u32[]{:S(2)}) %all-to-all-start) | async-done | bytes 1179680 | tf_op jit(solution)/shard_map/all_to_all | solution.py:559
  46.1 3.0 %block.1 = bf16[16,48,768]{2,1,0:T(8,128)(2,1)} custom-call(bf16[96,576]{1,0:T(8,128)(2,1)} %copy-done.2, bf16[96,576]{1,0:T(8,128)(2,1)} %copy-done.3, bf16[96,576]{1,0:T(8,128)(2,1)} %copy-done.7, bf16[96,576]{1,0:T(8,128)(2,1)} %copy-done.8, bf16[96,576]{1,0:T(8,128)(2,1)} %copy-done.10, ...), custom_call_target="tpu_custom_call", output_to_operand_aliasing={{}: (12, {})} | custom-call | flops 10000000 | bytes 100000 | tf_op jit(solution)/shard_map/block/pallas_call | solution.py:489
  49.1 6.0 %all-to-all-start.1 = ((bf16[16,48,768]{2,1,0:T(8,128)(2,1)}), bf16[16,48,768]{2,1,0:T(8,128)(2,1)S(1)}, u32[]{:S(2)}, u32[]{:S(2)}) async-start(bf16[16,48,768]{2,1,0:T(8,128)(2,1)} %block.1), calls=%async_computation.1 | async-start | bytes 2359296 | tf_op jit(solution)/shard_map/all_to_all | solution.py:575
  55.4 6.1 %first_points.1 = (f32[8,2048]{1,0:T(8,128)S(1)}, bf16[8,2048]{1,0:T(8,128)(2,1)S(1)}) custom-call(bf16[16,48,768]{2,1,0:T(8,128)(2,1)S(1)} %all-to-all-done.t_ref.refs_11_, bf16[384,384]{1,0:T(8,128)(2,1)S(1)} %copy-done.6, s32[1,2048]{1,0:T(1,128)S(1)} %bitcast.39, s32[1,2048]{1,0:T(1,128)S(1)} %bitcast.37, s32[1,2048]{1,0:T(1,128)S(1)} %get-tuple-element.35.far_ref, ...), custom_call_target="tpu_custom_call" | custom-call | flops 100000000 | bytes 100000 | tf_op jit(solution)/shard_map/first_points/pallas_call | solution.py:339
  61.5 10.8 %all-to-all-done.1.t_ref = bf16[16,48,768]{2,1,0:T(8,128)(2,1)S(1)} async-done(((bf16[16,48,768]{2,1,0:T(8,128)(2,1)}), bf16[16,48,768]{2,1,0:T(8,128)(2,1)S(1)}, u32[]{:S(2)}, u32[]{:S(2)}) %all-to-all-start.1) | async-done | bytes 1179680 | tf_op jit(solution)/shard_map/all_to_all | solution.py:575
  72.3 3.4 %second_far_points.1 = (bf16[16,2048]{1,0:T(8,128)(2,1)S(1)}, bf16[768,768]{1,0:T(8,128)(2,1)S(1)}, f32[16,128]{1,0:T(8,128)S(1)}) custom-call(bf16[16,48,768]{2,1,0:T(8,128)(2,1)S(1)} %all-to-all-done.1.t_ref, bf16[384,384]{1,0:T(8,128)(2,1)S(1)} %copy-done.6, s32[1,2048]{1,0:T(1,128)S(1)} %get-tuple-element.35.far_ref, ...), custom_call_target="tpu_custom_call" | custom-call | flops 100000000 | bytes 100000 | tf_op jit(solution)/shard_map/second_far_points/pallas_call | solution.py:355
  75.8 2.5 %collective-permute-start.9 = (bf16[16,2048]{1,0:T(8,128)(2,1)S(1)}, bf16[16,2048]{1,0:T(8,128)(2,1)S(1)}, u32[]{:S(2)}, u32[]{:S(2)}) collective-permute-start(bf16[16,2048]{1,0:T(8,128)(2,1)S(1)} %get-tuple-element.23), channel_id=1, source_target_pairs={{0,15},{1,14},{2,13},{3,12},{4,11},{5,10},{6,9},{7,8},{8,7},{9,6},... | collective-permute-start | bytes 196616 | tf_op jit(solution)/shard_map/ppermute | solution.py:602
  78.2 2.8 %second_own_points.1.own1_ref = f32[8,2048]{1,0:T(8,128)S(1)} custom-call(bf16[768,768]{1,0:T(8,128)(2,1)S(1)} %get-tuple-element.22.low, s32[1,2048]{1,0:T(1,128)S(1)} %bitcast.40, s32[1,2048]{1,0:T(1,128)S(1)} %bitcast.38), custom_call_target="tpu_custom_call" | custom-call | flops 2400000000 | bytes 1300000 | tf_op jit(solution)/shard_map/second_own_points/pallas_call | solution.py:371
  81.0 2.9 %collective-permute-done.9.far_ref = bf16[16,2048]{1,0:T(8,128)(2,1)S(1)} collective-permute-done((bf16[16,2048]{1,0:T(8,128)(2,1)S(1)}, bf16[16,2048]{1,0:T(8,128)(2,1)S(1)}, u32[]{:S(2)}, u32[]{:S(2)}) %collective-permute-start.9) | collective-permute-done | bytes 65568 | tf_op jit(solution)/shard_map/ppermute | solution.py:602
  83.9 0.8 split.1
  84.7 5.4 %all-to-all-start.2 = ((bf16[16,48,128]{2,1,0:T(8,128)(2,1)}), bf16[16,48,128]{2,1,0:T(8,128)(2,1)S(1)}, u32[]{:S(2)}, u32[]{:S(2)}) async-start(bf16[16,48,128]{2,1,0:T(8,128)(2,1)} %split.1), calls=%async_computation.2 | async-start | bytes 393216 | tf_op jit(solution)/shard_map/all_to_all | solution.py:605
  90.2 10.8 %all-to-all-done.2.pairs_ref = bf16[16,48,128]{2,1,0:T(8,128)(2,1)S(1)} async-done(((bf16[16,48,128]{2,1,0:T(8,128)(2,1)}), bf16[16,48,128]{2,1,0:T(8,128)(2,1)S(1)}, u32[]{:S(2)}, u32[]{:S(2)}) %all-to-all-start.2) | async-done | bytes 196640 | tf_op jit(solution)/shard_map/all_to_all | solution.py:605
  101.0 1.0 pair_sum.1
  (73 shorter events, 2.3 us)
Async XLA Ops:
  0.0 10.4 %copy-start.16 = (s32[2048]{0:T(1024)S(1)}, s32[2048]{0:T(1024)}, u32[]{:S(2)}) copy-start(s32[2048]{0:T(1024)} %param.23) | copy-start | bytes 24580
  1.1 12.6 %copy-start = (bf16[576,1536]{1,0:T(8,128)(2,1)S(1)}, bf16[576,1536]{1,0:T(8,128)(2,1)}, u32[]{:S(2)}) copy-start(bf16[576,1536]{1,0:T(8,128)(2,1)} %constant.108.clone.refs_4_) | copy-start | bytes 5308420
  1.1 12.6 %copy-start.1 = (bf16[384,384]{1,0:T(8,128)(2,1)S(1)}, bf16[384,384]{1,0:T(8,128)(2,1)}, u32[]{:S(2)}) copy-start(bf16[384,384]{1,0:T(8,128)(2,1)} %constant.110.clone.refs_6_) | copy-start | bytes 884740
  1.1 12.5 %copy-start.4 = (f32[2,16,768]{2,1,0:T(8,128)S(1)}, f32[2,16,768]{2,1,0:T(8,128)}, u32[]{:S(2)}) copy-start(f32[2,16,768]{2,1,0:T(8,128)} %constant.109.clone.refs_5_) | copy-start | bytes 294916
  1.4 14.7 %copy-start.7 = (bf16[96,576]{1,0:T(8,128)(2,1)}, bf16[96,576]{1,0:T(8,128)(2,1)S(1)}, u32[]{:S(2)}) copy-start(bf16[96,576]{1,0:T(8,128)(2,1)S(1)} %reshape.252.refs_2_) | copy-start | bytes 331780
  1.4 11.4 %collective-permute-start.2 = (bf16[96,576]{1,0:T(8,128)(2,1)S(1)}, bf16[96,576]{1,0:T(8,128)(2,1)S(1)}, u32[]{:S(2)}, u32[]{:S(2)}) collective-permute-start(bf16[96,576]{1,0:T(8,128)(2,1)S(1)} %reshape.252.refs_2_), channel_id=1, source_target_pairs={{0,32},{32,64},{64,96},{96,128},{128,160},{160,192},{192,224},{224... | collective-permute-start | bytes 331784 | tf_op jit(solution)/shard_map/ppermute | solution.py:549
  3.4 13.7 %collective-permute-start.1 = (bf16[96,576]{1,0:T(8,128)(2,1)S(1)}, bf16[96,576]{1,0:T(8,128)(2,1)S(1)}, u32[]{:S(2)}, u32[]{:S(2)}) collective-permute-start(bf16[96,576]{1,0:T(8,128)(2,1)S(1)} %reshape.252.refs_2_), channel_id=1, source_target_pairs={{0,224},{32,0},{64,32},{96,64},{128,96},{160,128},{192,160},{224,1... | collective-permute-start | bytes 331784 | tf_op jit(solution)/shard_map/ppermute | solution.py:551
  8.7 33.7 %copy-start.2 = (bf16[96,576]{1,0:T(8,128)(2,1)}, bf16[96,576]{1,0:T(8,128)(2,1)S(1)}, u32[]{:S(2)}) copy-start(bf16[96,576]{1,0:T(8,128)(2,1)S(1)} %reshape.250.refs_0_) | copy-start | bytes 331780
  8.7 5.0 %collective-permute-start = (bf16[96,576]{1,0:T(8,128)(2,1)S(1)}, bf16[96,576]{1,0:T(8,128)(2,1)S(1)}, u32[]{:S(2)}, u32[]{:S(2)}) collective-permute-start(bf16[96,576]{1,0:T(8,128)(2,1)S(1)} %reshape.250.refs_0_), channel_id=1, source_target_pairs={{0,16},{16,0},{1,17},{17,1},{2,18},{18,2},{3,19},{19,3},{4,20},{20... | collective-permute-start | bytes 331784 | tf_op jit(solution)/shard_map/ppermute | solution.py:546
  10.4 6.7 %collective-permute-start.4 = (s32[2048]{0:T(1024)S(1)}, s32[2048]{0:T(1024)S(1)}, u32[]{:S(2)}, u32[]{:S(2)}) collective-permute-start(s32[2048]{0:T(1024)S(1)} %copy-done.16), channel_id=1, source_target_pairs={{0,15},{1,14},{2,13},{3,12},{4,11},{5,10},{6,9},{7,8},{8,7},{9,6},... | collective-permute-start | bytes 24584 | tf_op jit(solution)/shard_map/ppermute | solution.py:554
  12.7 7.2 %collective-permute-start.3 = (bf16[96,576]{1,0:T(8,128)(2,1)S(1)}, bf16[96,576]{1,0:T(8,128)(2,1)S(1)}, u32[]{:S(2)}, u32[]{:S(2)}) collective-permute-start(bf16[96,576]{1,0:T(8,128)(2,1)S(1)} %collective-permute-done.2.refs_3_), channel_id=1, source_target_pairs={{0,32},{32,64},{64,96},{96,128},{128,160},{160,192},{192,224},{224... | collective-permute-start | bytes 331784 | tf_op jit(solution)/shard_map/ppermute | solution.py:549
  13.7 28.7 %copy-start.3 = (bf16[96,576]{1,0:T(8,128)(2,1)}, bf16[96,576]{1,0:T(8,128)(2,1)S(1)}, u32[]{:S(2)}) copy-start(bf16[96,576]{1,0:T(8,128)(2,1)S(1)} %collective-permute-done.refs_1_) | copy-start | bytes 331780
  22.4 6.6 %copy-start.22 = (f32[4]{0:T(128)S(1)}, f32[4]{0:T(128)}, u32[]{:S(2)}) copy-start(f32[4]{0:T(128)} %param.22) | copy-start | bytes 52
  22.4 6.7 %copy-start.23 = (pred[8,1]{0,1:T(4,128)(4,1)S(1)}, pred[8,1]{0,1:T(4,128)(4,1)}, u32[]{:S(2)}) copy-start(pred[8,1]{0,1:T(4,128)(4,1)} %constant.111.clone) | copy-start | bytes 28
  22.4 6.7 %copy-start.17 = (f32[8,128]{1,0:T(8,128)S(1)}, f32[8,128]{1,0:T(8,128)}, u32[]{:S(2)}) copy-start(f32[8,128]{1,0:T(8,128)} %constant.112.clone) | copy-start | bytes 12292
  22.4 8.8 %copy-start.15 = (f32[4096]{0:T(1024)S(1)}, f32[4096]{0:T(1024)}, u32[]{:S(2)}) copy-start(f32[4096]{0:T(1024)} %param.20) | copy-start | bytes 49156
  22.4 8.8 %copy-start.20 = (s32[16]{0:T(128)S(1)}, s32[16]{0:T(128)}, u32[]{:S(2)}) copy-start(s32[16]{0:T(128)} %param.19) | copy-start | bytes 196
  22.4 14.4 %copy-start.18 = (pred[256,16]{0,1:T(8,128)(4,1)S(1)}, pred[256,16]{0,1:T(8,128)(4,1)}, u32[]{:S(2)}) copy-start(pred[256,16]{0,1:T(8,128)(4,1)} %constant.113.clone) | copy-start | bytes 12292
  22.4 14.4 %copy-start.19 = (pred[256,16]{0,1:T(8,128)(4,1)S(1)}, pred[256,16]{0,1:T(8,128)(4,1)}, u32[]{:S(2)}) copy-start(pred[256,16]{0,1:T(8,128)(4,1)} %constant.114.clone) | copy-start | bytes 12292
  22.4 14.4 %copy-start.21 = (f32[16]{0:T(128)S(1)}, f32[16]{0:T(128)}, u32[]{:S(2)}) copy-start(f32[16]{0:T(128)} %param.21) | copy-start | bytes 196
  22.5 23.6 %all-to-all-start = ((bf16[16,48,768]{2,1,0:T(8,128)(2,1)}), bf16[16,48,768]{2,1,0:T(8,128)(2,1)S(1)}, u32[]{:S(2)}, u32[]{:S(2)}) async-start(bf16[16,48,768]{2,1,0:T(8,128)(2,1)} %get-tuple-element.15), calls=%async_computation | async-start | bytes 2359296 | tf_op jit(solution)/shard_map/all_to_all | solution.py:559
  29.2 5.6 %collective-permute-start.6 = (bf16[96,576]{1,0:T(8,128)(2,1)}, bf16[96,576]{1,0:T(8,128)(2,1)S(1)}, u32[]{:S(2)}, u32[]{:S(2)}) collective-permute-start(bf16[96,576]{1,0:T(8,128)(2,1)} %copy-done.9), channel_id=1, source_target_pairs={{0,224},{32,0},{64,32},{96,64},{128,96},{160,128},{192,160},{224,1... | collective-permute-start | bytes 331784 | tf_op jit(solution)/shard_map/ppermute | solution.py:551
  29.4 6.9 %collective-permute-start.5 = (bf16[96,576]{1,0:T(8,128)(2,1)}, bf16[96,576]{1,0:T(8,128)(2,1)S(1)}, u32[]{:S(2)}, u32[]{:S(2)}) collective-permute-start(bf16[96,576]{1,0:T(8,128)(2,1)} %copy-done.10), channel_id=1, source_target_pairs={{0,32},{32,64},{64,96},{96,128},{128,160},{160,192},{192,224},{224... | collective-permute-start | bytes 331784 | tf_op jit(solution)/shard_map/ppermute | solution.py:549
  34.8 5.4 %copy-start.11 = (bf16[96,576]{1,0:T(8,128)(2,1)}, bf16[96,576]{1,0:T(8,128)(2,1)S(1)}, u32[]{:S(2)}) copy-start(bf16[96,576]{1,0:T(8,128)(2,1)S(1)} %collective-permute-done.6.refs_2_.refs_8_) | copy-start | bytes 331780
  34.8 5.4 %collective-permute-start.7 = (bf16[96,576]{1,0:T(8,128)(2,1)S(1)}, bf16[96,576]{1,0:T(8,128)(2,1)S(1)}, u32[]{:S(2)}, u32[]{:S(2)}) collective-permute-start(bf16[96,576]{1,0:T(8,128)(2,1)S(1)} %collective-permute-done.6.refs_2_.refs_8_), channel_id=1, source_target_pairs={{0,224},{32,0},{64,32},{96,64},{128,96},{160,128},{192,160},{224,1... | collective-permute-start | bytes 331784 | tf_op jit(solution)/shard_map/ppermute | solution.py:551
  36.3 6.1 %collective-permute-start.8 = (bf16[96,576]{1,0:T(8,128)(2,1)S(1)}, bf16[96,576]{1,0:T(8,128)(2,1)S(1)}, u32[]{:S(2)}, u32[]{:S(2)}) collective-permute-start(bf16[96,576]{1,0:T(8,128)(2,1)S(1)} %collective-permute-done.5.refs_3_.refs_5_), channel_id=1, source_target_pairs={{0,32},{32,64},{64,96},{96,128},{128,160},{160,192},{192,224},{224... | collective-permute-start | bytes 331784 | tf_op jit(solution)/shard_map/ppermute | solution.py:549
  49.1 6.1 %copy-start.14 = (s32[16,128]{1,0:T(8,128)S(1)}, s32[16,128]{1,0:T(8,128)}, u32[]{:S(2)}) copy-start(s32[16,128]{1,0:T(8,128)} %get-tuple-element.16) | copy-start | bytes 24580
  49.1 6.3 %copy-start.6 = (bf16[384,384]{1,0:T(8,128)(2,1)S(1)}, bf16[384,384]{1,0:T(8,128)(2,1)}, u32[]{:S(2)}) copy-start(bf16[384,384]{1,0:T(8,128)(2,1)} %constant.115.clone.x_ref) | copy-start | bytes 884740
  49.1 23.2 %all-to-all-start.1 = ((bf16[16,48,768]{2,1,0:T(8,128)(2,1)}), bf16[16,48,768]{2,1,0:T(8,128)(2,1)S(1)}, u32[]{:S(2)}, u32[]{:S(2)}) async-start(bf16[16,48,768]{2,1,0:T(8,128)(2,1)} %block.1), calls=%async_computation.1 | async-start | bytes 2359296 | tf_op jit(solution)/shard_map/all_to_all | solution.py:575
  75.8 8.1 %collective-permute-start.9 = (bf16[16,2048]{1,0:T(8,128)(2,1)S(1)}, bf16[16,2048]{1,0:T(8,128)(2,1)S(1)}, u32[]{:S(2)}, u32[]{:S(2)}) collective-permute-start(bf16[16,2048]{1,0:T(8,128)(2,1)S(1)} %get-tuple-element.23), channel_id=1, source_target_pairs={{0,15},{1,14},{2,13},{3,12},{4,11},{5,10},{6,9},{7,8},{8,7},{9,6},... | collective-permute-start | bytes 196616 | tf_op jit(solution)/shard_map/ppermute | solution.py:602
  78.2 22.8 %copy-start.13 = (bf16[2,128,128]{2,1,0:T(8,128)(2,1)S(1)}, bf16[2,128,128]{2,1,0:T(8,128)(2,1)}, u32[]{:S(2)}) copy-start(bf16[2,128,128]{2,1,0:T(8,128)(2,1)} %constant.116.clone.column_ref) | copy-start | bytes 196612
  84.7 16.3 %all-to-all-start.2 = ((bf16[16,48,128]{2,1,0:T(8,128)(2,1)}), bf16[16,48,128]{2,1,0:T(8,128)(2,1)S(1)}, u32[]{:S(2)}, u32[]{:S(2)}) async-start(bf16[16,48,128]{2,1,0:T(8,128)(2,1)} %split.1), calls=%async_computation.2 | async-start | bytes 393216 | tf_op jit(solution)/shard_map/all_to_all | solution.py:605
  (5 other events, 15.8 us)

commit v14 on v12

--- a/solution.py
+++ b/solution.py
@@ -120,7 +120,7 @@
 VMEM = pl.BlockSpec(memory_space=pltpu.VMEM)
 HBM = pl.BlockSpec(memory_space=pltpu.HBM)
 ANY = pl.BlockSpec(memory_space=pl.ANY)
-SLAB_CUTS = 4
+SLAB_CUTS = 2
 
 
 def in_hbm(x):

time: 103 us -> 103 us (level)
  no operation moved by 1% of the time
where the time goes in v14:
time: 103 us; the launch traced here: 102 us
  waiting for transfers between devices  36.1 us (35%)
  starting transfers between devices  33.9 us (33%)
  Pallas kernels  26.4 us (26%)
  local copies, waits for them, and re-layouts  3.75 us (4%)
  between operations  1.08 us (1%)
    all_to_all x1, waiting for transfers between devices, per_device(): sent1 = lax.all_to_all(planes1, COL, 0, 0, tiled=True)  10.8 us
    all_to_all x1, waiting for transfers between devices, per_device(): pairs = lax.all_to_all(pairs, BAND, 0, 0, tiled=True)  10.8 us
    pallas_call x4, Pallas kernels, planes_of(): pl.pallas_call(functools.partial(plane_kernel, items=items, first=first,...  9.38 us
    all_to_all x1, starting transfers between devices, per_device(): sent0 = lax.all_to_all(planes0, COL, 0, 0, tiled=True)  6.46 us
    pallas_call x1, Pallas kernels, first_points(): pl.pallas_call(first_kernel, out_shape=(jax.ShapeDtypeStruct((FIRST, G_DE...  6.11 us
    all_to_all x1, starting transfers between devices, per_device(): sent1 = lax.all_to_all(planes1, COL, 0, 0, tiled=True)  6.02 us
    ppermute x3, starting transfers between devices, per_device(): c[8 - slot] = lax.ppermute(c[(9 - slot) % 8], 'z', behind)  5.77 us
    all_to_all x1, starting transfers between devices, per_device(): pairs = lax.all_to_all(pairs, BAND, 0, 0, tiled=True)  5.37 us
  transfers between devices with their start and end apart: 13, of which 9 were waited for; matrix products, arithmetic and copies ran while one was open for 2% of the time, Pallas kernels for 16%

profile of v14, /device:TPU:6, one launch (start us, length us, event | category | flops | bytes accessed | tf_op | source)
XLA Modules:
  0.0 101.9 jit_solution(12313328445819252183)
XLA Ops:
  0.0 1.1 %reshape.251 = bf16[6,6,16,96]{3,2,1,0:T(8,128)(2,1)S(1)} reshape(bf16[1,6,9216]{2,1,0:T(8,128)(2,1)} %param.18) | data formatting | bytes 221184 | tf_op jit(solution)/shard_map/reshape | solution.py:528
  1.4 2.0 %collective-permute-start.2 = (bf16[96,576]{1,0:T(8,128)(2,1)S(1)}, bf16[96,576]{1,0:T(8,128)(2,1)S(1)}, u32[]{:S(2)}, u32[]{:S(2)}) collective-permute-start(bf16[96,576]{1,0:T(8,128)(2,1)S(1)} %reshape.252.refs_2_), channel_id=1, source_target_pairs={{0,32},{32,64},{64,96},{96,128},{128,160},{160,192},{192,224},{224... | collective-permute-start | bytes 331784 | tf_op jit(solution)/shard_map/ppermute | solution.py:549
  3.4 4.0 %collective-permute-start.1 = (bf16[96,576]{1,0:T(8,128)(2,1)S(1)}, bf16[96,576]{1,0:T(8,128)(2,1)S(1)}, u32[]{:S(2)}, u32[]{:S(2)}) collective-permute-start(bf16[96,576]{1,0:T(8,128)(2,1)S(1)} %reshape.252.refs_2_), channel_id=1, source_target_pairs={{0,224},{32,0},{64,32},{96,64},{128,96},{160,128},{192,160},{224,1... | collective-permute-start | bytes 331784 | tf_op jit(solution)/shard_map/ppermute | solution.py:551
  7.4 1.1 %reshape.249 = bf16[6,6,16,96]{3,2,1,0:T(8,128)(2,1)S(1)} reshape(bf16[1,6,9216]{2,1,0:T(8,128)(2,1)} %param.17) | data formatting | bytes 221184 | tf_op jit(solution)/shard_map/reshape | solution.py:528
  8.7 1.7 %collective-permute-start = (bf16[96,576]{1,0:T(8,128)(2,1)S(1)}, bf16[96,576]{1,0:T(8,128)(2,1)S(1)}, u32[]{:S(2)}, u32[]{:S(2)}) collective-permute-start(bf16[96,576]{1,0:T(8,128)(2,1)S(1)} %reshape.250.refs_0_), channel_id=1, source_target_pairs={{0,16},{16,0},{1,17},{17,1},{2,18},{18,2},{3,19},{19,3},{4,20},{20... | collective-permute-start | bytes 331784 | tf_op jit(solution)/shard_map/ppermute | solution.py:546
  10.4 1.7 %collective-permute-start.4 = (s32[2048]{0:T(1024)S(1)}, s32[2048]{0:T(1024)S(1)}, u32[]{:S(2)}, u32[]{:S(2)}) collective-permute-start(s32[2048]{0:T(1024)S(1)} %copy-done.16), channel_id=1, source_target_pairs={{0,15},{1,14},{2,13},{3,12},{4,11},{5,10},{6,9},{7,8},{8,7},{9,6},... | collective-permute-start | bytes 24584 | tf_op jit(solution)/shard_map/ppermute | solution.py:554
  12.9 0.8 collective-permute-done.refs_1_
  13.7 2.4 %planes.4.refs_8_ = bf16[16,48,768]{2,1,0:T(8,128)(2,1)} custom-call(bf16[96,576]{1,0:T(8,128)(2,1)S(1)} %reshape.250.refs_0_, bf16[96,576]{1,0:T(8,128)(2,1)S(1)} %collective-permute-done.refs_1_, bf16[96,576]{1,0:T(8,128)(2,1)S(1)} %reshape.252.refs_2_, bf16[96,576]{1,0:T(8,128)(2,1)S(1)} %collective-permute-done.2.refs_3_, bf16[576,1536]{1,0:T(8,128)(2,1)S(1)} %copy-done, ...), custom_call_target="tpu_custom_call" | custom-call | flops 60000000 | bytes 100000 | tf_op jit(solution)/shard_map/planes/pallas_call | solution.py:210
  16.1 1.0 collective-permute-done.4
  17.1 2.9 %collective-permute-done.3.refs_3_.refs_4_ = bf16[96,576]{1,0:T(8,128)(2,1)S(1)} collective-permute-done((bf16[96,576]{1,0:T(8,128)(2,1)S(1)}, bf16[96,576]{1,0:T(8,128)(2,1)S(1)}, u32[]{:S(2)}, u32[]{:S(2)}) %collective-permute-start.3) | collective-permute-done | bytes 110624 | tf_op jit(solution)/shard_map/ppermute | solution.py:549
  20.0 2.4 %planes.5 = (bf16[16,48,768]{2,1,0:T(8,128)(2,1)}, s32[16,128]{1,0:T(8,128)}) custom-call(bf16[96,576]{1,0:T(8,128)(2,1)S(1)} %reshape.250.refs_0_, bf16[96,576]{1,0:T(8,128)(2,1)S(1)} %collective-permute-done.refs_1_, bf16[96,576]{1,0:T(8,128)(2,1)S(1)} %collective-permute-done.1.refs_2_.refs_9_, ...), custom_call_target="tpu_custom_call", output_to_operand_aliasing={{0}: (8, {})} | custom-call | flops 60000000 | bytes 100000 | tf_op jit(solution)/shard_map/planes/pallas_call | solution.py:210
  22.4 6.5 %all-to-all-start = ((bf16[16,48,768]{2,1,0:T(8,128)(2,1)}), bf16[16,48,768]{2,1,0:T(8,128)(2,1)S(1)}, u32[]{:S(2)}, u32[]{:S(2)}) async-start(bf16[16,48,768]{2,1,0:T(8,128)(2,1)} %get-tuple-element.15), calls=%async_computation | async-start | bytes 2359296 | tf_op jit(solution)/shard_map/all_to_all | solution.py:559
  29.4 1.8 %collective-permute-start.5 = (bf16[96,576]{1,0:T(8,128)(2,1)}, bf16[96,576]{1,0:T(8,128)(2,1)S(1)}, u32[]{:S(2)}, u32[]{:S(2)}) collective-permute-start(bf16[96,576]{1,0:T(8,128)(2,1)} %copy-done.10), channel_id=1, source_target_pairs={{0,32},{32,64},{64,96},{96,128},{128,160},{160,192},{192,224},{224... | collective-permute-start | bytes 331784 | tf_op jit(solution)/shard_map/ppermute | solution.py:549
  31.4 3.3 %collective-permute-done.6.refs_2_.refs_8_ = bf16[96,576]{1,0:T(8,128)(2,1)S(1)} collective-permute-done((bf16[96,576]{1,0:T(8,128)(2,1)}, bf16[96,576]{1,0:T(8,128)(2,1)S(1)}, u32[]{:S(2)}, u32[]{:S(2)}) %collective-permute-start.6) | collective-permute-done | bytes 110624 | tf_op jit(solution)/shard_map/ppermute | solution.py:551
  34.8 1.5 %collective-permute-start.7 = (bf16[96,576]{1,0:T(8,128)(2,1)S(1)}, bf16[96,576]{1,0:T(8,128)(2,1)S(1)}, u32[]{:S(2)}, u32[]{:S(2)}) collective-permute-start(bf16[96,576]{1,0:T(8,128)(2,1)S(1)} %collective-permute-done.6.refs_2_.refs_8_), channel_id=1, source_target_pairs={{0,224},{32,0},{64,32},{96,64},{128,96},{160,128},{192,160},{224,1... | collective-permute-start | bytes 331784 | tf_op jit(solution)/shard_map/ppermute | solution.py:551
  36.9 0.9 copy-done.5
  37.8 2.3 %planes.6.refs_7_ = bf16[16,48,768]{2,1,0:T(8,128)(2,1)} custom-call(bf16[96,576]{1,0:T(8,128)(2,1)S(1)} %reshape.250.refs_0_, bf16[96,576]{1,0:T(8,128)(2,1)S(1)} %collective-permute-done.refs_1_, bf16[96,576]{1,0:T(8,128)(2,1)S(1)} %collective-permute-done.6.refs_2_.refs_8_, bf16[96,576]{1,0:T(8,128)(2,1)S(1)} %collective-permute-done.5.refs_3_.refs_5_, ...), custom_call_target="tpu_custom_call" | custom-call | flops 60000000 | bytes 100000 | tf_op jit(solution)/shard_map/planes/pallas_call | solution.py:210
  40.2 2.2 %collective-permute-done.8.refs_3_ = bf16[96,576]{1,0:T(8,128)(2,1)S(1)} collective-permute-done((bf16[96,576]{1,0:T(8,128)(2,1)S(1)}, bf16[96,576]{1,0:T(8,128)(2,1)S(1)}, u32[]{:S(2)}, u32[]{:S(2)}) %collective-permute-start.8) | collective-permute-done | bytes 110624 | tf_op jit(solution)/shard_map/ppermute | solution.py:549
  42.4 2.4 %planes.7 = (bf16[16,48,768]{2,1,0:T(8,128)(2,1)}, bf16[96,576]{1,0:T(8,128)(2,1)}, bf16[96,576]{1,0:T(8,128)(2,1)}) custom-call(bf16[96,576]{1,0:T(8,128)(2,1)S(1)} %reshape.250.refs_0_, bf16[96,576]{1,0:T(8,128)(2,1)S(1)} %collective-permute-done.refs_1_, bf16[96,576]{1,0:T(8,128)(2,1)S(1)} %collective-permute-done.7.refs_2_, ...), custom_call_target="tpu_custom_call", output_to_operand_aliasing={{0}: (7, {})} | custom-call | flops 60000000 | bytes 100000 | tf_op jit(solution)/shard_map/planes/pallas_call | solution.py:210
  44.7 1.3 %all-to-all-done.t_ref.refs_11_ = bf16[16,48,768]{2,1,0:T(8,128)(2,1)S(1)} async-done(((bf16[16,48,768]{2,1,0:T(8,128)(2,1)}), bf16[16,48,768]{2,1,0:T(8,128)(2,1)S(1)}, u32[]{:S(2)}, u32[]{:S(2)}) %all-to-all-start) | async-done | bytes 1179680 | tf_op jit(solution)/shard_map/all_to_all | solution.py:559
  46.1 3.0 %block.1 = bf16[16,48,768]{2,1,0:T(8,128)(2,1)} custom-call(bf16[96,576]{1,0:T(8,128)(2,1)} %copy-done.2, bf16[96,576]{1,0:T(8,128)(2,1)} %copy-done.3, bf16[96,576]{1,0:T(8,128)(2,1)} %copy-done.7, bf16[96,576]{1,0:T(8,128)(2,1)} %copy-done.8, bf16[96,576]{1,0:T(8,128)(2,1)} %copy-done.10, ...), custom_call_target="tpu_custom_call", output_to_operand_aliasing={{}: (12, {})} | custom-call | flops 10000000 | bytes 100000 | tf_op jit(solution)/shard_map/block/pallas_call | solution.py:489
  49.1 6.0 %all-to-all-start.1 = ((bf16[16,48,768]{2,1,0:T(8,128)(2,1)}), bf16[16,48,768]{2,1,0:T(8,128)(2,1)S(1)}, u32[]{:S(2)}, u32[]{:S(2)}) async-start(bf16[16,48,768]{2,1,0:T(8,128)(2,1)} %block.1), calls=%async_computation.1 | async-start | bytes 2359296 | tf_op jit(solution)/shard_map/all_to_all | solution.py:575
  55.3 6.1 %first_points.1 = (f32[8,2048]{1,0:T(8,128)S(1)}, bf16[8,2048]{1,0:T(8,128)(2,1)S(1)}) custom-call(bf16[16,48,768]{2,1,0:T(8,128)(2,1)S(1)} %all-to-all-done.t_ref.refs_11_, bf16[384,384]{1,0:T(8,128)(2,1)S(1)} %copy-done.6, s32[1,2048]{1,0:T(1,128)S(1)} %bitcast.39, s32[1,2048]{1,0:T(1,128)S(1)} %bitcast.37, s32[1,2048]{1,0:T(1,128)S(1)} %get-tuple-element.35.far_ref, ...), custom_call_target="tpu_custom_call" | custom-call | flops 100000000 | bytes 100000 | tf_op jit(solution)/shard_map/first_points/pallas_call | solution.py:339
  61.5 10.8 %all-to-all-done.1.t_ref = bf16[16,48,768]{2,1,0:T(8,128)(2,1)S(1)} async-done(((bf16[16,48,768]{2,1,0:T(8,128)(2,1)}), bf16[16,48,768]{2,1,0:T(8,128)(2,1)S(1)}, u32[]{:S(2)}, u32[]{:S(2)}) %all-to-all-start.1) | async-done | bytes 1179680 | tf_op jit(solution)/shard_map/all_to_all | solution.py:575
  72.3 3.4 %second_far_points.1 = (bf16[16,2048]{1,0:T(8,128)(2,1)S(1)}, bf16[768,768]{1,0:T(8,128)(2,1)S(1)}, f32[16,128]{1,0:T(8,128)S(1)}) custom-call(bf16[16,48,768]{2,1,0:T(8,128)(2,1)S(1)} %all-to-all-done.1.t_ref, bf16[384,384]{1,0:T(8,128)(2,1)S(1)} %copy-done.6, s32[1,2048]{1,0:T(1,128)S(1)} %get-tuple-element.35.far_ref, ...), custom_call_target="tpu_custom_call" | custom-call | flops 100000000 | bytes 100000 | tf_op jit(solution)/shard_map/second_far_points/pallas_call | solution.py:355
  75.7 2.5 %collective-permute-start.9 = (bf16[16,2048]{1,0:T(8,128)(2,1)S(1)}, bf16[16,2048]{1,0:T(8,128)(2,1)S(1)}, u32[]{:S(2)}, u32[]{:S(2)}) collective-permute-start(bf16[16,2048]{1,0:T(8,128)(2,1)S(1)} %get-tuple-element.23), channel_id=1, source_target_pairs={{0,15},{1,14},{2,13},{3,12},{4,11},{5,10},{6,9},{7,8},{8,7},{9,6},... | collective-permute-start | bytes 196616 | tf_op jit(solution)/shard_map/ppermute | solution.py:602
  78.2 2.7 %second_own_points.1.own1_ref = f32[8,2048]{1,0:T(8,128)S(1)} custom-call(bf16[768,768]{1,0:T(8,128)(2,1)S(1)} %get-tuple-element.22.low, s32[1,2048]{1,0:T(1,128)S(1)} %bitcast.40, s32[1,2048]{1,0:T(1,128)S(1)} %bitcast.38), custom_call_target="tpu_custom_call" | custom-call | flops 2400000000 | bytes 1300000 | tf_op jit(solution)/shard_map/second_own_points/pallas_call | solution.py:371
  80.9 2.9 %collective-permute-done.9.far_ref = bf16[16,2048]{1,0:T(8,128)(2,1)S(1)} collective-permute-done((bf16[16,2048]{1,0:T(8,128)(2,1)S(1)}, bf16[16,2048]{1,0:T(8,128)(2,1)S(1)}, u32[]{:S(2)}, u32[]{:S(2)}) %collective-permute-start.9) | collective-permute-done | bytes 65568 | tf_op jit(solution)/shard_map/ppermute | solution.py:602
  83.8 0.8 split.1
  84.6 5.4 %all-to-all-start.2 = ((bf16[16,48,128]{2,1,0:T(8,128)(2,1)}), bf16[16,48,128]{2,1,0:T(8,128)(2,1)S(1)}, u32[]{:S(2)}, u32[]{:S(2)}) async-start(bf16[16,48,128]{2,1,0:T(8,128)(2,1)} %split.1), calls=%async_computation.2 | async-start | bytes 393216 | tf_op jit(solution)/shard_map/all_to_all | solution.py:605
  90.1 10.8 %all-to-all-done.2.pairs_ref = bf16[16,48,128]{2,1,0:T(8,128)(2,1)S(1)} async-done(((bf16[16,48,128]{2,1,0:T(8,128)(2,1)}), bf16[16,48,128]{2,1,0:T(8,128)(2,1)S(1)}, u32[]{:S(2)}, u32[]{:S(2)}) %all-to-all-start.2) | async-done | bytes 196640 | tf_op jit(solution)/shard_map/all_to_all | solution.py:605
  101.0 1.0 pair_sum.1
  (73 shorter events, 2.3 us)
Async XLA Ops:
  0.0 10.4 %copy-start.16 = (s32[2048]{0:T(1024)S(1)}, s32[2048]{0:T(1024)}, u32[]{:S(2)}) copy-start(s32[2048]{0:T(1024)} %param.23) | copy-start | bytes 24580
  1.1 12.6 %copy-start = (bf16[576,1536]{1,0:T(8,128)(2,1)S(1)}, bf16[576,1536]{1,0:T(8,128)(2,1)}, u32[]{:S(2)}) copy-start(bf16[576,1536]{1,0:T(8,128)(2,1)} %constant.108.clone.refs_4_) | copy-start | bytes 5308420
  1.1 12.6 %copy-start.1 = (bf16[384,384]{1,0:T(8,128)(2,1)S(1)}, bf16[384,384]{1,0:T(8,128)(2,1)}, u32[]{:S(2)}) copy-start(bf16[384,384]{1,0:T(8,128)(2,1)} %constant.110.clone.refs_6_) | copy-start | bytes 884740
  1.1 12.5 %copy-start.4 = (f32[2,16,768]{2,1,0:T(8,128)S(1)}, f32[2,16,768]{2,1,0:T(8,128)}, u32[]{:S(2)}) copy-start(f32[2,16,768]{2,1,0:T(8,128)} %constant.109.clone.refs_5_) | copy-start | bytes 294916
  1.4 14.7 %copy-start.7 = (bf16[96,576]{1,0:T(8,128)(2,1)}, bf16[96,576]{1,0:T(8,128)(2,1)S(1)}, u32[]{:S(2)}) copy-start(bf16[96,576]{1,0:T(8,128)(2,1)S(1)} %reshape.252.refs_2_) | copy-start | bytes 331780
  1.4 11.4 %collective-permute-start.2 = (bf16[96,576]{1,0:T(8,128)(2,1)S(1)}, bf16[96,576]{1,0:T(8,128)(2,1)S(1)}, u32[]{:S(2)}, u32[]{:S(2)}) collective-permute-start(bf16[96,576]{1,0:T(8,128)(2,1)S(1)} %reshape.252.refs_2_), channel_id=1, source_target_pairs={{0,32},{32,64},{64,96},{96,128},{128,160},{160,192},{192,224},{224... | collective-permute-start | bytes 331784 | tf_op jit(solution)/shard_map/ppermute | solution.py:549
  3.4 13.7 %collective-permute-start.1 = (bf16[96,576]{1,0:T(8,128)(2,1)S(1)}, bf16[96,576]{1,0:T(8,128)(2,1)S(1)}, u32[]{:S(2)}, u32[]{:S(2)}) collective-permute-start(bf16[96,576]{1,0:T(8,128)(2,1)S(1)} %reshape.252.refs_2_), channel_id=1, source_target_pairs={{0,224},{32,0},{64,32},{96,64},{128,96},{160,128},{192,160},{224,1... | collective-permute-start | bytes 331784 | tf_op jit(solution)/shard_map/ppermute | solution.py:551
  8.7 33.7 %copy-start.2 = (bf16[96,576]{1,0:T(8,128)(2,1)}, bf16[96,576]{1,0:T(8,128)(2,1)S(1)}, u32[]{:S(2)}) copy-start(bf16[96,576]{1,0:T(8,128)(2,1)S(1)} %reshape.250.refs_0_) | copy-start | bytes 331780
  8.7 5.0 %collective-permute-start = (bf16[96,576]{1,0:T(8,128)(2,1)S(1)}, bf16[96,576]{1,0:T(8,128)(2,1)S(1)}, u32[]{:S(2)}, u32[]{:S(2)}) collective-permute-start(bf16[96,576]{1,0:T(8,128)(2,1)S(1)} %reshape.250.refs_0_), channel_id=1, source_target_pairs={{0,16},{16,0},{1,17},{17,1},{2,18},{18,2},{3,19},{19,3},{4,20},{20... | collective-permute-start | bytes 331784 | tf_op jit(solution)/shard_map/ppermute | solution.py:546
  10.4 6.7 %collective-permute-start.4 = (s32[2048]{0:T(1024)S(1)}, s32[2048]{0:T(1024)S(1)}, u32[]{:S(2)}, u32[]{:S(2)}) collective-permute-start(s32[2048]{0:T(1024)S(1)} %copy-done.16), channel_id=1, source_target_pairs={{0,15},{1,14},{2,13},{3,12},{4,11},{5,10},{6,9},{7,8},{8,7},{9,6},... | collective-permute-start | bytes 24584 | tf_op jit(solution)/shard_map/ppermute | solution.py:554
  12.7 7.2 %collective-permute-start.3 = (bf16[96,576]{1,0:T(8,128)(2,1)S(1)}, bf16[96,576]{1,0:T(8,128)(2,1)S(1)}, u32[]{:S(2)}, u32[]{:S(2)}) collective-permute-start(bf16[96,576]{1,0:T(8,128)(2,1)S(1)} %collective-permute-done.2.refs_3_), channel_id=1, source_target_pairs={{0,32},{32,64},{64,96},{96,128},{128,160},{160,192},{192,224},{224... | collective-permute-start | bytes 331784 | tf_op jit(solution)/shard_map/ppermute | solution.py:549
  13.7 28.7 %copy-start.3 = (bf16[96,576]{1,0:T(8,128)(2,1)}, bf16[96,576]{1,0:T(8,128)(2,1)S(1)}, u32[]{:S(2)}) copy-start(bf16[96,576]{1,0:T(8,128)(2,1)S(1)} %collective-permute-done.refs_1_) | copy-start | bytes 331780
  22.3 6.6 %copy-start.22 = (f32[4]{0:T(128)S(1)}, f32[4]{0:T(128)}, u32[]{:S(2)}) copy-start(f32[4]{0:T(128)} %param.22) | copy-start | bytes 52
  22.4 6.7 %copy-start.23 = (pred[8,1]{0,1:T(4,128)(4,1)S(1)}, pred[8,1]{0,1:T(4,128)(4,1)}, u32[]{:S(2)}) copy-start(pred[8,1]{0,1:T(4,128)(4,1)} %constant.111.clone) | copy-start | bytes 28
  22.4 6.7 %copy-start.17 = (f32[8,128]{1,0:T(8,128)S(1)}, f32[8,128]{1,0:T(8,128)}, u32[]{:S(2)}) copy-start(f32[8,128]{1,0:T(8,128)} %constant.112.clone) | copy-start | bytes 12292
  22.4 8.8 %copy-start.15 = (f32[4096]{0:T(1024)S(1)}, f32[4096]{0:T(1024)}, u32[]{:S(2)}) copy-start(f32[4096]{0:T(1024)} %param.20) | copy-start | bytes 49156
  22.4 8.8 %copy-start.20 = (s32[16]{0:T(128)S(1)}, s32[16]{0:T(128)}, u32[]{:S(2)}) copy-start(s32[16]{0:T(128)} %param.19) | copy-start | bytes 196
  22.4 14.4 %copy-start.18 = (pred[256,16]{0,1:T(8,128)(4,1)S(1)}, pred[256,16]{0,1:T(8,128)(4,1)}, u32[]{:S(2)}) copy-start(pred[256,16]{0,1:T(8,128)(4,1)} %constant.113.clone) | copy-start | bytes 12292
  22.4 14.4 %copy-start.19 = (pred[256,16]{0,1:T(8,128)(4,1)S(1)}, pred[256,16]{0,1:T(8,128)(4,1)}, u32[]{:S(2)}) copy-start(pred[256,16]{0,1:T(8,128)(4,1)} %constant.114.clone) | copy-start | bytes 12292
  22.4 14.4 %copy-start.21 = (f32[16]{0:T(128)S(1)}, f32[16]{0:T(128)}, u32[]{:S(2)}) copy-start(f32[16]{0:T(128)} %param.21) | copy-start | bytes 196
  22.4 23.6 %all-to-all-start = ((bf16[16,48,768]{2,1,0:T(8,128)(2,1)}), bf16[16,48,768]{2,1,0:T(8,128)(2,1)S(1)}, u32[]{:S(2)}, u32[]{:S(2)}) async-start(bf16[16,48,768]{2,1,0:T(8,128)(2,1)} %get-tuple-element.15), calls=%async_computation | async-start | bytes 2359296 | tf_op jit(solution)/shard_map/all_to_all | solution.py:559
  29.2 5.6 %collective-permute-start.6 = (bf16[96,576]{1,0:T(8,128)(2,1)}, bf16[96,576]{1,0:T(8,128)(2,1)S(1)}, u32[]{:S(2)}, u32[]{:S(2)}) collective-permute-start(bf16[96,576]{1,0:T(8,128)(2,1)} %copy-done.9), channel_id=1, source_target_pairs={{0,224},{32,0},{64,32},{96,64},{128,96},{160,128},{192,160},{224,1... | collective-permute-start | bytes 331784 | tf_op jit(solution)/shard_map/ppermute | solution.py:551
  29.4 6.9 %collective-permute-start.5 = (bf16[96,576]{1,0:T(8,128)(2,1)}, bf16[96,576]{1,0:T(8,128)(2,1)S(1)}, u32[]{:S(2)}, u32[]{:S(2)}) collective-permute-start(bf16[96,576]{1,0:T(8,128)(2,1)} %copy-done.10), channel_id=1, source_target_pairs={{0,32},{32,64},{64,96},{96,128},{128,160},{160,192},{192,224},{224... | collective-permute-start | bytes 331784 | tf_op jit(solution)/shard_map/ppermute | solution.py:549
  34.8 5.4 %copy-start.11 = (bf16[96,576]{1,0:T(8,128)(2,1)}, bf16[96,576]{1,0:T(8,128)(2,1)S(1)}, u32[]{:S(2)}) copy-start(bf16[96,576]{1,0:T(8,128)(2,1)S(1)} %collective-permute-done.6.refs_2_.refs_8_) | copy-start | bytes 331780
  34.8 5.4 %collective-permute-start.7 = (bf16[96,576]{1,0:T(8,128)(2,1)S(1)}, bf16[96,576]{1,0:T(8,128)(2,1)S(1)}, u32[]{:S(2)}, u32[]{:S(2)}) collective-permute-start(bf16[96,576]{1,0:T(8,128)(2,1)S(1)} %collective-permute-done.6.refs_2_.refs_8_), channel_id=1, source_target_pairs={{0,224},{32,0},{64,32},{96,64},{128,96},{160,128},{192,160},{224,1... | collective-permute-start | bytes 331784 | tf_op jit(solution)/shard_map/ppermute | solution.py:551
  36.3 6.1 %collective-permute-start.8 = (bf16[96,576]{1,0:T(8,128)(2,1)S(1)}, bf16[96,576]{1,0:T(8,128)(2,1)S(1)}, u32[]{:S(2)}, u32[]{:S(2)}) collective-permute-start(bf16[96,576]{1,0:T(8,128)(2,1)S(1)} %collective-permute-done.5.refs_3_.refs_5_), channel_id=1, source_target_pairs={{0,32},{32,64},{64,96},{96,128},{128,160},{160,192},{192,224},{224... | collective-permute-start | bytes 331784 | tf_op jit(solution)/shard_map/ppermute | solution.py:549
  49.1 6.1 %copy-start.14 = (s32[16,128]{1,0:T(8,128)S(1)}, s32[16,128]{1,0:T(8,128)}, u32[]{:S(2)}) copy-start(s32[16,128]{1,0:T(8,128)} %get-tuple-element.16) | copy-start | bytes 24580
  49.1 6.3 %copy-start.6 = (bf16[384,384]{1,0:T(8,128)(2,1)S(1)}, bf16[384,384]{1,0:T(8,128)(2,1)}, u32[]{:S(2)}) copy-start(bf16[384,384]{1,0:T(8,128)(2,1)} %constant.115.clone.x_ref) | copy-start | bytes 884740
  49.1 23.2 %all-to-all-start.1 = ((bf16[16,48,768]{2,1,0:T(8,128)(2,1)}), bf16[16,48,768]{2,1,0:T(8,128)(2,1)S(1)}, u32[]{:S(2)}, u32[]{:S(2)}) async-start(bf16[16,48,768]{2,1,0:T(8,128)(2,1)} %block.1), calls=%async_computation.1 | async-start | bytes 2359296 | tf_op jit(solution)/shard_map/all_to_all | solution.py:575
  75.7 8.1 %collective-permute-start.9 = (bf16[16,2048]{1,0:T(8,128)(2,1)S(1)}, bf16[16,2048]{1,0:T(8,128)(2,1)S(1)}, u32[]{:S(2)}, u32[]{:S(2)}) collective-permute-start(bf16[16,2048]{1,0:T(8,128)(2,1)S(1)} %get-tuple-element.23), channel_id=1, source_target_pairs={{0,15},{1,14},{2,13},{3,12},{4,11},{5,10},{6,9},{7,8},{8,7},{9,6},... | collective-permute-start | bytes 196616 | tf_op jit(solution)/shard_map/ppermute | solution.py:602
  78.2 22.8 %copy-start.13 = (bf16[2,128,128]{2,1,0:T(8,128)(2,1)S(1)}, bf16[2,128,128]{2,1,0:T(8,128)(2,1)}, u32[]{:S(2)}) copy-start(bf16[2,128,128]{2,1,0:T(8,128)(2,1)} %constant.116.clone.column_ref) | copy-start | bytes 196612
  84.6 16.3 %all-to-all-start.2 = ((bf16[16,48,128]{2,1,0:T(8,128)(2,1)}), bf16[16,48,128]{2,1,0:T(8,128)(2,1)S(1)}, u32[]{:S(2)}, u32[]{:S(2)}) async-start(bf16[16,48,128]{2,1,0:T(8,128)(2,1)} %split.1), calls=%async_computation.2 | async-start | bytes 393216 | tf_op jit(solution)/shard_map/all_to_all | solution.py:605
  (5 other events, 15.7 us)
